TPU v7x, 32 devices: a whole 2x2x4 slice. The times are simulated.
32 devices in a mesh: mem: 2 (over x), hid: 4 (over z), tok: 4 (over y, core).
Axes of the slice: x: 2, y: 2, z: 4, core: 2. Of those that a mesh axis runs over, the one named last changes fastest.
Arguments:
- inputs: bfloat16 [256, 12288], P(('mem', 'hid'), 'tok'), may hold values from -6 to 6
- cotangent: bfloat16 [256, 12288], P(('mem', 'hid'), 'tok'), may hold values from -1.1953125 to 1.1953125
- blocks: float32 [2, 4, 4, 144, 128, 128], P(None, None, 'hid', ('mem', 'tok')), may hold values from -0.15625 to 0.15625
- first_moment: float32 [2, 4, 4, 144, 128, 128], P(None, None, 'hid', ('mem', 'tok')), may hold values from -18 to 18
- second_moment: float32 [2, 4, 4, 144, 128, 128], P(None, None, 'hid', ('mem', 'tok')), may hold values from 4 to 100
- places: int32 [2, 4, 4, 144], P(None, 'tok', 'hid'), may hold values from 0 to 1151, as said below
- kept_counts: int32 [2, 4, 4], P(None, None, 'hid'), may hold values from 18 to 144, as said below
Outputs:
- layer_out: bfloat16 [256, 12288], P(('mem', 'hid'), 'tok')
- grad_in: bfloat16 [256, 12288], P(('mem', 'hid'), 'tok')
- new_blocks: float32 [2, 4, 4, 144, 128, 128], P(None, None, 'hid', ('mem', 'tok'))
- new_first: float32 [2, 4, 4, 144, 128, 128], P(None, None, 'hid', ('mem', 'tok'))
- new_second: float32 [2, 4, 4, 144, 128, 128], P(None, None, 'hid', ('mem', 'tok'))
Inputs may be any that keep to these rules, and one draw needn't show every extreme that they name: Within each matrix and cell the 144 places are distinct. `kept_counts`: in every draw some cell of each matrix has all 144 slots live.
All inputs are finite; a program needn't handle non-finite values.
Results may differ from a plain program's by a relative error of at most 0.0015.
The roundings to bfloat16 on the way count: a program that leaves them out, or rounds other values in their place, can miss the bound.
Values may be sent and summed in bfloat16 or wider, within the bound.
No kernel may reach another device: no remote copies, remote signals or barrier semaphores. Data moves between devices by JAX's collectives and lax.ppermute only.
A program may use at most 128 MiB of HBM per device.

v0:
```python
import jax
import jax.numpy as jnp
from jax import lax
from jax.sharding import PartitionSpec as P

FFW = 24576
STEP = 10


GELU_ROOT = 0.7978845608028654
GELU_CUBIC = 0.044715
BETA_FIRST = 0.9
BETA_SECOND = 0.95
LEARN_RATE = 0.001
WEIGHT_DECAY = 0.1
ADAM_EPSILON = 1e-08


def activate(values):
    tangent = jnp.tanh(GELU_ROOT * (values + GELU_CUBIC * values * values * values))
    return 0.5 * values * (1.0 + tangent)


def gelu_slope(values):
    tangent = jnp.tanh(GELU_ROOT * (values + GELU_CUBIC * values * values * values))
    return 0.5 * (1.0 + tangent) + 0.5 * values * (1.0 - tangent * tangent) * GELU_ROOT * (
        1.0 + 3.0 * GELU_CUBIC * values * values
    )


def select(matrix, slot_index, groups):
    return jnp.take(matrix.reshape(matrix.shape[0], groups, -1), slot_index, axis=1)


def spread(values, slot_index, groups, live_mask):
    masked = values * live_mask[None, :, None]
    placed = (
        jnp.zeros((values.shape[0], groups, values.shape[2]), jnp.float32)
        .at[:, slot_index]
        .add(masked)
    )
    return placed.reshape(values.shape[0], -1)


def adam_step(weight, moment, variance, gradient, live_mask):
    new_moment = BETA_FIRST * moment + (1.0 - BETA_FIRST) * gradient
    new_variance = BETA_SECOND * variance + (1.0 - BETA_SECOND) * gradient * gradient
    scaled = (
        new_moment
        / (1.0 - BETA_FIRST**STEP)
        / (jnp.sqrt(new_variance / (1.0 - BETA_SECOND**STEP)) + ADAM_EPSILON)
    )
    new_weight = weight - LEARN_RATE * (scaled + WEIGHT_DECAY * weight)
    return (
        jnp.where(live_mask, new_weight, weight),
        jnp.where(live_mask, new_moment, moment),
        jnp.where(live_mask, new_variance, variance),
    )


def on_device(inputs, cotangent, blocks, first_moment, second_moment, places, kept_counts):
    mem_count = lax.axis_size("mem")
    tok_count = lax.axis_size("tok")
    hid_count = lax.axis_size("hid")
    mem_index = lax.axis_index("mem")
    tok_index = lax.axis_index("tok")
    block_size = blocks.shape[-1]
    owned_slots = blocks.shape[3]
    slot_count = owned_slots * mem_count * tok_count
    token_rows, grad_rows = (
        lax.all_gather(inputs, "hid", axis=0, tiled=True),
        lax.all_gather(cotangent, "hid", axis=0, tiled=True),
    )
    width_blocks = token_rows.shape[1] // block_size
    hidden_blocks = FFW // (block_size * hid_count)
    narrow = blocks[:, :, 0].astype(jnp.bfloat16)
    copies = jnp.broadcast_to(
        narrow[:, None], (2, mem_count, tok_count, owned_slots, block_size, block_size)
    )
    copies = copies.reshape(2, mem_count * tok_count, owned_slots, block_size, block_size)
    gathered = lax.all_to_all(copies, ("mem", "tok"), split_axis=1, concat_axis=2, tiled=True)
    weights = gathered.reshape(2, slot_count, block_size, block_size)
    place_ids = places[:, 0, 0]
    cell_kept = lax.dynamic_index_in_dim(kept_counts[:, :, 0], tok_index, 1, keepdims=False)
    live_mask = (jnp.arange(slot_count, dtype=jnp.int32)[None, :] < cell_kept[:, None]).astype(
        jnp.float32
    )
    width_index = place_ids % width_blocks
    hidden_index = place_ids // width_blocks
    first_rows = select(token_rows, width_index[0], width_blocks)
    pre_part = spread(
        jnp.einsum("tsi,sij->tsj", first_rows, weights[0], preferred_element_type=jnp.float32),
        hidden_index[0],
        hidden_blocks,
        live_mask[0],
    )
    preact = lax.psum_scatter(pre_part, "tok", scatter_dimension=1, tiled=True)
    hidden = lax.all_gather(activate(preact).astype(jnp.bfloat16), "tok", axis=1, tiled=True)
    hidden_cols = select(hidden, hidden_index[1], hidden_blocks)
    out_part = spread(
        jnp.einsum("tsi,sij->tsj", hidden_cols, weights[1], preferred_element_type=jnp.float32),
        width_index[1],
        width_blocks,
        live_mask[1],
    )
    layer_out = lax.psum_scatter(out_part, "hid", scatter_dimension=0, tiled=True).astype(
        jnp.bfloat16
    )
    grad_cols = select(grad_rows, width_index[1], width_blocks)
    back_part = spread(
        jnp.einsum("tsj,sij->tsi", grad_cols, weights[1], preferred_element_type=jnp.float32),
        hidden_index[1],
        hidden_blocks,
        live_mask[1],
    )
    hidden_grad = lax.psum_scatter(back_part, "tok", scatter_dimension=1, tiled=True)
    pre_grad = lax.all_gather(
        (hidden_grad * gelu_slope(preact)).astype(jnp.bfloat16), "tok", axis=1, tiled=True
    )
    pre_cols = select(pre_grad, hidden_index[0], hidden_blocks)
    in_part = spread(
        jnp.einsum("tsj,sij->tsi", pre_cols, weights[0], preferred_element_type=jnp.float32),
        width_index[0],
        width_blocks,
        live_mask[0],
    )
    grad_in = lax.psum_scatter(in_part, "hid", scatter_dimension=0, tiled=True).astype(jnp.bfloat16)
    first_grad = jnp.einsum(
        "tsi,tsj->sij", first_rows, pre_cols, preferred_element_type=jnp.float32
    )
    second_grad = jnp.einsum(
        "tsi,tsj->sij", hidden_cols, grad_cols, preferred_element_type=jnp.float32
    )
    grad_terms = jnp.stack([first_grad, second_grad]).astype(jnp.bfloat16)
    sendable = grad_terms.reshape(2, mem_count * tok_count, owned_slots, block_size, block_size)
    pieces = lax.all_to_all(sendable, ("mem", "tok"), split_axis=1, concat_axis=1, tiled=True)
    summed = (
        pieces.astype(jnp.float32)
        .reshape(2, mem_count, tok_count, owned_slots, block_size, block_size)
        .sum(axis=1)
    )
    slot_ids = (mem_index * tok_count + tok_index) * owned_slots + jnp.arange(
        owned_slots, dtype=jnp.int32
    )
    owner_live = slot_ids[None, None, :] < kept_counts[:, :, 0][:, :, None]
    new_blocks, new_first, new_second = adam_step(
        blocks,
        first_moment,
        second_moment,
        summed[:, :, None],
        owner_live[:, :, None, :, None, None],
    )
    return (layer_out, grad_in, new_blocks, new_first, new_second)


def solution(mesh):
    return jax.shard_map(
        on_device,
        mesh=mesh,
        in_specs=(
            P(("mem", "hid"), "tok"),
            P(("mem", "hid"), "tok"),
            P(None, None, "hid", ("mem", "tok"), None, None),
            P(None, None, "hid", ("mem", "tok"), None, None),
            P(None, None, "hid", ("mem", "tok"), None, None),
            P(None, "tok", "hid", None),
            P(None, None, "hid"),
        ),
        out_specs=(
            P(("mem", "hid"), "tok"),
            P(("mem", "hid"), "tok"),
            P(None, None, "hid", ("mem", "tok"), None, None),
            P(None, None, "hid", ("mem", "tok"), None, None),
            P(None, None, "hid", ("mem", "tok"), None, None),
        ),
        check_vma=False,
    )
```

profile of v0, /device:TPU:0, one launch (start us, length us, event | category | flops | bytes accessed | tf_op | source)
XLA Modules:
  0.0 526.5 jit_solution(5989168978866651771)
XLA Ops:
  7.2 4.8 convert_bitcast_fusion
  15.1 9.6 %broadcast_in_dim.47 = bf16[2,2,4,18,128,128]{5,4,3,0,2,1:T(8,128)(2,1)} broadcast(bf16[2,4,18,128,128]{4,3,2,0,1:T(8,128)(2,1)} %copy.70), dimensions={0,2,3,4,5} | broadcast | bytes 14155776 | tf_op jit(solution)/shard_map/broadcast_in_dim | solution.py:77
  24.8 5.3 %all-to-all-start = ((bf16[2,8,18,128,128]{4,3,2,0,1:T(8,128)(2,1)}), bf16[2,8,18,128,128]{4,3,2,0,1:T(8,128)(2,1)}, u32[]{:S(2)}, u32[]{:S(2)}) async-start(bf16[2,8,18,128,128]{4,3,2,0,1:T(8,128)(2,1)} %bitcast.112), calls=%async_computation | async-start | bytes 18874368 | tf_op jit(solution)/shard_map/all_to_all | solution.py:81
  30.2 21.4 %all_gather.14 = bf16[128,3072]{1,0:T(8,128)(2,1)S(1)} all-gather(bf16[32,3072]{1,0:T(8,128)(2,1)S(1)} %copy-done.3), channel_id=1, replica_groups=mesh['mem'=2,'hid'=4,'tok'=4] {'hid'}, dimensions={0}, use_global_device_ids=true | all-gather | bytes 983040 | tf_op jit(solution)/shard_map/all_gather | solution.py:72
  52.4 7.6 %gather_fusion.2 = bf16[144,128,128]{2,1,0:T(8,128)(2,1)} fusion(bf16[128,24,128]{2,0,1:T(8,128)(2,1)S(1)} %copy.75, s32[1024]{0:T(1024)S(1)} %pad_clamp_fusion.1), kind=kCustom, calls=%fused_computation.2.clone | custom fusion | bytes 9437760 | tf_op jit(solution)/shard_map/jit(_take)/gather | solution.py:32
  60.3 74.7 %all-to-all-done = bf16[2,8,18,128,128]{4,3,2,0,1:T(8,128)(2,1)} async-done(((bf16[2,8,18,128,128]{4,3,2,0,1:T(8,128)(2,1)}), bf16[2,8,18,128,128]{4,3,2,0,1:T(8,128)(2,1)}, u32[]{:S(2)}, u32[]{:S(2)}) %all-to-all-start) | async-done | bytes 9437216 | tf_op jit(solution)/shard_map/all_to_all | solution.py:81
  135.0 9.3 %fusion.48 = (bf16[1,8,18,128,128]{4,3,2,0,1:T(8,128)(2,1)}, bf16[1,8,18,128,128]{4,3,2,0,1:T(8,128)(2,1)S(1)}) fusion(bf16[2,8,18,128,128]{4,3,2,0,1:T(8,128)(2,1)} %all-to-all-done), kind=kLoop, calls=%fused_computation.83 | loop fusion | bytes 18874368 | tf_op jit(solution)/shard_map/slice | solution.py:92
  144.3 5.9 %broadcast_multiply_fusion = f32[144,128,128]{2,1,0:T(8,128)} fusion(f32[144]{0:T(256)S(1)} %bitcast.127, bf16[144,128,128]{2,1,0:T(8,128)(2,1)S(1)} %bitcast.110, bf16[144,128,128]{2,1,0:T(8,128)(2,1)S(1)} %copy-done.1, pred[144]{0:T(512)(128)(4,1)S(1)} %compare_and_fusion.1), kind=kOutput, calls=%fused_computation.31 | convolution fusion | flops 608698368 | bytes 18875088 | tf_op jit(solution)/shard_map/tsj,sij->tsi/dot_general | solution.py:111
  150.5 19.1 %scatter_fusion.2 = f32[128,48,128]{2,0,1:T(8,128)S(1)} fusion(f32[128,48,128]{2,0,1:T(8,128)S(1)} %broadcast.138.clone, s32[144]{0:T(256)S(1)} %bitcast.132, f32[144,128,128]{2,1,0:T(8,128)} %broadcast_multiply_fusion), kind=kCustom, calls=%fused_computation.6 | custom fusion | flops 2359296 | bytes 28312128 | tf_op jit(solution)/shard_map/scatter-add | solution.py:40
  172.1 20.9 %all_gather.12 = bf16[128,3072]{1,0:T(8,128)(2,1)S(1)} all-gather(bf16[32,3072]{1,0:T(8,128)(2,1)S(1)} %copy-done.4), channel_id=1, replica_groups=mesh['mem'=2,'hid'=4,'tok'=4] {'hid'}, dimensions={0}, use_global_device_ids=true | all-gather | bytes 983040 | tf_op jit(solution)/shard_map/all_gather | solution.py:71
  193.8 7.5 %gather_fusion = bf16[144,128,128]{2,1,0:T(8,128)(2,1)} fusion(bf16[128,24,128]{2,0,1:T(8,128)(2,1)S(1)} %copy.69, s32[1024]{0:T(1024)S(1)} %pad_clamp_fusion.3), kind=kCustom, calls=%fused_computation.clone | custom fusion | bytes 9437760 | tf_op jit(solution)/shard_map/jit(_take)/gather | solution.py:32
  201.3 9.1 %broadcast_multiply_fusion.3 = f32[144,128,128]{2,1,0:T(8,128)} fusion(f32[144]{0:T(256)S(1)} %bitcast.125, bf16[144,128,128]{2,1,0:T(8,128)(2,1)} %bitcast.108, bf16[144,128,128]{2,1,0:T(8,128)(2,1)} %gather_fusion, pred[144]{0:T(512)(128)(4,1)S(1)} %compare_and_fusion.3), kind=kOutput, calls=%fused_computation.34 | convolution fusion | flops 608698368 | bytes 18875088 | tf_op jit(solution)/shard_map/tsi,sij->tsj/dot_general | solution.py:92
  210.8 19.1 %scatter_fusion = f32[128,48,128]{2,0,1:T(8,128)S(1)} fusion(f32[128,48,128]{2,0,1:T(8,128)S(1)} %broadcast.138.clone.1, s32[144]{0:T(256)S(1)} %bitcast.131, f32[144,128,128]{2,1,0:T(8,128)} %broadcast_multiply_fusion.3), kind=kCustom, calls=%fused_computation.4 | custom fusion | flops 2359296 | bytes 28312128 | tf_op jit(solution)/shard_map/scatter-add | solution.py:40
  232.4 36.3 %reduce-scatter.9.cloned.1.call-done = f32[128,1536]{0,1:T(8,128)} async-done(((f32[128,6144]{0,1:T(8,128)}), f32[128,1536]{0,1:T(8,128)}) %reduce-scatter.9.cloned.1.call-update) | async-done | bytes 786448 | tf_op jit(solution)/shard_map/reduce_scatter | solution.py:97
  272.2 19.1 %all-gather.3.cloned.1.call-done = bf16[128,6144]{0,1:T(8,128)(2,1)} async-done(((bf16[128,1536]{0,1:T(8,128)(2,1)}), bf16[128,6144]{0,1:T(8,128)(2,1)}) %all-gather.3.cloned.1.call-update) | async-done | bytes 1572880 | tf_op jit(solution)/shard_map/all_gather | solution.py:98
  293.3 19.7 %all-gather.5.cloned.1.call-done = bf16[128,6144]{0,1:T(8,128)(2,1)} async-done(((bf16[128,1536]{0,1:T(8,128)(2,1)}), bf16[128,6144]{0,1:T(8,128)(2,1)}) %all-gather.5.cloned.1.call-update) | async-done | bytes 1572880 | tf_op jit(solution)/shard_map/all_gather | solution.py:117
  315.0 7.6 %gather_fusion.1 = bf16[144,128,128]{2,1,0:T(8,128)(2,1)} fusion(bf16[128,48,128]{2,0,1:T(8,128)(2,1)S(1)} %copy.72, s32[1024]{0:T(1024)S(1)} %pad_clamp_fusion.2), kind=kCustom, calls=%fused_computation.1.clone | custom fusion | bytes 9437760 | tf_op jit(solution)/shard_map/jit(_take)/gather | solution.py:32
  322.5 7.5 %gather_fusion.3 = bf16[144,128,128]{2,1,0:T(8,128)(2,1)} fusion(bf16[128,48,128]{2,0,1:T(8,128)(2,1)S(1)} %copy.77, s32[1024]{0:T(1024)S(1)} %pad_clamp_fusion), kind=kCustom, calls=%fused_computation.3.clone | custom fusion | bytes 9437760 | tf_op jit(solution)/shard_map/jit(_take)/gather | solution.py:32
  330.1 8.1 %fusion.24 = bf16[144,128,128]{2,1,0:T(8,128)(2,1)} fusion(bf16[144,128,128]{2,1,0:T(8,128)(2,1)} %gather_fusion.1, pred[144]{0:T(512)(128)(4,1)S(1)} %compare_and_fusion.2, bf16[144,128,128]{2,1,0:T(8,128)(2,1)} %gather_fusion.2, pred[144]{0:T(512)(128)(4,1)S(1)} %compare_and_fusion.1), kind=kOutput, calls=%fused_computation.40 | convolution fusion | flops 611057664 | bytes 14156064 | tf_op jit(solution)/shard_map/tsi,tsj->sij/dot_general | solution.py:131
  342.3 8.4 %pad_maximum_fusion = bf16[2,8,18,128,128]{4,3,2,0,1:T(8,128)(2,1)} fusion(bf16[1,8,18,128,128]{4,3,2,0,1:T(8,128)(2,1)} %bitcast.119, bf16[1,8,18,128,128]{4,3,2,0,1:T(8,128)(2,1)} %bitcast.120), kind=kLoop, calls=%fused_computation.12 | loop fusion | flops 4718592 | bytes 18874368 | tf_op jit(solution)/shard_map/stack | solution.py:134
  350.7 5.0 all-to-all-start.1
  355.9 9.0 %broadcast_multiply_fusion.1 = f32[144,128,128]{2,1,0:T(8,128)} fusion(f32[144]{0:T(256)S(1)} %bitcast.128, bf16[144,128,128]{2,1,0:T(8,128)(2,1)} %bitcast.111, bf16[144,128,128]{2,1,0:T(8,128)(2,1)} %gather_fusion.1, pred[144]{0:T(512)(128)(4,1)S(1)} %compare_and_fusion.2), kind=kOutput, calls=%fused_computation.32 | convolution fusion | flops 608698368 | bytes 18875088 | tf_op jit(solution)/shard_map/tsi,sij->tsj/dot_general | solution.py:101
  365.1 19.1 %scatter_fusion.1 = f32[128,24,128]{2,0,1:T(8,128)S(1)} fusion(f32[128,24,128]{2,0,1:T(8,128)S(1)} %broadcast.135.clone, s32[144]{0:T(256)S(1)} %bitcast.130, f32[144,128,128]{2,1,0:T(8,128)} %broadcast_multiply_fusion.1), kind=kCustom, calls=%fused_computation.5 | custom fusion | flops 2359296 | bytes 28312128 | tf_op jit(solution)/shard_map/scatter-add | solution.py:40
  386.4 11.0 %broadcast_multiply_fusion.2 = f32[144,128,128]{2,1,0:T(8,128)} fusion(f32[144]{0:T(256)S(1)} %bitcast.126, bf16[144,128,128]{2,1,0:T(8,128)(2,1)} %bitcast.109, bf16[144,128,128]{2,1,0:T(8,128)(2,1)} %gather_fusion.3, pred[144]{0:T(512)(128)(4,1)S(1)} %compare_and_fusion), kind=kOutput, calls=%fused_computation.33 | convolution fusion | flops 608698368 | bytes 18875088 | tf_op jit(solution)/shard_map/tsj,sij->tsi/dot_general | solution.py:122
  397.6 19.2 %scatter_fusion.3 = f32[128,24,128]{2,0,1:T(8,128)S(1)} fusion(f32[128,24,128]{2,0,1:T(8,128)S(1)} %broadcast.135.clone.1, s32[144]{0:T(256)S(1)} %bitcast.129, f32[144,128,128]{2,1,0:T(8,128)} %broadcast_multiply_fusion.2), kind=kCustom, calls=%fused_computation.7 | custom fusion | flops 2359296 | bytes 28312128 | tf_op jit(solution)/shard_map/scatter-add | solution.py:40
  419.1 4.2 reduce-scatter.13.cloned.1.call-done
  425.6 34.7 %reduce-scatter.15.cloned.1.call-done = f32[32,3072]{1,0:T(8,128)} async-done(((f32[128,3072]{1,0:T(8,128)}), f32[32,3072]{1,0:T(8,128)}) %reduce-scatter.15.cloned.1.call-update) | async-done | bytes 393232
  462.6 11.1 %convert_reduce_fusion = f32[2,4,18,128,128]{4,3,2,0,1:T(8,128)} fusion(bf16[2,2,4,18,128,128]{5,4,3,0,2,1:T(8,128)(2,1)} %bitcast.43), kind=kLoop, calls=%fused_computation.8 | loop fusion | flops 7077888 | bytes 18874368 | tf_op jit(solution)/shard_map/reduce_sum | solution.py:140
  473.8 22.9 %copy_select_fusion = (f32[2,4,1,18,128,128]{5,4,3,0,1,2:T(8,128)S(1)}, f32[2,4,1,18,128,128]{5,4,3,0,1,2:T(8,128)}, f32[2,4,1,18,128,128]{5,4,3,0,1,2:T(8,128)}) fusion(f32[2,4,1,18,128,128]{5,4,3,2,1,0:T(8,128)} %param.15, f32[2,4,18,128,128]{4,3,2,0,1:T(8,128)} %convert_reduce_fusion, pred[2,4,18]{2,0,1:T(4,128)(4,1)S(1)} %broadcast_compare_fusion, ...), kind=kLoop, calls=%fused_computation.15 | loop fusion | flops 42467328 | bytes 66060432 | tf_op jit(solution)/shard_map/jit(_where)/select_n | solution.py:57
  496.7 8.8 %copy.93 = f32[2,4,1,18,128,128]{5,4,3,2,1,0:T(8,128)} copy(f32[2,4,1,18,128,128]{5,4,3,0,1,2:T(8,128)} %get-tuple-element.28) | data formatting | bytes 18874368
  505.5 8.8 %copy.94 = f32[2,4,1,18,128,128]{5,4,3,2,1,0:T(8,128)} copy(f32[2,4,1,18,128,128]{5,4,3,0,1,2:T(8,128)} %get-tuple-element.29) | data formatting | bytes 18874368
  514.3 5.1 copy.95
  (78 shorter events, 31.5 us)
Async XLA Ops:
  24.8 5.4 %copy-start.3 = (bf16[32,3072]{1,0:T(8,128)(2,1)S(1)}, bf16[32,3072]{1,0:T(8,128)(2,1)}, u32[]{:S(2)}) copy-start(bf16[32,3072]{1,0:T(8,128)(2,1)} %param.12) | copy-start | bytes 589828
  24.8 27.5 %copy-start.5 = (s32[2,1,1,144]{3,2,1,0:T(1,128)S(1)}, s32[2,1,1,144]{3,2,1,0:T(1,128)}, u32[]{:S(2)}) copy-start(s32[2,1,1,144]{3,2,1,0:T(1,128)} %param.16) | copy-start | bytes 3460
  24.8 110.2 %all-to-all-start = ((bf16[2,8,18,128,128]{4,3,2,0,1:T(8,128)(2,1)}), bf16[2,8,18,128,128]{4,3,2,0,1:T(8,128)(2,1)}, u32[]{:S(2)}, u32[]{:S(2)}) async-start(bf16[2,8,18,128,128]{4,3,2,0,1:T(8,128)(2,1)} %bitcast.112), calls=%async_computation | async-start | bytes 18874368 | tf_op jit(solution)/shard_map/all_to_all | solution.py:81
  30.1 202.3 %reduce-scatter.11.cloned.1.call-start = ((), (), s32[]{:S(2)}) async-start(), calls=%async_computation.8 | async-start | bytes 3932160 | tf_op jit(solution)/shard_map/reduce_scatter | solution.py:116
  52.4 7.6 %copy-start.6 = (s32[2,4,1]{1,2,0:T(1,128)S(1)}, s32[2,4,1]{1,2,0:T(1,128)}, u32[]{:S(2)}) copy-start(s32[2,4,1]{1,2,0:T(1,128)} %param.17) | copy-start | bytes 100
  135.0 9.3 %copy-start.1 = (bf16[144,128,128]{2,1,0:T(8,128)(2,1)S(1)}, bf16[144,128,128]{2,1,0:T(8,128)(2,1)}, u32[]{:S(2)}) copy-start(bf16[144,128,128]{2,1,0:T(8,128)(2,1)} %gather_fusion.2) | copy-start | bytes 14155780
  144.3 5.9 %copy-start = (bf16[1,8,18,128,128]{4,3,2,0,1:T(8,128)(2,1)}, bf16[1,8,18,128,128]{4,3,2,0,1:T(8,128)(2,1)S(1)}, u32[]{:S(2)}) copy-start(bf16[1,8,18,128,128]{4,3,2,0,1:T(8,128)(2,1)S(1)} %get-tuple-element.31) | copy-start | bytes 14155780
  169.7 2.4 copy-start.4
  172.1 96.7 %reduce-scatter.9.cloned.1.call-start = ((), (), s32[]{:S(2)}) async-start(), calls=%async_computation.6 | async-start | bytes 3932160 | tf_op jit(solution)/shard_map/reduce_scatter | solution.py:97
  232.3 59.0 %all-gather.3.cloned.1.call-start = ((), (), s32[]{:S(2)}) async-start(), calls=%async_computation.7 | async-start | bytes 1966080 | tf_op jit(solution)/shard_map/all_gather | solution.py:98
  271.6 41.4 %all-gather.5.cloned.1.call-start = ((), (), s32[]{:S(2)}) async-start(), calls=%async_computation.9 | async-start | bytes 1966080 | tf_op jit(solution)/shard_map/all_gather | solution.py:117
  322.5 15.7 %slice-start = ((s8[4718592]{0:T(1024)(128)(4,1)}), s8[524288]{0:T(1024)(128)(4,1)S(1)}, s32[]{:S(2)}) async-start(s8[4718592]{0:T(1024)(128)(4,1)} %bitcast.113), calls=%async_computation.12 | async-start | bytes 1048576
  330.1 8.2 %slice-start.1 = ((s8[4718592]{0:T(1024)(128)(4,1)}), s8[4194304]{0:T(1024)(128)(4,1)S(1)}, s32[]{:S(2)}) async-start(s8[4718592]{0:T(1024)(128)(4,1)} %bitcast.113), calls=%async_computation.13 | async-start | bytes 8388608
  330.1 8.1 %copy-start.2 = (bf16[144,128,128]{2,1,0:T(8,128)(2,1)S(1)}, bf16[144,128,128]{2,1,0:T(8,128)(2,1)}, u32[]{:S(2)}) copy-start(bf16[144,128,128]{2,1,0:T(8,128)(2,1)} %gather_fusion.3) | copy-start | bytes 14155780
  350.7 112.0 %all-to-all-start.1 = ((bf16[2,8,18,128,128]{4,3,2,0,1:T(8,128)(2,1)}), bf16[2,8,18,128,128]{4,3,2,0,1:T(8,128)(2,1)}, u32[]{:S(2)}, u32[]{:S(2)}) async-start(bf16[2,8,18,128,128]{4,3,2,0,1:T(8,128)(2,1)} %pad_maximum_fusion), calls=%async_computation.3 | async-start | bytes 18874368 | tf_op jit(solution)/shard_map/all_to_all | solution.py:136
  355.7 67.6 %reduce-scatter.13.cloned.1.call-start = ((), (), s32[]{:S(2)}) async-start(), calls=%async_computation.10 | async-start | bytes 1966080
  386.4 74.0 %reduce-scatter.15.cloned.1.call-start = ((), (), s32[]{:S(2)}) async-start(), calls=%async_computation.11 | async-start | bytes 1966080
Sparse Core Ops, SparseCore 0:
  172.2 38.9 reduce-scatter.10
  232.5 36.2 reduce-scatter.8
  271.7 19.6 all-gather.2
  293.4 19.6 all-gather.4
  386.5 36.7 reduce-scatter.12
  426.0 34.2 reduce-scatter.14
where the time goes:
time: 532 us; the launch traced here: 526 us
  waiting for transfers between devices  189 us (36%)
  other arithmetic  127 us (24%)
  local copies, waits for them, and re-layouts  95.1 us (18%)
  matrix products  47.2 us (9%)
  blocking collectives  42.3 us (8%)
  between operations  14.7 us (3%)
  starting transfers between devices  11.3 us (2%)
    scatter-add x4, other arithmetic, spread(): placed = jnp.zeros((values.shape[0], groups, values.shape[2]), jnp.float3...  76.6 us
    all_to_all x1, waiting for transfers between devices, on_device(): lax.all_to_all(copies, ('mem', 'tok'), split_axis=1, concat_axis=2, tiled...  74.7 us
    unnamed x8, waiting for transfers between devices  39.1 us
    reduce_scatter x1, waiting for transfers between devices, on_device(): preact = lax.psum_scatter(pre_part, 'tok', scatter_dimension=1, tiled=True)  36.3 us
    unnamed x27, local copies, waits for them, and re-layouts  30.6 us
    gather x4, local copies, waits for them, and re-layouts, select(): jnp.take(matrix.reshape(matrix.shape[0], groups, -1), slot_index, axis=1)  30.2 us
    select_n x1, other arithmetic, adam_step(): jnp.where(live_mask, new_variance, variance)  22.9 us
    all_gather x1, blocking collectives, on_device(): lax.all_gather(cotangent, 'hid', axis=0, tiled=True)  21.4 us
  transfers between devices with their start and end apart: 8, of which 6 were waited for; matrix products, arithmetic and copies ran while one was open for 22% of the time, Pallas kernels for 0%

commit v1 on v0

v1 whole, which is shorter than its diff:
```python
import functools

import jax
import jax.numpy as jnp
from jax import lax
from jax.experimental import pallas as pl
from jax.experimental.pallas import tpu as pltpu
from jax.sharding import PartitionSpec as P

FFW = 24576
STEP = 10


GELU_ROOT = 0.7978845608028654
GELU_CUBIC = 0.044715
BETA_FIRST = 0.9
BETA_SECOND = 0.95
LEARN_RATE = 0.001
WEIGHT_DECAY = 0.1
ADAM_EPSILON = 1e-08
VMEM_BYTES = 56 * 2**20
UNROLL = 4


def activate(values):
    tangent = jnp.tanh(GELU_ROOT * (values + GELU_CUBIC * values * values * values))
    return 0.5 * values * (1.0 + tangent)


def gelu_slope(values):
    tangent = jnp.tanh(GELU_ROOT * (values + GELU_CUBIC * values * values * values))
    return 0.5 * (1.0 + tangent) + 0.5 * values * (1.0 - tangent * tangent) * GELU_ROOT * (
        1.0 + 3.0 * GELU_CUBIC * values * values
    )


def adam_step(weight, moment, variance, gradient):
    new_moment = BETA_FIRST * moment + (1.0 - BETA_FIRST) * gradient
    new_variance = BETA_SECOND * variance + (1.0 - BETA_SECOND) * gradient * gradient
    scaled = (
        new_moment
        / (1.0 - BETA_FIRST**STEP)
        / (jnp.sqrt(new_variance / (1.0 - BETA_SECOND**STEP)) + ADAM_EPSILON)
    )
    new_weight = weight - LEARN_RATE * (scaled + WEIGHT_DECAY * weight)
    return new_weight, new_moment, new_variance


def dot(left, right, left_dim, right_dim):
    return lax.dot_general(
        left, right, (((left_dim,), (right_dim,)), ((), ())), preferred_element_type=jnp.float32
    )


def lanes(index, size):
    return pl.ds(pl.multiple_of(index * size, size), size)


def live_range(kept_ref, matrix, local_slots):
    first = lax.axis_index("mem") * local_slots
    count = jnp.clip(kept_ref[matrix, lax.axis_index("tok")] - first, 0, local_slots)
    return first, count


def over_slots(count, body):
    groups = count // UNROLL

    def run(group, carry):
        body([group * UNROLL + lane for lane in range(UNROLL)])
        return carry

    lax.fori_loop(0, groups, run, 0)

    def single(slot, carry):
        body([slot])
        return carry

    lax.fori_loop(groups * UNROLL, count, single, 0)


def relative(tok_count):
    tok = lax.axis_index("tok")
    return (tok % 2) * (tok_count // 2) + tok // 2


def forward_kernel(
    matrix, transposed, width_blocks, tok_count, hid_count, mem_count, kept_ref, place_ref, *refs
):
    own_refs, (weight_ref, row_ref, keep_ref, send_ref) = refs[:mem_count], refs[mem_count:]
    half = keep_ref.shape[1]
    size = weight_ref.shape[-1]
    rows = own_refs[0].shape[0]
    step = rows // hid_count
    part = rows // tok_count
    turn = relative(tok_count)
    for group in range(mem_count):
        for block in range(hid_count):
            start = block * step
            spot = ((start // part) ^ turn) * part + start % part + group * rows
            row_ref[pl.ds(pl.multiple_of(spot, step), step), :] = own_refs[group][
                start : start + step, :
            ]
    keep_ref[...] = jnp.zeros(keep_ref.shape, jnp.float32)
    send_ref[...] = jnp.zeros(send_ref.shape, jnp.float32)
    first, count = live_range(kept_ref, matrix, weight_ref.shape[0])

    def body(slots):
        found = []
        for slot in slots:
            place = place_ref[matrix, first + slot]
            left = row_ref[:, lanes(place % width_blocks, size)]
            product = dot(left, weight_ref[slot], 1, 1 if transposed else 0)
            found.append((lanes(place // width_blocks, size), product))
        for spot, product in found:
            for group in range(mem_count):
                start = group * rows
                keep_ref[group, :, spot] += product[start : start + half]
                send_ref[group, :, spot] += product[start + half : start + rows]

    over_slots(count, body)


def backward_kernel(
    matrix, transposed, width_blocks, mem_count, kept_ref, place_ref, own_ref, pair_ref, weight_ref, *out_refs
):
    size = weight_ref.shape[-1]
    half = own_ref.shape[1]
    for out_ref in out_refs:
        out_ref[...] = jnp.zeros(out_ref.shape, jnp.float32)
    first, count = live_range(kept_ref, matrix, weight_ref.shape[0])

    def body(slots):
        found = []
        for slot in slots:
            place = place_ref[matrix, first + slot]
            spot = lanes(place // width_blocks, size)
            pieces = []
            for group in range(mem_count):
                pieces += [own_ref[group, :, spot], pair_ref[group, :, spot]]
            product = dot(
                jnp.concatenate(pieces, axis=0), weight_ref[slot], 1, 1 if transposed else 0
            )
            found.append((lanes(place % width_blocks, size), product))
        for spot, product in found:
            for group, out_ref in enumerate(out_refs):
                out_ref[:, spot] += product[group * 2 * half : (group + 1) * 2 * half]

    over_slots(count, body)


def gradient_kernel(
    matrix, width_blocks, mem_count, kept_ref, place_ref, row_ref, own_ref, pair_ref, out_ref
):
    size = out_ref.shape[-1]
    rows = row_ref.shape[0] // mem_count
    first, count = live_range(kept_ref, matrix, out_ref.shape[0])

    def body(slots):
        for slot in slots:
            place = place_ref[matrix, first + slot]
            hidden = lanes(place // width_blocks, size)
            width = lanes(place % width_blocks, size)
            total = None
            for group in range(mem_count):
                wide = row_ref[group * rows : (group + 1) * rows, width]
                deep = jnp.concatenate(
                    [own_ref[group, :, hidden], pair_ref[group, :, hidden]], axis=0
                )
                left, right = (wide, deep) if matrix == 0 else (deep, wide)
                term = dot(left, right, 0, 0).astype(jnp.bfloat16).astype(jnp.float32)
                total = term if total is None else total + term
            out_ref[slot] = total

    over_slots(count, body)

    def clear(slot, carry):
        out_ref[slot] = jnp.zeros(out_ref.shape[1:], jnp.float32)
        return carry

    lax.fori_loop(count, out_ref.shape[0], clear, 0)


def adam_kernel(matrix, tok_count, kept_ref, grad_ref, weight_ref, moment_ref, variance_ref, *refs):
    out_refs = refs[-3:]
    cell = pl.program_id(0)
    owned = weight_ref.shape[3]
    first = (lax.axis_index("mem") * tok_count + lax.axis_index("tok")) * owned
    count = jnp.clip(kept_ref[matrix, cell] - first, 0, owned)

    def update(slot, carry):
        at = (0, 0, 0, slot)
        fresh = adam_step(weight_ref[at], moment_ref[at], variance_ref[at], grad_ref[0, slot])
        for out_ref, value in zip(out_refs, fresh):
            out_ref[at] = value
        return carry

    lax.fori_loop(0, count, update, 0)

    def keep(slot, carry):
        at = (0, 0, 0, slot)
        for out_ref, value_ref in zip(out_refs, (weight_ref, moment_ref, variance_ref)):
            out_ref[at] = value_ref[at]
        return carry

    lax.fori_loop(count, owned, keep, 0)


SCALARS = pl.BlockSpec(memory_space=pltpu.SMEM)
WHOLE = pl.BlockSpec(memory_space=pltpu.VMEM)
ANYWHERE = pl.BlockSpec(memory_space=pl.ANY)


def call(kernel, name, outs, scalars, arrays, flops):
    moved = sum(a.size * a.dtype.itemsize for a in arrays)
    moved += sum(math_size(o) for o in outs)
    return pl.pallas_call(
        kernel,
        out_shape=outs,
        in_specs=[SCALARS] * len(scalars) + [WHOLE] * len(arrays),
        out_specs=[WHOLE] * len(outs),
        compiler_params=pltpu.CompilerParams(vmem_limit_bytes=VMEM_BYTES),
        cost_estimate=pl.CostEstimate(flops=flops, bytes_accessed=moved, transcendentals=0),
        name=name,
    )(*scalars, *arrays)


def math_size(shape):
    total = shape.dtype.itemsize
    for dim in shape.shape:
        total *= dim
    return total


def on_device(inputs, cotangent, blocks, first_moment, second_moment, places, kept_counts):
    mem_count = lax.axis_size("mem")
    tok_count = lax.axis_size("tok")
    hid_count = lax.axis_size("hid")
    block_size = blocks.shape[-1]
    owned_slots = blocks.shape[3]
    local_slots = owned_slots * tok_count
    width_blocks = inputs.shape[1] // block_size
    hidden_span = FFW // hid_count
    rows = inputs.shape[0] * hid_count
    other = tok_count // 2
    half = rows // 2
    part = rows // tok_count
    kept = kept_counts[:, :, 0]
    place_ids = places[:, 0, 0]
    scalars = (kept, place_ids)
    f32, bf16 = jnp.float32, jnp.bfloat16

    def shift_hid(array, shift):
        return lax.ppermute(array, "hid", [(i, (i + shift) % hid_count) for i in range(hid_count)])

    def shift_mem(array, shift):
        return lax.ppermute(array, "mem", [(i, (i + shift) % mem_count) for i in range(mem_count)])

    def pair(array):
        return lax.ppermute(array, "tok", [(i, i ^ 1) for i in range(tok_count)])

    def across(array, mem_shift, tok_shift):
        table = []
        for m in range(mem_count):
            for t in range(tok_count):
                to = ((m - mem_shift) % mem_count) * tok_count + (t ^ (2 * tok_shift))
                table.append((m * tok_count + t, to))
        return lax.ppermute(array, ("mem", "tok"), table)

    peers = [(j, b) for j in range(mem_count) for b in range(other)][1:]

    def gather_rows(array):
        pieces = [array] + [shift_hid(array, k) for k in range(1, hid_count)]
        near = jnp.concatenate(pieces, axis=0)
        return [near] + [shift_mem(near, j) for j in range(1, mem_count)]

    def gather_weights(matrix):
        narrow = blocks[matrix, :, 0].astype(bf16)
        moved = lax.all_to_all(narrow, "tok", split_axis=0, concat_axis=0, tiled=True)
        return moved.reshape(local_slots, block_size, block_size)

    def forward(matrix, transposed, row_groups, weights):
        kernel = functools.partial(
            forward_kernel, matrix, transposed, width_blocks, tok_count, hid_count, mem_count
        )
        width = row_groups[0].shape[1]
        outs = [
            jax.ShapeDtypeStruct((mem_count * rows, width), bf16),
            jax.ShapeDtypeStruct((mem_count, half, hidden_span), f32),
            jax.ShapeDtypeStruct((mem_count, half, hidden_span), f32),
        ]
        flops = 2 * mem_count * rows * local_slots * block_size * block_size
        return call(kernel, f"forward_{matrix}", outs, scalars, [*row_groups, weights], flops)

    def reduce_plane(keep, send):
        total = (keep + pair(send)).reshape(mem_count, other, part, hidden_span)
        result = total[0, 0]
        for j, b in peers:
            result = result + across(total[j, b], j, b)
        return result

    def gather_plane(piece):
        found = {(0, 0): piece}
        for j, b in peers:
            found[(-j) % mem_count, b] = across(piece, j, b)
        near = jnp.concatenate(
            [found[j, b] for j in range(mem_count) for b in range(other)], axis=0
        ).reshape(mem_count, half, hidden_span)
        return near, pair(near)

    def backward(matrix, transposed, near, far, weights):
        kernel = functools.partial(backward_kernel, matrix, transposed, width_blocks, mem_count)
        outs = [jax.ShapeDtypeStruct((rows, width_blocks * block_size), f32)] * mem_count
        flops = 2 * mem_count * rows * local_slots * block_size * block_size
        return call(kernel, f"backward_{matrix}", outs, scalars, [near, far, weights], flops)

    turn = relative(tok_count)
    step = inputs.shape[0]

    def reduce_rows(groups):
        total = groups[0]
        for j in range(1, mem_count):
            total = total + shift_mem(groups[j], -j)
        result = None
        for k in range(hid_count):
            start = k * step
            spot = ((start // part) ^ turn) * part + start % part
            piece = lax.dynamic_slice_in_dim(total, spot, step, 0)
            if k:
                piece = shift_hid(piece, -k)
            result = piece if result is None else result + piece
        return result.astype(bf16)

    def gradient(matrix, row_values, near, far):
        kernel = functools.partial(gradient_kernel, matrix, width_blocks, mem_count)
        outs = [jax.ShapeDtypeStruct((local_slots, block_size, block_size), f32)]
        flops = 2 * mem_count * rows * local_slots * block_size * block_size
        (found,) = call(
            kernel, f"gradient_{matrix}", outs, scalars, [row_values, near, far], flops
        )
        sendable = found.reshape(tok_count, owned_slots, block_size, block_size)
        return lax.all_to_all(sendable, "tok", split_axis=0, concat_axis=0, tiled=True)

    def update(matrix, grads, held):
        state_spec = pl.BlockSpec(
            (1, 1, 1, owned_slots, block_size, block_size), lambda i: (matrix, i, 0, 0, 0, 0)
        )
        grad_spec = pl.BlockSpec((1, owned_slots, block_size, block_size), lambda i: (i, 0, 0, 0))
        state = (blocks, first_moment, second_moment)
        return pl.pallas_call(
            functools.partial(adam_kernel, matrix, tok_count),
            grid=(tok_count,),
            out_shape=[jax.ShapeDtypeStruct(s.shape, f32) for s in state],
            in_specs=[SCALARS, grad_spec] + [state_spec] * 3 + [ANYWHERE] * len(held),
            out_specs=[state_spec] * 3,
            input_output_aliases={5 + i: i for i in range(len(held))},
            compiler_params=pltpu.CompilerParams(vmem_limit_bytes=VMEM_BYTES),
            cost_estimate=pl.CostEstimate(
                flops=grads.size * 12, bytes_accessed=grads.size * 28, transcendentals=grads.size
            ),
            name=f"update_{matrix}",
        )(kept, grads, *state, *held)

    input_groups = gather_rows(inputs)
    weights_first = gather_weights(0)
    cotangent_groups = gather_rows(cotangent)
    weights_second = gather_weights(1)
    token_rows, *pre_part = forward(0, False, input_groups, weights_first)
    preact = reduce_plane(*pre_part)
    grad_rows, *back_part = forward(1, True, cotangent_groups, weights_second)
    hidden = gather_plane(activate(preact).astype(bf16))
    hidden_grad = reduce_plane(*back_part)
    pre_grad = gather_plane((hidden_grad * gelu_slope(preact)).astype(bf16))
    layer_out = reduce_rows(backward(1, False, *hidden, weights_second))
    second_grad = gradient(1, grad_rows, *hidden)
    grad_in = reduce_rows(backward(0, True, *pre_grad, weights_first))
    first_grad = gradient(0, token_rows, *pre_grad)
    held = update(1, second_grad, ())
    return (layer_out, grad_in, *update(0, first_grad, held))


def solution(mesh):
    return jax.shard_map(
        on_device,
        mesh=mesh,
        in_specs=(
            P(("mem", "hid"), "tok"),
            P(("mem", "hid"), "tok"),
            P(None, None, "hid", ("mem", "tok"), None, None),
            P(None, None, "hid", ("mem", "tok"), None, None),
            P(None, None, "hid", ("mem", "tok"), None, None),
            P(None, "tok", "hid", None),
            P(None, None, "hid"),
        ),
        out_specs=(
            P(("mem", "hid"), "tok"),
            P(("mem", "hid"), "tok"),
            P(None, None, "hid", ("mem", "tok"), None, None),
            P(None, None, "hid", ("mem", "tok"), None, None),
            P(None, None, "hid", ("mem", "tok"), None, None),
        ),
        check_vma=False,
    )
```

time: 532 us -> 436 us (0.82)
  other arithmetic: 127 us -> 15.1 us
  Pallas kernels: 0 us -> 82.2 us
  local copies, waits for them, and re-layouts: 95.1 us -> 15.6 us
  waiting for transfers between devices: 189 us -> 267 us
  matrix products: 47.2 us -> 0 us
  starting transfers between devices: 11.3 us -> 53.9 us
  blocking collectives: 42.3 us -> 0 us
  between operations: 14.7 us -> 0.9 us
    ppermute x0 -> x32, waiting for transfers between devices: none -> 251 us  [the longest x12 149 us: across(): return lax.ppermute(array, ('mem', 'tok'), table)]
    pallas_call x0 -> x8, Pallas kernels: none -> 82.2 us  [the longest x6 56.6 us: call(): pl.pallas_call(kernel, out_shape=outs, in_specs=[SCALARS] * len(scalars)...]
    scatter-add x4 -> x0, other arithmetic: 76.6 us -> none  [spread(): placed = jnp.zeros((values.shape[0], groups, values.shape[2]), jnp.float3...]
    all_to_all x2 -> x4, waiting for transfers between devices: 74.7 us -> 15.6 us  [the longest x2 15.6 us: gather_weights(): lax.all_to_all(narrow, 'tok', split_axis=0, concat_axis=0, tiled=True)]
    dot_general x6 -> x0, matrix products: 47.2 us -> none  [the longest x1 11 us: on_device(): jnp.einsum('tsj,sij->tsi', pre_cols, weights[0], preferred_element_type=j...]
    all_gather x2 -> x0, blocking collectives: 42.3 us -> none  [the longest x1 21.4 us: on_device(): lax.all_gather(cotangent, 'hid', axis=0, tiled=True)]
    unnamed x8 -> x0, waiting for transfers between devices: 39.1 us -> none
    all_gather x2 -> x0, waiting for transfers between devices: 38.9 us -> none  [the longest x1 19.7 us: on_device(): lax.all_gather((hidden_grad * gelu_slope(preact)).astype(jnp.bfloat16), '...]
  transfers between devices with their start and end apart: 8 -> 36, of which waited for: 6 -> 19; matrix products, arithmetic and copies ran while one was open for 22% -> 6% of each run, Pallas kernels for 0% -> 14%
where the time goes in v1:
time: 436 us; the launch traced here: 435 us
  waiting for transfers between devices  267 us (61%)
  Pallas kernels  82.2 us (19%)
  starting transfers between devices  53.9 us (12%)
  local copies, waits for them, and re-layouts  15.6 us (4%)
  other arithmetic  15.1 us (3%)
    ppermute x12, waiting for transfers between devices, across(): return lax.ppermute(array, ('mem', 'tok'), table)  149 us
    ppermute x4, waiting for transfers between devices, shift_mem(): lax.ppermute(array, 'mem', [(i, (i + shift) % mem_count) for i in range(m...  60.9 us
    pallas_call x6, Pallas kernels, call(): pl.pallas_call(kernel, out_shape=outs, in_specs=[SCALARS] * len(scalars)...  56.6 us
    ppermute x12, waiting for transfers between devices, shift_hid(): lax.ppermute(array, 'hid', [(i, (i + shift) % hid_count) for i in range(h...  34.8 us
    pallas_call x2, Pallas kernels, update(): pl.pallas_call(functools.partial(adam_kernel, matrix, tok_count), grid=(t...  25.6 us
    ppermute x12, starting transfers between devices, shift_hid(): lax.ppermute(array, 'hid', [(i, (i + shift) % hid_count) for i in range(h...  20.3 us
    all_to_all x2, waiting for transfers between devices, gather_weights(): lax.all_to_all(narrow, 'tok', split_axis=0, concat_axis=0, tiled=True)  15.6 us
    ppermute x12, starting transfers between devices, across(): return lax.ppermute(array, ('mem', 'tok'), table)  12.8 us
  transfers between devices with their start and end apart: 36, of which 19 were waited for; matrix products, arithmetic and copies ran while one was open for 6% of the time, Pallas kernels for 14%

profile of v1, /device:TPU:0, one launch (start us, length us, event | category | flops | bytes accessed | tf_op | source)
XLA Modules:
  0.0 434.7 jit_solution(14112205162751475867)
XLA Ops:
  0.6 4.1 collective-permute-start.17
  8.6 4.8 %convert.4 = bf16[2,4,1,18,128,128]{5,4,3,2,1,0:T(8,128)(2,1)S(1)} convert(f32[2,4,1,18,128,128]{5,4,3,2,1,0:T(8,128)} %weight_ref.3) | non-fusion elementwise | flops 2359296 | bytes 14155776 | tf_op jit(solution)/shard_map/convert.1
  16.6 3.8 all-to-all-start.1
  24.6 4.1 collective-permute-start.1
  28.7 3.8 collective-permute-start.2
  33.1 15.6 %all-to-all-done.1 = bf16[4,18,128,128]{3,2,1,0:T(8,128)(2,1)S(1)} async-done(((bf16[4,18,128,128]{3,2,1,0:T(8,128)(2,1)}), bf16[4,18,128,128]{3,2,1,0:T(8,128)(2,1)S(1)}, u32[]{:S(2)}, u32[]{:S(2)}) %all-to-all-start.1) | async-done | bytes 2359328 | tf_op jit(solution)/shard_map/all_to_all | solution.py:278
  48.8 4.5 %all-to-all-start = ((bf16[4,18,128,128]{3,2,1,0:T(8,128)(2,1)}), bf16[4,18,128,128]{3,2,1,0:T(8,128)(2,1)}, u32[]{:S(2)}, u32[]{:S(2)}) async-start(bf16[4,18,128,128]{3,2,1,0:T(8,128)(2,1)} %get-tuple-element.39), calls=%async_computation | async-start | bytes 4718592 | tf_op jit(solution)/shard_map/all_to_all | solution.py:278
  55.2 9.7 %forward_1.1 = (bf16[256,3072]{1,0:T(8,128)(2,1)}, f32[2,64,6144]{2,1,0:T(8,128)}, f32[2,64,6144]{2,1,0:T(8,128)}) custom-call(s32[2,4]{1,0:T(2,128)} %bitcast.67, s32[2,144]{1,0:T(2,128)} %bitcast.61, bf16[128,3072]{1,0:T(8,128)(2,1)} %constant_dynamic-update-slice_fusion.4.refs_0_, bf16[128,3072]{1,0:T(8,128)(2,1)} %collective-permute-done.19.refs_1_, ...), custom_call_target="tpu_custom_call" | custom-call | flops 603979776 | bytes 11796480 | tf_op jit(solution)/shard_map/forward_1/pallas_call | solution.py:216
  68.3 20.1 %collective-permute-done.3.refs_1_ = bf16[128,3072]{1,0:T(8,128)(2,1)} collective-permute-done((bf16[128,3072]{1,0:T(8,128)(2,1)}, bf16[128,3072]{1,0:T(8,128)(2,1)}, u32[]{:S(2)}, u32[]{:S(2)}) %collective-permute-start.3) | collective-permute-done | bytes 786464 | tf_op jit(solution)/shard_map/ppermute | solution.py:256
  88.3 10.5 %forward_0.1 = (bf16[256,3072]{1,0:T(8,128)(2,1)}, f32[2,64,6144]{2,1,0:T(8,128)}, f32[2,64,6144]{2,1,0:T(8,128)}) custom-call(s32[2,4]{1,0:T(2,128)} %bitcast.68, s32[2,144]{1,0:T(2,128)} %bitcast.62, bf16[128,3072]{1,0:T(8,128)(2,1)} %constant_dynamic-update-slice_fusion.refs_0_, bf16[128,3072]{1,0:T(8,128)(2,1)} %collective-permute-done.3.refs_1_, ...), custom_call_target="tpu_custom_call" | custom-call | flops 603979776 | bytes 11796480 | tf_op jit(solution)/shard_map/forward_0/pallas_call | solution.py:216
  107.2 31.4 %collective-permute-done.21 = f32[32,6144]{1,0:T(8,128)S(1)} collective-permute-done((f32[32,6144]{1,0:T(8,128)S(1)}, f32[32,6144]{1,0:T(8,128)S(1)}, u32[]{:S(2)}, u32[]{:S(2)}) %collective-permute-start.21) | collective-permute-done | bytes 786464 | tf_op jit(solution)/shard_map/ppermute | solution.py:267
  140.1 31.7 %collective-permute-done.5 = f32[32,6144]{1,0:T(8,128)S(1)} collective-permute-done((f32[32,6144]{1,0:T(8,128)S(1)}, f32[32,6144]{1,0:T(8,128)S(1)}, u32[]{:S(2)}, u32[]{:S(2)}) %collective-permute-start.5) | collective-permute-done | bytes 786464 | tf_op jit(solution)/shard_map/ppermute | solution.py:267
  177.7 9.4 %collective-permute-done.10 = bf16[32,6144]{1,0:T(8,128)(2,1)S(1)} collective-permute-done((bf16[32,6144]{1,0:T(8,128)(2,1)S(1)}, bf16[32,6144]{1,0:T(8,128)(2,1)S(1)}, u32[]{:S(2)}, u32[]{:S(2)}) %collective-permute-start.10) | collective-permute-done | bytes 393248 | tf_op jit(solution)/shard_map/ppermute | solution.py:267
  187.1 6.4 %collective-permute-done.9 = bf16[32,6144]{1,0:T(8,128)(2,1)S(1)} collective-permute-done((bf16[32,6144]{1,0:T(8,128)(2,1)S(1)}, bf16[32,6144]{1,0:T(8,128)(2,1)S(1)}, u32[]{:S(2)}, u32[]{:S(2)}) %collective-permute-start.9) | collective-permute-done | bytes 393248 | tf_op jit(solution)/shard_map/ppermute | solution.py:267
  194.1 3.4 collective-permute-done.11.pair_ref
  198.7 9.1 %gradient_1.1 = f32[72,128,128]{2,1,0:T(8,128)} custom-call(s32[2,4]{1,0:T(2,128)} %bitcast.69, s32[2,144]{1,0:T(2,128)} %bitcast.63, bf16[256,3072]{1,0:T(8,128)(2,1)} %get-tuple-element.30.row_ref, bf16[2,64,6144]{2,1,0:T(8,128)(2,1)} %bitcast.52, bf16[2,64,6144]{2,1,0:T(8,128)(2,1)} %copy-done.3), custom_call_target="tpu_custom_call" | custom-call | flops 603979776 | bytes 9437184 | tf_op jit(solution)/shard_map/gradient_1/pallas_call | solution.py:216
  207.8 5.0 %all-to-all-start.3 = ((f32[4,18,128,128]{3,2,1,0:T(8,128)}), f32[4,18,128,128]{3,2,1,0:T(8,128)}, u32[]{:S(2)}, u32[]{:S(2)}) async-start(f32[4,18,128,128]{3,2,1,0:T(8,128)} %bitcast.50), calls=%async_computation.3 | async-start | bytes 9437184 | tf_op jit(solution)/shard_map/all_to_all | solution.py:341
  216.4 9.4 %collective-permute-done.26 = bf16[32,6144]{1,0:T(8,128)(2,1)S(1)} collective-permute-done((bf16[32,6144]{1,0:T(8,128)(2,1)S(1)}, bf16[32,6144]{1,0:T(8,128)(2,1)S(1)}, u32[]{:S(2)}, u32[]{:S(2)}) %collective-permute-start.26) | collective-permute-done | bytes 393248 | tf_op jit(solution)/shard_map/ppermute | solution.py:267
  225.8 8.2 %collective-permute-done.25 = bf16[32,6144]{1,0:T(8,128)(2,1)S(1)} collective-permute-done((bf16[32,6144]{1,0:T(8,128)(2,1)S(1)}, bf16[32,6144]{1,0:T(8,128)(2,1)S(1)}, u32[]{:S(2)}, u32[]{:S(2)}) %collective-permute-start.25) | collective-permute-done | bytes 393248 | tf_op jit(solution)/shard_map/ppermute | solution.py:267
  234.0 49.4 %collective-permute-done.24 = bf16[32,6144]{1,0:T(8,128)(2,1)S(1)} collective-permute-done((bf16[32,6144]{1,0:T(8,128)(2,1)S(1)}, bf16[32,6144]{1,0:T(8,128)(2,1)S(1)}, u32[]{:S(2)}, u32[]{:S(2)}) %collective-permute-start.24) | collective-permute-done | bytes 393248 | tf_op jit(solution)/shard_map/ppermute | solution.py:267
  283.7 3.4 collective-permute-done.27.pair_ref
  288.2 9.2 %backward_0.1 = (f32[128,3072]{1,0:T(8,128)}, f32[128,3072]{1,0:T(8,128)}) custom-call(s32[2,4]{1,0:T(2,128)} %bitcast.70, s32[2,144]{1,0:T(2,128)} %bitcast.64, bf16[2,64,6144]{2,1,0:T(8,128)(2,1)} %bitcast.55, bf16[2,64,6144]{2,1,0:T(8,128)(2,1)} %copy-done.4, bf16[72,128,128]{2,1,0:T(8,128)(2,1)} %bitcast.2.refs_2_.weight_ref), custom_call_target="tpu_custom_call" | custom-call | flops 603979776 | bytes 8650752 | tf_op jit(solution)/shard_map/backward_0/pallas_call | solution.py:216
  297.4 10.1 %gradient_0.1 = f32[72,128,128]{2,1,0:T(8,128)} custom-call(s32[2,4]{1,0:T(2,128)} %bitcast.71, s32[2,144]{1,0:T(2,128)} %bitcast.65, bf16[256,3072]{1,0:T(8,128)(2,1)} %get-tuple-element.29.row_ref, bf16[2,64,6144]{2,1,0:T(8,128)(2,1)} %bitcast.56, bf16[2,64,6144]{2,1,0:T(8,128)(2,1)} %copy-done.4), custom_call_target="tpu_custom_call" | custom-call | flops 603979776 | bytes 9437184 | tf_op jit(solution)/shard_map/gradient_0/pallas_call | solution.py:216
  307.5 4.9 %all-to-all-start.2 = ((f32[4,18,128,128]{3,2,1,0:T(8,128)}), f32[4,18,128,128]{3,2,1,0:T(8,128)}, u32[]{:S(2)}, u32[]{:S(2)}) async-start(f32[4,18,128,128]{3,2,1,0:T(8,128)} %bitcast.49), calls=%async_computation.2 | async-start | bytes 9437184 | tf_op jit(solution)/shard_map/all_to_all | solution.py:341
  312.5 7.9 %backward_1.1 = (f32[128,3072]{1,0:T(8,128)}, f32[128,3072]{1,0:T(8,128)}) custom-call(s32[2,4]{1,0:T(2,128)} %bitcast.72, s32[2,144]{1,0:T(2,128)} %bitcast.66, bf16[2,64,6144]{2,1,0:T(8,128)(2,1)} %bitcast.53, bf16[2,64,6144]{2,1,0:T(8,128)(2,1)} %copy-done.3, bf16[72,128,128]{2,1,0:T(8,128)(2,1)} %bitcast.48), custom_call_target="tpu_custom_call" | custom-call | flops 603979776 | bytes 8650752 | tf_op jit(solution)/shard_map/backward_1/pallas_call | solution.py:216
  320.4 14.5 %collective-permute-done.28 = f32[128,3072]{1,0:T(8,128)S(1)} collective-permute-done((f32[128,3072]{1,0:T(8,128)}, f32[128,3072]{1,0:T(8,128)S(1)}, u32[]{:S(2)}, u32[]{:S(2)}) %collective-permute-start.28) | collective-permute-done | bytes 1572896 | tf_op jit(solution)/shard_map/ppermute | solution.py:256
  341.5 26.3 %collective-permute-done.12 = f32[128,3072]{1,0:T(8,128)} collective-permute-done((f32[128,3072]{1,0:T(8,128)}, f32[128,3072]{1,0:T(8,128)}, u32[]{:S(2)}, u32[]{:S(2)}) %collective-permute-start.12) | collective-permute-done | bytes 1572896 | tf_op jit(solution)/shard_map/ppermute | solution.py:256
  371.6 4.6 %collective-permute-done.30 = f32[32,3072]{1,0:T(8,128)} collective-permute-done((f32[32,3072]{1,0:T(8,128)S(1)}, f32[32,3072]{1,0:T(8,128)}, u32[]{:S(2)}, u32[]{:S(2)}) %collective-permute-start.30) | collective-permute-done | bytes 393248 | tf_op jit(solution)/shard_map/ppermute | solution.py:253
  378.2 13.3 %collective-permute-done.13 = f32[32,3072]{1,0:T(8,128)S(1)} collective-permute-done((f32[32,3072]{1,0:T(8,128)S(1)}, f32[32,3072]{1,0:T(8,128)S(1)}, u32[]{:S(2)}, u32[]{:S(2)}) %collective-permute-start.13) | collective-permute-done | bytes 393248 | tf_op jit(solution)/shard_map/ppermute | solution.py:253
  391.5 16.9 %collective-permute-done.14 = f32[32,3072]{1,0:T(8,128)S(1)} collective-permute-done((f32[32,3072]{1,0:T(8,128)S(1)}, f32[32,3072]{1,0:T(8,128)S(1)}, u32[]{:S(2)}, u32[]{:S(2)}) %collective-permute-start.14) | collective-permute-done | bytes 393248 | tf_op jit(solution)/shard_map/ppermute | solution.py:253
  409.2 12.8 %update_1.1 = (f32[2,4,1,18,128,128]{5,4,3,2,1,0:T(8,128)}, f32[2,4,1,18,128,128]{5,4,3,2,1,0:T(8,128)}, f32[2,4,1,18,128,128]{5,4,3,2,1,0:T(8,128)}) custom-call(s32[2,4]{1,0:T(2,128)} %bitcast.73, f32[4,18,128,128]{3,2,1,0:T(8,128)} %all-to-all-done.3.grad_ref, f32[2,4,1,18,128,128]{5,4,3,2,1,0:T(8,128)} %weight_ref.3, ...), custom_call_target="tpu_custom_call" | custom-call | flops 14155776 | bytes 33030144 | tf_op jit(solution)/shard_map/update_1/pallas_call | solution.py:349
  422.0 12.8 %update_0.1 = (f32[2,4,1,18,128,128]{5,4,3,2,1,0:T(8,128)}, f32[2,4,1,18,128,128]{5,4,3,2,1,0:T(8,128)}, f32[2,4,1,18,128,128]{5,4,3,2,1,0:T(8,128)}) custom-call(s32[2,4]{1,0:T(2,128)} %bitcast.74, f32[4,18,128,128]{3,2,1,0:T(8,128)} %all-to-all-done.2.grad_ref, ...), custom_call_target="tpu_custom_call", output_to_operand_aliasing={{0}: (5, {}), {1}: (6, {}), {2}: (7, {})} | custom-call | flops 14155776 | bytes 33030144 | tf_op jit(solution)/shard_map/update_0/pallas_call | solution.py:349
  (99 shorter events, 52.5 us)
Async XLA Ops:
  0.6 21.1 %collective-permute-start.17 = (bf16[32,3072]{1,0:T(8,128)(2,1)}, bf16[32,3072]{1,0:T(8,128)(2,1)S(1)}, u32[]{:S(2)}, u32[]{:S(2)}) collective-permute-start(bf16[32,3072]{1,0:T(8,128)(2,1)} %param.8), channel_id=1, source_target_pairs={{0,8},{4,12},{8,0},{12,4},{1,9},{5,13},{9,1},{13,5},{2,10},{6,14},... | collective-permute-start | bytes 589832 | tf_op jit(solution)/shard_map/ppermute | solution.py:253
  4.8 16.3 %collective-permute-start.16 = (bf16[32,3072]{1,0:T(8,128)(2,1)}, bf16[32,3072]{1,0:T(8,128)(2,1)S(1)}, u32[]{:S(2)}, u32[]{:S(2)}) collective-permute-start(bf16[32,3072]{1,0:T(8,128)(2,1)} %param.8), channel_id=1, source_target_pairs={{0,4},{4,8},{8,12},{12,0},{1,5},{5,9},{9,13},{13,1},{2,6},{6,10},{... | collective-permute-start | bytes 589832 | tf_op jit(solution)/shard_map/ppermute | solution.py:253
  6.3 16.1 %collective-permute-start.18 = (bf16[32,3072]{1,0:T(8,128)(2,1)}, bf16[32,3072]{1,0:T(8,128)(2,1)S(1)}, u32[]{:S(2)}, u32[]{:S(2)}) collective-permute-start(bf16[32,3072]{1,0:T(8,128)(2,1)} %param.8), channel_id=1, source_target_pairs={{0,12},{4,0},{8,4},{12,8},{1,13},{5,1},{9,5},{13,9},{2,14},{6,2},{... | collective-permute-start | bytes 589832 | tf_op jit(solution)/shard_map/ppermute | solution.py:253
  16.6 32.2 %all-to-all-start.1 = ((bf16[4,18,128,128]{3,2,1,0:T(8,128)(2,1)}), bf16[4,18,128,128]{3,2,1,0:T(8,128)(2,1)S(1)}, u32[]{:S(2)}, u32[]{:S(2)}) async-start(bf16[4,18,128,128]{3,2,1,0:T(8,128)(2,1)} %get-tuple-element.40), calls=%async_computation.1 | async-start | bytes 4718592 | tf_op jit(solution)/shard_map/all_to_all | solution.py:278
  23.1 31.1 %collective-permute-start.19 = (bf16[128,3072]{1,0:T(8,128)(2,1)}, bf16[128,3072]{1,0:T(8,128)(2,1)}, u32[]{:S(2)}, u32[]{:S(2)}) collective-permute-start(bf16[128,3072]{1,0:T(8,128)(2,1)} %constant_dynamic-update-slice_fusion.4.refs_0_), channel_id=1, source_target_pairs={{0,16},{16,0},{1,17},{17,1},{2,18},{18,2},{3,19},{19,3},{4,20},{20... | collective-permute-start | bytes 2359304 | tf_op jit(solution)/shard_map/ppermute | solution.py:256
  24.6 41.3 %collective-permute-start.1 = (bf16[32,3072]{1,0:T(8,128)(2,1)S(1)}, bf16[32,3072]{1,0:T(8,128)(2,1)S(1)}, u32[]{:S(2)}, u32[]{:S(2)}) collective-permute-start(bf16[32,3072]{1,0:T(8,128)(2,1)S(1)} %copy-done.11), channel_id=1, source_target_pairs={{0,8},{4,12},{8,0},{12,4},{1,9},{5,13},{9,1},{13,5},{2,10},{6,14},... | collective-permute-start | bytes 589832 | tf_op jit(solution)/shard_map/ppermute | solution.py:253
  28.7 24.5 %collective-permute-start = (bf16[32,3072]{1,0:T(8,128)(2,1)S(1)}, bf16[32,3072]{1,0:T(8,128)(2,1)}, u32[]{:S(2)}, u32[]{:S(2)}) collective-permute-start(bf16[32,3072]{1,0:T(8,128)(2,1)S(1)} %copy-done.11), channel_id=1, source_target_pairs={{0,4},{4,8},{8,12},{12,0},{1,5},{5,9},{9,13},{13,1},{2,6},{6,10},{... | collective-permute-start | bytes 589832 | tf_op jit(solution)/shard_map/ppermute | solution.py:253
  28.7 37.9 %collective-permute-start.2 = (bf16[32,3072]{1,0:T(8,128)(2,1)S(1)}, bf16[32,3072]{1,0:T(8,128)(2,1)}, u32[]{:S(2)}, u32[]{:S(2)}) collective-permute-start(bf16[32,3072]{1,0:T(8,128)(2,1)S(1)} %copy-done.11), channel_id=1, source_target_pairs={{0,12},{4,0},{8,4},{12,8},{1,13},{5,1},{9,5},{13,9},{2,14},{6,2},{... | collective-permute-start | bytes 589832 | tf_op jit(solution)/shard_map/ppermute | solution.py:253
  48.8 39.6 %all-to-all-start = ((bf16[4,18,128,128]{3,2,1,0:T(8,128)(2,1)}), bf16[4,18,128,128]{3,2,1,0:T(8,128)(2,1)}, u32[]{:S(2)}, u32[]{:S(2)}) async-start(bf16[4,18,128,128]{3,2,1,0:T(8,128)(2,1)} %get-tuple-element.39), calls=%async_computation | async-start | bytes 4718592 | tf_op jit(solution)/shard_map/all_to_all | solution.py:278
  64.9 34.0 %collective-permute-start.20 = (f32[2,64,6144]{2,1,0:T(8,128)}, f32[2,64,6144]{2,1,0:T(8,128)}, u32[]{:S(2)}, u32[]{:S(2)}) collective-permute-start(f32[2,64,6144]{2,1,0:T(8,128)} %get-tuple-element.26), channel_id=1, source_target_pairs={{0,1},{1,0},{2,3},{3,2},{4,5},{5,4},{6,7},{7,6},{8,9},{9,8},{10,11... | collective-permute-start | bytes 9437192 | tf_op jit(solution)/shard_map/ppermute | solution.py:259
  68.3 20.1 %collective-permute-start.3 = (bf16[128,3072]{1,0:T(8,128)(2,1)}, bf16[128,3072]{1,0:T(8,128)(2,1)}, u32[]{:S(2)}, u32[]{:S(2)}) collective-permute-start(bf16[128,3072]{1,0:T(8,128)(2,1)} %constant_dynamic-update-slice_fusion.refs_0_), channel_id=1, source_target_pairs={{0,16},{16,0},{1,17},{17,1},{2,18},{18,2},{3,19},{19,3},{4,20},{20... | collective-permute-start | bytes 2359304 | tf_op jit(solution)/shard_map/ppermute | solution.py:256
  101.3 37.3 %collective-permute-start.21 = (f32[32,6144]{1,0:T(8,128)S(1)}, f32[32,6144]{1,0:T(8,128)S(1)}, u32[]{:S(2)}, u32[]{:S(2)}) collective-permute-start(f32[32,6144]{1,0:T(8,128)S(1)} %get-tuple-element.44), channel_id=1, source_target_pairs={{0,2},{1,3},{2,0},{3,1},{16,18},{17,19},{18,16},{19,17},{4,6},{5,7... | collective-permute-start | bytes 2359304 | tf_op jit(solution)/shard_map/ppermute | solution.py:267
  103.0 35.9 %collective-permute-start.23 = (f32[32,6144]{1,0:T(8,128)S(1)}, f32[32,6144]{1,0:T(8,128)S(1)}, u32[]{:S(2)}, u32[]{:S(2)}) collective-permute-start(f32[32,6144]{1,0:T(8,128)S(1)} %get-tuple-element.45), channel_id=1, source_target_pairs={{0,18},{1,19},{2,16},{3,17},{16,2},{17,3},{18,0},{19,1},{4,22},{5,... | collective-permute-start | bytes 2359304 | tf_op jit(solution)/shard_map/ppermute | solution.py:267
  103.1 37.0 %collective-permute-start.22 = (f32[32,6144]{1,0:T(8,128)S(1)}, f32[32,6144]{1,0:T(8,128)S(1)}, u32[]{:S(2)}, u32[]{:S(2)}) collective-permute-start(f32[32,6144]{1,0:T(8,128)S(1)} %get-tuple-element.46), channel_id=1, source_target_pairs={{0,16},{1,17},{2,18},{3,19},{16,0},{17,1},{18,2},{19,3},{4,20},{5,... | collective-permute-start | bytes 2359304 | tf_op jit(solution)/shard_map/ppermute | solution.py:267
  105.4 66.4 %collective-permute-start.5 = (f32[32,6144]{1,0:T(8,128)S(1)}, f32[32,6144]{1,0:T(8,128)S(1)}, u32[]{:S(2)}, u32[]{:S(2)}) collective-permute-start(f32[32,6144]{1,0:T(8,128)S(1)} %get-tuple-element.41), channel_id=1, source_target_pairs={{0,2},{1,3},{2,0},{3,1},{16,18},{17,19},{18,16},{19,17},{4,6},{5,7... | collective-permute-start | bytes 2359304 | tf_op jit(solution)/shard_map/ppermute | solution.py:267
  107.1 64.8 %collective-permute-start.7 = (f32[32,6144]{1,0:T(8,128)S(1)}, f32[32,6144]{1,0:T(8,128)S(1)}, u32[]{:S(2)}, u32[]{:S(2)}) collective-permute-start(f32[32,6144]{1,0:T(8,128)S(1)} %get-tuple-element.42), channel_id=1, source_target_pairs={{0,18},{1,19},{2,16},{3,17},{16,2},{17,3},{18,0},{19,1},{4,22},{5,... | collective-permute-start | bytes 2359304 | tf_op jit(solution)/shard_map/ppermute | solution.py:267
  138.6 34.5 %collective-permute-start.6 = (f32[32,6144]{1,0:T(8,128)S(1)}, f32[32,6144]{1,0:T(8,128)S(1)}, u32[]{:S(2)}, u32[]{:S(2)}) collective-permute-start(f32[32,6144]{1,0:T(8,128)S(1)} %get-tuple-element.43), channel_id=1, source_target_pairs={{0,16},{1,17},{2,18},{3,19},{16,0},{17,1},{18,2},{19,3},{4,20},{5,... | collective-permute-start | bytes 2359304 | tf_op jit(solution)/shard_map/ppermute | solution.py:267
  174.5 19.0 %collective-permute-start.9 = (bf16[32,6144]{1,0:T(8,128)(2,1)S(1)}, bf16[32,6144]{1,0:T(8,128)(2,1)S(1)}, u32[]{:S(2)}, u32[]{:S(2)}) collective-permute-start(bf16[32,6144]{1,0:T(8,128)(2,1)S(1)} %multiply_convert_fusion), channel_id=1, source_target_pairs={{0,16},{1,17},{2,18},{3,19},{16,0},{17,1},{18,2},{19,3},{4,20},{5,... | collective-permute-start | bytes 1179656 | tf_op jit(solution)/shard_map/ppermute | solution.py:267
  176.9 16.9 %collective-permute-start.8 = (bf16[32,6144]{1,0:T(8,128)(2,1)S(1)}, bf16[32,6144]{1,0:T(8,128)(2,1)S(1)}, u32[]{:S(2)}, u32[]{:S(2)}) collective-permute-start(bf16[32,6144]{1,0:T(8,128)(2,1)S(1)} %multiply_convert_fusion), channel_id=1, source_target_pairs={{0,2},{1,3},{2,0},{3,1},{16,18},{17,19},{18,16},{19,17},{4,6},{5,7... | collective-permute-start | bytes 1179656 | tf_op jit(solution)/shard_map/ppermute | solution.py:267
  207.8 99.8 %all-to-all-start.3 = ((f32[4,18,128,128]{3,2,1,0:T(8,128)}), f32[4,18,128,128]{3,2,1,0:T(8,128)}, u32[]{:S(2)}, u32[]{:S(2)}) async-start(f32[4,18,128,128]{3,2,1,0:T(8,128)} %bitcast.50), calls=%async_computation.3 | async-start | bytes 9437184 | tf_op jit(solution)/shard_map/all_to_all | solution.py:341
  212.8 13.0 %collective-permute-start.26 = (bf16[32,6144]{1,0:T(8,128)(2,1)S(1)}, bf16[32,6144]{1,0:T(8,128)(2,1)S(1)}, u32[]{:S(2)}, u32[]{:S(2)}) collective-permute-start(bf16[32,6144]{1,0:T(8,128)(2,1)S(1)} %get-tuple-element.37), channel_id=1, source_target_pairs={{0,18},{1,19},{2,16},{3,17},{16,2},{17,3},{18,0},{19,1},{4,22},{5,... | collective-permute-start | bytes 1179656 | tf_op jit(solution)/shard_map/ppermute | solution.py:267
  213.4 20.6 %collective-permute-start.25 = (bf16[32,6144]{1,0:T(8,128)(2,1)S(1)}, bf16[32,6144]{1,0:T(8,128)(2,1)S(1)}, u32[]{:S(2)}, u32[]{:S(2)}) collective-permute-start(bf16[32,6144]{1,0:T(8,128)(2,1)S(1)} %get-tuple-element.37), channel_id=1, source_target_pairs={{0,16},{1,17},{2,18},{3,19},{16,0},{17,1},{18,2},{19,3},{4,20},{5,... | collective-permute-start | bytes 1179656 | tf_op jit(solution)/shard_map/ppermute | solution.py:267
  216.4 67.1 %collective-permute-start.24 = (bf16[32,6144]{1,0:T(8,128)(2,1)S(1)}, bf16[32,6144]{1,0:T(8,128)(2,1)S(1)}, u32[]{:S(2)}, u32[]{:S(2)}) collective-permute-start(bf16[32,6144]{1,0:T(8,128)(2,1)S(1)} %get-tuple-element.37), channel_id=1, source_target_pairs={{0,2},{1,3},{2,0},{3,1},{16,18},{17,19},{18,16},{19,17},{4,6},{5,7... | collective-permute-start | bytes 1179656 | tf_op jit(solution)/shard_map/ppermute | solution.py:267
  297.4 37.5 %collective-permute-start.28 = (f32[128,3072]{1,0:T(8,128)}, f32[128,3072]{1,0:T(8,128)S(1)}, u32[]{:S(2)}, u32[]{:S(2)}) collective-permute-start(f32[128,3072]{1,0:T(8,128)} %get-tuple-element.28), channel_id=1, source_target_pairs={{0,16},{16,0},{1,17},{17,1},{2,18},{18,2},{3,19},{19,3},{4,20},{20... | collective-permute-start | bytes 4718600 | tf_op jit(solution)/shard_map/ppermute | solution.py:256
  307.5 114.4 %all-to-all-start.2 = ((f32[4,18,128,128]{3,2,1,0:T(8,128)}), f32[4,18,128,128]{3,2,1,0:T(8,128)}, u32[]{:S(2)}, u32[]{:S(2)}) async-start(f32[4,18,128,128]{3,2,1,0:T(8,128)} %bitcast.49), calls=%async_computation.2 | async-start | bytes 9437184 | tf_op jit(solution)/shard_map/all_to_all | solution.py:341
  320.4 47.4 %collective-permute-start.12 = (f32[128,3072]{1,0:T(8,128)}, f32[128,3072]{1,0:T(8,128)}, u32[]{:S(2)}, u32[]{:S(2)}) collective-permute-start(f32[128,3072]{1,0:T(8,128)} %get-tuple-element.24), channel_id=1, source_target_pairs={{0,16},{16,0},{1,17},{17,1},{2,18},{18,2},{3,19},{19,3},{4,20},{20... | collective-permute-start | bytes 4718600 | tf_op jit(solution)/shard_map/ppermute | solution.py:256
  339.2 32.4 %collective-permute-start.29 = (f32[32,3072]{1,0:T(8,128)}, f32[32,3072]{1,0:T(8,128)}, u32[]{:S(2)}, u32[]{:S(2)}) collective-permute-start(f32[32,3072]{1,0:T(8,128)} %get-tuple-element.47), channel_id=1, source_target_pairs={{0,12},{4,0},{8,4},{12,8},{1,13},{5,1},{9,5},{13,9},{2,14},{6,2},{... | collective-permute-start | bytes 1179656 | tf_op jit(solution)/shard_map/ppermute | solution.py:253
  340.9 30.7 %collective-permute-start.31 = (f32[32,3072]{1,0:T(8,128)}, f32[32,3072]{1,0:T(8,128)}, u32[]{:S(2)}, u32[]{:S(2)}) collective-permute-start(f32[32,3072]{1,0:T(8,128)} %get-tuple-element.48), channel_id=1, source_target_pairs={{0,4},{4,8},{8,12},{12,0},{1,5},{5,9},{9,13},{13,1},{2,6},{6,10},{... | collective-permute-start | bytes 1179656 | tf_op jit(solution)/shard_map/ppermute | solution.py:253
  341.2 35.0 %collective-permute-start.30 = (f32[32,3072]{1,0:T(8,128)S(1)}, f32[32,3072]{1,0:T(8,128)}, u32[]{:S(2)}, u32[]{:S(2)}) collective-permute-start(f32[32,3072]{1,0:T(8,128)S(1)} %get-tuple-element.49), channel_id=1, source_target_pairs={{0,8},{4,12},{8,0},{12,4},{1,9},{5,13},{9,1},{13,5},{2,10},{6,14},... | collective-permute-start | bytes 1179656 | tf_op jit(solution)/shard_map/ppermute | solution.py:253
  369.5 22.0 %collective-permute-start.13 = (f32[32,3072]{1,0:T(8,128)S(1)}, f32[32,3072]{1,0:T(8,128)S(1)}, u32[]{:S(2)}, u32[]{:S(2)}) collective-permute-start(f32[32,3072]{1,0:T(8,128)S(1)} %get-tuple-element.50), channel_id=1, source_target_pairs={{0,12},{4,0},{8,4},{12,8},{1,13},{5,1},{9,5},{13,9},{2,14},{6,2},{... | collective-permute-start | bytes 1179656 | tf_op jit(solution)/shard_map/ppermute | solution.py:253
  369.6 21.9 %collective-permute-start.15 = (f32[32,3072]{1,0:T(8,128)S(1)}, f32[32,3072]{1,0:T(8,128)S(1)}, u32[]{:S(2)}, u32[]{:S(2)}) collective-permute-start(f32[32,3072]{1,0:T(8,128)S(1)} %get-tuple-element.51), channel_id=1, source_target_pairs={{0,4},{4,8},{8,12},{12,0},{1,5},{5,9},{9,13},{13,1},{2,6},{6,10},{... | collective-permute-start | bytes 1179656 | tf_op jit(solution)/shard_map/ppermute | solution.py:253
  371.6 36.8 %collective-permute-start.14 = (f32[32,3072]{1,0:T(8,128)S(1)}, f32[32,3072]{1,0:T(8,128)S(1)}, u32[]{:S(2)}, u32[]{:S(2)}) collective-permute-start(f32[32,3072]{1,0:T(8,128)S(1)} %get-tuple-element.52), channel_id=1, source_target_pairs={{0,8},{4,12},{8,0},{12,4},{1,9},{5,13},{9,1},{13,5},{2,10},{6,14},... | collective-permute-start | bytes 1179656 | tf_op jit(solution)/shard_map/ppermute | solution.py:253
  (17 other events, 140.1 us)

commit v2 on v1

--- a/solution.py
+++ b/solution.py
@@ -6,6 +6,7 @@
 from jax.experimental import pallas as pl
 from jax.experimental.pallas import tpu as pltpu
 from jax.sharding import PartitionSpec as P
+
 
 FFW = 24576
 STEP = 10
@@ -20,6 +21,7 @@
 ADAM_EPSILON = 1e-08
 VMEM_BYTES = 56 * 2**20
 UNROLL = 4
+CHUNKS = 2
 
 
 def activate(values):
@@ -121,12 +123,21 @@
 
 
 def backward_kernel(
-    matrix, transposed, width_blocks, mem_count, kept_ref, place_ref, own_ref, pair_ref, weight_ref, *out_refs
+    matrix,
+    transposed,
+    width_blocks,
+    mem_count,
+    kept_ref,
+    place_ref,
+    own_ref,
+    pair_ref,
+    weight_ref,
+    *refs,
 ):
+    out_refs, total_ref = refs[:-1], refs[-1]
     size = weight_ref.shape[-1]
     half = own_ref.shape[1]
-    for out_ref in out_refs:
-        out_ref[...] = jnp.zeros(out_ref.shape, jnp.float32)
+    total_ref[...] = jnp.zeros(total_ref.shape, jnp.float32)
     first, count = live_range(kept_ref, matrix, weight_ref.shape[0])
 
     def body(slots):
@@ -142,59 +153,88 @@
             )
             found.append((lanes(place % width_blocks, size), product))
         for spot, product in found:
-            for group, out_ref in enumerate(out_refs):
-                out_ref[:, spot] += product[group * 2 * half : (group + 1) * 2 * half]
+            total_ref[:, spot] += product
 
     over_slots(count, body)
-
-
-def gradient_kernel(
-    matrix, width_blocks, mem_count, kept_ref, place_ref, row_ref, own_ref, pair_ref, out_ref
-):
-    size = out_ref.shape[-1]
+    for index, out_ref in enumerate(out_refs):
+        chunk, group = index // mem_count, index % mem_count
+        span = out_ref.shape[1]
+        out_ref[...] = total_ref[
+            group * 2 * half : (group + 1) * 2 * half, chunk * span : (chunk + 1) * span
+        ]
+
+
+def owner_count(kept_ref, matrix, cell, owner, owned):
+    first = (lax.axis_index("mem") * lax.axis_size("tok") + owner) * owned
+    return first, jnp.clip(kept_ref[matrix, cell] - first, 0, owned)
+
+
+def gradient_kernel(matrix, width_blocks, mem_count, hid_count, kept_ref, place_ref, far_place_ref, *refs):
+    row_ref, own_ref, pair_ref = refs[:3]
+    late_refs = refs[3 : 3 + hid_count]
+    keep_ref, send_ref, late_ref = refs[3 + hid_count :]
+    cells, owned, size = keep_ref.shape[:3]
+    tok_count = lax.axis_size("tok")
+    tok = lax.axis_index("tok")
     rows = row_ref.shape[0] // mem_count
-    first, count = live_range(kept_ref, matrix, out_ref.shape[0])
-
-    def body(slots):
-        for slot in slots:
-            place = place_ref[matrix, first + slot]
-            hidden = lanes(place // width_blocks, size)
-            width = lanes(place % width_blocks, size)
-            total = None
-            for group in range(mem_count):
-                wide = row_ref[group * rows : (group + 1) * rows, width]
-                deep = jnp.concatenate(
-                    [own_ref[group, :, hidden], pair_ref[group, :, hidden]], axis=0
-                )
-                left, right = (wide, deep) if matrix == 0 else (deep, wide)
-                term = dot(left, right, 0, 0).astype(jnp.bfloat16).astype(jnp.float32)
-                total = term if total is None else total + term
-            out_ref[slot] = total
-
-    over_slots(count, body)
-
-    def clear(slot, carry):
-        out_ref[slot] = jnp.zeros(out_ref.shape[1:], jnp.float32)
-        return carry
-
-    lax.fori_loop(count, out_ref.shape[0], clear, 0)
-
-
-def adam_kernel(matrix, tok_count, kept_ref, grad_ref, weight_ref, moment_ref, variance_ref, *refs):
+    part = rows // tok_count
+    step = rows // hid_count
+    turn = relative(tok_count)
+    for block, source in enumerate(late_refs):
+        start = block * step
+        spot = ((start // part) ^ turn) * part + start % part
+        for group in range(mem_count):
+            late_ref[pl.ds(pl.multiple_of(spot + group * rows, step), step), :] = source[matrix, group]
+
+    for cell in range(cells):
+        places, values = ((place_ref, row_ref), (far_place_ref, late_ref))[cell]
+        for side, out_ref in enumerate((keep_ref, send_ref)):
+            first, count = owner_count(kept_ref, matrix, tok ^ (2 * cell), tok ^ side, owned)
+
+            def body(slots):
+                for slot in slots:
+                    place = places[matrix, first + slot]
+                    hidden = lanes(place // width_blocks, size)
+                    width = lanes(place % width_blocks, size)
+                    total = None
+                    for group in range(mem_count):
+                        wide = values[group * rows : (group + 1) * rows, width]
+                        deep = jnp.concatenate(
+                            [own_ref[group, :, hidden], pair_ref[group, :, hidden]], axis=0
+                        )
+                        left, right = (wide, deep) if matrix == 0 else (deep, wide)
+                        term = dot(left, right, 0, 0).astype(jnp.bfloat16).astype(jnp.float32)
+                        total = term if total is None else total + term
+                    out_ref[cell, slot] = total
+
+            over_slots(count, body)
+
+            def clear(slot, carry):
+                out_ref[cell, slot] = jnp.zeros((size, size), jnp.float32)
+                return carry
+
+            lax.fori_loop(count, owned, clear, 0)
+
+
+def update_kernel(matrix, kept_ref, keep_ref, swap_ref, weight_ref, moment_ref, variance_ref, *refs):
     out_refs = refs[-3:]
-    cell = pl.program_id(0)
+    turn = pl.program_id(0)
+    tok = lax.axis_index("tok")
     owned = weight_ref.shape[3]
-    first = (lax.axis_index("mem") * tok_count + lax.axis_index("tok")) * owned
-    count = jnp.clip(kept_ref[matrix, cell] - first, 0, owned)
-
-    def update(slot, carry):
-        at = (0, 0, 0, slot)
-        fresh = adam_step(weight_ref[at], moment_ref[at], variance_ref[at], grad_ref[0, slot])
-        for out_ref, value in zip(out_refs, fresh):
-            out_ref[at] = value
-        return carry
-
-    lax.fori_loop(0, count, update, 0)
+    _, count = owner_count(kept_ref, matrix, tok ^ turn, tok, owned)
+
+    def update_from(grad_ref):
+        def update(slot, carry):
+            at = (0, 0, 0, slot)
+            fresh = adam_step(weight_ref[at], moment_ref[at], variance_ref[at], grad_ref[0, slot])
+            for out_ref, value in zip(out_refs, fresh):
+                out_ref[at] = value
+            return carry
+
+        lax.fori_loop(0, count, update, 0)
+
+    pl.when(turn % 2 == 0)(functools.partial(update_from, keep_ref))
+    pl.when(turn % 2 == 1)(functools.partial(update_from, swap_ref))
 
     def keep(slot, carry):
         at = (0, 0, 0, slot)
@@ -205,12 +245,43 @@
     lax.fori_loop(count, owned, keep, 0)
 
 
+def join_kernel(keep_ref, swap_ref, *out_refs):
+    groups = keep_ref.shape[0]
+    part = out_refs[0].shape[0]
+    for index, out_ref in enumerate(out_refs):
+        group, start = index % groups, index // groups * part
+        out_ref[...] = keep_ref[group, start : start + part] + swap_ref[group, start : start + part]
+
+
+def total_of(refs):
+    total = refs[0][...]
+    for ref in refs[1:]:
+        total = total + ref[...]
+    return total
+
+
+def activate_kernel(*refs):
+    *part_refs, hidden_ref, preact_ref = refs
+    preact = total_of(part_refs)
+    preact_ref[...] = preact
+    hidden_ref[...] = activate(preact).astype(jnp.bfloat16)
+
+
+def slope_kernel(*refs):
+    *part_refs, preact_ref, out_ref = refs
+    out_ref[...] = (total_of(part_refs) * gelu_slope(preact_ref[...])).astype(jnp.bfloat16)
+
+
+def narrow_kernel(block_ref, out_ref):
+    out_ref[...] = block_ref[0, :, 0].astype(jnp.bfloat16)
+
+
 SCALARS = pl.BlockSpec(memory_space=pltpu.SMEM)
 WHOLE = pl.BlockSpec(memory_space=pltpu.VMEM)
 ANYWHERE = pl.BlockSpec(memory_space=pl.ANY)
 
 
-def call(kernel, name, outs, scalars, arrays, flops):
+def call(kernel, outs, scalars, arrays, flops, scratch=()):
     moved = sum(a.size * a.dtype.itemsize for a in arrays)
     moved += sum(math_size(o) for o in outs)
     return pl.pallas_call(
@@ -218,9 +289,9 @@
         out_shape=outs,
         in_specs=[SCALARS] * len(scalars) + [WHOLE] * len(arrays),
         out_specs=[WHOLE] * len(outs),
+        scratch_shapes=scratch,
         compiler_params=pltpu.CompilerParams(vmem_limit_bytes=VMEM_BYTES),
         cost_estimate=pl.CostEstimate(flops=flops, bytes_accessed=moved, transcendentals=0),
-        name=name,
     )(*scalars, *arrays)
 
 
@@ -244,6 +315,7 @@
     other = tok_count // 2
     half = rows // 2
     part = rows // tok_count
+    chunks = CHUNKS
     kept = kept_counts[:, :, 0]
     place_ids = places[:, 0, 0]
     scalars = (kept, place_ids)
@@ -255,8 +327,8 @@
     def shift_mem(array, shift):
         return lax.ppermute(array, "mem", [(i, (i + shift) % mem_count) for i in range(mem_count)])
 
-    def pair(array):
-        return lax.ppermute(array, "tok", [(i, i ^ 1) for i in range(tok_count)])
+    def flip_tok(array, bit):
+        return lax.ppermute(array, "tok", [(i, i ^ bit) for i in range(tok_count)])
 
     def across(array, mem_shift, tok_shift):
         table = []
@@ -273,8 +345,24 @@
         near = jnp.concatenate(pieces, axis=0)
         return [near] + [shift_mem(near, j) for j in range(1, mem_count)]
 
+    def gather_late():
+        both = flip_tok(jnp.stack([inputs, cotangent]), 2)
+        found = [both] + [shift_mem(both, j) for j in range(1, mem_count)]
+        moved = jnp.stack(found, axis=1)
+        return [moved] + [shift_hid(moved, k) for k in range(1, hid_count)]
+
     def gather_weights(matrix):
-        narrow = blocks[matrix, :, 0].astype(bf16)
+        shape = (tok_count, owned_slots, block_size, block_size)
+        narrow = pl.pallas_call(
+            narrow_kernel,
+            grid=(tok_count,),
+            out_shape=jax.ShapeDtypeStruct(shape, bf16),
+            in_specs=[
+                pl.BlockSpec((1, 1, 1) + blocks.shape[3:], lambda i: (matrix, i, 0, 0, 0, 0))
+            ],
+            out_specs=pl.BlockSpec((1,) + shape[1:], lambda i: (i, 0, 0, 0)),
+            compiler_params=pltpu.CompilerParams(vmem_limit_bytes=VMEM_BYTES),
+        )(blocks)
         moved = lax.all_to_all(narrow, "tok", split_axis=0, concat_axis=0, tiled=True)
         return moved.reshape(local_slots, block_size, block_size)
 
@@ -289,14 +377,37 @@
             jax.ShapeDtypeStruct((mem_count, half, hidden_span), f32),
         ]
         flops = 2 * mem_count * rows * local_slots * block_size * block_size
-        return call(kernel, f"forward_{matrix}", outs, scalars, [*row_groups, weights], flops)
+        return call(kernel, outs, scalars, [*row_groups, weights], flops)
+
+    def over_columns(kernel, outs, arrays, steps):
+        def spec(shape):
+            lead = len(shape) - 1
+            return pl.BlockSpec(
+                tuple(shape[:-1]) + (shape[-1] // steps,), lambda i: (0,) * lead + (i,)
+            )
+
+        return pl.pallas_call(
+            kernel,
+            grid=(steps,),
+            out_shape=outs,
+            in_specs=[spec(a.shape) for a in arrays],
+            out_specs=[spec(o.shape) for o in outs],
+            compiler_params=pltpu.CompilerParams(vmem_limit_bytes=VMEM_BYTES),
+            cost_estimate=pl.CostEstimate(
+                flops=sum(o.size for o in outs) * 4,
+                bytes_accessed=sum(a.size * a.dtype.itemsize for a in (*arrays, *outs)),
+                transcendentals=0,
+            ),
+        )(*arrays)
 
     def reduce_plane(keep, send):
-        total = (keep + pair(send)).reshape(mem_count, other, part, hidden_span)
-        result = total[0, 0]
+        outs = [jax.ShapeDtypeStruct((part, hidden_span), f32)] * (mem_count * other)
+        swap = flip_tok(send, 1)
+        found = over_columns(join_kernel, outs, [keep, swap], 4)
+        terms = [found[0]]
         for j, b in peers:
-            result = result + across(total[j, b], j, b)
-        return result
+            terms.append(across(found[b * mem_count + j], j, b))
+        return terms
 
     def gather_plane(piece):
         found = {(0, 0): piece}
@@ -305,75 +416,93 @@
         near = jnp.concatenate(
             [found[j, b] for j in range(mem_count) for b in range(other)], axis=0
         ).reshape(mem_count, half, hidden_span)
-        return near, pair(near)
+        return near, flip_tok(near, 1)
 
     def backward(matrix, transposed, near, far, weights):
         kernel = functools.partial(backward_kernel, matrix, transposed, width_blocks, mem_count)
-        outs = [jax.ShapeDtypeStruct((rows, width_blocks * block_size), f32)] * mem_count
+        span = inputs.shape[1] // chunks
+        outs = [jax.ShapeDtypeStruct((rows, span), f32)] * (mem_count * chunks)
         flops = 2 * mem_count * rows * local_slots * block_size * block_size
-        return call(kernel, f"backward_{matrix}", outs, scalars, [near, far, weights], flops)
+        scratch = [pltpu.VMEM((mem_count * rows, inputs.shape[1]), f32)]
+        return call(kernel, outs, scalars, [near, far, weights], flops, scratch)
 
     turn = relative(tok_count)
     step = inputs.shape[0]
 
-    def reduce_rows(groups):
-        total = groups[0]
-        for j in range(1, mem_count):
-            total = total + shift_mem(groups[j], -j)
-        result = None
-        for k in range(hid_count):
-            start = k * step
-            spot = ((start // part) ^ turn) * part + start % part
-            piece = lax.dynamic_slice_in_dim(total, spot, step, 0)
-            if k:
-                piece = shift_hid(piece, -k)
-            result = piece if result is None else result + piece
-        return result.astype(bf16)
-
-    def gradient(matrix, row_values, near, far):
-        kernel = functools.partial(gradient_kernel, matrix, width_blocks, mem_count)
-        outs = [jax.ShapeDtypeStruct((local_slots, block_size, block_size), f32)]
+    def reduce_rows(found):
+        results = []
+        for chunk in range(chunks):
+            groups = found[chunk * mem_count : (chunk + 1) * mem_count]
+            total = groups[0]
+            for j in range(1, mem_count):
+                total = total + shift_mem(groups[j], -j)
+            result = None
+            for k in range(hid_count):
+                start = k * step
+                spot = ((start // part) ^ turn) * part + start % part
+                piece = lax.dynamic_slice_in_dim(total, spot, step, 0)
+                if k:
+                    piece = shift_hid(piece, -k)
+                result = piece if result is None else result + piece
+            results.append(result.astype(bf16))
+        return jnp.concatenate(results, axis=1)
+
+    def gradient(matrix, row_values, near, far, late):
+        kernel = functools.partial(gradient_kernel, matrix, width_blocks, mem_count, hid_count)
+        outs = [
+            jax.ShapeDtypeStruct((other, owned_slots, block_size, block_size), f32),
+            jax.ShapeDtypeStruct((other, owned_slots, block_size, block_size), f32),
+        ]
         flops = 2 * mem_count * rows * local_slots * block_size * block_size
-        (found,) = call(
-            kernel, f"gradient_{matrix}", outs, scalars, [row_values, near, far], flops
+        keep, send = call(
+            kernel,
+            outs,
+            (kept, place_ids, far_place_ids),
+            [row_values, near, far, *late],
+            flops,
+            [pltpu.VMEM(row_values.shape, bf16)],
         )
-        sendable = found.reshape(tok_count, owned_slots, block_size, block_size)
-        return lax.all_to_all(sendable, "tok", split_axis=0, concat_axis=0, tiled=True)
+        return keep, flip_tok(send, 1)
 
     def update(matrix, grads, held):
-        state_spec = pl.BlockSpec(
-            (1, 1, 1, owned_slots, block_size, block_size), lambda i: (matrix, i, 0, 0, 0, 0)
-        )
-        grad_spec = pl.BlockSpec((1, owned_slots, block_size, block_size), lambda i: (i, 0, 0, 0))
+        state_shape = (1, 1, 1, owned_slots, block_size, block_size)
+        state_spec = pl.BlockSpec(state_shape, lambda i: (matrix, lax.axis_index("tok") ^ i, 0, 0, 0, 0))
+        grad_spec = pl.BlockSpec((1, owned_slots, block_size, block_size), lambda i: (i // 2, 0, 0, 0))
         state = (blocks, first_moment, second_moment)
+        size = local_slots * block_size * block_size
         return pl.pallas_call(
-            functools.partial(adam_kernel, matrix, tok_count),
+            functools.partial(update_kernel, matrix),
             grid=(tok_count,),
             out_shape=[jax.ShapeDtypeStruct(s.shape, f32) for s in state],
-            in_specs=[SCALARS, grad_spec] + [state_spec] * 3 + [ANYWHERE] * len(held),
+            in_specs=[SCALARS, grad_spec, grad_spec] + [state_spec] * 3 + [ANYWHERE] * len(held),
             out_specs=[state_spec] * 3,
-            input_output_aliases={5 + i: i for i in range(len(held))},
+            input_output_aliases={6 + i: i for i in range(len(held))},
             compiler_params=pltpu.CompilerParams(vmem_limit_bytes=VMEM_BYTES),
             cost_estimate=pl.CostEstimate(
-                flops=grads.size * 12, bytes_accessed=grads.size * 28, transcendentals=grads.size
+                flops=size * 12, bytes_accessed=size * 28, transcendentals=size
             ),
-            name=f"update_{matrix}",
-        )(kept, grads, *state, *held)
-
+        )(kept, *grads, *state, *held)
+
+    far_place_ids = flip_tok(place_ids, 2)
     input_groups = gather_rows(inputs)
     weights_first = gather_weights(0)
     cotangent_groups = gather_rows(cotangent)
     weights_second = gather_weights(1)
+    late = gather_late()
     token_rows, *pre_part = forward(0, False, input_groups, weights_first)
-    preact = reduce_plane(*pre_part)
+    pre_terms = reduce_plane(*pre_part)
     grad_rows, *back_part = forward(1, True, cotangent_groups, weights_second)
-    hidden = gather_plane(activate(preact).astype(bf16))
-    hidden_grad = reduce_plane(*back_part)
-    pre_grad = gather_plane((hidden_grad * gelu_slope(preact)).astype(bf16))
+    back_terms = reduce_plane(*back_part)
+    piece = (part, hidden_span)
+    outs = [jax.ShapeDtypeStruct(piece, bf16), jax.ShapeDtypeStruct(piece, f32)]
+    hidden_piece, preact = over_columns(activate_kernel, outs, pre_terms, 2)
+    hidden = gather_plane(hidden_piece)
+    (grad_piece,) = over_columns(slope_kernel, outs[:1], [*back_terms, preact], 2)
+    pre_grad = gather_plane(grad_piece)
     layer_out = reduce_rows(backward(1, False, *hidden, weights_second))
-    second_grad = gradient(1, grad_rows, *hidden)
     grad_in = reduce_rows(backward(0, True, *pre_grad, weights_first))
-    first_grad = gradient(0, token_rows, *pre_grad)
+    second_grad = gradient(1, grad_rows, *hidden, late)
+    first_grad = gradient(0, token_rows, *pre_grad, late)
     held = update(1, second_grad, ())
     return (layer_out, grad_in, *update(0, first_grad, held))
 

time: 436 us -> 418 us (0.959)
  waiting for transfers between devices: 267 us -> 202 us
  starting transfers between devices: 53.9 us -> 87.6 us
  Pallas kernels: 82.2 us -> 108 us
  other arithmetic: 15.1 us -> 4.3 us
    ppermute x12, waiting for transfers between devices: 149 us -> 85.6 us  [across(): return lax.ppermute(array, ('mem', 'tok'), table)]
    ppermute x12 -> x21, waiting for transfers between devices: 34.8 us -> 88.8 us  [shift_hid(): lax.ppermute(array, 'hid', [(i, (i + shift) % hid_count) for i in range(h...]
    ppermute x12 -> x21, starting transfers between devices: 20.3 us -> 58.5 us  [shift_hid(): lax.ppermute(array, 'hid', [(i, (i + shift) % hid_count) for i in range(h...]
    ppermute x4 -> x7, waiting for transfers between devices: 60.9 us -> 27.3 us  [shift_mem(): lax.ppermute(array, 'mem', [(i, (i + shift) % mem_count) for i in range(m...]
    pallas_call x2 -> x8, Pallas kernels: 25.6 us -> 51.2 us  [the longest x2 26.8 us: update(): pl.pallas_call(functools.partial(update_kernel, matrix), grid=(tok_count,...]
    all_to_all x2, waiting for transfers between devices: 15.6 us -> 0.01 us  [gather_weights(): lax.all_to_all(narrow, 'tok', split_axis=0, concat_axis=0, tiled=True)]
    all_to_all x2 -> x0, starting transfers between devices: 9.93 us -> none  [gradient(): lax.all_to_all(sendable, 'tok', split_axis=0, concat_axis=0, tiled=True)]
    ppermute x4 -> x8, waiting for transfers between devices: 6.8 us -> 0.02 us  [flip_tok(): return lax.ppermute(array, 'tok', [(i, i ^ bit) for i in range(tok_count)])]
  transfers between devices with their start and end apart: 36 -> 50, of which waited for: 19 -> 24; matrix products, arithmetic and copies ran while one was open for 6% -> 3% of each run, Pallas kernels for 14% -> 22%
where the time goes in v2:
time: 418 us; the launch traced here: 417 us
  waiting for transfers between devices  202 us (48%)
  Pallas kernels  108 us (26%)
  starting transfers between devices  87.6 us (21%)
  local copies, waits for them, and re-layouts  14.5 us (3%)
  other arithmetic  4.3 us (1%)
    ppermute x21, waiting for transfers between devices, shift_hid(): lax.ppermute(array, 'hid', [(i, (i + shift) % hid_count) for i in range(h...  88.8 us
    ppermute x12, waiting for transfers between devices, across(): return lax.ppermute(array, ('mem', 'tok'), table)  85.6 us
    ppermute x21, starting transfers between devices, shift_hid(): lax.ppermute(array, 'hid', [(i, (i + shift) % hid_count) for i in range(h...  58.5 us
    pallas_call x6, Pallas kernels, call(): pl.pallas_call(kernel, out_shape=outs, in_specs=[SCALARS] * len(scalars)...  56.6 us
    ppermute x7, waiting for transfers between devices, shift_mem(): lax.ppermute(array, 'mem', [(i, (i + shift) % mem_count) for i in range(m...  27.3 us
    pallas_call x2, Pallas kernels, update(): pl.pallas_call(functools.partial(update_kernel, matrix), grid=(tok_count,...  26.8 us
    pallas_call x4, Pallas kernels, over_columns(): pl.pallas_call(kernel, grid=(steps,), out_shape=outs, in_specs=[spec(a.sh...  15.6 us
    ppermute x12, starting transfers between devices, across(): return lax.ppermute(array, ('mem', 'tok'), table)  13.4 us
  transfers between devices with their start and end apart: 50, of which 24 were waited for; matrix products, arithmetic and copies ran while one was open for 3% of the time, Pallas kernels for 22%

profile of v2, /device:TPU:0, one launch (start us, length us, event | category | flops | bytes accessed | tf_op | source)
XLA Modules:
  0.0 416.9 jit_solution(2519985994039517742)
XLA Ops:
  9.4 4.5 %collective-permute-start.2 = (bf16[32,3072]{1,0:T(8,128)(2,1)S(1)}, bf16[32,3072]{1,0:T(8,128)(2,1)S(1)}, u32[]{:S(2)}, u32[]{:S(2)}) collective-permute-start(bf16[32,3072]{1,0:T(8,128)(2,1)S(1)} %copy-done.13), channel_id=1, source_target_pairs={{0,12},{4,0},{8,4},{12,8},{1,13},{5,1},{9,5},{13,9},{2,14},{6,2},{... | collective-permute-start | bytes 589832 | tf_op jit(solution)/shard_map/ppermute | solution.py:325
  23.9 4.6 %collective-permute-done = bf16[32,3072]{1,0:T(8,128)(2,1)S(1)} collective-permute-done((bf16[32,3072]{1,0:T(8,128)(2,1)S(1)}, bf16[32,3072]{1,0:T(8,128)(2,1)S(1)}, u32[]{:S(2)}, u32[]{:S(2)}) %collective-permute-start) | collective-permute-done | bytes 196640 | tf_op jit(solution)/shard_map/ppermute | solution.py:325
  28.6 12.7 %collective-permute-start.20 = (bf16[32,3072]{1,0:T(8,128)(2,1)S(1)}, bf16[32,3072]{1,0:T(8,128)(2,1)}, u32[]{:S(2)}, u32[]{:S(2)}) collective-permute-start(bf16[32,3072]{1,0:T(8,128)(2,1)S(1)} %copy-done.14), channel_id=1, source_target_pairs={{0,4},{4,8},{8,12},{12,0},{1,5},{5,9},{9,13},{13,1},{2,6},{6,10},{... | collective-permute-start | bytes 589832 | tf_op jit(solution)/shard_map/ppermute | solution.py:325
  43.0 4.5 %all-to-all-start.1 = ((bf16[4,18,128,128]{3,2,1,0:T(8,128)(2,1)}), bf16[4,18,128,128]{3,2,1,0:T(8,128)(2,1)}, u32[]{:S(2)}, u32[]{:S(2)}) async-start(bf16[4,18,128,128]{3,2,1,0:T(8,128)(2,1)} %shard_map.114), calls=%async_computation.1 | async-start | bytes 4718592 | tf_op jit(solution)/shard_map/all_to_all | solution.py:366
  53.5 8.5 %collective-permute-done.3.refs_1_ = bf16[128,3072]{1,0:T(8,128)(2,1)} collective-permute-done((bf16[128,3072]{1,0:T(8,128)(2,1)S(1)}, bf16[128,3072]{1,0:T(8,128)(2,1)}, u32[]{:S(2)}, u32[]{:S(2)}) %collective-permute-start.3) | collective-permute-done | bytes 786464 | tf_op jit(solution)/shard_map/ppermute | solution.py:328
  62.0 10.4 %shard_map.111 = (bf16[256,3072]{1,0:T(8,128)(2,1)}, f32[2,64,6144]{2,1,0:T(8,128)}, f32[2,64,6144]{2,1,0:T(8,128)}) custom-call(s32[2,4]{1,0:T(2,128)} %bitcast.33, s32[2,144]{1,0:T(2,128)} %bitcast.26, bf16[128,3072]{1,0:T(8,128)(2,1)} %copy-done.12, bf16[128,3072]{1,0:T(8,128)(2,1)} %collective-permute-done.3.refs_1_, bf16[72,128,128]{2,1,0:T(8,128)(2,1)} %bitcast.14), custom_call_target="tpu_custom_call" | custom-call | flops 603979776 | bytes 11796480 | tf_op jit(solution)/shard_map/pallas_call | solution.py:287
  76.1 7.4 %shard_map.116 = (bf16[256,3072]{1,0:T(8,128)(2,1)}, f32[2,64,6144]{2,1,0:T(8,128)}, f32[2,64,6144]{2,1,0:T(8,128)}) custom-call(s32[2,4]{1,0:T(2,128)} %bitcast.34, s32[2,144]{1,0:T(2,128)} %bitcast.27, bf16[128,3072]{1,0:T(8,128)(2,1)} %constant_dynamic-update-slice_fusion.4.refs_0_, bf16[128,3072]{1,0:T(8,128)(2,1)} %collective-permute-done.23.refs_1_, ...), custom_call_target="tpu_custom_call" | custom-call | flops 603979776 | bytes 11796480 | tf_op jit(solution)/shard_map/pallas_call | solution.py:287
  85.2 4.9 %shard_map.112 = (f32[32,6144]{1,0:T(8,128)}, f32[32,6144]{1,0:T(8,128)}, f32[32,6144]{1,0:T(8,128)}, f32[32,6144]{1,0:T(8,128)}) custom-call(f32[2,64,6144]{2,1,0:T(8,128)} %get-tuple-element.39.keep_ref, f32[2,64,6144]{2,1,0:T(8,128)} %copy-done.7), custom_call_target="tpu_custom_call" | custom-call | flops 3145728 | bytes 9437184 | tf_op jit(solution)/shard_map/pallas_call | solution.py:389
  95.3 4.9 %shard_map.117 = (f32[32,6144]{1,0:T(8,128)}, f32[32,6144]{1,0:T(8,128)}, f32[32,6144]{1,0:T(8,128)}, f32[32,6144]{1,0:T(8,128)}) custom-call(f32[2,64,6144]{2,1,0:T(8,128)} %get-tuple-element.50.keep_ref, f32[2,64,6144]{2,1,0:T(8,128)} %copy-done.6), custom_call_target="tpu_custom_call" | custom-call | flops 3145728 | bytes 9437184 | tf_op jit(solution)/shard_map/pallas_call | solution.py:389
  102.2 8.5 %collective-permute-done.5.refs_1_ = f32[32,6144]{1,0:T(8,128)S(1)} collective-permute-done((f32[32,6144]{1,0:T(8,128)}, f32[32,6144]{1,0:T(8,128)S(1)}, u32[]{:S(2)}, u32[]{:S(2)}) %collective-permute-start.5) | collective-permute-done | bytes 786464 | tf_op jit(solution)/shard_map/ppermute | solution.py:339
  112.7 16.4 %collective-permute-done.7.refs_3_ = f32[32,6144]{1,0:T(8,128)S(1)} collective-permute-done((f32[32,6144]{1,0:T(8,128)}, f32[32,6144]{1,0:T(8,128)S(1)}, u32[]{:S(2)}, u32[]{:S(2)}) %collective-permute-start.7) | collective-permute-done | bytes 786464 | tf_op jit(solution)/shard_map/ppermute | solution.py:339
  136.3 8.0 %collective-permute-done.25.refs_1_ = f32[32,6144]{1,0:T(8,128)S(1)} collective-permute-done((f32[32,6144]{1,0:T(8,128)}, f32[32,6144]{1,0:T(8,128)S(1)}, u32[]{:S(2)}, u32[]{:S(2)}) %collective-permute-start.25) | collective-permute-done | bytes 786464 | tf_op jit(solution)/shard_map/ppermute | solution.py:339
  147.0 15.9 %collective-permute-done.27.refs_3_ = f32[32,6144]{1,0:T(8,128)S(1)} collective-permute-done((f32[32,6144]{1,0:T(8,128)}, f32[32,6144]{1,0:T(8,128)S(1)}, u32[]{:S(2)}, u32[]{:S(2)}) %collective-permute-start.27) | collective-permute-done | bytes 786464 | tf_op jit(solution)/shard_map/ppermute | solution.py:339
  171.5 8.8 %collective-permute-done.9 = bf16[32,6144]{1,0:T(8,128)(2,1)S(1)} collective-permute-done((bf16[32,6144]{1,0:T(8,128)(2,1)}, bf16[32,6144]{1,0:T(8,128)(2,1)S(1)}, u32[]{:S(2)}, u32[]{:S(2)}) %collective-permute-start.9) | collective-permute-done | bytes 393248 | tf_op jit(solution)/shard_map/ppermute | solution.py:339
  180.5 7.7 %collective-permute-done.30 = bf16[32,6144]{1,0:T(8,128)(2,1)S(1)} collective-permute-done((bf16[32,6144]{1,0:T(8,128)(2,1)}, bf16[32,6144]{1,0:T(8,128)(2,1)S(1)}, u32[]{:S(2)}, u32[]{:S(2)}) %collective-permute-start.30) | collective-permute-done | bytes 393248 | tf_op jit(solution)/shard_map/ppermute | solution.py:339
  188.2 8.2 %collective-permute-done.29 = bf16[32,6144]{1,0:T(8,128)(2,1)S(1)} collective-permute-done((bf16[32,6144]{1,0:T(8,128)(2,1)}, bf16[32,6144]{1,0:T(8,128)(2,1)S(1)}, u32[]{:S(2)}, u32[]{:S(2)}) %collective-permute-start.29) | collective-permute-done | bytes 393248 | tf_op jit(solution)/shard_map/ppermute | solution.py:339
  196.4 8.1 %collective-permute-done.28 = bf16[32,6144]{1,0:T(8,128)(2,1)S(1)} collective-permute-done((bf16[32,6144]{1,0:T(8,128)(2,1)}, bf16[32,6144]{1,0:T(8,128)(2,1)S(1)}, u32[]{:S(2)}, u32[]{:S(2)}) %collective-permute-start.28) | collective-permute-done | bytes 393248 | tf_op jit(solution)/shard_map/ppermute | solution.py:339
  205.1 11.2 %collective-permute-done.42 = bf16[2,32,3072]{2,1,0:T(8,128)(2,1)S(1)} collective-permute-done((bf16[2,32,3072]{2,1,0:T(8,128)(2,1)S(1)}, bf16[2,32,3072]{2,1,0:T(8,128)(2,1)S(1)}, u32[]{:S(2)}, u32[]{:S(2)}) %collective-permute-start.42) | collective-permute-done | bytes 393248 | tf_op jit(solution)/shard_map/ppermute | solution.py:328
  225.4 6.1 %shard_map.115 = (f32[128,1536]{1,0:T(8,128)}, f32[128,1536]{1,0:T(8,128)}, f32[128,1536]{1,0:T(8,128)}, f32[128,1536]{1,0:T(8,128)}) custom-call(s32[2,4]{1,0:T(2,128)} %bitcast.35, s32[2,144]{1,0:T(2,128)} %bitcast.28, bf16[2,64,6144]{2,1,0:T(8,128)(2,1)} %bitcast.17, bf16[2,64,6144]{2,1,0:T(8,128)(2,1)} %copy-done.4, ...), custom_call_target="tpu_custom_call" | custom-call | flops 603979776 | bytes 8650752 | tf_op jit(solution)/shard_map/pallas_call | solution.py:287
  233.6 9.7 %shard_map.119 = (f32[128,1536]{1,0:T(8,128)}, f32[128,1536]{1,0:T(8,128)}, f32[128,1536]{1,0:T(8,128)}, f32[128,1536]{1,0:T(8,128)}) custom-call(s32[2,4]{1,0:T(2,128)} %bitcast.36, s32[2,144]{1,0:T(2,128)} %bitcast.29, bf16[2,64,6144]{2,1,0:T(8,128)(2,1)} %bitcast.20, bf16[2,64,6144]{2,1,0:T(8,128)(2,1)} %copy-done.5, bf16[72,128,128]{2,1,0:T(8,128)(2,1)} %bitcast.15), custom_call_target="tpu_custom_call" | custom-call | flops 603979776 | bytes 8650752 | tf_op jit(solution)/shard_map/pallas_call | solution.py:287
  243.3 47.7 %collective-permute-done.44.refs_5_ = bf16[2,2,32,3072]{3,2,1,0:T(8,128)(2,1)} collective-permute-done((bf16[2,2,32,3072]{3,2,1,0:T(8,128)(2,1)S(1)}, bf16[2,2,32,3072]{3,2,1,0:T(8,128)(2,1)}, u32[]{:S(2)}, u32[]{:S(2)}) %collective-permute-start.44) | collective-permute-done | bytes 786464 | tf_op jit(solution)/shard_map/ppermute | solution.py:325
  291.0 10.8 %shard_map.121 = (f32[2,18,128,128]{3,2,1,0:T(8,128)}, f32[2,18,128,128]{3,2,1,0:T(8,128)}) custom-call(s32[2,4]{1,0:T(2,128)} %bitcast.37, s32[2,144]{1,0:T(2,128)} %bitcast.30, s32[2,144]{1,0:T(2,128)} %copy-done.27, bf16[256,3072]{1,0:T(8,128)(2,1)} %get-tuple-element.64.refs_0_, bf16[2,64,6144]{2,1,0:T(8,128)(2,1)} %bitcast.18, ...), custom_call_target="tpu_custom_call" | custom-call | flops 603979776 | bytes 12582912 | tf_op jit(solution)/shard_map/pallas_call | solution.py:287
  301.9 12.3 %shard_map.120 = (f32[2,18,128,128]{3,2,1,0:T(8,128)}, f32[2,18,128,128]{3,2,1,0:T(8,128)}) custom-call(s32[2,4]{1,0:T(2,128)} %bitcast.38, s32[2,144]{1,0:T(2,128)} %bitcast.31, s32[2,144]{1,0:T(2,128)} %copy-done.27, bf16[256,3072]{1,0:T(8,128)(2,1)} %get-tuple-element.61.refs_0_, bf16[2,64,6144]{2,1,0:T(8,128)(2,1)} %bitcast.21, ...), custom_call_target="tpu_custom_call" | custom-call | flops 603979776 | bytes 12582912 | tf_op jit(solution)/shard_map/pallas_call | solution.py:287
  328.3 8.4 %collective-permute-done.14 = f32[32,1536]{1,0:T(8,128)S(1)} collective-permute-done((f32[32,1536]{1,0:T(8,128)S(1)}, f32[32,1536]{1,0:T(8,128)S(1)}, u32[]{:S(2)}, u32[]{:S(2)}) %collective-permute-start.14) | collective-permute-done | bytes 196640 | tf_op jit(solution)/shard_map/ppermute | solution.py:325
  336.8 5.5 %collective-permute-start.33 = (f32[32,1536]{1,0:T(8,128)S(1)}, f32[32,1536]{1,0:T(8,128)S(1)}, u32[]{:S(2)}, u32[]{:S(2)}) collective-permute-start(f32[32,1536]{1,0:T(8,128)S(1)} %get-tuple-element.73), channel_id=1, source_target_pairs={{0,12},{4,0},{8,4},{12,8},{1,13},{5,1},{9,5},{13,9},{2,14},{6,2},{... | collective-permute-start | bytes 589832 | tf_op jit(solution)/shard_map/ppermute | solution.py:325
  342.3 9.4 %collective-permute-start.35 = (f32[32,1536]{1,0:T(8,128)S(1)}, f32[32,1536]{1,0:T(8,128)S(1)}, u32[]{:S(2)}, u32[]{:S(2)}) collective-permute-start(f32[32,1536]{1,0:T(8,128)S(1)} %get-tuple-element.74), channel_id=1, source_target_pairs={{0,4},{4,8},{8,12},{12,0},{1,5},{5,9},{9,13},{13,1},{2,6},{6,10},{... | collective-permute-start | bytes 589832 | tf_op jit(solution)/shard_map/ppermute | solution.py:325
  353.8 7.3 %collective-permute-done.33 = f32[32,1536]{1,0:T(8,128)S(1)} collective-permute-done((f32[32,1536]{1,0:T(8,128)S(1)}, f32[32,1536]{1,0:T(8,128)S(1)}, u32[]{:S(2)}, u32[]{:S(2)}) %collective-permute-start.33) | collective-permute-done | bytes 196640 | tf_op jit(solution)/shard_map/ppermute | solution.py:325
  361.1 7.6 %collective-permute-start.39 = (f32[32,1536]{1,0:T(8,128)S(1)}, f32[32,1536]{1,0:T(8,128)S(1)}, u32[]{:S(2)}, u32[]{:S(2)}) collective-permute-start(f32[32,1536]{1,0:T(8,128)S(1)} %get-tuple-element.77), channel_id=1, source_target_pairs={{0,4},{4,8},{8,12},{12,0},{1,5},{5,9},{9,13},{13,1},{2,6},{6,10},{... | collective-permute-start | bytes 589832 | tf_op jit(solution)/shard_map/ppermute | solution.py:325
  371.3 6.6 %collective-permute-done.37 = f32[32,1536]{1,0:T(8,128)S(1)} collective-permute-done((f32[32,1536]{1,0:T(8,128)S(1)}, f32[32,1536]{1,0:T(8,128)S(1)}, u32[]{:S(2)}, u32[]{:S(2)}) %collective-permute-start.37) | collective-permute-done | bytes 196640 | tf_op jit(solution)/shard_map/ppermute | solution.py:325
  378.0 8.5 %collective-permute-done.38 = f32[32,1536]{1,0:T(8,128)S(1)} collective-permute-done((f32[32,1536]{1,0:T(8,128)S(1)}, f32[32,1536]{1,0:T(8,128)S(1)}, u32[]{:S(2)}, u32[]{:S(2)}) %collective-permute-start.38) | collective-permute-done | bytes 196640 | tf_op jit(solution)/shard_map/ppermute | solution.py:325
  388.7 13.4 %shard_map.122 = (f32[2,4,1,18,128,128]{5,4,3,2,1,0:T(8,128)}, f32[2,4,1,18,128,128]{5,4,3,2,1,0:T(8,128)}, f32[2,4,1,18,128,128]{5,4,3,2,1,0:T(8,128)}) custom-call(s32[2,4]{1,0:T(2,128)} %bitcast.39, f32[2,18,128,128]{3,2,1,0:T(8,128)} %get-tuple-element.65.keep_ref, f32[2,18,128,128]{3,2,1,0:T(8,128)} %copy-done.9, ...), custom_call_target="tpu_custom_call" | custom-call | flops 14155776 | bytes 33030144 | tf_op jit(solution)/shard_map/pallas_call | solution.py:473
  403.5 13.4 %shard_map.123 = (f32[2,4,1,18,128,128]{5,4,3,2,1,0:T(8,128)}, f32[2,4,1,18,128,128]{5,4,3,2,1,0:T(8,128)}, f32[2,4,1,18,128,128]{5,4,3,2,1,0:T(8,128)}) custom-call(s32[2,4]{1,0:T(2,128)} %bitcast.40, f32[2,18,128,128]{3,2,1,0:T(8,128)} %get-tuple-element.62.keep_ref, ...), custom_call_target="tpu_custom_call", output_to_operand_aliasing={{0}: (6, {}), {1}: (7, {}), {2}: (8, {})} | custom-call | flops 14155776 | bytes 33030144 | tf_op jit(solution)/shard_map/pallas_call | solution.py:473
  (167 shorter events, 93.9 us)
Async XLA Ops:
  5.0 38.0 %all-to-all-start = ((bf16[4,18,128,128]{3,2,1,0:T(8,128)(2,1)}), bf16[4,18,128,128]{3,2,1,0:T(8,128)(2,1)S(1)}, u32[]{:S(2)}, u32[]{:S(2)}) async-start(bf16[4,18,128,128]{3,2,1,0:T(8,128)(2,1)} %shard_map.110), calls=%async_computation | async-start | bytes 4718592 | tf_op jit(solution)/shard_map/all_to_all | solution.py:366
  9.4 32.0 %collective-permute-start.2 = (bf16[32,3072]{1,0:T(8,128)(2,1)S(1)}, bf16[32,3072]{1,0:T(8,128)(2,1)S(1)}, u32[]{:S(2)}, u32[]{:S(2)}) collective-permute-start(bf16[32,3072]{1,0:T(8,128)(2,1)S(1)} %copy-done.13), channel_id=1, source_target_pairs={{0,12},{4,0},{8,4},{12,8},{1,13},{5,1},{9,5},{13,9},{2,14},{6,2},{... | collective-permute-start | bytes 589832 | tf_op jit(solution)/shard_map/ppermute | solution.py:325
  13.9 27.4 %collective-permute-start.1 = (bf16[32,3072]{1,0:T(8,128)(2,1)S(1)}, bf16[32,3072]{1,0:T(8,128)(2,1)S(1)}, u32[]{:S(2)}, u32[]{:S(2)}) collective-permute-start(bf16[32,3072]{1,0:T(8,128)(2,1)S(1)} %copy-done.13), channel_id=1, source_target_pairs={{0,8},{4,12},{8,0},{12,4},{1,9},{5,13},{9,1},{13,5},{2,10},{6,14},... | collective-permute-start | bytes 589832 | tf_op jit(solution)/shard_map/ppermute | solution.py:325
  14.9 35.8 %collective-permute-start.22 = (bf16[32,3072]{1,0:T(8,128)(2,1)S(1)}, bf16[32,3072]{1,0:T(8,128)(2,1)}, u32[]{:S(2)}, u32[]{:S(2)}) collective-permute-start(bf16[32,3072]{1,0:T(8,128)(2,1)S(1)} %copy-done.14), channel_id=1, source_target_pairs={{0,12},{4,0},{8,4},{12,8},{1,13},{5,1},{9,5},{13,9},{2,14},{6,2},{... | collective-permute-start | bytes 589832 | tf_op jit(solution)/shard_map/ppermute | solution.py:325
  17.7 31.4 %collective-permute-start.21 = (bf16[32,3072]{1,0:T(8,128)(2,1)S(1)}, bf16[32,3072]{1,0:T(8,128)(2,1)}, u32[]{:S(2)}, u32[]{:S(2)}) collective-permute-start(bf16[32,3072]{1,0:T(8,128)(2,1)S(1)} %copy-done.14), channel_id=1, source_target_pairs={{0,8},{4,12},{8,0},{12,4},{1,9},{5,13},{9,1},{13,5},{2,10},{6,14},... | collective-permute-start | bytes 589832 | tf_op jit(solution)/shard_map/ppermute | solution.py:325
  41.4 20.6 %collective-permute-start.3 = (bf16[128,3072]{1,0:T(8,128)(2,1)S(1)}, bf16[128,3072]{1,0:T(8,128)(2,1)}, u32[]{:S(2)}, u32[]{:S(2)}) collective-permute-start(bf16[128,3072]{1,0:T(8,128)(2,1)S(1)} %constant_dynamic-update-slice_fusion.refs_0_), channel_id=1, source_target_pairs={{0,16},{16,0},{1,17},{17,1},{2,18},{18,2},{3,19},{19,3},{4,20},{20... | collective-permute-start | bytes 2359304 | tf_op jit(solution)/shard_map/ppermute | solution.py:328
  43.0 33.1 %all-to-all-start.1 = ((bf16[4,18,128,128]{3,2,1,0:T(8,128)(2,1)}), bf16[4,18,128,128]{3,2,1,0:T(8,128)(2,1)}, u32[]{:S(2)}, u32[]{:S(2)}) async-start(bf16[4,18,128,128]{3,2,1,0:T(8,128)(2,1)} %shard_map.114), calls=%async_computation.1 | async-start | bytes 4718592 | tf_op jit(solution)/shard_map/all_to_all | solution.py:366
  52.4 23.7 %collective-permute-start.23 = (bf16[128,3072]{1,0:T(8,128)(2,1)}, bf16[128,3072]{1,0:T(8,128)(2,1)}, u32[]{:S(2)}, u32[]{:S(2)}) collective-permute-start(bf16[128,3072]{1,0:T(8,128)(2,1)} %constant_dynamic-update-slice_fusion.4.refs_0_), channel_id=1, source_target_pairs={{0,16},{16,0},{1,17},{17,1},{2,18},{18,2},{3,19},{19,3},{4,20},{20... | collective-permute-start | bytes 2359304 | tf_op jit(solution)/shard_map/ppermute | solution.py:328
  90.1 20.6 %collective-permute-start.5 = (f32[32,6144]{1,0:T(8,128)}, f32[32,6144]{1,0:T(8,128)S(1)}, u32[]{:S(2)}, u32[]{:S(2)}) collective-permute-start(f32[32,6144]{1,0:T(8,128)} %get-tuple-element.42), channel_id=1, source_target_pairs={{0,2},{1,3},{2,0},{3,1},{16,18},{17,19},{18,16},{19,17},{4,6},{5,7... | collective-permute-start | bytes 2359304 | tf_op jit(solution)/shard_map/ppermute | solution.py:339
  92.1 20.6 %collective-permute-start.6 = (f32[32,6144]{1,0:T(8,128)}, f32[32,6144]{1,0:T(8,128)S(1)}, u32[]{:S(2)}, u32[]{:S(2)}) collective-permute-start(f32[32,6144]{1,0:T(8,128)} %get-tuple-element.43), channel_id=1, source_target_pairs={{0,16},{1,17},{2,18},{3,19},{16,0},{17,1},{18,2},{19,3},{4,20},{5,... | collective-permute-start | bytes 2359304 | tf_op jit(solution)/shard_map/ppermute | solution.py:339
  92.1 37.0 %collective-permute-start.7 = (f32[32,6144]{1,0:T(8,128)}, f32[32,6144]{1,0:T(8,128)S(1)}, u32[]{:S(2)}, u32[]{:S(2)}) collective-permute-start(f32[32,6144]{1,0:T(8,128)} %get-tuple-element.44), channel_id=1, source_target_pairs={{0,18},{1,19},{2,16},{3,17},{16,2},{17,3},{18,0},{19,1},{4,22},{5,... | collective-permute-start | bytes 2359304 | tf_op jit(solution)/shard_map/ppermute | solution.py:339
  100.2 44.0 %collective-permute-start.25 = (f32[32,6144]{1,0:T(8,128)}, f32[32,6144]{1,0:T(8,128)S(1)}, u32[]{:S(2)}, u32[]{:S(2)}) collective-permute-start(f32[32,6144]{1,0:T(8,128)} %get-tuple-element.53), channel_id=1, source_target_pairs={{0,2},{1,3},{2,0},{3,1},{16,18},{17,19},{18,16},{19,17},{4,6},{5,7... | collective-permute-start | bytes 2359304 | tf_op jit(solution)/shard_map/ppermute | solution.py:339
  102.2 44.6 %collective-permute-start.26 = (f32[32,6144]{1,0:T(8,128)}, f32[32,6144]{1,0:T(8,128)S(1)}, u32[]{:S(2)}, u32[]{:S(2)}) collective-permute-start(f32[32,6144]{1,0:T(8,128)} %get-tuple-element.54), channel_id=1, source_target_pairs={{0,16},{1,17},{2,18},{3,19},{16,0},{17,1},{18,2},{19,3},{4,20},{5,... | collective-permute-start | bytes 2359304 | tf_op jit(solution)/shard_map/ppermute | solution.py:339
  110.7 52.2 %collective-permute-start.27 = (f32[32,6144]{1,0:T(8,128)}, f32[32,6144]{1,0:T(8,128)S(1)}, u32[]{:S(2)}, u32[]{:S(2)}) collective-permute-start(f32[32,6144]{1,0:T(8,128)} %get-tuple-element.55), channel_id=1, source_target_pairs={{0,18},{1,19},{2,16},{3,17},{16,2},{17,3},{18,0},{19,1},{4,22},{5,... | collective-permute-start | bytes 2359304 | tf_op jit(solution)/shard_map/ppermute | solution.py:339
  132.8 38.5 %collective-permute-start.10 = (bf16[32,6144]{1,0:T(8,128)(2,1)}, bf16[32,6144]{1,0:T(8,128)(2,1)S(1)}, u32[]{:S(2)}, u32[]{:S(2)}) collective-permute-start(bf16[32,6144]{1,0:T(8,128)(2,1)} %get-tuple-element.45), channel_id=1, source_target_pairs={{0,18},{1,19},{2,16},{3,17},{16,2},{17,3},{18,0},{19,1},{4,22},{5,... | collective-permute-start | bytes 1179656 | tf_op jit(solution)/shard_map/ppermute | solution.py:339
  134.2 46.0 %collective-permute-start.9 = (bf16[32,6144]{1,0:T(8,128)(2,1)}, bf16[32,6144]{1,0:T(8,128)(2,1)S(1)}, u32[]{:S(2)}, u32[]{:S(2)}) collective-permute-start(bf16[32,6144]{1,0:T(8,128)(2,1)} %get-tuple-element.45), channel_id=1, source_target_pairs={{0,16},{1,17},{2,18},{3,19},{16,0},{17,1},{18,2},{19,3},{4,20},{5,... | collective-permute-start | bytes 1179656 | tf_op jit(solution)/shard_map/ppermute | solution.py:339
  144.2 36.1 %collective-permute-start.8 = (bf16[32,6144]{1,0:T(8,128)(2,1)}, bf16[32,6144]{1,0:T(8,128)(2,1)S(1)}, u32[]{:S(2)}, u32[]{:S(2)}) collective-permute-start(bf16[32,6144]{1,0:T(8,128)(2,1)} %get-tuple-element.45), channel_id=1, source_target_pairs={{0,2},{1,3},{2,0},{3,1},{16,18},{17,19},{18,16},{19,17},{4,6},{5,7... | collective-permute-start | bytes 1179656 | tf_op jit(solution)/shard_map/ppermute | solution.py:339
  146.7 58.0 %collective-permute-start.41 = (bf16[2,32,3072]{2,1,0:T(8,128)(2,1)}, bf16[2,32,3072]{2,1,0:T(8,128)(2,1)S(1)}, u32[]{:S(2)}, u32[]{:S(2)}) collective-permute-start(bf16[2,32,3072]{2,1,0:T(8,128)(2,1)} %pad_maximum_fusion.3), channel_id=1, source_target_pairs={{0,2},{1,3},{2,0},{3,1},{4,6},{5,7},{6,4},{7,5},{8,10},{9,11},{10,... | collective-permute-start | bytes 1179656 | tf_op jit(solution)/shard_map/ppermute | solution.py:331
  166.9 21.3 %collective-permute-start.30 = (bf16[32,6144]{1,0:T(8,128)(2,1)}, bf16[32,6144]{1,0:T(8,128)(2,1)S(1)}, u32[]{:S(2)}, u32[]{:S(2)}) collective-permute-start(bf16[32,6144]{1,0:T(8,128)(2,1)} %shard_map.118), channel_id=1, source_target_pairs={{0,18},{1,19},{2,16},{3,17},{16,2},{17,3},{18,0},{19,1},{4,22},{5,... | collective-permute-start | bytes 1179656 | tf_op jit(solution)/shard_map/ppermute | solution.py:339
  171.3 25.1 %collective-permute-start.29 = (bf16[32,6144]{1,0:T(8,128)(2,1)}, bf16[32,6144]{1,0:T(8,128)(2,1)S(1)}, u32[]{:S(2)}, u32[]{:S(2)}) collective-permute-start(bf16[32,6144]{1,0:T(8,128)(2,1)} %shard_map.118), channel_id=1, source_target_pairs={{0,16},{1,17},{2,18},{3,19},{16,0},{17,1},{18,2},{19,3},{4,20},{5,... | collective-permute-start | bytes 1179656 | tf_op jit(solution)/shard_map/ppermute | solution.py:339
  180.2 24.3 %collective-permute-start.28 = (bf16[32,6144]{1,0:T(8,128)(2,1)}, bf16[32,6144]{1,0:T(8,128)(2,1)S(1)}, u32[]{:S(2)}, u32[]{:S(2)}) collective-permute-start(bf16[32,6144]{1,0:T(8,128)(2,1)} %shard_map.118), channel_id=1, source_target_pairs={{0,2},{1,3},{2,0},{3,1},{16,18},{17,19},{18,16},{19,17},{4,6},{5,7... | collective-permute-start | bytes 1179656 | tf_op jit(solution)/shard_map/ppermute | solution.py:339
  180.5 43.2 %collective-permute-start.11 = (bf16[2,64,6144]{2,1,0:T(8,128)(2,1)S(1)}, bf16[2,64,6144]{2,1,0:T(8,128)(2,1)S(1)}, u32[]{:S(2)}, u32[]{:S(2)}) collective-permute-start(bf16[2,64,6144]{2,1,0:T(8,128)(2,1)S(1)} %bitcast.16), channel_id=1, source_target_pairs={{0,1},{1,0},{2,3},{3,2},{4,5},{5,4},{6,7},{7,6},{8,9},{9,8},{10,11... | collective-permute-start | bytes 4718600 | tf_op jit(solution)/shard_map/ppermute | solution.py:331
  204.7 26.9 %collective-permute-start.31 = (bf16[2,64,6144]{2,1,0:T(8,128)(2,1)S(1)}, bf16[2,64,6144]{2,1,0:T(8,128)(2,1)S(1)}, u32[]{:S(2)}, u32[]{:S(2)}) collective-permute-start(bf16[2,64,6144]{2,1,0:T(8,128)(2,1)S(1)} %bitcast.19), channel_id=1, source_target_pairs={{0,1},{1,0},{2,3},{3,2},{4,5},{5,4},{6,7},{7,6},{8,9},{9,8},{10,11... | collective-permute-start | bytes 4718600 | tf_op jit(solution)/shard_map/ppermute | solution.py:331
  216.3 26.9 %collective-permute-start.45 = (bf16[2,2,32,3072]{3,2,1,0:T(8,128)(2,1)S(1)}, bf16[2,2,32,3072]{3,2,1,0:T(8,128)(2,1)S(1)}, u32[]{:S(2)}, u32[]{:S(2)}) collective-permute-start(bf16[2,2,32,3072]{3,2,1,0:T(8,128)(2,1)S(1)} %pad_maximum_fusion.2.refs_3_), channel_id=1, source_target_pairs={{0,12},{4,0},{8,4},{12,8},{1,13},{5,1},{9,5},{13,9},{2,14},{6,2},{... | collective-permute-start | bytes 2359304 | tf_op jit(solution)/shard_map/ppermute | solution.py:325
  219.8 71.2 %collective-permute-start.44 = (bf16[2,2,32,3072]{3,2,1,0:T(8,128)(2,1)S(1)}, bf16[2,2,32,3072]{3,2,1,0:T(8,128)(2,1)}, u32[]{:S(2)}, u32[]{:S(2)}) collective-permute-start(bf16[2,2,32,3072]{3,2,1,0:T(8,128)(2,1)S(1)} %pad_maximum_fusion.2.refs_3_), channel_id=1, source_target_pairs={{0,8},{4,12},{8,0},{12,4},{1,9},{5,13},{9,1},{13,5},{2,10},{6,14},... | collective-permute-start | bytes 2359304 | tf_op jit(solution)/shard_map/ppermute | solution.py:325
  223.4 67.7 %collective-permute-start.43 = (bf16[2,2,32,3072]{3,2,1,0:T(8,128)(2,1)S(1)}, bf16[2,2,32,3072]{3,2,1,0:T(8,128)(2,1)}, u32[]{:S(2)}, u32[]{:S(2)}) collective-permute-start(bf16[2,2,32,3072]{3,2,1,0:T(8,128)(2,1)S(1)} %pad_maximum_fusion.2.refs_3_), channel_id=1, source_target_pairs={{0,4},{4,8},{8,12},{12,0},{1,5},{5,9},{9,13},{13,1},{2,6},{6,10},{... | collective-permute-start | bytes 2359304 | tf_op jit(solution)/shard_map/ppermute | solution.py:325
  231.5 82.7 %collective-permute-start.12 = (f32[128,1536]{1,0:T(8,128)}, f32[128,1536]{1,0:T(8,128)}, u32[]{:S(2)}, u32[]{:S(2)}) collective-permute-start(f32[128,1536]{1,0:T(8,128)} %get-tuple-element.47), channel_id=1, source_target_pairs={{0,16},{16,0},{1,17},{17,1},{2,18},{18,2},{3,19},{19,3},{4,20},{20... | collective-permute-start | bytes 2359304 | tf_op jit(solution)/shard_map/ppermute | solution.py:328
  231.6 84.1 %collective-permute-start.16 = (f32[128,1536]{1,0:T(8,128)}, f32[128,1536]{1,0:T(8,128)S(1)}, u32[]{:S(2)}, u32[]{:S(2)}) collective-permute-start(f32[128,1536]{1,0:T(8,128)} %get-tuple-element.49), channel_id=1, source_target_pairs={{0,16},{16,0},{1,17},{17,1},{2,18},{18,2},{3,19},{19,3},{4,20},{20... | collective-permute-start | bytes 2359304 | tf_op jit(solution)/shard_map/ppermute | solution.py:328
  243.2 72.6 %collective-permute-start.32 = (f32[128,1536]{1,0:T(8,128)}, f32[128,1536]{1,0:T(8,128)S(1)}, u32[]{:S(2)}, u32[]{:S(2)}) collective-permute-start(f32[128,1536]{1,0:T(8,128)} %get-tuple-element.58), channel_id=1, source_target_pairs={{0,16},{16,0},{1,17},{17,1},{2,18},{18,2},{3,19},{19,3},{4,20},{20... | collective-permute-start | bytes 2359304 | tf_op jit(solution)/shard_map/ppermute | solution.py:328
  301.9 85.3 %collective-permute-start.47 = (f32[2,18,128,128]{3,2,1,0:T(8,128)}, f32[2,18,128,128]{3,2,1,0:T(8,128)S(1)}, u32[]{:S(2)}, u32[]{:S(2)}) collective-permute-start(f32[2,18,128,128]{3,2,1,0:T(8,128)} %get-tuple-element.66), channel_id=1, source_target_pairs={{0,1},{1,0},{2,3},{3,2},{4,5},{5,4},{6,7},{7,6},{8,9},{9,8},{10,11... | collective-permute-start | bytes 7077896 | tf_op jit(solution)/shard_map/ppermute | solution.py:331
  314.2 87.9 %collective-permute-start.46 = (f32[2,18,128,128]{3,2,1,0:T(8,128)}, f32[2,18,128,128]{3,2,1,0:T(8,128)S(1)}, u32[]{:S(2)}, u32[]{:S(2)}) collective-permute-start(f32[2,18,128,128]{3,2,1,0:T(8,128)} %get-tuple-element.63), channel_id=1, source_target_pairs={{0,1},{1,0},{2,3},{3,2},{4,5},{5,4},{6,7},{7,6},{8,9},{9,8},{10,11... | collective-permute-start | bytes 7077896 | tf_op jit(solution)/shard_map/ppermute | solution.py:331
  336.8 24.3 %collective-permute-start.33 = (f32[32,1536]{1,0:T(8,128)S(1)}, f32[32,1536]{1,0:T(8,128)S(1)}, u32[]{:S(2)}, u32[]{:S(2)}) collective-permute-start(f32[32,1536]{1,0:T(8,128)S(1)} %get-tuple-element.73), channel_id=1, source_target_pairs={{0,12},{4,0},{8,4},{12,8},{1,13},{5,1},{9,5},{13,9},{2,14},{6,2},{... | collective-permute-start | bytes 589832 | tf_op jit(solution)/shard_map/ppermute | solution.py:325
  (47 other events, 764.8 us)

commit v3 on v2

--- a/solution.py
+++ b/solution.py
@@ -22,6 +22,7 @@
 VMEM_BYTES = 56 * 2**20
 UNROLL = 4
 CHUNKS = 2
+MEM, HID, TOK = "mem", "hid", "tok"
 
 
 def activate(values):
@@ -58,10 +59,9 @@
     return pl.ds(pl.multiple_of(index * size, size), size)
 
 
-def live_range(kept_ref, matrix, local_slots):
-    first = lax.axis_index("mem") * local_slots
-    count = jnp.clip(kept_ref[matrix, lax.axis_index("tok")] - first, 0, local_slots)
-    return first, count
+def owner_count(kept_ref, matrix, cell, owner, owned):
+    first = (lax.axis_index(MEM) * lax.axis_size(TOK) + owner) * owned
+    return first, jnp.clip(kept_ref[matrix, cell] - first, 0, owned)
 
 
 def over_slots(count, body):
@@ -80,17 +80,29 @@
     lax.fori_loop(groups * UNROLL, count, single, 0)
 
 
+def over_owners(matrix, kept_ref, weight_refs, body):
+    tok = lax.axis_index(TOK)
+    for turn, weight_ref in enumerate(weight_refs):
+        owned = weight_ref.shape[0]
+        first, count = owner_count(kept_ref, matrix, tok, tok ^ turn, owned)
+        over_slots(count, functools.partial(body, weight_ref, first))
+
+
 def relative(tok_count):
-    tok = lax.axis_index("tok")
+    tok = lax.axis_index(TOK)
     return (tok % 2) * (tok_count // 2) + tok // 2
 
 
 def forward_kernel(
     matrix, transposed, width_blocks, tok_count, hid_count, mem_count, kept_ref, place_ref, *refs
 ):
-    own_refs, (weight_ref, row_ref, keep_ref, send_ref) = refs[:mem_count], refs[mem_count:]
+    own_refs, weight_refs, (row_ref, keep_ref, send_ref) = (
+        refs[:mem_count],
+        refs[mem_count:-3],
+        refs[-3:],
+    )
     half = keep_ref.shape[1]
-    size = weight_ref.shape[-1]
+    _, size = weight_refs[0].shape[:2]
     rows = own_refs[0].shape[0]
     step = rows // hid_count
     part = rows // tok_count
@@ -104,9 +116,8 @@
             ]
     keep_ref[...] = jnp.zeros(keep_ref.shape, jnp.float32)
     send_ref[...] = jnp.zeros(send_ref.shape, jnp.float32)
-    first, count = live_range(kept_ref, matrix, weight_ref.shape[0])
-
-    def body(slots):
+
+    def body(weight_ref, first, slots):
         found = []
         for slot in slots:
             place = place_ref[matrix, first + slot]
@@ -119,28 +130,19 @@
                 keep_ref[group, :, spot] += product[start : start + half]
                 send_ref[group, :, spot] += product[start + half : start + rows]
 
-    over_slots(count, body)
+    over_owners(matrix, kept_ref, weight_refs, body)
 
 
 def backward_kernel(
-    matrix,
-    transposed,
-    width_blocks,
-    mem_count,
-    kept_ref,
-    place_ref,
-    own_ref,
-    pair_ref,
-    weight_ref,
-    *refs,
+    matrix, transposed, width_blocks, mem_count, kept_ref, place_ref, own_ref, pair_ref, *refs
 ):
-    out_refs, total_ref = refs[:-1], refs[-1]
-    size = weight_ref.shape[-1]
+    tok_count = lax.axis_size(TOK)
+    weight_refs, out_refs, total_ref = refs[:tok_count], refs[tok_count:-1], refs[-1]
+    size = weight_refs[0].shape[-1]
     half = own_ref.shape[1]
     total_ref[...] = jnp.zeros(total_ref.shape, jnp.float32)
-    first, count = live_range(kept_ref, matrix, weight_ref.shape[0])
-
-    def body(slots):
+
+    def body(weight_ref, first, slots):
         found = []
         for slot in slots:
             place = place_ref[matrix, first + slot]
@@ -155,7 +157,7 @@
         for spot, product in found:
             total_ref[:, spot] += product
 
-    over_slots(count, body)
+    over_owners(matrix, kept_ref, weight_refs, body)
     for index, out_ref in enumerate(out_refs):
         chunk, group = index // mem_count, index % mem_count
         span = out_ref.shape[1]
@@ -164,18 +166,13 @@
         ]
 
 
-def owner_count(kept_ref, matrix, cell, owner, owned):
-    first = (lax.axis_index("mem") * lax.axis_size("tok") + owner) * owned
-    return first, jnp.clip(kept_ref[matrix, cell] - first, 0, owned)
-
-
 def gradient_kernel(matrix, width_blocks, mem_count, hid_count, kept_ref, place_ref, far_place_ref, *refs):
     row_ref, own_ref, pair_ref = refs[:3]
     late_refs = refs[3 : 3 + hid_count]
     keep_ref, send_ref, late_ref = refs[3 + hid_count :]
     cells, owned, size = keep_ref.shape[:3]
-    tok_count = lax.axis_size("tok")
-    tok = lax.axis_index("tok")
+    tok_count = lax.axis_size(TOK)
+    tok = lax.axis_index(TOK)
     rows = row_ref.shape[0] // mem_count
     part = rows // tok_count
     step = rows // hid_count
@@ -219,7 +216,7 @@
 def update_kernel(matrix, kept_ref, keep_ref, swap_ref, weight_ref, moment_ref, variance_ref, *refs):
     out_refs = refs[-3:]
     turn = pl.program_id(0)
-    tok = lax.axis_index("tok")
+    tok = lax.axis_index(TOK)
     owned = weight_ref.shape[3]
     _, count = owner_count(kept_ref, matrix, tok ^ turn, tok, owned)
 
@@ -272,8 +269,12 @@
     out_ref[...] = (total_of(part_refs) * gelu_slope(preact_ref[...])).astype(jnp.bfloat16)
 
 
-def narrow_kernel(block_ref, out_ref):
-    out_ref[...] = block_ref[0, :, 0].astype(jnp.bfloat16)
+def narrow_kernel(block_ref, *out_refs):
+    for turn, out_ref in enumerate(out_refs):
+
+        @pl.when(pl.program_id(0) == turn)
+        def _():
+            out_ref[...] = block_ref[0, 0, 0].astype(jnp.bfloat16)
 
 
 SCALARS = pl.BlockSpec(memory_space=pltpu.SMEM)
@@ -303,9 +304,9 @@
 
 
 def on_device(inputs, cotangent, blocks, first_moment, second_moment, places, kept_counts):
-    mem_count = lax.axis_size("mem")
-    tok_count = lax.axis_size("tok")
-    hid_count = lax.axis_size("hid")
+    mem_count = lax.axis_size(MEM)
+    tok_count = lax.axis_size(TOK)
+    hid_count = lax.axis_size(HID)
     block_size = blocks.shape[-1]
     owned_slots = blocks.shape[3]
     local_slots = owned_slots * tok_count
@@ -322,13 +323,13 @@
     f32, bf16 = jnp.float32, jnp.bfloat16
 
     def shift_hid(array, shift):
-        return lax.ppermute(array, "hid", [(i, (i + shift) % hid_count) for i in range(hid_count)])
+        return lax.ppermute(array, HID, [(i, (i + shift) % hid_count) for i in range(hid_count)])
 
     def shift_mem(array, shift):
-        return lax.ppermute(array, "mem", [(i, (i + shift) % mem_count) for i in range(mem_count)])
+        return lax.ppermute(array, MEM, [(i, (i + shift) % mem_count) for i in range(mem_count)])
 
     def flip_tok(array, bit):
-        return lax.ppermute(array, "tok", [(i, i ^ bit) for i in range(tok_count)])
+        return lax.ppermute(array, TOK, [(i, i ^ bit) for i in range(tok_count)])
 
     def across(array, mem_shift, tok_shift):
         table = []
@@ -336,7 +337,7 @@
             for t in range(tok_count):
                 to = ((m - mem_shift) % mem_count) * tok_count + (t ^ (2 * tok_shift))
                 table.append((m * tok_count + t, to))
-        return lax.ppermute(array, ("mem", "tok"), table)
+        return lax.ppermute(array, (MEM, TOK), table)
 
     peers = [(j, b) for j in range(mem_count) for b in range(other)][1:]
 
@@ -352,19 +353,22 @@
         return [moved] + [shift_hid(moved, k) for k in range(1, hid_count)]
 
     def gather_weights(matrix):
-        shape = (tok_count, owned_slots, block_size, block_size)
+        shape = (owned_slots, block_size, block_size)
         narrow = pl.pallas_call(
             narrow_kernel,
             grid=(tok_count,),
-            out_shape=jax.ShapeDtypeStruct(shape, bf16),
+            out_shape=[jax.ShapeDtypeStruct(shape, bf16)] * tok_count,
             in_specs=[
-                pl.BlockSpec((1, 1, 1) + blocks.shape[3:], lambda i: (matrix, i, 0, 0, 0, 0))
+                pl.BlockSpec(
+                    (1, 1, 1) + blocks.shape[3:],
+                    lambda i: (matrix, lax.axis_index(TOK) ^ i, 0, 0, 0, 0),
+                )
             ],
-            out_specs=pl.BlockSpec((1,) + shape[1:], lambda i: (i, 0, 0, 0)),
+            out_specs=[pl.BlockSpec(shape, lambda i: (0, 0, 0))] * tok_count,
             compiler_params=pltpu.CompilerParams(vmem_limit_bytes=VMEM_BYTES),
         )(blocks)
-        moved = lax.all_to_all(narrow, "tok", split_axis=0, concat_axis=0, tiled=True)
-        return moved.reshape(local_slots, block_size, block_size)
+        moved = [flip_tok(narrow[r], r) for r in range(1, tok_count)]
+        return [narrow[0], *moved]
 
     def forward(matrix, transposed, row_groups, weights):
         kernel = functools.partial(
@@ -377,7 +381,7 @@
             jax.ShapeDtypeStruct((mem_count, half, hidden_span), f32),
         ]
         flops = 2 * mem_count * rows * local_slots * block_size * block_size
-        return call(kernel, outs, scalars, [*row_groups, weights], flops)
+        return call(kernel, outs, scalars, [*row_groups, *weights], flops)
 
     def over_columns(kernel, outs, arrays, steps):
         def spec(shape):
@@ -424,7 +428,7 @@
         outs = [jax.ShapeDtypeStruct((rows, span), f32)] * (mem_count * chunks)
         flops = 2 * mem_count * rows * local_slots * block_size * block_size
         scratch = [pltpu.VMEM((mem_count * rows, inputs.shape[1]), f32)]
-        return call(kernel, outs, scalars, [near, far, weights], flops, scratch)
+        return call(kernel, outs, scalars, [near, far, *weights], flops, scratch)
 
     turn = relative(tok_count)
     step = inputs.shape[0]
@@ -466,7 +470,7 @@
 
     def update(matrix, grads, held):
         state_shape = (1, 1, 1, owned_slots, block_size, block_size)
-        state_spec = pl.BlockSpec(state_shape, lambda i: (matrix, lax.axis_index("tok") ^ i, 0, 0, 0, 0))
+        state_spec = pl.BlockSpec(state_shape, lambda i: (matrix, lax.axis_index(TOK) ^ i, 0, 0, 0, 0))
         grad_spec = pl.BlockSpec((1, owned_slots, block_size, block_size), lambda i: (i // 2, 0, 0, 0))
         state = (blocks, first_moment, second_moment)
         size = local_slots * block_size * block_size
@@ -512,20 +516,20 @@
         on_device,
         mesh=mesh,
         in_specs=(
-            P(("mem", "hid"), "tok"),
-            P(("mem", "hid"), "tok"),
-            P(None, None, "hid", ("mem", "tok"), None, None),
-            P(None, None, "hid", ("mem", "tok"), None, None),
-            P(None, None, "hid", ("mem", "tok"), None, None),
-            P(None, "tok", "hid", None),
-            P(None, None, "hid"),
+            P((MEM, HID), TOK),
+            P((MEM, HID), TOK),
+            P(None, None, HID, (MEM, TOK), None, None),
+            P(None, None, HID, (MEM, TOK), None, None),
+            P(None, None, HID, (MEM, TOK), None, None),
+            P(None, TOK, HID, None),
+            P(None, None, HID),
         ),
         out_specs=(
-            P(("mem", "hid"), "tok"),
-            P(("mem", "hid"), "tok"),
-            P(None, None, "hid", ("mem", "tok"), None, None),
-            P(None, None, "hid", ("mem", "tok"), None, None),
-            P(None, None, "hid", ("mem", "tok"), None, None),
+            P((MEM, HID), TOK),
+            P((MEM, HID), TOK),
+            P(None, None, HID, (MEM, TOK), None, None),
+            P(None, None, HID, (MEM, TOK), None, None),
+            P(None, None, HID, (MEM, TOK), None, None),
         ),
         check_vma=False,
     )

time: 418 us -> 430 us (1.029)
  waiting for transfers between devices: 202 us -> 224 us
  starting transfers between devices: 87.6 us -> 77.3 us
    ppermute x48 -> x54, waiting for transfers between devices: 202 us -> 224 us  [the longest x21 96.2 us: shift_hid(): lax.ppermute(array, HID, [(i, (i + shift) % hid_count) for i in range(hid...]
    all_to_all x2 -> x0, starting transfers between devices: 8.89 us -> none  [gather_weights(): lax.all_to_all(narrow, 'tok', split_axis=0, concat_axis=0, tiled=True)]
    ppermute x48 -> x54, starting transfers between devices: 78.7 us -> 77.3 us  [the longest x21 52.3 us: shift_hid(): lax.ppermute(array, HID, [(i, (i + shift) % hid_count) for i in range(hid...]
    unnamed x65 -> x75, local copies, waits for them, and re-layouts: 12.6 us -> 12.1 us
  transfers between devices with their start and end apart: 50 -> 54, of which waited for: 24 -> 28; matrix products, arithmetic and copies ran while one was open for 3% -> 2% of each run, Pallas kernels for 22% -> 22%
where the time goes in v3:
time: 430 us
  waiting for transfers between devices  224 us (52%)
  Pallas kernels  110 us (26%)
  starting transfers between devices  77.3 us (18%)
  local copies, waits for them, and re-layouts  12.4 us (3%)
  other arithmetic  5.36 us (1%)
    ppermute x21, waiting for transfers between devices, shift_hid(): lax.ppermute(array, HID, [(i, (i + shift) % hid_count) for i in range(hid...  96.2 us
    ppermute x12, waiting for transfers between devices, across(): return lax.ppermute(array, (MEM, TOK), table)  86.6 us
    pallas_call x6, Pallas kernels, call(): pl.pallas_call(kernel, out_shape=outs, in_specs=[SCALARS] * len(scalars)...  58 us
    ppermute x21, starting transfers between devices, shift_hid(): lax.ppermute(array, HID, [(i, (i + shift) % hid_count) for i in range(hid...  52.3 us
    pallas_call x2, Pallas kernels, update(): pl.pallas_call(functools.partial(update_kernel, matrix), grid=(tok_count,...  26.8 us
    ppermute x14, waiting for transfers between devices, flip_tok(): return lax.ppermute(array, TOK, [(i, i ^ bit) for i in range(tok_count)])  24.3 us
    ppermute x7, waiting for transfers between devices, shift_mem(): lax.ppermute(array, MEM, [(i, (i + shift) % mem_count) for i in range(mem...  16.8 us
    pallas_call x4, Pallas kernels, over_columns(): pl.pallas_call(kernel, grid=(steps,), out_shape=outs, in_specs=[spec(a.sh...  15.8 us
  transfers between devices with their start and end apart: 54, of which 28 were waited for; matrix products, arithmetic and copies ran while one was open for 2% of the time, Pallas kernels for 22%

profile of v3, /device:TPU:0, one launch (start us, length us, event | category | flops | bytes accessed | tf_op | source)
XLA Modules:
  0.0 429.8 jit_solution(168496580899731425)
XLA Ops:
  0.6 5.1 %collective-permute-start.2 = (bf16[32,3072]{1,0:T(8,128)(2,1)}, bf16[32,3072]{1,0:T(8,128)(2,1)S(1)}, u32[]{:S(2)}, u32[]{:S(2)}) collective-permute-start(bf16[32,3072]{1,0:T(8,128)(2,1)} %param.7), channel_id=1, source_target_pairs={{0,12},{4,0},{8,4},{12,8},{1,13},{5,1},{9,5},{13,9},{2,14},{6,2},{... | collective-permute-start | bytes 589832 | tf_op jit(solution)/shard_map/ppermute | solution.py:326
  20.6 12.3 %collective-permute-start.26 = (bf16[32,3072]{1,0:T(8,128)(2,1)S(1)}, bf16[32,3072]{1,0:T(8,128)(2,1)S(1)}, u32[]{:S(2)}, u32[]{:S(2)}) collective-permute-start(bf16[32,3072]{1,0:T(8,128)(2,1)S(1)} %copy-done.18), channel_id=1, source_target_pairs={{0,4},{4,8},{8,12},{12,0},{1,5},{5,9},{9,13},{13,1},{2,6},{6,10},{... | collective-permute-start | bytes 589832 | tf_op jit(solution)/shard_map/ppermute | solution.py:326
  51.0 10.3 %collective-permute-done.6.refs_5_.refs_3_ = bf16[18,128,128]{2,1,0:T(8,128)(2,1)S(1)} collective-permute-done((bf16[18,128,128]{2,1,0:T(8,128)(2,1)}, bf16[18,128,128]{2,1,0:T(8,128)(2,1)S(1)}, u32[]{:S(2)}, u32[]{:S(2)}) %collective-permute-start.6) | collective-permute-done | bytes 589856 | tf_op jit(solution)/shard_map/ppermute | solution.py:332
  65.0 10.6 %shard_map.111 = (bf16[256,3072]{1,0:T(8,128)(2,1)}, f32[2,64,6144]{2,1,0:T(8,128)}, f32[2,64,6144]{2,1,0:T(8,128)}) custom-call(s32[2,4]{1,0:T(2,128)} %bitcast.28, s32[2,144]{1,0:T(2,128)} %bitcast.21, bf16[128,3072]{1,0:T(8,128)(2,1)} %copy-done.16, bf16[128,3072]{1,0:T(8,128)(2,1)} %copy-done.28, ...), custom_call_target="tpu_custom_call" | custom-call | flops 603979776 | bytes 11796480 | tf_op jit(solution)/shard_map/pallas_call | solution.py:288
  75.7 10.8 %collective-permute-done.17.refs_3_.refs_5_ = bf16[18,128,128]{2,1,0:T(8,128)(2,1)S(1)} collective-permute-done((bf16[18,128,128]{2,1,0:T(8,128)(2,1)}, bf16[18,128,128]{2,1,0:T(8,128)(2,1)S(1)}, u32[]{:S(2)}, u32[]{:S(2)}) %collective-permute-start.17) | collective-permute-done | bytes 589856 | tf_op jit(solution)/shard_map/ppermute | solution.py:332
  87.3 7.8 %shard_map.116 = (bf16[256,3072]{1,0:T(8,128)(2,1)}, f32[2,64,6144]{2,1,0:T(8,128)}, f32[2,64,6144]{2,1,0:T(8,128)}) custom-call(s32[2,4]{1,0:T(2,128)} %bitcast.29, s32[2,144]{1,0:T(2,128)} %bitcast.22, bf16[128,3072]{1,0:T(8,128)(2,1)} %copy-done.15, bf16[128,3072]{1,0:T(8,128)(2,1)} %collective-permute-done.29.refs_1_, ...), custom_call_target="tpu_custom_call" | custom-call | flops 603979776 | bytes 11796480 | tf_op jit(solution)/shard_map/pallas_call | solution.py:288
  96.8 4.9 %shard_map.112 = (f32[32,6144]{1,0:T(8,128)}, f32[32,6144]{1,0:T(8,128)}, f32[32,6144]{1,0:T(8,128)}, f32[32,6144]{1,0:T(8,128)}) custom-call(f32[2,64,6144]{2,1,0:T(8,128)} %get-tuple-element.51.keep_ref, f32[2,64,6144]{2,1,0:T(8,128)} %copy-done.4), custom_call_target="tpu_custom_call" | custom-call | flops 3145728 | bytes 9437184 | tf_op jit(solution)/shard_map/pallas_call | solution.py:393
  106.9 5.0 %shard_map.117 = (f32[32,6144]{1,0:T(8,128)}, f32[32,6144]{1,0:T(8,128)}, f32[32,6144]{1,0:T(8,128)}, f32[32,6144]{1,0:T(8,128)}) custom-call(f32[2,64,6144]{2,1,0:T(8,128)} %get-tuple-element.66.keep_ref, f32[2,64,6144]{2,1,0:T(8,128)} %copy-done.5), custom_call_target="tpu_custom_call" | custom-call | flops 3145728 | bytes 9437184 | tf_op jit(solution)/shard_map/pallas_call | solution.py:393
  113.8 8.5 %collective-permute-done.8.refs_1_ = f32[32,6144]{1,0:T(8,128)S(1)} collective-permute-done((f32[32,6144]{1,0:T(8,128)}, f32[32,6144]{1,0:T(8,128)S(1)}, u32[]{:S(2)}, u32[]{:S(2)}) %collective-permute-start.8) | collective-permute-done | bytes 786464 | tf_op jit(solution)/shard_map/ppermute | solution.py:340
  124.3 16.4 %collective-permute-done.10.refs_3_ = f32[32,6144]{1,0:T(8,128)S(1)} collective-permute-done((f32[32,6144]{1,0:T(8,128)}, f32[32,6144]{1,0:T(8,128)S(1)}, u32[]{:S(2)}, u32[]{:S(2)}) %collective-permute-start.10) | collective-permute-done | bytes 786464 | tf_op jit(solution)/shard_map/ppermute | solution.py:340
  147.8 7.9 %collective-permute-done.31.refs_1_ = f32[32,6144]{1,0:T(8,128)S(1)} collective-permute-done((f32[32,6144]{1,0:T(8,128)}, f32[32,6144]{1,0:T(8,128)S(1)}, u32[]{:S(2)}, u32[]{:S(2)}) %collective-permute-start.31) | collective-permute-done | bytes 786464 | tf_op jit(solution)/shard_map/ppermute | solution.py:340
  158.1 16.4 %collective-permute-done.33.refs_3_ = f32[32,6144]{1,0:T(8,128)S(1)} collective-permute-done((f32[32,6144]{1,0:T(8,128)}, f32[32,6144]{1,0:T(8,128)S(1)}, u32[]{:S(2)}, u32[]{:S(2)}) %collective-permute-start.33) | collective-permute-done | bytes 786464 | tf_op jit(solution)/shard_map/ppermute | solution.py:340
  183.0 8.8 %collective-permute-done.12 = bf16[32,6144]{1,0:T(8,128)(2,1)S(1)} collective-permute-done((bf16[32,6144]{1,0:T(8,128)(2,1)}, bf16[32,6144]{1,0:T(8,128)(2,1)S(1)}, u32[]{:S(2)}, u32[]{:S(2)}) %collective-permute-start.12) | collective-permute-done | bytes 393248 | tf_op jit(solution)/shard_map/ppermute | solution.py:340
  192.1 7.7 %collective-permute-done.36 = bf16[32,6144]{1,0:T(8,128)(2,1)S(1)} collective-permute-done((bf16[32,6144]{1,0:T(8,128)(2,1)}, bf16[32,6144]{1,0:T(8,128)(2,1)S(1)}, u32[]{:S(2)}, u32[]{:S(2)}) %collective-permute-start.36) | collective-permute-done | bytes 393248 | tf_op jit(solution)/shard_map/ppermute | solution.py:340
  199.8 8.1 %collective-permute-done.35 = bf16[32,6144]{1,0:T(8,128)(2,1)S(1)} collective-permute-done((bf16[32,6144]{1,0:T(8,128)(2,1)}, bf16[32,6144]{1,0:T(8,128)(2,1)S(1)}, u32[]{:S(2)}, u32[]{:S(2)}) %collective-permute-start.35) | collective-permute-done | bytes 393248 | tf_op jit(solution)/shard_map/ppermute | solution.py:340
  207.9 8.1 %collective-permute-done.34 = bf16[32,6144]{1,0:T(8,128)(2,1)S(1)} collective-permute-done((bf16[32,6144]{1,0:T(8,128)(2,1)}, bf16[32,6144]{1,0:T(8,128)(2,1)S(1)}, u32[]{:S(2)}, u32[]{:S(2)}) %collective-permute-start.34) | collective-permute-done | bytes 393248 | tf_op jit(solution)/shard_map/ppermute | solution.py:340
  216.5 11.5 %collective-permute-done.48 = bf16[2,32,3072]{2,1,0:T(8,128)(2,1)S(1)} collective-permute-done((bf16[2,32,3072]{2,1,0:T(8,128)(2,1)}, bf16[2,32,3072]{2,1,0:T(8,128)(2,1)S(1)}, u32[]{:S(2)}, u32[]{:S(2)}) %collective-permute-start.48) | collective-permute-done | bytes 393248 | tf_op jit(solution)/shard_map/ppermute | solution.py:329
  231.2 6.0 %collective-permute-start.50 = (bf16[2,2,32,3072]{3,2,1,0:T(8,128)(2,1)}, bf16[2,2,32,3072]{3,2,1,0:T(8,128)(2,1)}, u32[]{:S(2)}, u32[]{:S(2)}) collective-permute-start(bf16[2,2,32,3072]{3,2,1,0:T(8,128)(2,1)} %pad_maximum_fusion.2.refs_3_), channel_id=1, source_target_pairs={{0,8},{4,12},{8,0},{12,4},{1,9},{5,13},{9,1},{13,5},{2,10},{6,14},... | collective-permute-start | bytes 2359304 | tf_op jit(solution)/shard_map/ppermute | solution.py:326
  238.9 6.4 %shard_map.115 = (f32[128,1536]{1,0:T(8,128)}, f32[128,1536]{1,0:T(8,128)}, f32[128,1536]{1,0:T(8,128)}, f32[128,1536]{1,0:T(8,128)}) custom-call(s32[2,4]{1,0:T(2,128)} %bitcast.30, s32[2,144]{1,0:T(2,128)} %bitcast.23, bf16[2,64,6144]{2,1,0:T(8,128)(2,1)} %bitcast.13, bf16[2,64,6144]{2,1,0:T(8,128)(2,1)} %copy-done.2, ...), custom_call_target="tpu_custom_call" | custom-call | flops 603979776 | bytes 8650752 | tf_op jit(solution)/shard_map/pallas_call | solution.py:288
  247.4 10.1 %shard_map.119 = (f32[128,1536]{1,0:T(8,128)}, f32[128,1536]{1,0:T(8,128)}, f32[128,1536]{1,0:T(8,128)}, f32[128,1536]{1,0:T(8,128)}) custom-call(s32[2,4]{1,0:T(2,128)} %bitcast.31, s32[2,144]{1,0:T(2,128)} %bitcast.24, bf16[2,64,6144]{2,1,0:T(8,128)(2,1)} %bitcast.16, bf16[2,64,6144]{2,1,0:T(8,128)(2,1)} %copy-done.3, ...), custom_call_target="tpu_custom_call" | custom-call | flops 603979776 | bytes 8650752 | tf_op jit(solution)/shard_map/pallas_call | solution.py:288
  257.6 47.5 %collective-permute-done.50.refs_5_ = bf16[2,2,32,3072]{3,2,1,0:T(8,128)(2,1)} collective-permute-done((bf16[2,2,32,3072]{3,2,1,0:T(8,128)(2,1)}, bf16[2,2,32,3072]{3,2,1,0:T(8,128)(2,1)}, u32[]{:S(2)}, u32[]{:S(2)}) %collective-permute-start.50) | collective-permute-done | bytes 786464 | tf_op jit(solution)/shard_map/ppermute | solution.py:326
  305.0 10.8 %shard_map.121 = (f32[2,18,128,128]{3,2,1,0:T(8,128)}, f32[2,18,128,128]{3,2,1,0:T(8,128)}) custom-call(s32[2,4]{1,0:T(2,128)} %bitcast.32, s32[2,144]{1,0:T(2,128)} %bitcast.25, s32[2,144]{1,0:T(2,128)} %copy-done.32, bf16[256,3072]{1,0:T(8,128)(2,1)} %get-tuple-element.80.refs_0_, bf16[2,64,6144]{2,1,0:T(8,128)(2,1)} %bitcast.14, ...), custom_call_target="tpu_custom_call" | custom-call | flops 603979776 | bytes 12582912 | tf_op jit(solution)/shard_map/pallas_call | solution.py:288
  315.9 12.3 %shard_map.120 = (f32[2,18,128,128]{3,2,1,0:T(8,128)}, f32[2,18,128,128]{3,2,1,0:T(8,128)}) custom-call(s32[2,4]{1,0:T(2,128)} %bitcast.33, s32[2,144]{1,0:T(2,128)} %bitcast.26, s32[2,144]{1,0:T(2,128)} %copy-done.32, bf16[256,3072]{1,0:T(8,128)(2,1)} %get-tuple-element.77.refs_0_, bf16[2,64,6144]{2,1,0:T(8,128)(2,1)} %bitcast.17, ...), custom_call_target="tpu_custom_call" | custom-call | flops 603979776 | bytes 12582912 | tf_op jit(solution)/shard_map/pallas_call | solution.py:288
  330.8 5.3 %collective-permute-done.42 = f32[128,1536]{1,0:T(8,128)} collective-permute-done((f32[128,1536]{1,0:T(8,128)}, f32[128,1536]{1,0:T(8,128)}, u32[]{:S(2)}, u32[]{:S(2)}) %collective-permute-start.42) | collective-permute-done | bytes 786464 | tf_op jit(solution)/shard_map/ppermute | solution.py:329
  341.2 8.5 %collective-permute-done.20 = f32[32,1536]{1,0:T(8,128)S(1)} collective-permute-done((f32[32,1536]{1,0:T(8,128)S(1)}, f32[32,1536]{1,0:T(8,128)S(1)}, u32[]{:S(2)}, u32[]{:S(2)}) %collective-permute-start.20) | collective-permute-done | bytes 196640 | tf_op jit(solution)/shard_map/ppermute | solution.py:326
  355.0 9.6 %collective-permute-start.41 = (f32[32,1536]{1,0:T(8,128)S(1)}, f32[32,1536]{1,0:T(8,128)S(1)}, u32[]{:S(2)}, u32[]{:S(2)}) collective-permute-start(f32[32,1536]{1,0:T(8,128)S(1)} %get-tuple-element.90), channel_id=1, source_target_pairs={{0,4},{4,8},{8,12},{12,0},{1,5},{5,9},{9,13},{13,1},{2,6},{6,10},{... | collective-permute-start | bytes 589832 | tf_op jit(solution)/shard_map/ppermute | solution.py:326
  366.6 7.4 %collective-permute-done.39 = f32[32,1536]{1,0:T(8,128)S(1)} collective-permute-done((f32[32,1536]{1,0:T(8,128)S(1)}, f32[32,1536]{1,0:T(8,128)S(1)}, u32[]{:S(2)}, u32[]{:S(2)}) %collective-permute-start.39) | collective-permute-done | bytes 196640 | tf_op jit(solution)/shard_map/ppermute | solution.py:326
  373.9 7.5 %collective-permute-start.45 = (f32[32,1536]{1,0:T(8,128)S(1)}, f32[32,1536]{1,0:T(8,128)S(1)}, u32[]{:S(2)}, u32[]{:S(2)}) collective-permute-start(f32[32,1536]{1,0:T(8,128)S(1)} %get-tuple-element.93), channel_id=1, source_target_pairs={{0,4},{4,8},{8,12},{12,0},{1,5},{5,9},{9,13},{13,1},{2,6},{6,10},{... | collective-permute-start | bytes 589832 | tf_op jit(solution)/shard_map/ppermute | solution.py:326
  384.2 6.7 %collective-permute-done.43 = f32[32,1536]{1,0:T(8,128)S(1)} collective-permute-done((f32[32,1536]{1,0:T(8,128)S(1)}, f32[32,1536]{1,0:T(8,128)S(1)}, u32[]{:S(2)}, u32[]{:S(2)}) %collective-permute-start.43) | collective-permute-done | bytes 196640 | tf_op jit(solution)/shard_map/ppermute | solution.py:326
  390.8 8.5 %collective-permute-done.44 = f32[32,1536]{1,0:T(8,128)S(1)} collective-permute-done((f32[32,1536]{1,0:T(8,128)S(1)}, f32[32,1536]{1,0:T(8,128)S(1)}, u32[]{:S(2)}, u32[]{:S(2)}) %collective-permute-start.44) | collective-permute-done | bytes 196640 | tf_op jit(solution)/shard_map/ppermute | solution.py:326
  401.5 13.4 %shard_map.122 = (f32[2,4,1,18,128,128]{5,4,3,2,1,0:T(8,128)}, f32[2,4,1,18,128,128]{5,4,3,2,1,0:T(8,128)}, f32[2,4,1,18,128,128]{5,4,3,2,1,0:T(8,128)}) custom-call(s32[2,4]{1,0:T(2,128)} %bitcast.34, f32[2,18,128,128]{3,2,1,0:T(8,128)} %get-tuple-element.81.keep_ref, f32[2,18,128,128]{3,2,1,0:T(8,128)} %copy-done.6, ...), custom_call_target="tpu_custom_call" | custom-call | flops 14155776 | bytes 33030144 | tf_op jit(solution)/shard_map/pallas_call | solution.py:477
  416.4 13.4 %shard_map.123 = (f32[2,4,1,18,128,128]{5,4,3,2,1,0:T(8,128)}, f32[2,4,1,18,128,128]{5,4,3,2,1,0:T(8,128)}, f32[2,4,1,18,128,128]{5,4,3,2,1,0:T(8,128)}) custom-call(s32[2,4]{1,0:T(2,128)} %bitcast.35, f32[2,18,128,128]{3,2,1,0:T(8,128)} %get-tuple-element.78.keep_ref, ...), custom_call_target="tpu_custom_call", output_to_operand_aliasing={{0}: (6, {}), {1}: (7, {}), {2}: (8, {})} | custom-call | flops 14155776 | bytes 33030144 | tf_op jit(solution)/shard_map/pallas_call | solution.py:477
  (185 shorter events, 95.2 us)
Async XLA Ops:
  0.6 32.4 %collective-permute-start.2 = (bf16[32,3072]{1,0:T(8,128)(2,1)}, bf16[32,3072]{1,0:T(8,128)(2,1)S(1)}, u32[]{:S(2)}, u32[]{:S(2)}) collective-permute-start(bf16[32,3072]{1,0:T(8,128)(2,1)} %param.7), channel_id=1, source_target_pairs={{0,12},{4,0},{8,4},{12,8},{1,13},{5,1},{9,5},{13,9},{2,14},{6,2},{... | collective-permute-start | bytes 589832 | tf_op jit(solution)/shard_map/ppermute | solution.py:326
  5.8 27.2 %collective-permute-start.1 = (bf16[32,3072]{1,0:T(8,128)(2,1)}, bf16[32,3072]{1,0:T(8,128)(2,1)S(1)}, u32[]{:S(2)}, u32[]{:S(2)}) collective-permute-start(bf16[32,3072]{1,0:T(8,128)(2,1)} %param.7), channel_id=1, source_target_pairs={{0,8},{4,12},{8,0},{12,4},{1,9},{5,13},{9,1},{13,5},{2,10},{6,14},... | collective-permute-start | bytes 589832 | tf_op jit(solution)/shard_map/ppermute | solution.py:326
  6.8 34.3 %collective-permute-start.28 = (bf16[32,3072]{1,0:T(8,128)(2,1)}, bf16[32,3072]{1,0:T(8,128)(2,1)S(1)}, u32[]{:S(2)}, u32[]{:S(2)}) collective-permute-start(bf16[32,3072]{1,0:T(8,128)(2,1)} %param.8), channel_id=1, source_target_pairs={{0,12},{4,0},{8,4},{12,8},{1,13},{5,1},{9,5},{13,9},{2,14},{6,2},{... | collective-permute-start | bytes 589832 | tf_op jit(solution)/shard_map/ppermute | solution.py:326
  9.6 29.9 %collective-permute-start.27 = (bf16[32,3072]{1,0:T(8,128)(2,1)}, bf16[32,3072]{1,0:T(8,128)(2,1)S(1)}, u32[]{:S(2)}, u32[]{:S(2)}) collective-permute-start(bf16[32,3072]{1,0:T(8,128)(2,1)} %param.8), channel_id=1, source_target_pairs={{0,8},{4,12},{8,0},{12,4},{1,9},{5,13},{9,1},{13,5},{2,10},{6,14},... | collective-permute-start | bytes 589832 | tf_op jit(solution)/shard_map/ppermute | solution.py:326
  36.1 25.2 %collective-permute-start.6 = (bf16[18,128,128]{2,1,0:T(8,128)(2,1)}, bf16[18,128,128]{2,1,0:T(8,128)(2,1)S(1)}, u32[]{:S(2)}, u32[]{:S(2)}) collective-permute-start(bf16[18,128,128]{2,1,0:T(8,128)(2,1)} %get-tuple-element.50), channel_id=1, source_target_pairs={{0,3},{1,2},{2,1},{3,0},{4,7},{5,6},{6,5},{7,4},{8,11},{9,10},{10,... | collective-permute-start | bytes 1769480 | tf_op jit(solution)/shard_map/ppermute | solution.py:332
  39.5 24.6 %collective-permute-start.3 = (bf16[128,3072]{1,0:T(8,128)(2,1)S(1)}, bf16[128,3072]{1,0:T(8,128)(2,1)S(1)}, u32[]{:S(2)}, u32[]{:S(2)}) collective-permute-start(bf16[128,3072]{1,0:T(8,128)(2,1)S(1)} %constant_dynamic-update-slice_fusion.refs_0_), channel_id=1, source_target_pairs={{0,16},{16,0},{1,17},{17,1},{2,18},{18,2},{3,19},{19,3},{4,20},{20... | collective-permute-start | bytes 2359304 | tf_op jit(solution)/shard_map/ppermute | solution.py:329
  41.1 45.4 %collective-permute-start.29 = (bf16[128,3072]{1,0:T(8,128)(2,1)S(1)}, bf16[128,3072]{1,0:T(8,128)(2,1)}, u32[]{:S(2)}, u32[]{:S(2)}) collective-permute-start(bf16[128,3072]{1,0:T(8,128)(2,1)S(1)} %constant_dynamic-update-slice_fusion.4.refs_0_), channel_id=1, source_target_pairs={{0,16},{16,0},{1,17},{17,1},{2,18},{18,2},{3,19},{19,3},{4,20},{20... | collective-permute-start | bytes 2359304 | tf_op jit(solution)/shard_map/ppermute | solution.py:329
  46.3 29.4 %collective-permute-start.15 = (bf16[18,128,128]{2,1,0:T(8,128)(2,1)}, bf16[18,128,128]{2,1,0:T(8,128)(2,1)S(1)}, u32[]{:S(2)}, u32[]{:S(2)}) collective-permute-start(bf16[18,128,128]{2,1,0:T(8,128)(2,1)} %get-tuple-element.59), channel_id=1, source_target_pairs={{0,1},{1,0},{2,3},{3,2},{4,5},{5,4},{6,7},{7,6},{8,9},{9,8},{10,11... | collective-permute-start | bytes 1769480 | tf_op jit(solution)/shard_map/ppermute | solution.py:332
  49.5 26.1 %collective-permute-start.16 = (bf16[18,128,128]{2,1,0:T(8,128)(2,1)}, bf16[18,128,128]{2,1,0:T(8,128)(2,1)S(1)}, u32[]{:S(2)}, u32[]{:S(2)}) collective-permute-start(bf16[18,128,128]{2,1,0:T(8,128)(2,1)} %get-tuple-element.60), channel_id=1, source_target_pairs={{0,2},{1,3},{2,0},{3,1},{4,6},{5,7},{6,4},{7,5},{8,10},{9,11},{10,... | collective-permute-start | bytes 1769480 | tf_op jit(solution)/shard_map/ppermute | solution.py:332
  61.3 25.2 %collective-permute-start.17 = (bf16[18,128,128]{2,1,0:T(8,128)(2,1)}, bf16[18,128,128]{2,1,0:T(8,128)(2,1)S(1)}, u32[]{:S(2)}, u32[]{:S(2)}) collective-permute-start(bf16[18,128,128]{2,1,0:T(8,128)(2,1)} %get-tuple-element.61), channel_id=1, source_target_pairs={{0,3},{1,2},{2,1},{3,0},{4,7},{5,6},{6,5},{7,4},{8,11},{9,10},{10,... | collective-permute-start | bytes 1769480 | tf_op jit(solution)/shard_map/ppermute | solution.py:332
  103.6 37.1 %collective-permute-start.10 = (f32[32,6144]{1,0:T(8,128)}, f32[32,6144]{1,0:T(8,128)S(1)}, u32[]{:S(2)}, u32[]{:S(2)}) collective-permute-start(f32[32,6144]{1,0:T(8,128)} %get-tuple-element.56), channel_id=1, source_target_pairs={{0,18},{1,19},{2,16},{3,17},{16,2},{17,3},{18,0},{19,1},{4,22},{5,... | collective-permute-start | bytes 2359304 | tf_op jit(solution)/shard_map/ppermute | solution.py:340
  111.9 43.9 %collective-permute-start.31 = (f32[32,6144]{1,0:T(8,128)}, f32[32,6144]{1,0:T(8,128)S(1)}, u32[]{:S(2)}, u32[]{:S(2)}) collective-permute-start(f32[32,6144]{1,0:T(8,128)} %get-tuple-element.69), channel_id=1, source_target_pairs={{0,2},{1,3},{2,0},{3,1},{16,18},{17,19},{18,16},{19,17},{4,6},{5,7... | collective-permute-start | bytes 2359304 | tf_op jit(solution)/shard_map/ppermute | solution.py:340
  113.8 44.2 %collective-permute-start.32 = (f32[32,6144]{1,0:T(8,128)}, f32[32,6144]{1,0:T(8,128)S(1)}, u32[]{:S(2)}, u32[]{:S(2)}) collective-permute-start(f32[32,6144]{1,0:T(8,128)} %get-tuple-element.70), channel_id=1, source_target_pairs={{0,16},{1,17},{2,18},{3,19},{16,0},{17,1},{18,2},{19,3},{4,20},{5,... | collective-permute-start | bytes 2359304 | tf_op jit(solution)/shard_map/ppermute | solution.py:340
  122.3 52.2 %collective-permute-start.33 = (f32[32,6144]{1,0:T(8,128)}, f32[32,6144]{1,0:T(8,128)S(1)}, u32[]{:S(2)}, u32[]{:S(2)}) collective-permute-start(f32[32,6144]{1,0:T(8,128)} %get-tuple-element.71), channel_id=1, source_target_pairs={{0,18},{1,19},{2,16},{3,17},{16,2},{17,3},{18,0},{19,1},{4,22},{5,... | collective-permute-start | bytes 2359304 | tf_op jit(solution)/shard_map/ppermute | solution.py:340
  144.4 38.5 %collective-permute-start.13 = (bf16[32,6144]{1,0:T(8,128)(2,1)}, bf16[32,6144]{1,0:T(8,128)(2,1)S(1)}, u32[]{:S(2)}, u32[]{:S(2)}) collective-permute-start(bf16[32,6144]{1,0:T(8,128)(2,1)} %get-tuple-element.57), channel_id=1, source_target_pairs={{0,18},{1,19},{2,16},{3,17},{16,2},{17,3},{18,0},{19,1},{4,22},{5,... | collective-permute-start | bytes 1179656 | tf_op jit(solution)/shard_map/ppermute | solution.py:340
  145.8 46.0 %collective-permute-start.12 = (bf16[32,6144]{1,0:T(8,128)(2,1)}, bf16[32,6144]{1,0:T(8,128)(2,1)S(1)}, u32[]{:S(2)}, u32[]{:S(2)}) collective-permute-start(bf16[32,6144]{1,0:T(8,128)(2,1)} %get-tuple-element.57), channel_id=1, source_target_pairs={{0,16},{1,17},{2,18},{3,19},{16,0},{17,1},{18,2},{19,3},{4,20},{5,... | collective-permute-start | bytes 1179656 | tf_op jit(solution)/shard_map/ppermute | solution.py:340
  155.7 36.1 %collective-permute-start.11 = (bf16[32,6144]{1,0:T(8,128)(2,1)}, bf16[32,6144]{1,0:T(8,128)(2,1)S(1)}, u32[]{:S(2)}, u32[]{:S(2)}) collective-permute-start(bf16[32,6144]{1,0:T(8,128)(2,1)} %get-tuple-element.57), channel_id=1, source_target_pairs={{0,2},{1,3},{2,0},{3,1},{16,18},{17,19},{18,16},{19,17},{4,6},{5,7... | collective-permute-start | bytes 1179656 | tf_op jit(solution)/shard_map/ppermute | solution.py:340
  158.0 58.3 %collective-permute-start.47 = (bf16[2,32,3072]{2,1,0:T(8,128)(2,1)S(1)}, bf16[2,32,3072]{2,1,0:T(8,128)(2,1)}, u32[]{:S(2)}, u32[]{:S(2)}) collective-permute-start(bf16[2,32,3072]{2,1,0:T(8,128)(2,1)S(1)} %pad_maximum_fusion.3), channel_id=1, source_target_pairs={{0,2},{1,3},{2,0},{3,1},{4,6},{5,7},{6,4},{7,5},{8,10},{9,11},{10,... | collective-permute-start | bytes 1179656 | tf_op jit(solution)/shard_map/ppermute | solution.py:332
  178.4 21.3 %collective-permute-start.36 = (bf16[32,6144]{1,0:T(8,128)(2,1)}, bf16[32,6144]{1,0:T(8,128)(2,1)S(1)}, u32[]{:S(2)}, u32[]{:S(2)}) collective-permute-start(bf16[32,6144]{1,0:T(8,128)(2,1)} %shard_map.118), channel_id=1, source_target_pairs={{0,18},{1,19},{2,16},{3,17},{16,2},{17,3},{18,0},{19,1},{4,22},{5,... | collective-permute-start | bytes 1179656 | tf_op jit(solution)/shard_map/ppermute | solution.py:340
  182.9 25.0 %collective-permute-start.35 = (bf16[32,6144]{1,0:T(8,128)(2,1)}, bf16[32,6144]{1,0:T(8,128)(2,1)S(1)}, u32[]{:S(2)}, u32[]{:S(2)}) collective-permute-start(bf16[32,6144]{1,0:T(8,128)(2,1)} %shard_map.118), channel_id=1, source_target_pairs={{0,16},{1,17},{2,18},{3,19},{16,0},{17,1},{18,2},{19,3},{4,20},{5,... | collective-permute-start | bytes 1179656 | tf_op jit(solution)/shard_map/ppermute | solution.py:340
  191.8 24.3 %collective-permute-start.34 = (bf16[32,6144]{1,0:T(8,128)(2,1)}, bf16[32,6144]{1,0:T(8,128)(2,1)S(1)}, u32[]{:S(2)}, u32[]{:S(2)}) collective-permute-start(bf16[32,6144]{1,0:T(8,128)(2,1)} %shard_map.118), channel_id=1, source_target_pairs={{0,2},{1,3},{2,0},{3,1},{16,18},{17,19},{18,16},{19,17},{4,6},{5,7... | collective-permute-start | bytes 1179656 | tf_op jit(solution)/shard_map/ppermute | solution.py:340
  192.0 45.1 %collective-permute-start.14 = (bf16[2,64,6144]{2,1,0:T(8,128)(2,1)S(1)}, bf16[2,64,6144]{2,1,0:T(8,128)(2,1)S(1)}, u32[]{:S(2)}, u32[]{:S(2)}) collective-permute-start(bf16[2,64,6144]{2,1,0:T(8,128)(2,1)S(1)} %bitcast.12), channel_id=1, source_target_pairs={{0,1},{1,0},{2,3},{3,2},{4,5},{5,4},{6,7},{7,6},{8,9},{9,8},{10,11... | collective-permute-start | bytes 4718600 | tf_op jit(solution)/shard_map/ppermute | solution.py:332
  216.2 29.2 %collective-permute-start.37 = (bf16[2,64,6144]{2,1,0:T(8,128)(2,1)S(1)}, bf16[2,64,6144]{2,1,0:T(8,128)(2,1)S(1)}, u32[]{:S(2)}, u32[]{:S(2)}) collective-permute-start(bf16[2,64,6144]{2,1,0:T(8,128)(2,1)S(1)} %bitcast.15), channel_id=1, source_target_pairs={{0,1},{1,0},{2,3},{3,2},{4,5},{5,4},{6,7},{7,6},{8,9},{9,8},{10,11... | collective-permute-start | bytes 4718600 | tf_op jit(solution)/shard_map/ppermute | solution.py:332
  230.0 27.5 %collective-permute-start.51 = (bf16[2,2,32,3072]{3,2,1,0:T(8,128)(2,1)}, bf16[2,2,32,3072]{3,2,1,0:T(8,128)(2,1)}, u32[]{:S(2)}, u32[]{:S(2)}) collective-permute-start(bf16[2,2,32,3072]{3,2,1,0:T(8,128)(2,1)} %pad_maximum_fusion.2.refs_3_), channel_id=1, source_target_pairs={{0,12},{4,0},{8,4},{12,8},{1,13},{5,1},{9,5},{13,9},{2,14},{6,2},{... | collective-permute-start | bytes 2359304 | tf_op jit(solution)/shard_map/ppermute | solution.py:326
  231.2 73.8 %collective-permute-start.50 = (bf16[2,2,32,3072]{3,2,1,0:T(8,128)(2,1)}, bf16[2,2,32,3072]{3,2,1,0:T(8,128)(2,1)}, u32[]{:S(2)}, u32[]{:S(2)}) collective-permute-start(bf16[2,2,32,3072]{3,2,1,0:T(8,128)(2,1)} %pad_maximum_fusion.2.refs_3_), channel_id=1, source_target_pairs={{0,8},{4,12},{8,0},{12,4},{1,9},{5,13},{9,1},{13,5},{2,10},{6,14},... | collective-permute-start | bytes 2359304 | tf_op jit(solution)/shard_map/ppermute | solution.py:326
  237.2 67.9 %collective-permute-start.49 = (bf16[2,2,32,3072]{3,2,1,0:T(8,128)(2,1)}, bf16[2,2,32,3072]{3,2,1,0:T(8,128)(2,1)}, u32[]{:S(2)}, u32[]{:S(2)}) collective-permute-start(bf16[2,2,32,3072]{3,2,1,0:T(8,128)(2,1)} %pad_maximum_fusion.2.refs_3_), channel_id=1, source_target_pairs={{0,4},{4,8},{8,12},{12,0},{1,5},{5,9},{9,13},{13,1},{2,6},{6,10},{... | collective-permute-start | bytes 2359304 | tf_op jit(solution)/shard_map/ppermute | solution.py:326
  245.3 82.8 %collective-permute-start.18 = (f32[128,1536]{1,0:T(8,128)}, f32[128,1536]{1,0:T(8,128)S(1)}, u32[]{:S(2)}, u32[]{:S(2)}) collective-permute-start(f32[128,1536]{1,0:T(8,128)} %get-tuple-element.63), channel_id=1, source_target_pairs={{0,16},{16,0},{1,17},{17,1},{2,18},{18,2},{3,19},{19,3},{4,20},{20... | collective-permute-start | bytes 2359304 | tf_op jit(solution)/shard_map/ppermute | solution.py:329
  245.4 83.0 %collective-permute-start.22 = (f32[128,1536]{1,0:T(8,128)}, f32[128,1536]{1,0:T(8,128)S(1)}, u32[]{:S(2)}, u32[]{:S(2)}) collective-permute-start(f32[128,1536]{1,0:T(8,128)} %get-tuple-element.65), channel_id=1, source_target_pairs={{0,16},{16,0},{1,17},{17,1},{2,18},{18,2},{3,19},{19,3},{4,20},{20... | collective-permute-start | bytes 2359304 | tf_op jit(solution)/shard_map/ppermute | solution.py:329
  257.5 71.9 %collective-permute-start.38 = (f32[128,1536]{1,0:T(8,128)}, f32[128,1536]{1,0:T(8,128)S(1)}, u32[]{:S(2)}, u32[]{:S(2)}) collective-permute-start(f32[128,1536]{1,0:T(8,128)} %get-tuple-element.74), channel_id=1, source_target_pairs={{0,16},{16,0},{1,17},{17,1},{2,18},{18,2},{3,19},{19,3},{4,20},{20... | collective-permute-start | bytes 2359304 | tf_op jit(solution)/shard_map/ppermute | solution.py:329
  315.8 84.2 %collective-permute-start.53 = (f32[2,18,128,128]{3,2,1,0:T(8,128)}, f32[2,18,128,128]{3,2,1,0:T(8,128)S(1)}, u32[]{:S(2)}, u32[]{:S(2)}) collective-permute-start(f32[2,18,128,128]{3,2,1,0:T(8,128)} %get-tuple-element.82), channel_id=1, source_target_pairs={{0,1},{1,0},{2,3},{3,2},{4,5},{5,4},{6,7},{7,6},{8,9},{9,8},{10,11... | collective-permute-start | bytes 7077896 | tf_op jit(solution)/shard_map/ppermute | solution.py:332
  328.1 86.8 %collective-permute-start.52 = (f32[2,18,128,128]{3,2,1,0:T(8,128)}, f32[2,18,128,128]{3,2,1,0:T(8,128)S(1)}, u32[]{:S(2)}, u32[]{:S(2)}) collective-permute-start(f32[2,18,128,128]{3,2,1,0:T(8,128)} %get-tuple-element.79), channel_id=1, source_target_pairs={{0,1},{1,0},{2,3},{3,2},{4,5},{5,4},{6,7},{7,6},{8,9},{9,8},{10,11... | collective-permute-start | bytes 7077896 | tf_op jit(solution)/shard_map/ppermute | solution.py:332
  353.3 20.7 %collective-permute-start.39 = (f32[32,1536]{1,0:T(8,128)S(1)}, f32[32,1536]{1,0:T(8,128)S(1)}, u32[]{:S(2)}, u32[]{:S(2)}) collective-permute-start(f32[32,1536]{1,0:T(8,128)S(1)} %get-tuple-element.89), channel_id=1, source_target_pairs={{0,12},{4,0},{8,4},{12,8},{1,13},{5,1},{9,5},{13,9},{2,14},{6,2},{... | collective-permute-start | bytes 589832 | tf_op jit(solution)/shard_map/ppermute | solution.py:326
  (56 other events, 857.1 us)

commit v4 on v3

--- a/solution.py
+++ b/solution.py
@@ -1,4 +1,5 @@
 import functools
+import math
 
 import jax
 import jax.numpy as jnp
@@ -19,7 +20,7 @@
 LEARN_RATE = 0.001
 WEIGHT_DECAY = 0.1
 ADAM_EPSILON = 1e-08
-VMEM_BYTES = 56 * 2**20
+VMEM_SPARE = 3 * 2**19
 UNROLL = 4
 CHUNKS = 2
 MEM, HID, TOK = "mem", "hid", "tok"
@@ -213,12 +214,13 @@
             lax.fori_loop(count, owned, clear, 0)
 
 
-def update_kernel(matrix, kept_ref, keep_ref, swap_ref, weight_ref, moment_ref, variance_ref, *refs):
+def update_kernel(matrix, owned, kept_ref, keep_ref, swap_ref, weight_ref, moment_ref, variance_ref, *refs):
     out_refs = refs[-3:]
     turn = pl.program_id(0)
     tok = lax.axis_index(TOK)
-    owned = weight_ref.shape[3]
+    run = weight_ref.shape[3]
     _, count = owner_count(kept_ref, matrix, tok ^ turn, tok, owned)
+    count = jnp.clip(count - pl.program_id(1) * run, 0, run)
 
     def update_from(grad_ref):
         def update(slot, carry):
@@ -239,15 +241,25 @@
             out_ref[at] = value_ref[at]
         return carry
 
-    lax.fori_loop(count, owned, keep, 0)
-
-
-def join_kernel(keep_ref, swap_ref, *out_refs):
-    groups = keep_ref.shape[0]
-    part = out_refs[0].shape[0]
+    lax.fori_loop(count, run, keep, 0)
+
+
+def join_kernel(pair_major, keep_ref, swap_ref, *out_refs):
+    part = out_refs[0].shape[1]
     for index, out_ref in enumerate(out_refs):
-        group, start = index % groups, index // groups * part
-        out_ref[...] = keep_ref[group, start : start + part] + swap_ref[group, start : start + part]
+        for inner in range(out_ref.shape[0]):
+            group, shift = (inner, index) if pair_major else (index, inner)
+            at = slice(shift * part, (shift + 1) * part)
+            out_ref[inner] = keep_ref[group, at] + swap_ref[group, at]
+
+
+def split_kernel(*refs):
+    inner = refs[0].shape[0]
+    for index, out_ref in enumerate(refs[-inner:]):
+        total = refs[0][index]
+        for ref in refs[1:-inner]:
+            total = total + ref[index]
+        out_ref[...] = total
 
 
 def total_of(refs):
@@ -257,16 +269,23 @@
     return total
 
 
-def activate_kernel(*refs):
+def activate_kernel(split, *refs):
     *part_refs, hidden_ref, preact_ref = refs
-    preact = total_of(part_refs)
-    preact_ref[...] = preact
-    hidden_ref[...] = activate(preact).astype(jnp.bfloat16)
-
-
-def slope_kernel(*refs):
+    span = preact_ref.shape[1] // 2
+    for side, side_refs in enumerate((part_refs[:split], part_refs[split:])):
+        at = slice(side * span, (side + 1) * span)
+        preact = total_of(side_refs)
+        preact_ref[:, at] = preact
+        hidden_ref[:, at] = activate(preact).astype(jnp.bfloat16)
+
+
+def slope_kernel(split, *refs):
     *part_refs, preact_ref, out_ref = refs
-    out_ref[...] = (total_of(part_refs) * gelu_slope(preact_ref[...])).astype(jnp.bfloat16)
+    span = preact_ref.shape[1] // 2
+    for side, side_refs in enumerate((part_refs[:split], part_refs[split:])):
+        at = slice(side * span, (side + 1) * span)
+        slope = gelu_slope(preact_ref[:, at])
+        out_ref[:, at] = (total_of(side_refs) * slope).astype(jnp.bfloat16)
 
 
 def narrow_kernel(block_ref, *out_refs):
@@ -282,25 +301,25 @@
 ANYWHERE = pl.BlockSpec(memory_space=pl.ANY)
 
 
-def call(kernel, outs, scalars, arrays, flops, scratch=()):
-    moved = sum(a.size * a.dtype.itemsize for a in arrays)
-    moved += sum(math_size(o) for o in outs)
+def call(kernel, outs, scalars, arrays, flops, scratch=(), scratch_sizes=()):
+    moved = sum(math_size(a) for a in (*arrays, *outs))
     return pl.pallas_call(
         kernel,
         out_shape=outs,
         in_specs=[SCALARS] * len(scalars) + [WHOLE] * len(arrays),
         out_specs=[WHOLE] * len(outs),
         scratch_shapes=scratch,
-        compiler_params=pltpu.CompilerParams(vmem_limit_bytes=VMEM_BYTES),
+        compiler_params=grant(moved + sum(scratch_sizes)),
         cost_estimate=pl.CostEstimate(flops=flops, bytes_accessed=moved, transcendentals=0),
     )(*scalars, *arrays)
 
 
-def math_size(shape):
-    total = shape.dtype.itemsize
-    for dim in shape.shape:
-        total *= dim
-    return total
+def math_size(array):
+    return math.prod(array.shape) * array.dtype.itemsize
+
+
+def grant(needed):
+    return pltpu.CompilerParams(vmem_limit_bytes=needed + VMEM_SPARE)
 
 
 def on_device(inputs, cotangent, blocks, first_moment, second_moment, places, kept_counts):
@@ -365,7 +384,7 @@
                 )
             ],
             out_specs=[pl.BlockSpec(shape, lambda i: (0, 0, 0))] * tok_count,
-            compiler_params=pltpu.CompilerParams(vmem_limit_bytes=VMEM_BYTES),
+            compiler_params=grant(owned_slots * block_size**2 * 4 * (2 + tok_count)),
         )(blocks)
         moved = [flip_tok(narrow[r], r) for r in range(1, tok_count)]
         return [narrow[0], *moved]
@@ -383,35 +402,58 @@
         flops = 2 * mem_count * rows * local_slots * block_size * block_size
         return call(kernel, outs, scalars, [*row_groups, *weights], flops)
 
-    def over_columns(kernel, outs, arrays, steps):
-        def spec(shape):
+    def half_columns(kernel, outs, arrays, side, steps):
+        span = hidden_span // 2 // steps
+
+        def spec(shape, shift):
             lead = len(shape) - 1
-            return pl.BlockSpec(
-                tuple(shape[:-1]) + (shape[-1] // steps,), lambda i: (0,) * lead + (i,)
-            )
-
+            return pl.BlockSpec(tuple(shape[:-1]) + (span,), lambda i: (0,) * lead + (i + shift,))
+
+        shift = side * steps
+        needed = sum(math_size(a) for a in outs) // steps * 2
+        needed += sum(math_size(a) for a in arrays) // steps
         return pl.pallas_call(
             kernel,
             grid=(steps,),
             out_shape=outs,
-            in_specs=[spec(a.shape) for a in arrays],
-            out_specs=[spec(o.shape) for o in outs],
-            compiler_params=pltpu.CompilerParams(vmem_limit_bytes=VMEM_BYTES),
+            in_specs=[spec(a.shape, shift) for a in arrays],
+            out_specs=[spec(o.shape, 0) for o in outs],
+            compiler_params=grant(needed),
             cost_estimate=pl.CostEstimate(
-                flops=sum(o.size for o in outs) * 4,
-                bytes_accessed=sum(a.size * a.dtype.itemsize for a in (*arrays, *outs)),
+                flops=sum(math.prod(o.shape) for o in outs) * 2,
+                bytes_accessed=needed * steps // 2,
                 transcendentals=0,
             ),
         )(*arrays)
 
     def reduce_plane(keep, send):
-        outs = [jax.ShapeDtypeStruct((part, hidden_span), f32)] * (mem_count * other)
         swap = flip_tok(send, 1)
-        found = over_columns(join_kernel, outs, [keep, swap], 4)
-        terms = [found[0]]
-        for j, b in peers:
-            terms.append(across(found[b * mem_count + j], j, b))
-        return terms
+        span = hidden_span // 2
+
+        def array(*lead):
+            return jax.ShapeDtypeStruct((*lead, span), f32)
+
+        by_mem = half_columns(
+            functools.partial(join_kernel, False),
+            [array(other, part)] * mem_count,
+            [keep, swap],
+            0,
+            2,
+        )
+        by_pair = half_columns(
+            functools.partial(join_kernel, True),
+            [array(mem_count, part)] * other,
+            [keep, swap],
+            1,
+            2,
+        )
+        mem_terms = [by_mem[0]] + [shift_mem(by_mem[j], -j) for j in range(1, mem_count)]
+        pair_terms = [by_pair[0]] + [flip_tok(by_pair[b], 2 * b) for b in range(1, other)]
+        mine, *rest = call(split_kernel, [array(part)] * other, (), mem_terms, part)
+        first = [mine] + [flip_tok(x, 2 * b) for b, x in enumerate(rest, 1)]
+        mine, *rest = call(split_kernel, [array(part)] * mem_count, (), pair_terms, part)
+        second = [mine] + [shift_mem(x, -j) for j, x in enumerate(rest, 1)]
+        return first, second
 
     def gather_plane(piece):
         found = {(0, 0): piece}
@@ -428,7 +470,8 @@
         outs = [jax.ShapeDtypeStruct((rows, span), f32)] * (mem_count * chunks)
         flops = 2 * mem_count * rows * local_slots * block_size * block_size
         scratch = [pltpu.VMEM((mem_count * rows, inputs.shape[1]), f32)]
-        return call(kernel, outs, scalars, [near, far, *weights], flops, scratch)
+        sizes = [mem_count * rows * inputs.shape[1] * 4]
+        return call(kernel, outs, scalars, [near, far, *weights], flops, scratch, sizes)
 
     turn = relative(tok_count)
     step = inputs.shape[0]
@@ -465,23 +508,28 @@
             [row_values, near, far, *late],
             flops,
             [pltpu.VMEM(row_values.shape, bf16)],
+            [math_size(row_values)],
         )
         return keep, flip_tok(send, 1)
 
     def update(matrix, grads, held):
-        state_shape = (1, 1, 1, owned_slots, block_size, block_size)
-        state_spec = pl.BlockSpec(state_shape, lambda i: (matrix, lax.axis_index(TOK) ^ i, 0, 0, 0, 0))
-        grad_spec = pl.BlockSpec((1, owned_slots, block_size, block_size), lambda i: (i // 2, 0, 0, 0))
+        splits = 2 if owned_slots % 2 == 0 else 1
+        run = owned_slots // splits
+        state_spec = pl.BlockSpec(
+            (1, 1, 1, run, block_size, block_size),
+            lambda i, j: (matrix, lax.axis_index(TOK) ^ i, 0, j, 0, 0),
+        )
+        grad_spec = pl.BlockSpec((1, run, block_size, block_size), lambda i, j: (i // 2, j, 0, 0))
         state = (blocks, first_moment, second_moment)
         size = local_slots * block_size * block_size
         return pl.pallas_call(
-            functools.partial(update_kernel, matrix),
-            grid=(tok_count,),
+            functools.partial(update_kernel, matrix, owned_slots),
+            grid=(tok_count, splits),
             out_shape=[jax.ShapeDtypeStruct(s.shape, f32) for s in state],
             in_specs=[SCALARS, grad_spec, grad_spec] + [state_spec] * 3 + [ANYWHERE] * len(held),
             out_specs=[state_spec] * 3,
             input_output_aliases={6 + i: i for i in range(len(held))},
-            compiler_params=pltpu.CompilerParams(vmem_limit_bytes=VMEM_BYTES),
+            compiler_params=grant(16 * run * block_size**2 * 4),
             cost_estimate=pl.CostEstimate(
                 flops=size * 12, bytes_accessed=size * 28, transcendentals=size
             ),
@@ -499,9 +547,12 @@
     back_terms = reduce_plane(*back_part)
     piece = (part, hidden_span)
     outs = [jax.ShapeDtypeStruct(piece, bf16), jax.ShapeDtypeStruct(piece, f32)]
-    hidden_piece, preact = over_columns(activate_kernel, outs, pre_terms, 2)
+    kernel = functools.partial(activate_kernel, len(pre_terms[0]))
+    hidden_piece, preact = call(kernel, outs, (), [*pre_terms[0], *pre_terms[1]], part)
     hidden = gather_plane(hidden_piece)
-    (grad_piece,) = over_columns(slope_kernel, outs[:1], [*back_terms, preact], 2)
+    kernel = functools.partial(slope_kernel, len(back_terms[0]))
+    arrays = [*back_terms[0], *back_terms[1], preact]
+    (grad_piece,) = call(kernel, outs[:1], (), arrays, part)
     pre_grad = gather_plane(grad_piece)
     layer_out = reduce_rows(backward(1, False, *hidden, weights_second))
     grad_in = reduce_rows(backward(0, True, *pre_grad, weights_first))

time: 430 us -> 388 us (0.902)
  Pallas kernels: 110 us -> 57.4 us
  local copies, waits for them, and re-layouts: 12.4 us -> 19.6 us
    ppermute x12 -> x6, waiting for transfers between devices: 86.6 us -> 36.5 us  [across(): return lax.ppermute(array, (MEM, TOK), table)]
    ppermute x14 -> x18, waiting for transfers between devices: 24.3 us -> 62.2 us  [flip_tok(): return lax.ppermute(array, TOK, [(i, i ^ bit) for i in range(tok_count)])]
    pallas_call x6, Pallas kernels: 42.6 us -> 19.5 us  [the longest x2 17.3 us: update(): pl.pallas_call(functools.partial(update_kernel, matrix, owned_slots), gri...]
    pallas_call x6 -> x12, Pallas kernels: 58 us -> 37.2 us  [call(): pl.pallas_call(kernel, out_shape=outs, in_specs=[SCALARS] * len(scalars)...]
    ppermute x7 -> x11, waiting for transfers between devices: 16.8 us -> 33.7 us  [shift_mem(): lax.ppermute(array, MEM, [(i, (i + shift) % mem_count) for i in range(mem...]
    pallas_call x2, Pallas kernels: 9.17 us -> 0.69 us  [gather_weights(): pl.pallas_call(narrow_kernel, grid=(tok_count,), out_shape=[jax.ShapeDtyp...]
    ppermute x12 -> x6, starting transfers between devices: 13 us -> 5.09 us  [across(): return lax.ppermute(array, (MEM, TOK), table)]
    unnamed x75 -> x71, local copies, waits for them, and re-layouts: 12.1 us -> 19.4 us
  transfers between devices with their start and end apart: 54 -> 56, of which waited for: 28 -> 30; matrix products, arithmetic and copies ran while one was open for 2% -> 2% of each run, Pallas kernels for 22% -> 13%
where the time goes in v4:
time: 388 us
  waiting for transfers between devices  228 us (59%)
  starting transfers between devices  74.6 us (19%)
  Pallas kernels  57.4 us (15%)
  local copies, waits for them, and re-layouts  19.6 us (5%)
  other arithmetic  7.22 us (2%)
    ppermute x21, waiting for transfers between devices, shift_hid(): lax.ppermute(array, HID, [(i, (i + shift) % hid_count) for i in range(hid...  95.5 us
    ppermute x18, waiting for transfers between devices, flip_tok(): return lax.ppermute(array, TOK, [(i, i ^ bit) for i in range(tok_count)])  62.2 us
    ppermute x21, starting transfers between devices, shift_hid(): lax.ppermute(array, HID, [(i, (i + shift) % hid_count) for i in range(hid...  53 us
    pallas_call x12, Pallas kernels, call(): pl.pallas_call(kernel, out_shape=outs, in_specs=[SCALARS] * len(scalars)...  37.2 us
    ppermute x6, waiting for transfers between devices, across(): return lax.ppermute(array, (MEM, TOK), table)  36.5 us
    ppermute x11, waiting for transfers between devices, shift_mem(): lax.ppermute(array, MEM, [(i, (i + shift) % mem_count) for i in range(mem...  33.7 us
    unnamed x71, local copies, waits for them, and re-layouts  19.4 us
    pallas_call x2, Pallas kernels, update(): pl.pallas_call(functools.partial(update_kernel, matrix, owned_slots), gri...  17.3 us
  transfers between devices with their start and end apart: 56, of which 30 were waited for; matrix products, arithmetic and copies ran while one was open for 2% of the time, Pallas kernels for 13%

profile of v4, /device:TPU:0, one launch (start us, length us, event | category | flops | bytes accessed | tf_op | source)
XLA Modules:
  0.0 388.0 jit_solution(16673051448523599872)
XLA Ops:
  0.6 5.1 %collective-permute-start.2 = (bf16[32,3072]{1,0:T(8,128)(2,1)}, bf16[32,3072]{1,0:T(8,128)(2,1)S(1)}, u32[]{:S(2)}, u32[]{:S(2)}) collective-permute-start(bf16[32,3072]{1,0:T(8,128)(2,1)} %param.7), channel_id=1, source_target_pairs={{0,12},{4,0},{8,4},{12,8},{1,13},{5,1},{9,5},{13,9},{2,14},{6,2},{... | collective-permute-start | bytes 589832 | tf_op jit(solution)/shard_map/ppermute | solution.py:345
  15.8 4.9 %collective-permute-done = bf16[32,3072]{1,0:T(8,128)(2,1)S(1)} collective-permute-done((bf16[32,3072]{1,0:T(8,128)(2,1)}, bf16[32,3072]{1,0:T(8,128)(2,1)S(1)}, u32[]{:S(2)}, u32[]{:S(2)}) %collective-permute-start) | collective-permute-done | bytes 196640 | tf_op jit(solution)/shard_map/ppermute | solution.py:345
  20.6 12.3 %collective-permute-start.27 = (bf16[32,3072]{1,0:T(8,128)(2,1)S(1)}, bf16[32,3072]{1,0:T(8,128)(2,1)S(1)}, u32[]{:S(2)}, u32[]{:S(2)}) collective-permute-start(bf16[32,3072]{1,0:T(8,128)(2,1)S(1)} %copy-done.24), channel_id=1, source_target_pairs={{0,4},{4,8},{8,12},{12,0},{1,5},{5,9},{9,13},{13,1},{2,6},{6,10},{... | collective-permute-start | bytes 589832 | tf_op jit(solution)/shard_map/ppermute | solution.py:345
  42.1 7.2 %collective-permute-done.5.refs_4_.refs_2_ = bf16[18,128,128]{2,1,0:T(8,128)(2,1)S(1)} collective-permute-done((bf16[18,128,128]{2,1,0:T(8,128)(2,1)S(1)}, bf16[18,128,128]{2,1,0:T(8,128)(2,1)S(1)}, u32[]{:S(2)}, u32[]{:S(2)}) %collective-permute-start.5) | collective-permute-done | bytes 589856 | tf_op jit(solution)/shard_map/ppermute | solution.py:351
  50.8 10.2 %collective-permute-done.6.refs_5_.refs_3_ = bf16[18,128,128]{2,1,0:T(8,128)(2,1)S(1)} collective-permute-done((bf16[18,128,128]{2,1,0:T(8,128)(2,1)S(1)}, bf16[18,128,128]{2,1,0:T(8,128)(2,1)S(1)}, u32[]{:S(2)}, u32[]{:S(2)}) %collective-permute-start.6) | collective-permute-done | bytes 589856 | tf_op jit(solution)/shard_map/ppermute | solution.py:351
  63.2 5.9 %shard_map.111 = (bf16[256,3072]{1,0:T(8,128)(2,1)S(1)}, f32[2,64,6144]{2,1,0:T(8,128)S(1)}, f32[2,64,6144]{2,1,0:T(8,128)S(1)}) custom-call(s32[2,4]{1,0:T(2,128)S(1)} %bitcast.29, s32[2,144]{1,0:T(2,128)S(1)} %bitcast.22, bf16[128,3072]{1,0:T(8,128)(2,1)S(1)} %constant_dynamic-update-slice_fusion.refs_0_, ...), custom_call_target="tpu_custom_call" | custom-call | flops 603979776 | bytes 11796480 | tf_op jit(solution)/shard_map/pallas_call | solution.py:306
  70.3 4.3 %collective-permute-done.17.refs_2_.refs_4_ = bf16[18,128,128]{2,1,0:T(8,128)(2,1)S(1)} collective-permute-done((bf16[18,128,128]{2,1,0:T(8,128)(2,1)S(1)}, bf16[18,128,128]{2,1,0:T(8,128)(2,1)S(1)}, u32[]{:S(2)}, u32[]{:S(2)}) %collective-permute-start.17) | collective-permute-done | bytes 589856 | tf_op jit(solution)/shard_map/ppermute | solution.py:351
  74.6 11.7 %collective-permute-done.18.refs_3_.refs_5_ = bf16[18,128,128]{2,1,0:T(8,128)(2,1)S(1)} collective-permute-done((bf16[18,128,128]{2,1,0:T(8,128)(2,1)S(1)}, bf16[18,128,128]{2,1,0:T(8,128)(2,1)S(1)}, u32[]{:S(2)}, u32[]{:S(2)}) %collective-permute-start.18) | collective-permute-done | bytes 589856 | tf_op jit(solution)/shard_map/ppermute | solution.py:351
  98.2 12.7 %collective-permute-done.10.refs_1_ = f32[2,32,3072]{2,1,0:T(8,128)S(1)} collective-permute-done((f32[2,32,3072]{2,1,0:T(8,128)S(1)}, f32[2,32,3072]{2,1,0:T(8,128)S(1)}, u32[]{:S(2)}, u32[]{:S(2)}) %collective-permute-start.10) | collective-permute-done | bytes 786464 | tf_op jit(solution)/shard_map/ppermute | solution.py:351
  113.7 14.1 %collective-permute-done.34.refs_1_ = f32[2,32,3072]{2,1,0:T(8,128)S(1)} collective-permute-done((f32[2,32,3072]{2,1,0:T(8,128)S(1)}, f32[2,32,3072]{2,1,0:T(8,128)S(1)}, u32[]{:S(2)}, u32[]{:S(2)}) %collective-permute-start.34) | collective-permute-done | bytes 786464 | tf_op jit(solution)/shard_map/ppermute | solution.py:351
  130.6 8.2 %collective-permute-done.11.refs_3_ = f32[32,3072]{1,0:T(8,128)S(1)} collective-permute-done((f32[32,3072]{1,0:T(8,128)S(1)}, f32[32,3072]{1,0:T(8,128)S(1)}, u32[]{:S(2)}, u32[]{:S(2)}) %collective-permute-start.11) | collective-permute-done | bytes 393248 | tf_op jit(solution)/shard_map/ppermute | solution.py:348
  142.6 4.5 %collective-permute-done.35.refs_3_ = f32[32,3072]{1,0:T(8,128)S(1)} collective-permute-done((f32[32,3072]{1,0:T(8,128)S(1)}, f32[32,3072]{1,0:T(8,128)S(1)}, u32[]{:S(2)}, u32[]{:S(2)}) %collective-permute-start.35) | collective-permute-done | bytes 393248 | tf_op jit(solution)/shard_map/ppermute | solution.py:348
  149.2 6.0 %collective-permute-done.14 = bf16[32,6144]{1,0:T(8,128)(2,1)S(1)} collective-permute-done((bf16[32,6144]{1,0:T(8,128)(2,1)S(1)}, bf16[32,6144]{1,0:T(8,128)(2,1)S(1)}, u32[]{:S(2)}, u32[]{:S(2)}) %collective-permute-start.14) | collective-permute-done | bytes 393248 | tf_op jit(solution)/shard_map/ppermute | solution.py:359
  155.2 8.9 %collective-permute-done.13 = bf16[32,6144]{1,0:T(8,128)(2,1)S(1)} collective-permute-done((bf16[32,6144]{1,0:T(8,128)(2,1)S(1)}, bf16[32,6144]{1,0:T(8,128)(2,1)S(1)}, u32[]{:S(2)}, u32[]{:S(2)}) %collective-permute-start.13) | collective-permute-done | bytes 393248 | tf_op jit(solution)/shard_map/ppermute | solution.py:359
  164.4 7.7 %collective-permute-done.38 = bf16[32,6144]{1,0:T(8,128)(2,1)S(1)} collective-permute-done((bf16[32,6144]{1,0:T(8,128)(2,1)S(1)}, bf16[32,6144]{1,0:T(8,128)(2,1)S(1)}, u32[]{:S(2)}, u32[]{:S(2)}) %collective-permute-start.38) | collective-permute-done | bytes 393248 | tf_op jit(solution)/shard_map/ppermute | solution.py:359
  172.1 7.7 %collective-permute-done.37 = bf16[32,6144]{1,0:T(8,128)(2,1)S(1)} collective-permute-done((bf16[32,6144]{1,0:T(8,128)(2,1)S(1)}, bf16[32,6144]{1,0:T(8,128)(2,1)S(1)}, u32[]{:S(2)}, u32[]{:S(2)}) %collective-permute-start.37) | collective-permute-done | bytes 393248 | tf_op jit(solution)/shard_map/ppermute | solution.py:359
  179.8 6.3 %collective-permute-done.36 = bf16[32,6144]{1,0:T(8,128)(2,1)S(1)} collective-permute-done((bf16[32,6144]{1,0:T(8,128)(2,1)S(1)}, bf16[32,6144]{1,0:T(8,128)(2,1)S(1)}, u32[]{:S(2)}, u32[]{:S(2)}) %collective-permute-start.36) | collective-permute-done | bytes 393248 | tf_op jit(solution)/shard_map/ppermute | solution.py:359
  186.3 11.4 %collective-permute-done.50 = bf16[2,32,3072]{2,1,0:T(8,128)(2,1)S(1)} collective-permute-done((bf16[2,32,3072]{2,1,0:T(8,128)(2,1)S(1)}, bf16[2,32,3072]{2,1,0:T(8,128)(2,1)S(1)}, u32[]{:S(2)}, u32[]{:S(2)}) %collective-permute-start.50) | collective-permute-done | bytes 393248 | tf_op jit(solution)/shard_map/ppermute | solution.py:348
  200.1 5.9 %collective-permute-start.52 = (bf16[2,2,32,3072]{3,2,1,0:T(8,128)(2,1)}, bf16[2,2,32,3072]{3,2,1,0:T(8,128)(2,1)}, u32[]{:S(2)}, u32[]{:S(2)}) collective-permute-start(bf16[2,2,32,3072]{3,2,1,0:T(8,128)(2,1)} %pad_maximum_fusion.2.refs_3_), channel_id=1, source_target_pairs={{0,8},{4,12},{8,0},{12,4},{1,9},{5,13},{9,1},{13,5},{2,10},{6,14},... | collective-permute-start | bytes 2359304 | tf_op jit(solution)/shard_map/ppermute | solution.py:345
  215.8 7.3 %shard_map.125 = (f32[128,1536]{1,0:T(8,128)S(1)}, f32[128,1536]{1,0:T(8,128)}, f32[128,1536]{1,0:T(8,128)S(1)}, f32[128,1536]{1,0:T(8,128)S(1)}) custom-call(s32[2,4]{1,0:T(2,128)S(1)} %bitcast.32, s32[2,144]{1,0:T(2,128)S(1)} %bitcast.26, bf16[2,64,6144]{2,1,0:T(8,128)(2,1)S(1)} %bitcast.20, ...), custom_call_target="tpu_custom_call" | custom-call | flops 603979776 | bytes 8650752 | tf_op jit(solution)/shard_map/pallas_call | solution.py:306
  226.7 47.1 %collective-permute-done.52.refs_5_ = bf16[2,2,32,3072]{3,2,1,0:T(8,128)(2,1)} collective-permute-done((bf16[2,2,32,3072]{3,2,1,0:T(8,128)(2,1)}, bf16[2,2,32,3072]{3,2,1,0:T(8,128)(2,1)}, u32[]{:S(2)}, u32[]{:S(2)}) %collective-permute-start.52) | collective-permute-done | bytes 786464 | tf_op jit(solution)/shard_map/ppermute | solution.py:345
  277.7 7.2 %shard_map.127 = (f32[2,18,128,128]{3,2,1,0:T(8,128)S(1)}, f32[2,18,128,128]{3,2,1,0:T(8,128)S(1)}) custom-call(s32[2,4]{1,0:T(2,128)S(1)} %bitcast.33, s32[2,144]{1,0:T(2,128)S(1)} %bitcast.27, s32[2,144]{1,0:T(2,128)S(1)} %collective-permute-done.48.far_place_ref, bf16[256,3072]{1,0:T(8,128)(2,1)S(1)} %copy-done.12, bf16[2,64,6144]{2,1,0:T(8,128)(2,1)S(1)} %bitcast.18, ...), custom_call_target="tpu_custom_call" | custom-call | flops 603979776 | bytes 12582912 | tf_op jit(solution)/shard_map/pallas_call | solution.py:306
  285.2 8.6 %shard_map.126 = (f32[2,18,128,128]{3,2,1,0:T(8,128)S(1)}, f32[2,18,128,128]{3,2,1,0:T(8,128)S(1)}) custom-call(s32[2,4]{1,0:T(2,128)S(1)} %bitcast.34, s32[2,144]{1,0:T(2,128)S(1)} %bitcast.28, s32[2,144]{1,0:T(2,128)S(1)} %collective-permute-done.48.far_place_ref, bf16[256,3072]{1,0:T(8,128)(2,1)S(1)} %copy-done.10, bf16[2,64,6144]{2,1,0:T(8,128)(2,1)S(1)} %bitcast.21, ...), custom_call_target="tpu_custom_call" | custom-call | flops 603979776 | bytes 12582912 | tf_op jit(solution)/shard_map/pallas_call | solution.py:306
  300.3 4.9 %collective-permute-done.44 = f32[128,1536]{1,0:T(8,128)S(1)} collective-permute-done((f32[128,1536]{1,0:T(8,128)}, f32[128,1536]{1,0:T(8,128)S(1)}, u32[]{:S(2)}, u32[]{:S(2)}) %collective-permute-start.44) | collective-permute-done | bytes 786464 | tf_op jit(solution)/shard_map/ppermute | solution.py:348
  308.2 8.3 %collective-permute-done.21 = f32[32,1536]{1,0:T(8,128)S(1)} collective-permute-done((f32[32,1536]{1,0:T(8,128)S(1)}, f32[32,1536]{1,0:T(8,128)S(1)}, u32[]{:S(2)}, u32[]{:S(2)}) %collective-permute-start.21) | collective-permute-done | bytes 196640 | tf_op jit(solution)/shard_map/ppermute | solution.py:345
  322.3 9.3 %collective-permute-start.43 = (f32[32,1536]{1,0:T(8,128)S(1)}, f32[32,1536]{1,0:T(8,128)S(1)}, u32[]{:S(2)}, u32[]{:S(2)}) collective-permute-start(f32[32,1536]{1,0:T(8,128)S(1)} %get-tuple-element.106), channel_id=1, source_target_pairs={{0,4},{4,8},{8,12},{12,0},{1,5},{5,9},{9,13},{13,1},{2,6},{6,10},{... | collective-permute-start | bytes 589832 | tf_op jit(solution)/shard_map/ppermute | solution.py:345
  333.5 7.3 %collective-permute-done.41 = f32[32,1536]{1,0:T(8,128)S(1)} collective-permute-done((f32[32,1536]{1,0:T(8,128)S(1)}, f32[32,1536]{1,0:T(8,128)S(1)}, u32[]{:S(2)}, u32[]{:S(2)}) %collective-permute-start.41) | collective-permute-done | bytes 196640 | tf_op jit(solution)/shard_map/ppermute | solution.py:345
  340.8 7.6 %collective-permute-start.47 = (f32[32,1536]{1,0:T(8,128)S(1)}, f32[32,1536]{1,0:T(8,128)S(1)}, u32[]{:S(2)}, u32[]{:S(2)}) collective-permute-start(f32[32,1536]{1,0:T(8,128)S(1)} %get-tuple-element.109), channel_id=1, source_target_pairs={{0,4},{4,8},{8,12},{12,0},{1,5},{5,9},{9,13},{13,1},{2,6},{6,10},{... | collective-permute-start | bytes 589832 | tf_op jit(solution)/shard_map/ppermute | solution.py:345
  351.1 6.6 %collective-permute-done.45 = f32[32,1536]{1,0:T(8,128)S(1)} collective-permute-done((f32[32,1536]{1,0:T(8,128)S(1)}, f32[32,1536]{1,0:T(8,128)S(1)}, u32[]{:S(2)}, u32[]{:S(2)}) %collective-permute-start.45) | collective-permute-done | bytes 196640 | tf_op jit(solution)/shard_map/ppermute | solution.py:345
  357.7 8.5 %collective-permute-done.46 = f32[32,1536]{1,0:T(8,128)S(1)} collective-permute-done((f32[32,1536]{1,0:T(8,128)S(1)}, f32[32,1536]{1,0:T(8,128)S(1)}, u32[]{:S(2)}, u32[]{:S(2)}) %collective-permute-start.46) | collective-permute-done | bytes 196640 | tf_op jit(solution)/shard_map/ppermute | solution.py:345
  370.7 8.7 %shard_map.128 = (f32[2,4,1,18,128,128]{5,4,3,2,1,0:T(8,128)}, f32[2,4,1,18,128,128]{5,4,3,2,1,0:T(8,128)}, f32[2,4,1,18,128,128]{5,4,3,2,1,0:T(8,128)}) custom-call(s32[2,4]{1,0:T(2,128)S(1)} %bitcast.35, f32[2,18,128,128]{3,2,1,0:T(8,128)S(1)} %get-tuple-element.97.keep_ref, f32[2,18,128,128]{3,2,1,0:T(8,128)S(1)} %collective-permute-done.55.swap_ref, ...), custom_call_target="tpu_custom_call" | custom-call | flops 14155776 | bytes 33030144 | tf_op jit(solution)/shard_map/pallas_call | solution.py:525
  379.3 8.6 %shard_map.129 = (f32[2,4,1,18,128,128]{5,4,3,2,1,0:T(8,128)}, f32[2,4,1,18,128,128]{5,4,3,2,1,0:T(8,128)}, f32[2,4,1,18,128,128]{5,4,3,2,1,0:T(8,128)}) custom-call(s32[2,4]{1,0:T(2,128)S(1)} %bitcast.36, f32[2,18,128,128]{3,2,1,0:T(8,128)S(1)} %get-tuple-element.94.keep_ref, ...), custom_call_target="tpu_custom_call", output_to_operand_aliasing={{0}: (6, {}), {1}: (7, {}), {2}: (8, {})} | custom-call | flops 14155776 | bytes 33030144 | tf_op jit(solution)/shard_map/pallas_call | solution.py:525
  (193 shorter events, 92.0 us)
Async XLA Ops:
  0.6 32.4 %collective-permute-start.2 = (bf16[32,3072]{1,0:T(8,128)(2,1)}, bf16[32,3072]{1,0:T(8,128)(2,1)S(1)}, u32[]{:S(2)}, u32[]{:S(2)}) collective-permute-start(bf16[32,3072]{1,0:T(8,128)(2,1)} %param.7), channel_id=1, source_target_pairs={{0,12},{4,0},{8,4},{12,8},{1,13},{5,1},{9,5},{13,9},{2,14},{6,2},{... | collective-permute-start | bytes 589832 | tf_op jit(solution)/shard_map/ppermute | solution.py:345
  5.8 27.2 %collective-permute-start.1 = (bf16[32,3072]{1,0:T(8,128)(2,1)}, bf16[32,3072]{1,0:T(8,128)(2,1)S(1)}, u32[]{:S(2)}, u32[]{:S(2)}) collective-permute-start(bf16[32,3072]{1,0:T(8,128)(2,1)} %param.7), channel_id=1, source_target_pairs={{0,8},{4,12},{8,0},{12,4},{1,9},{5,13},{9,1},{13,5},{2,10},{6,14},... | collective-permute-start | bytes 589832 | tf_op jit(solution)/shard_map/ppermute | solution.py:345
  6.8 34.3 %collective-permute-start.29 = (bf16[32,3072]{1,0:T(8,128)(2,1)}, bf16[32,3072]{1,0:T(8,128)(2,1)S(1)}, u32[]{:S(2)}, u32[]{:S(2)}) collective-permute-start(bf16[32,3072]{1,0:T(8,128)(2,1)} %param.8), channel_id=1, source_target_pairs={{0,12},{4,0},{8,4},{12,8},{1,13},{5,1},{9,5},{13,9},{2,14},{6,2},{... | collective-permute-start | bytes 589832 | tf_op jit(solution)/shard_map/ppermute | solution.py:345
  9.6 29.9 %collective-permute-start.28 = (bf16[32,3072]{1,0:T(8,128)(2,1)}, bf16[32,3072]{1,0:T(8,128)(2,1)S(1)}, u32[]{:S(2)}, u32[]{:S(2)}) collective-permute-start(bf16[32,3072]{1,0:T(8,128)(2,1)} %param.8), channel_id=1, source_target_pairs={{0,8},{4,12},{8,0},{12,4},{1,9},{5,13},{9,1},{13,5},{2,10},{6,14},... | collective-permute-start | bytes 589832 | tf_op jit(solution)/shard_map/ppermute | solution.py:345
  36.1 24.9 %collective-permute-start.6 = (bf16[18,128,128]{2,1,0:T(8,128)(2,1)S(1)}, bf16[18,128,128]{2,1,0:T(8,128)(2,1)S(1)}, u32[]{:S(2)}, u32[]{:S(2)}) collective-permute-start(bf16[18,128,128]{2,1,0:T(8,128)(2,1)S(1)} %get-tuple-element.58), channel_id=1, source_target_pairs={{0,3},{1,2},{2,1},{3,0},{4,7},{5,6},{6,5},{7,4},{8,11},{9,10},{10,... | collective-permute-start | bytes 1769480 | tf_op jit(solution)/shard_map/ppermute | solution.py:351
  39.5 23.7 %collective-permute-start.3 = (bf16[128,3072]{1,0:T(8,128)(2,1)S(1)}, bf16[128,3072]{1,0:T(8,128)(2,1)S(1)}, u32[]{:S(2)}, u32[]{:S(2)}) collective-permute-start(bf16[128,3072]{1,0:T(8,128)(2,1)S(1)} %constant_dynamic-update-slice_fusion.refs_0_), channel_id=1, source_target_pairs={{0,16},{16,0},{1,17},{17,1},{2,18},{18,2},{3,19},{19,3},{4,20},{20... | collective-permute-start | bytes 2359304 | tf_op jit(solution)/shard_map/ppermute | solution.py:348
  41.1 45.2 %collective-permute-start.30 = (bf16[128,3072]{1,0:T(8,128)(2,1)S(1)}, bf16[128,3072]{1,0:T(8,128)(2,1)S(1)}, u32[]{:S(2)}, u32[]{:S(2)}) collective-permute-start(bf16[128,3072]{1,0:T(8,128)(2,1)S(1)} %constant_dynamic-update-slice_fusion.4.refs_0_), channel_id=1, source_target_pairs={{0,16},{16,0},{1,17},{17,1},{2,18},{18,2},{3,19},{19,3},{4,20},{20... | collective-permute-start | bytes 2359304 | tf_op jit(solution)/shard_map/ppermute | solution.py:348
  42.0 28.2 %collective-permute-start.16 = (bf16[18,128,128]{2,1,0:T(8,128)(2,1)S(1)}, bf16[18,128,128]{2,1,0:T(8,128)(2,1)S(1)}, u32[]{:S(2)}, u32[]{:S(2)}) collective-permute-start(bf16[18,128,128]{2,1,0:T(8,128)(2,1)S(1)} %get-tuple-element.71), channel_id=1, source_target_pairs={{0,1},{1,0},{2,3},{3,2},{4,5},{5,4},{6,7},{7,6},{8,9},{9,8},{10,11... | collective-permute-start | bytes 1769480 | tf_op jit(solution)/shard_map/ppermute | solution.py:351
  49.3 25.3 %collective-permute-start.17 = (bf16[18,128,128]{2,1,0:T(8,128)(2,1)S(1)}, bf16[18,128,128]{2,1,0:T(8,128)(2,1)S(1)}, u32[]{:S(2)}, u32[]{:S(2)}) collective-permute-start(bf16[18,128,128]{2,1,0:T(8,128)(2,1)S(1)} %get-tuple-element.72), channel_id=1, source_target_pairs={{0,2},{1,3},{2,0},{3,1},{4,6},{5,7},{6,4},{7,5},{8,10},{9,11},{10,... | collective-permute-start | bytes 1769480 | tf_op jit(solution)/shard_map/ppermute | solution.py:351
  61.0 25.3 %collective-permute-start.18 = (bf16[18,128,128]{2,1,0:T(8,128)(2,1)S(1)}, bf16[18,128,128]{2,1,0:T(8,128)(2,1)S(1)}, u32[]{:S(2)}, u32[]{:S(2)}) collective-permute-start(bf16[18,128,128]{2,1,0:T(8,128)(2,1)S(1)} %get-tuple-element.73), channel_id=1, source_target_pairs={{0,3},{1,2},{2,1},{3,0},{4,7},{5,6},{6,5},{7,4},{8,11},{9,10},{10,... | collective-permute-start | bytes 1769480 | tf_op jit(solution)/shard_map/ppermute | solution.py:351
  90.5 20.4 %collective-permute-start.10 = (f32[2,32,3072]{2,1,0:T(8,128)S(1)}, f32[2,32,3072]{2,1,0:T(8,128)S(1)}, u32[]{:S(2)}, u32[]{:S(2)}) collective-permute-start(f32[2,32,3072]{2,1,0:T(8,128)S(1)} %get-tuple-element.66), channel_id=1, source_target_pairs={{0,2},{1,3},{2,0},{3,1},{4,6},{5,7},{6,4},{7,5},{8,10},{9,11},{10,... | collective-permute-start | bytes 2359304 | tf_op jit(solution)/shard_map/ppermute | solution.py:351
  93.0 20.5 %collective-permute-start.8 = (f32[2,32,3072]{2,1,0:T(8,128)S(1)}, f32[2,32,3072]{2,1,0:T(8,128)S(1)}, u32[]{:S(2)}, u32[]{:S(2)}) collective-permute-start(f32[2,32,3072]{2,1,0:T(8,128)S(1)} %get-tuple-element.62), channel_id=1, source_target_pairs={{0,16},{16,0},{1,17},{17,1},{2,18},{18,2},{3,19},{19,3},{4,20},{20... | collective-permute-start | bytes 2359304 | tf_op jit(solution)/shard_map/ppermute | solution.py:348
  95.7 32.1 %collective-permute-start.34 = (f32[2,32,3072]{2,1,0:T(8,128)S(1)}, f32[2,32,3072]{2,1,0:T(8,128)S(1)}, u32[]{:S(2)}, u32[]{:S(2)}) collective-permute-start(f32[2,32,3072]{2,1,0:T(8,128)S(1)} %get-tuple-element.85), channel_id=1, source_target_pairs={{0,2},{1,3},{2,0},{3,1},{4,6},{5,7},{6,4},{7,5},{8,10},{9,11},{10,... | collective-permute-start | bytes 2359304 | tf_op jit(solution)/shard_map/ppermute | solution.py:351
  98.2 32.1 %collective-permute-start.32 = (f32[2,32,3072]{2,1,0:T(8,128)S(1)}, f32[2,32,3072]{2,1,0:T(8,128)S(1)}, u32[]{:S(2)}, u32[]{:S(2)}) collective-permute-start(f32[2,32,3072]{2,1,0:T(8,128)S(1)} %get-tuple-element.81), channel_id=1, source_target_pairs={{0,16},{16,0},{1,17},{17,1},{2,18},{18,2},{3,19},{19,3},{4,20},{20... | collective-permute-start | bytes 2359304 | tf_op jit(solution)/shard_map/ppermute | solution.py:348
  111.0 27.7 %collective-permute-start.11 = (f32[32,3072]{1,0:T(8,128)S(1)}, f32[32,3072]{1,0:T(8,128)S(1)}, u32[]{:S(2)}, u32[]{:S(2)}) collective-permute-start(f32[32,3072]{1,0:T(8,128)S(1)} %get-tuple-element.68), channel_id=1, source_target_pairs={{0,16},{16,0},{1,17},{17,1},{2,18},{18,2},{3,19},{19,3},{4,20},{20... | collective-permute-start | bytes 1179656 | tf_op jit(solution)/shard_map/ppermute | solution.py:348
  113.5 25.2 %collective-permute-start.9 = (f32[32,3072]{1,0:T(8,128)S(1)}, f32[32,3072]{1,0:T(8,128)S(1)}, u32[]{:S(2)}, u32[]{:S(2)}) collective-permute-start(f32[32,3072]{1,0:T(8,128)S(1)} %get-tuple-element.64), channel_id=1, source_target_pairs={{0,2},{1,3},{2,0},{3,1},{4,6},{5,7},{6,4},{7,5},{8,10},{9,11},{10,... | collective-permute-start | bytes 1179656 | tf_op jit(solution)/shard_map/ppermute | solution.py:351
  139.1 24.9 %collective-permute-start.13 = (bf16[32,6144]{1,0:T(8,128)(2,1)S(1)}, bf16[32,6144]{1,0:T(8,128)(2,1)S(1)}, u32[]{:S(2)}, u32[]{:S(2)}) collective-permute-start(bf16[32,6144]{1,0:T(8,128)(2,1)S(1)} %get-tuple-element.69), channel_id=1, source_target_pairs={{0,16},{1,17},{2,18},{3,19},{16,0},{17,1},{18,2},{19,3},{4,20},{5,... | collective-permute-start | bytes 1179656 | tf_op jit(solution)/shard_map/ppermute | solution.py:359
  140.7 23.5 %collective-permute-start.12 = (bf16[32,6144]{1,0:T(8,128)(2,1)S(1)}, bf16[32,6144]{1,0:T(8,128)(2,1)S(1)}, u32[]{:S(2)}, u32[]{:S(2)}) collective-permute-start(bf16[32,6144]{1,0:T(8,128)(2,1)S(1)} %get-tuple-element.69), channel_id=1, source_target_pairs={{0,2},{1,3},{2,0},{3,1},{16,18},{17,19},{18,16},{19,17},{4,6},{5,7... | collective-permute-start | bytes 1179656 | tf_op jit(solution)/shard_map/ppermute | solution.py:359
  147.1 39.1 %collective-permute-start.49 = (bf16[2,32,3072]{2,1,0:T(8,128)(2,1)S(1)}, bf16[2,32,3072]{2,1,0:T(8,128)(2,1)S(1)}, u32[]{:S(2)}, u32[]{:S(2)}) collective-permute-start(bf16[2,32,3072]{2,1,0:T(8,128)(2,1)S(1)} %pad_maximum_fusion.3), channel_id=1, source_target_pairs={{0,2},{1,3},{2,0},{3,1},{4,6},{5,7},{6,4},{7,5},{8,10},{9,11},{10,... | collective-permute-start | bytes 1179656 | tf_op jit(solution)/shard_map/ppermute | solution.py:351
  147.8 24.3 %collective-permute-start.38 = (bf16[32,6144]{1,0:T(8,128)(2,1)S(1)}, bf16[32,6144]{1,0:T(8,128)(2,1)S(1)}, u32[]{:S(2)}, u32[]{:S(2)}) collective-permute-start(bf16[32,6144]{1,0:T(8,128)(2,1)S(1)} %shard_map.124), channel_id=1, source_target_pairs={{0,18},{1,19},{2,16},{3,17},{16,2},{17,3},{18,0},{19,1},{4,22},{5,... | collective-permute-start | bytes 1179656 | tf_op jit(solution)/shard_map/ppermute | solution.py:359
  155.2 24.6 %collective-permute-start.37 = (bf16[32,6144]{1,0:T(8,128)(2,1)S(1)}, bf16[32,6144]{1,0:T(8,128)(2,1)S(1)}, u32[]{:S(2)}, u32[]{:S(2)}) collective-permute-start(bf16[32,6144]{1,0:T(8,128)(2,1)S(1)} %shard_map.124), channel_id=1, source_target_pairs={{0,16},{1,17},{2,18},{3,19},{16,0},{17,1},{18,2},{19,3},{4,20},{5,... | collective-permute-start | bytes 1179656 | tf_op jit(solution)/shard_map/ppermute | solution.py:359
  164.0 22.0 %collective-permute-start.36 = (bf16[32,6144]{1,0:T(8,128)(2,1)S(1)}, bf16[32,6144]{1,0:T(8,128)(2,1)S(1)}, u32[]{:S(2)}, u32[]{:S(2)}) collective-permute-start(bf16[32,6144]{1,0:T(8,128)(2,1)S(1)} %shard_map.124), channel_id=1, source_target_pairs={{0,2},{1,3},{2,0},{3,1},{16,18},{17,19},{18,16},{19,17},{4,6},{5,7... | collective-permute-start | bytes 1179656 | tf_op jit(solution)/shard_map/ppermute | solution.py:359
  164.3 41.9 %collective-permute-start.15 = (bf16[2,64,6144]{2,1,0:T(8,128)(2,1)S(1)}, bf16[2,64,6144]{2,1,0:T(8,128)(2,1)S(1)}, u32[]{:S(2)}, u32[]{:S(2)}) collective-permute-start(bf16[2,64,6144]{2,1,0:T(8,128)(2,1)S(1)} %bitcast.16), channel_id=1, source_target_pairs={{0,1},{1,0},{2,3},{3,2},{4,5},{5,4},{6,7},{7,6},{8,9},{9,8},{10,11... | collective-permute-start | bytes 4718600 | tf_op jit(solution)/shard_map/ppermute | solution.py:351
  186.2 27.6 %collective-permute-start.39 = (bf16[2,64,6144]{2,1,0:T(8,128)(2,1)S(1)}, bf16[2,64,6144]{2,1,0:T(8,128)(2,1)S(1)}, u32[]{:S(2)}, u32[]{:S(2)}) collective-permute-start(bf16[2,64,6144]{2,1,0:T(8,128)(2,1)S(1)} %bitcast.19), channel_id=1, source_target_pairs={{0,1},{1,0},{2,3},{3,2},{4,5},{5,4},{6,7},{7,6},{8,9},{9,8},{10,11... | collective-permute-start | bytes 4718600 | tf_op jit(solution)/shard_map/ppermute | solution.py:351
  198.7 27.0 %collective-permute-start.53 = (bf16[2,2,32,3072]{3,2,1,0:T(8,128)(2,1)}, bf16[2,2,32,3072]{3,2,1,0:T(8,128)(2,1)S(1)}, u32[]{:S(2)}, u32[]{:S(2)}) collective-permute-start(bf16[2,2,32,3072]{3,2,1,0:T(8,128)(2,1)} %pad_maximum_fusion.2.refs_3_), channel_id=1, source_target_pairs={{0,12},{4,0},{8,4},{12,8},{1,13},{5,1},{9,5},{13,9},{2,14},{6,2},{... | collective-permute-start | bytes 2359304 | tf_op jit(solution)/shard_map/ppermute | solution.py:345
  200.1 73.7 %collective-permute-start.52 = (bf16[2,2,32,3072]{3,2,1,0:T(8,128)(2,1)}, bf16[2,2,32,3072]{3,2,1,0:T(8,128)(2,1)}, u32[]{:S(2)}, u32[]{:S(2)}) collective-permute-start(bf16[2,2,32,3072]{3,2,1,0:T(8,128)(2,1)} %pad_maximum_fusion.2.refs_3_), channel_id=1, source_target_pairs={{0,8},{4,12},{8,0},{12,4},{1,9},{5,13},{9,1},{13,5},{2,10},{6,14},... | collective-permute-start | bytes 2359304 | tf_op jit(solution)/shard_map/ppermute | solution.py:345
  205.9 67.9 %collective-permute-start.51 = (bf16[2,2,32,3072]{3,2,1,0:T(8,128)(2,1)}, bf16[2,2,32,3072]{3,2,1,0:T(8,128)(2,1)}, u32[]{:S(2)}, u32[]{:S(2)}) collective-permute-start(bf16[2,2,32,3072]{3,2,1,0:T(8,128)(2,1)} %pad_maximum_fusion.2.refs_3_), channel_id=1, source_target_pairs={{0,4},{4,8},{8,12},{12,0},{1,5},{5,9},{9,13},{13,1},{2,6},{6,10},{... | collective-permute-start | bytes 2359304 | tf_op jit(solution)/shard_map/ppermute | solution.py:345
  213.8 80.0 %collective-permute-start.19 = (f32[128,1536]{1,0:T(8,128)}, f32[128,1536]{1,0:T(8,128)}, u32[]{:S(2)}, u32[]{:S(2)}) collective-permute-start(f32[128,1536]{1,0:T(8,128)} %get-tuple-element.75), channel_id=1, source_target_pairs={{0,16},{16,0},{1,17},{17,1},{2,18},{18,2},{3,19},{19,3},{4,20},{20... | collective-permute-start | bytes 2359304 | tf_op jit(solution)/shard_map/ppermute | solution.py:348
  213.8 81.5 %collective-permute-start.23 = (f32[128,1536]{1,0:T(8,128)}, f32[128,1536]{1,0:T(8,128)}, u32[]{:S(2)}, u32[]{:S(2)}) collective-permute-start(f32[128,1536]{1,0:T(8,128)} %get-tuple-element.77), channel_id=1, source_target_pairs={{0,16},{16,0},{1,17},{17,1},{2,18},{18,2},{3,19},{19,3},{4,20},{20... | collective-permute-start | bytes 2359304 | tf_op jit(solution)/shard_map/ppermute | solution.py:348
  226.7 70.3 %collective-permute-start.40 = (f32[128,1536]{1,0:T(8,128)}, f32[128,1536]{1,0:T(8,128)}, u32[]{:S(2)}, u32[]{:S(2)}) collective-permute-start(f32[128,1536]{1,0:T(8,128)} %get-tuple-element.90), channel_id=1, source_target_pairs={{0,16},{16,0},{1,17},{17,1},{2,18},{18,2},{3,19},{19,3},{4,20},{20... | collective-permute-start | bytes 2359304 | tf_op jit(solution)/shard_map/ppermute | solution.py:348
  285.0 82.0 %collective-permute-start.55 = (f32[2,18,128,128]{3,2,1,0:T(8,128)S(1)}, f32[2,18,128,128]{3,2,1,0:T(8,128)S(1)}, u32[]{:S(2)}, u32[]{:S(2)}) collective-permute-start(f32[2,18,128,128]{3,2,1,0:T(8,128)S(1)} %get-tuple-element.98), channel_id=1, source_target_pairs={{0,1},{1,0},{2,3},{3,2},{4,5},{5,4},{6,7},{7,6},{8,9},{9,8},{10,11... | collective-permute-start | bytes 7077896 | tf_op jit(solution)/shard_map/ppermute | solution.py:351
  293.8 85.6 %collective-permute-start.54 = (f32[2,18,128,128]{3,2,1,0:T(8,128)S(1)}, f32[2,18,128,128]{3,2,1,0:T(8,128)S(1)}, u32[]{:S(2)}, u32[]{:S(2)}) collective-permute-start(f32[2,18,128,128]{3,2,1,0:T(8,128)S(1)} %get-tuple-element.95), channel_id=1, source_target_pairs={{0,1},{1,0},{2,3},{3,2},{4,5},{5,4},{6,7},{7,6},{8,9},{9,8},{10,11... | collective-permute-start | bytes 7077896 | tf_op jit(solution)/shard_map/ppermute | solution.py:351
  (56 other events, 1017.8 us)

commit v5 on v4

--- a/solution.py
+++ b/solution.py
@@ -97,14 +97,15 @@
 def forward_kernel(
     matrix, transposed, width_blocks, tok_count, hid_count, mem_count, kept_ref, place_ref, *refs
 ):
+    sources = hid_count if matrix else mem_count
     own_refs, weight_refs, (row_ref, keep_ref, send_ref) = (
-        refs[:mem_count],
-        refs[mem_count:-3],
+        refs[:sources],
+        refs[sources:-3],
         refs[-3:],
     )
     half = keep_ref.shape[1]
     _, size = weight_refs[0].shape[:2]
-    rows = own_refs[0].shape[0]
+    rows = row_ref.shape[0] // mem_count
     step = rows // hid_count
     part = rows // tok_count
     turn = relative(tok_count)
@@ -112,9 +113,9 @@
         for block in range(hid_count):
             start = block * step
             spot = ((start // part) ^ turn) * part + start % part + group * rows
-            row_ref[pl.ds(pl.multiple_of(spot, step), step), :] = own_refs[group][
-                start : start + step, :
-            ]
+            row_ref[pl.ds(pl.multiple_of(spot, step), step), :] = (
+                own_refs[block][group] if matrix else own_refs[group][start : start + step, :]
+            )
     keep_ref[...] = jnp.zeros(keep_ref.shape, jnp.float32)
     send_ref[...] = jnp.zeros(send_ref.shape, jnp.float32)
 
@@ -365,6 +366,11 @@
         near = jnp.concatenate(pieces, axis=0)
         return [near] + [shift_mem(near, j) for j in range(1, mem_count)]
 
+    def gather_small(array):
+        found = [array] + [shift_mem(array, j) for j in range(1, mem_count)]
+        own = jnp.stack(found)
+        return [own] + [shift_hid(own, k) for k in range(1, hid_count)]
+
     def gather_late():
         both = flip_tok(jnp.stack([inputs, cotangent]), 2)
         found = [both] + [shift_mem(both, j) for j in range(1, mem_count)]
@@ -393,7 +399,7 @@
         kernel = functools.partial(
             forward_kernel, matrix, transposed, width_blocks, tok_count, hid_count, mem_count
         )
-        width = row_groups[0].shape[1]
+        width = row_groups[0].shape[-1]
         outs = [
             jax.ShapeDtypeStruct((mem_count * rows, width), bf16),
             jax.ShapeDtypeStruct((mem_count, half, hidden_span), f32),
@@ -529,7 +535,7 @@
             in_specs=[SCALARS, grad_spec, grad_spec] + [state_spec] * 3 + [ANYWHERE] * len(held),
             out_specs=[state_spec] * 3,
             input_output_aliases={6 + i: i for i in range(len(held))},
-            compiler_params=grant(16 * run * block_size**2 * 4),
+            compiler_params=grant(44 * 2**20),
             cost_estimate=pl.CostEstimate(
                 flops=size * 12, bytes_accessed=size * 28, transcendentals=size
             ),
@@ -538,7 +544,7 @@
     far_place_ids = flip_tok(place_ids, 2)
     input_groups = gather_rows(inputs)
     weights_first = gather_weights(0)
-    cotangent_groups = gather_rows(cotangent)
+    cotangent_groups = gather_small(cotangent)
     weights_second = gather_weights(1)
     late = gather_late()
     token_rows, *pre_part = forward(0, False, input_groups, weights_first)

time: 388 us -> 384 us (0.990)
  Pallas kernels: 57.4 us -> 68.3 us
  waiting for transfers between devices: 228 us -> 220 us
  local copies, waits for them, and re-layouts: 19.6 us -> 15.7 us
    ppermute x18, waiting for transfers between devices: 62.2 us -> 39.3 us  [flip_tok(): return lax.ppermute(array, TOK, [(i, i ^ bit) for i in range(tok_count)])]
    ppermute x21, waiting for transfers between devices: 95.5 us -> 109 us  [shift_hid(): lax.ppermute(array, HID, [(i, (i + shift) % hid_count) for i in range(hid...]
    pallas_call x2, Pallas kernels: 17.3 us -> 28.3 us  [update(): pl.pallas_call(functools.partial(update_kernel, matrix, owned_slots), gri...]
    ppermute x21, starting transfers between devices: 53 us -> 48.7 us  [shift_hid(): lax.ppermute(array, HID, [(i, (i + shift) % hid_count) for i in range(hid...]
    unnamed x71 -> x56, local copies, waits for them, and re-layouts: 19.4 us -> 15.5 us
  transfers between devices with their start and end apart: 56 -> 56, of which waited for: 30 -> 29; matrix products, arithmetic and copies ran while one was open for 2% -> 2% of each run, Pallas kernels for 13% -> 14%
where the time goes in v5:
time: 384 us; the launch traced here: 383 us
  waiting for transfers between devices  220 us (57%)
  starting transfers between devices  71.3 us (19%)
  Pallas kernels  68.3 us (18%)
  local copies, waits for them, and re-layouts  15.7 us (4%)
  other arithmetic  6.85 us (2%)
    ppermute x21, waiting for transfers between devices, shift_hid(): lax.ppermute(array, HID, [(i, (i + shift) % hid_count) for i in range(hid...  109 us
    ppermute x21, starting transfers between devices, shift_hid(): lax.ppermute(array, HID, [(i, (i + shift) % hid_count) for i in range(hid...  48.7 us
    ppermute x18, waiting for transfers between devices, flip_tok(): return lax.ppermute(array, TOK, [(i, i ^ bit) for i in range(tok_count)])  39.3 us
    pallas_call x12, Pallas kernels, call(): pl.pallas_call(kernel, out_shape=outs, in_specs=[SCALARS] * len(scalars)...  37.1 us
    ppermute x6, waiting for transfers between devices, across(): return lax.ppermute(array, (MEM, TOK), table)  36.8 us
    ppermute x11, waiting for transfers between devices, shift_mem(): lax.ppermute(array, MEM, [(i, (i + shift) % mem_count) for i in range(mem...  34 us
    pallas_call x2, Pallas kernels, update(): pl.pallas_call(functools.partial(update_kernel, matrix, owned_slots), gri...  28.3 us
    unnamed x56, local copies, waits for them, and re-layouts  15.5 us
  transfers between devices with their start and end apart: 56, of which 29 were waited for; matrix products, arithmetic and copies ran while one was open for 2% of the time, Pallas kernels for 14%

profile of v5, /device:TPU:0, one launch (start us, length us, event | category | flops | bytes accessed | tf_op | source)
XLA Modules:
  0.0 383.0 jit_solution(2241153837138542939)
XLA Ops:
  0.6 5.1 %collective-permute-start.2 = (bf16[32,3072]{1,0:T(8,128)(2,1)}, bf16[32,3072]{1,0:T(8,128)(2,1)S(1)}, u32[]{:S(2)}, u32[]{:S(2)}) collective-permute-start(bf16[32,3072]{1,0:T(8,128)(2,1)} %param.7), channel_id=1, source_target_pairs={{0,12},{4,0},{8,4},{12,8},{1,13},{5,1},{9,5},{13,9},{2,14},{6,2},{... | collective-permute-start | bytes 589832 | tf_op jit(solution)/shard_map/ppermute | solution.py:346
  13.6 6.0 %collective-permute-done = bf16[32,3072]{1,0:T(8,128)(2,1)S(1)} collective-permute-done((bf16[32,3072]{1,0:T(8,128)(2,1)}, bf16[32,3072]{1,0:T(8,128)(2,1)S(1)}, u32[]{:S(2)}, u32[]{:S(2)}) %collective-permute-start) | collective-permute-done | bytes 196640 | tf_op jit(solution)/shard_map/ppermute | solution.py:346
  24.7 12.1 %collective-permute-done.30.refs_3_ = bf16[2,32,3072]{2,1,0:T(8,128)(2,1)S(1)} collective-permute-done((bf16[2,32,3072]{2,1,0:T(8,128)(2,1)S(1)}, bf16[2,32,3072]{2,1,0:T(8,128)(2,1)S(1)}, u32[]{:S(2)}, u32[]{:S(2)}) %collective-permute-start.30) | collective-permute-done | bytes 393248 | tf_op jit(solution)/shard_map/ppermute | solution.py:346
  41.7 5.7 %collective-permute-done.6.refs_5_.refs_3_ = bf16[18,128,128]{2,1,0:T(8,128)(2,1)S(1)} collective-permute-done((bf16[18,128,128]{2,1,0:T(8,128)(2,1)S(1)}, bf16[18,128,128]{2,1,0:T(8,128)(2,1)S(1)}, u32[]{:S(2)}, u32[]{:S(2)}) %collective-permute-start.6) | collective-permute-done | bytes 589856 | tf_op jit(solution)/shard_map/ppermute | solution.py:352
  53.5 5.9 %shard_map.111 = (bf16[256,3072]{1,0:T(8,128)(2,1)S(1)}, f32[2,64,6144]{2,1,0:T(8,128)S(1)}, f32[2,64,6144]{2,1,0:T(8,128)S(1)}) custom-call(s32[2,4]{1,0:T(2,128)S(1)} %bitcast.26, s32[2,144]{1,0:T(2,128)S(1)} %bitcast.19, bf16[128,3072]{1,0:T(8,128)(2,1)S(1)} %constant_dynamic-update-slice_fusion.refs_0_, ...), custom_call_target="tpu_custom_call" | custom-call | flops 603979776 | bytes 11796480 | tf_op jit(solution)/shard_map/pallas_call | solution.py:307
  60.5 5.3 %collective-permute-done.29.refs_2_ = bf16[2,32,3072]{2,1,0:T(8,128)(2,1)S(1)} collective-permute-done((bf16[2,32,3072]{2,1,0:T(8,128)(2,1)S(1)}, bf16[2,32,3072]{2,1,0:T(8,128)(2,1)S(1)}, u32[]{:S(2)}, u32[]{:S(2)}) %collective-permute-start.29) | collective-permute-done | bytes 393248 | tf_op jit(solution)/shard_map/ppermute | solution.py:346
  65.8 4.9 %collective-permute-done.18.refs_3_.refs_7_ = bf16[18,128,128]{2,1,0:T(8,128)(2,1)S(1)} collective-permute-done((bf16[18,128,128]{2,1,0:T(8,128)(2,1)S(1)}, bf16[18,128,128]{2,1,0:T(8,128)(2,1)S(1)}, u32[]{:S(2)}, u32[]{:S(2)}) %collective-permute-start.18) | collective-permute-done | bytes 589856 | tf_op jit(solution)/shard_map/ppermute | solution.py:352
  82.8 12.6 %collective-permute-done.10.refs_1_ = f32[2,32,3072]{2,1,0:T(8,128)S(1)} collective-permute-done((f32[2,32,3072]{2,1,0:T(8,128)S(1)}, f32[2,32,3072]{2,1,0:T(8,128)S(1)}, u32[]{:S(2)}, u32[]{:S(2)}) %collective-permute-start.10) | collective-permute-done | bytes 786464 | tf_op jit(solution)/shard_map/ppermute | solution.py:352
  98.1 14.1 %collective-permute-done.34.refs_1_ = f32[2,32,3072]{2,1,0:T(8,128)S(1)} collective-permute-done((f32[2,32,3072]{2,1,0:T(8,128)S(1)}, f32[2,32,3072]{2,1,0:T(8,128)S(1)}, u32[]{:S(2)}, u32[]{:S(2)}) %collective-permute-start.34) | collective-permute-done | bytes 786464 | tf_op jit(solution)/shard_map/ppermute | solution.py:352
  115.0 8.2 %collective-permute-done.11.refs_3_ = f32[32,3072]{1,0:T(8,128)S(1)} collective-permute-done((f32[32,3072]{1,0:T(8,128)S(1)}, f32[32,3072]{1,0:T(8,128)S(1)}, u32[]{:S(2)}, u32[]{:S(2)}) %collective-permute-start.11) | collective-permute-done | bytes 393248 | tf_op jit(solution)/shard_map/ppermute | solution.py:349
  127.1 4.5 %collective-permute-done.35.refs_3_ = f32[32,3072]{1,0:T(8,128)S(1)} collective-permute-done((f32[32,3072]{1,0:T(8,128)S(1)}, f32[32,3072]{1,0:T(8,128)S(1)}, u32[]{:S(2)}, u32[]{:S(2)}) %collective-permute-start.35) | collective-permute-done | bytes 393248 | tf_op jit(solution)/shard_map/ppermute | solution.py:349
  133.7 5.9 %collective-permute-done.14 = bf16[32,6144]{1,0:T(8,128)(2,1)S(1)} collective-permute-done((bf16[32,6144]{1,0:T(8,128)(2,1)S(1)}, bf16[32,6144]{1,0:T(8,128)(2,1)S(1)}, u32[]{:S(2)}, u32[]{:S(2)}) %collective-permute-start.14) | collective-permute-done | bytes 393248 | tf_op jit(solution)/shard_map/ppermute | solution.py:360
  139.6 8.9 %collective-permute-done.13 = bf16[32,6144]{1,0:T(8,128)(2,1)S(1)} collective-permute-done((bf16[32,6144]{1,0:T(8,128)(2,1)S(1)}, bf16[32,6144]{1,0:T(8,128)(2,1)S(1)}, u32[]{:S(2)}, u32[]{:S(2)}) %collective-permute-start.13) | collective-permute-done | bytes 393248 | tf_op jit(solution)/shard_map/ppermute | solution.py:360
  148.8 7.7 %collective-permute-done.38 = bf16[32,6144]{1,0:T(8,128)(2,1)S(1)} collective-permute-done((bf16[32,6144]{1,0:T(8,128)(2,1)S(1)}, bf16[32,6144]{1,0:T(8,128)(2,1)S(1)}, u32[]{:S(2)}, u32[]{:S(2)}) %collective-permute-start.38) | collective-permute-done | bytes 393248 | tf_op jit(solution)/shard_map/ppermute | solution.py:360
  156.5 8.1 %collective-permute-done.37 = bf16[32,6144]{1,0:T(8,128)(2,1)S(1)} collective-permute-done((bf16[32,6144]{1,0:T(8,128)(2,1)S(1)}, bf16[32,6144]{1,0:T(8,128)(2,1)S(1)}, u32[]{:S(2)}, u32[]{:S(2)}) %collective-permute-start.37) | collective-permute-done | bytes 393248 | tf_op jit(solution)/shard_map/ppermute | solution.py:360
  164.6 6.3 %collective-permute-done.36 = bf16[32,6144]{1,0:T(8,128)(2,1)S(1)} collective-permute-done((bf16[32,6144]{1,0:T(8,128)(2,1)S(1)}, bf16[32,6144]{1,0:T(8,128)(2,1)S(1)}, u32[]{:S(2)}, u32[]{:S(2)}) %collective-permute-start.36) | collective-permute-done | bytes 393248 | tf_op jit(solution)/shard_map/ppermute | solution.py:360
  171.2 11.4 %collective-permute-done.50 = bf16[2,32,3072]{2,1,0:T(8,128)(2,1)S(1)} collective-permute-done((bf16[2,32,3072]{2,1,0:T(8,128)(2,1)S(1)}, bf16[2,32,3072]{2,1,0:T(8,128)(2,1)S(1)}, u32[]{:S(2)}, u32[]{:S(2)}) %collective-permute-start.50) | collective-permute-done | bytes 393248 | tf_op jit(solution)/shard_map/ppermute | solution.py:349
  183.6 5.0 %collective-permute-start.53 = (bf16[2,2,32,3072]{3,2,1,0:T(8,128)(2,1)}, bf16[2,2,32,3072]{3,2,1,0:T(8,128)(2,1)S(1)}, u32[]{:S(2)}, u32[]{:S(2)}) collective-permute-start(bf16[2,2,32,3072]{3,2,1,0:T(8,128)(2,1)} %pad_maximum_fusion.2.refs_3_), channel_id=1, source_target_pairs={{0,12},{4,0},{8,4},{12,8},{1,13},{5,1},{9,5},{13,9},{2,14},{6,2},{... | collective-permute-start | bytes 2359304 | tf_op jit(solution)/shard_map/ppermute | solution.py:346
  188.6 4.9 %collective-permute-start.52 = (bf16[2,2,32,3072]{3,2,1,0:T(8,128)(2,1)}, bf16[2,2,32,3072]{3,2,1,0:T(8,128)(2,1)}, u32[]{:S(2)}, u32[]{:S(2)}) collective-permute-start(bf16[2,2,32,3072]{3,2,1,0:T(8,128)(2,1)} %pad_maximum_fusion.2.refs_3_), channel_id=1, source_target_pairs={{0,8},{4,12},{8,0},{12,4},{1,9},{5,13},{9,1},{13,5},{2,10},{6,14},... | collective-permute-start | bytes 2359304 | tf_op jit(solution)/shard_map/ppermute | solution.py:346
  205.1 7.3 %shard_map.125 = (f32[128,1536]{1,0:T(8,128)S(1)}, f32[128,1536]{1,0:T(8,128)}, f32[128,1536]{1,0:T(8,128)S(1)}, f32[128,1536]{1,0:T(8,128)S(1)}) custom-call(s32[2,4]{1,0:T(2,128)S(1)} %bitcast.29, s32[2,144]{1,0:T(2,128)S(1)} %bitcast.23, bf16[2,64,6144]{2,1,0:T(8,128)(2,1)S(1)} %bitcast.17, ...), custom_call_target="tpu_custom_call" | custom-call | flops 603979776 | bytes 8650752 | tf_op jit(solution)/shard_map/pallas_call | solution.py:307
  216.0 45.7 %collective-permute-done.52.refs_5_ = bf16[2,2,32,3072]{3,2,1,0:T(8,128)(2,1)} collective-permute-done((bf16[2,2,32,3072]{3,2,1,0:T(8,128)(2,1)}, bf16[2,2,32,3072]{3,2,1,0:T(8,128)(2,1)}, u32[]{:S(2)}, u32[]{:S(2)}) %collective-permute-start.52) | collective-permute-done | bytes 786464 | tf_op jit(solution)/shard_map/ppermute | solution.py:346
  265.6 7.2 %shard_map.127 = (f32[2,18,128,128]{3,2,1,0:T(8,128)S(1)}, f32[2,18,128,128]{3,2,1,0:T(8,128)S(1)}) custom-call(s32[2,4]{1,0:T(2,128)S(1)} %bitcast.30, s32[2,144]{1,0:T(2,128)S(1)} %bitcast.24, s32[2,144]{1,0:T(2,128)S(1)} %collective-permute-done.48.far_place_ref, bf16[256,3072]{1,0:T(8,128)(2,1)S(1)} %copy-done.11, bf16[2,64,6144]{2,1,0:T(8,128)(2,1)S(1)} %bitcast.15, ...), custom_call_target="tpu_custom_call" | custom-call | flops 603979776 | bytes 12582912 | tf_op jit(solution)/shard_map/pallas_call | solution.py:307
  273.0 8.5 %shard_map.126 = (f32[2,18,128,128]{3,2,1,0:T(8,128)S(1)}, f32[2,18,128,128]{3,2,1,0:T(8,128)S(1)}) custom-call(s32[2,4]{1,0:T(2,128)S(1)} %bitcast.31, s32[2,144]{1,0:T(2,128)S(1)} %bitcast.25, s32[2,144]{1,0:T(2,128)S(1)} %collective-permute-done.48.far_place_ref, bf16[256,3072]{1,0:T(8,128)(2,1)S(1)} %copy-done.9, bf16[2,64,6144]{2,1,0:T(8,128)(2,1)S(1)} %bitcast.18, ...), custom_call_target="tpu_custom_call" | custom-call | flops 603979776 | bytes 12582912 | tf_op jit(solution)/shard_map/pallas_call | solution.py:307
  287.9 5.0 %collective-permute-done.44 = f32[128,1536]{1,0:T(8,128)S(1)} collective-permute-done((f32[128,1536]{1,0:T(8,128)S(1)}, f32[128,1536]{1,0:T(8,128)S(1)}, u32[]{:S(2)}, u32[]{:S(2)}) %collective-permute-start.44) | collective-permute-done | bytes 786464 | tf_op jit(solution)/shard_map/ppermute | solution.py:349
  295.9 8.3 %collective-permute-done.21 = f32[32,1536]{1,0:T(8,128)S(1)} collective-permute-done((f32[32,1536]{1,0:T(8,128)S(1)}, f32[32,1536]{1,0:T(8,128)S(1)}, u32[]{:S(2)}, u32[]{:S(2)}) %collective-permute-start.21) | collective-permute-done | bytes 196640 | tf_op jit(solution)/shard_map/ppermute | solution.py:346
  309.9 9.3 %collective-permute-start.43 = (f32[32,1536]{1,0:T(8,128)S(1)}, f32[32,1536]{1,0:T(8,128)S(1)}, u32[]{:S(2)}, u32[]{:S(2)}) collective-permute-start(f32[32,1536]{1,0:T(8,128)S(1)} %get-tuple-element.106), channel_id=1, source_target_pairs={{0,4},{4,8},{8,12},{12,0},{1,5},{5,9},{9,13},{13,1},{2,6},{6,10},{... | collective-permute-start | bytes 589832 | tf_op jit(solution)/shard_map/ppermute | solution.py:346
  321.2 7.4 %collective-permute-done.41 = f32[32,1536]{1,0:T(8,128)S(1)} collective-permute-done((f32[32,1536]{1,0:T(8,128)S(1)}, f32[32,1536]{1,0:T(8,128)S(1)}, u32[]{:S(2)}, u32[]{:S(2)}) %collective-permute-start.41) | collective-permute-done | bytes 196640 | tf_op jit(solution)/shard_map/ppermute | solution.py:346
  328.6 7.5 %collective-permute-start.47 = (f32[32,1536]{1,0:T(8,128)S(1)}, f32[32,1536]{1,0:T(8,128)S(1)}, u32[]{:S(2)}, u32[]{:S(2)}) collective-permute-start(f32[32,1536]{1,0:T(8,128)S(1)} %get-tuple-element.109), channel_id=1, source_target_pairs={{0,4},{4,8},{8,12},{12,0},{1,5},{5,9},{9,13},{13,1},{2,6},{6,10},{... | collective-permute-start | bytes 589832 | tf_op jit(solution)/shard_map/ppermute | solution.py:346
  338.7 6.7 %collective-permute-done.45 = f32[32,1536]{1,0:T(8,128)S(1)} collective-permute-done((f32[32,1536]{1,0:T(8,128)S(1)}, f32[32,1536]{1,0:T(8,128)S(1)}, u32[]{:S(2)}, u32[]{:S(2)}) %collective-permute-start.45) | collective-permute-done | bytes 196640 | tf_op jit(solution)/shard_map/ppermute | solution.py:346
  345.5 8.5 %collective-permute-done.46 = f32[32,1536]{1,0:T(8,128)S(1)} collective-permute-done((f32[32,1536]{1,0:T(8,128)S(1)}, f32[32,1536]{1,0:T(8,128)S(1)}, u32[]{:S(2)}, u32[]{:S(2)}) %collective-permute-start.46) | collective-permute-done | bytes 196640 | tf_op jit(solution)/shard_map/ppermute | solution.py:346
  354.7 14.2 %shard_map.128 = (f32[2,4,1,18,128,128]{5,4,3,2,1,0:T(8,128)}, f32[2,4,1,18,128,128]{5,4,3,2,1,0:T(8,128)}, f32[2,4,1,18,128,128]{5,4,3,2,1,0:T(8,128)}) custom-call(s32[2,4]{1,0:T(2,128)S(1)} %bitcast.32, f32[2,18,128,128]{3,2,1,0:T(8,128)S(1)} %get-tuple-element.97.keep_ref, f32[2,18,128,128]{3,2,1,0:T(8,128)S(1)} %collective-permute-done.55.swap_ref, ...), custom_call_target="tpu_custom_call" | custom-call | flops 14155776 | bytes 33030144 | tf_op jit(solution)/shard_map/pallas_call | solution.py:531
  368.8 14.1 %shard_map.129 = (f32[2,4,1,18,128,128]{5,4,3,2,1,0:T(8,128)}, f32[2,4,1,18,128,128]{5,4,3,2,1,0:T(8,128)}, f32[2,4,1,18,128,128]{5,4,3,2,1,0:T(8,128)}) custom-call(s32[2,4]{1,0:T(2,128)S(1)} %bitcast.33, f32[2,18,128,128]{3,2,1,0:T(8,128)S(1)} %get-tuple-element.94.keep_ref, ...), custom_call_target="tpu_custom_call", output_to_operand_aliasing={{0}: (6, {}), {1}: (7, {}), {2}: (8, {})} | custom-call | flops 14155776 | bytes 33030144 | tf_op jit(solution)/shard_map/pallas_call | solution.py:531
  (175 shorter events, 89.7 us)
Async XLA Ops:
  0.6 22.3 %collective-permute-start.2 = (bf16[32,3072]{1,0:T(8,128)(2,1)}, bf16[32,3072]{1,0:T(8,128)(2,1)S(1)}, u32[]{:S(2)}, u32[]{:S(2)}) collective-permute-start(bf16[32,3072]{1,0:T(8,128)(2,1)} %param.7), channel_id=1, source_target_pairs={{0,12},{4,0},{8,4},{12,8},{1,13},{5,1},{9,5},{13,9},{2,14},{6,2},{... | collective-permute-start | bytes 589832 | tf_op jit(solution)/shard_map/ppermute | solution.py:346
  12.3 28.3 %collective-permute-start.4 = (bf16[18,128,128]{2,1,0:T(8,128)(2,1)S(1)}, bf16[18,128,128]{2,1,0:T(8,128)(2,1)S(1)}, u32[]{:S(2)}, u32[]{:S(2)}) collective-permute-start(bf16[18,128,128]{2,1,0:T(8,128)(2,1)S(1)} %get-tuple-element.56), channel_id=1, source_target_pairs={{0,1},{1,0},{2,3},{3,2},{4,5},{5,4},{6,7},{7,6},{8,9},{9,8},{10,11... | collective-permute-start | bytes 1769480 | tf_op jit(solution)/shard_map/ppermute | solution.py:352
  19.6 21.1 %collective-permute-start.5 = (bf16[18,128,128]{2,1,0:T(8,128)(2,1)S(1)}, bf16[18,128,128]{2,1,0:T(8,128)(2,1)S(1)}, u32[]{:S(2)}, u32[]{:S(2)}) collective-permute-start(bf16[18,128,128]{2,1,0:T(8,128)(2,1)S(1)} %get-tuple-element.57), channel_id=1, source_target_pairs={{0,2},{1,3},{2,0},{3,1},{4,6},{5,7},{6,4},{7,5},{8,10},{9,11},{10,... | collective-permute-start | bytes 1769480 | tf_op jit(solution)/shard_map/ppermute | solution.py:352
  22.7 24.8 %collective-permute-start.6 = (bf16[18,128,128]{2,1,0:T(8,128)(2,1)S(1)}, bf16[18,128,128]{2,1,0:T(8,128)(2,1)S(1)}, u32[]{:S(2)}, u32[]{:S(2)}) collective-permute-start(bf16[18,128,128]{2,1,0:T(8,128)(2,1)S(1)} %get-tuple-element.58), channel_id=1, source_target_pairs={{0,3},{1,2},{2,1},{3,0},{4,7},{5,6},{6,5},{7,4},{8,11},{9,10},{10,... | collective-permute-start | bytes 1769480 | tf_op jit(solution)/shard_map/ppermute | solution.py:352
  22.9 26.7 %collective-permute-start.3 = (bf16[128,3072]{1,0:T(8,128)(2,1)S(1)}, bf16[128,3072]{1,0:T(8,128)(2,1)S(1)}, u32[]{:S(2)}, u32[]{:S(2)}) collective-permute-start(bf16[128,3072]{1,0:T(8,128)(2,1)S(1)} %constant_dynamic-update-slice_fusion.refs_0_), channel_id=1, source_target_pairs={{0,16},{16,0},{1,17},{17,1},{2,18},{18,2},{3,19},{19,3},{4,20},{20... | collective-permute-start | bytes 2359304 | tf_op jit(solution)/shard_map/ppermute | solution.py:349
  36.8 29.0 %collective-permute-start.29 = (bf16[2,32,3072]{2,1,0:T(8,128)(2,1)S(1)}, bf16[2,32,3072]{2,1,0:T(8,128)(2,1)S(1)}, u32[]{:S(2)}, u32[]{:S(2)}) collective-permute-start(bf16[2,32,3072]{2,1,0:T(8,128)(2,1)S(1)} %get-tuple-element.118.refs_0_), channel_id=1, source_target_pairs={{0,8},{4,12},{8,0},{12,4},{1,9},{5,13},{9,1},{13,5},{2,10},{6,14},... | collective-permute-start | bytes 1179656 | tf_op jit(solution)/shard_map/ppermute | solution.py:346
  40.6 25.2 %collective-permute-start.16 = (bf16[18,128,128]{2,1,0:T(8,128)(2,1)S(1)}, bf16[18,128,128]{2,1,0:T(8,128)(2,1)S(1)}, u32[]{:S(2)}, u32[]{:S(2)}) collective-permute-start(bf16[18,128,128]{2,1,0:T(8,128)(2,1)S(1)} %get-tuple-element.71), channel_id=1, source_target_pairs={{0,1},{1,0},{2,3},{3,2},{4,5},{5,4},{6,7},{7,6},{8,9},{9,8},{10,11... | collective-permute-start | bytes 1769480 | tf_op jit(solution)/shard_map/ppermute | solution.py:352
  40.7 25.2 %collective-permute-start.17 = (bf16[18,128,128]{2,1,0:T(8,128)(2,1)S(1)}, bf16[18,128,128]{2,1,0:T(8,128)(2,1)S(1)}, u32[]{:S(2)}, u32[]{:S(2)}) collective-permute-start(bf16[18,128,128]{2,1,0:T(8,128)(2,1)S(1)} %get-tuple-element.72), channel_id=1, source_target_pairs={{0,2},{1,3},{2,0},{3,1},{4,6},{5,7},{6,4},{7,5},{8,10},{9,11},{10,... | collective-permute-start | bytes 1769480 | tf_op jit(solution)/shard_map/ppermute | solution.py:352
  47.4 23.2 %collective-permute-start.18 = (bf16[18,128,128]{2,1,0:T(8,128)(2,1)S(1)}, bf16[18,128,128]{2,1,0:T(8,128)(2,1)S(1)}, u32[]{:S(2)}, u32[]{:S(2)}) collective-permute-start(bf16[18,128,128]{2,1,0:T(8,128)(2,1)S(1)} %get-tuple-element.73), channel_id=1, source_target_pairs={{0,3},{1,2},{2,1},{3,0},{4,7},{5,6},{6,5},{7,4},{8,11},{9,10},{10,... | collective-permute-start | bytes 1769480 | tf_op jit(solution)/shard_map/ppermute | solution.py:352
  74.9 20.4 %collective-permute-start.10 = (f32[2,32,3072]{2,1,0:T(8,128)S(1)}, f32[2,32,3072]{2,1,0:T(8,128)S(1)}, u32[]{:S(2)}, u32[]{:S(2)}) collective-permute-start(f32[2,32,3072]{2,1,0:T(8,128)S(1)} %get-tuple-element.66), channel_id=1, source_target_pairs={{0,2},{1,3},{2,0},{3,1},{4,6},{5,7},{6,4},{7,5},{8,10},{9,11},{10,... | collective-permute-start | bytes 2359304 | tf_op jit(solution)/shard_map/ppermute | solution.py:352
  77.4 20.5 %collective-permute-start.8 = (f32[2,32,3072]{2,1,0:T(8,128)S(1)}, f32[2,32,3072]{2,1,0:T(8,128)S(1)}, u32[]{:S(2)}, u32[]{:S(2)}) collective-permute-start(f32[2,32,3072]{2,1,0:T(8,128)S(1)} %get-tuple-element.62), channel_id=1, source_target_pairs={{0,16},{16,0},{1,17},{17,1},{2,18},{18,2},{3,19},{19,3},{4,20},{20... | collective-permute-start | bytes 2359304 | tf_op jit(solution)/shard_map/ppermute | solution.py:349
  80.1 32.1 %collective-permute-start.34 = (f32[2,32,3072]{2,1,0:T(8,128)S(1)}, f32[2,32,3072]{2,1,0:T(8,128)S(1)}, u32[]{:S(2)}, u32[]{:S(2)}) collective-permute-start(f32[2,32,3072]{2,1,0:T(8,128)S(1)} %get-tuple-element.85), channel_id=1, source_target_pairs={{0,2},{1,3},{2,0},{3,1},{4,6},{5,7},{6,4},{7,5},{8,10},{9,11},{10,... | collective-permute-start | bytes 2359304 | tf_op jit(solution)/shard_map/ppermute | solution.py:352
  82.7 32.1 %collective-permute-start.32 = (f32[2,32,3072]{2,1,0:T(8,128)S(1)}, f32[2,32,3072]{2,1,0:T(8,128)S(1)}, u32[]{:S(2)}, u32[]{:S(2)}) collective-permute-start(f32[2,32,3072]{2,1,0:T(8,128)S(1)} %get-tuple-element.81), channel_id=1, source_target_pairs={{0,16},{16,0},{1,17},{17,1},{2,18},{18,2},{3,19},{19,3},{4,20},{20... | collective-permute-start | bytes 2359304 | tf_op jit(solution)/shard_map/ppermute | solution.py:349
  95.4 27.8 %collective-permute-start.11 = (f32[32,3072]{1,0:T(8,128)S(1)}, f32[32,3072]{1,0:T(8,128)S(1)}, u32[]{:S(2)}, u32[]{:S(2)}) collective-permute-start(f32[32,3072]{1,0:T(8,128)S(1)} %get-tuple-element.68), channel_id=1, source_target_pairs={{0,16},{16,0},{1,17},{17,1},{2,18},{18,2},{3,19},{19,3},{4,20},{20... | collective-permute-start | bytes 1179656 | tf_op jit(solution)/shard_map/ppermute | solution.py:349
  98.0 25.2 %collective-permute-start.9 = (f32[32,3072]{1,0:T(8,128)S(1)}, f32[32,3072]{1,0:T(8,128)S(1)}, u32[]{:S(2)}, u32[]{:S(2)}) collective-permute-start(f32[32,3072]{1,0:T(8,128)S(1)} %get-tuple-element.64), channel_id=1, source_target_pairs={{0,2},{1,3},{2,0},{3,1},{4,6},{5,7},{6,4},{7,5},{8,10},{9,11},{10,... | collective-permute-start | bytes 1179656 | tf_op jit(solution)/shard_map/ppermute | solution.py:352
  123.6 24.9 %collective-permute-start.13 = (bf16[32,6144]{1,0:T(8,128)(2,1)S(1)}, bf16[32,6144]{1,0:T(8,128)(2,1)S(1)}, u32[]{:S(2)}, u32[]{:S(2)}) collective-permute-start(bf16[32,6144]{1,0:T(8,128)(2,1)S(1)} %get-tuple-element.69), channel_id=1, source_target_pairs={{0,16},{1,17},{2,18},{3,19},{16,0},{17,1},{18,2},{19,3},{4,20},{5,... | collective-permute-start | bytes 1179656 | tf_op jit(solution)/shard_map/ppermute | solution.py:360
  125.1 23.5 %collective-permute-start.12 = (bf16[32,6144]{1,0:T(8,128)(2,1)S(1)}, bf16[32,6144]{1,0:T(8,128)(2,1)S(1)}, u32[]{:S(2)}, u32[]{:S(2)}) collective-permute-start(bf16[32,6144]{1,0:T(8,128)(2,1)S(1)} %get-tuple-element.69), channel_id=1, source_target_pairs={{0,2},{1,3},{2,0},{3,1},{16,18},{17,19},{18,16},{19,17},{4,6},{5,7... | collective-permute-start | bytes 1179656 | tf_op jit(solution)/shard_map/ppermute | solution.py:360
  131.6 39.5 %collective-permute-start.49 = (bf16[2,32,3072]{2,1,0:T(8,128)(2,1)S(1)}, bf16[2,32,3072]{2,1,0:T(8,128)(2,1)S(1)}, u32[]{:S(2)}, u32[]{:S(2)}) collective-permute-start(bf16[2,32,3072]{2,1,0:T(8,128)(2,1)S(1)} %get-tuple-element.117), channel_id=1, source_target_pairs={{0,2},{1,3},{2,0},{3,1},{4,6},{5,7},{6,4},{7,5},{8,10},{9,11},{10,... | collective-permute-start | bytes 1179656 | tf_op jit(solution)/shard_map/ppermute | solution.py:352
  132.2 24.2 %collective-permute-start.38 = (bf16[32,6144]{1,0:T(8,128)(2,1)S(1)}, bf16[32,6144]{1,0:T(8,128)(2,1)S(1)}, u32[]{:S(2)}, u32[]{:S(2)}) collective-permute-start(bf16[32,6144]{1,0:T(8,128)(2,1)S(1)} %shard_map.124), channel_id=1, source_target_pairs={{0,18},{1,19},{2,16},{3,17},{16,2},{17,3},{18,0},{19,1},{4,22},{5,... | collective-permute-start | bytes 1179656 | tf_op jit(solution)/shard_map/ppermute | solution.py:360
  139.6 25.0 %collective-permute-start.37 = (bf16[32,6144]{1,0:T(8,128)(2,1)S(1)}, bf16[32,6144]{1,0:T(8,128)(2,1)S(1)}, u32[]{:S(2)}, u32[]{:S(2)}) collective-permute-start(bf16[32,6144]{1,0:T(8,128)(2,1)S(1)} %shard_map.124), channel_id=1, source_target_pairs={{0,16},{1,17},{2,18},{3,19},{16,0},{17,1},{18,2},{19,3},{4,20},{5,... | collective-permute-start | bytes 1179656 | tf_op jit(solution)/shard_map/ppermute | solution.py:360
  148.5 22.4 %collective-permute-start.36 = (bf16[32,6144]{1,0:T(8,128)(2,1)S(1)}, bf16[32,6144]{1,0:T(8,128)(2,1)S(1)}, u32[]{:S(2)}, u32[]{:S(2)}) collective-permute-start(bf16[32,6144]{1,0:T(8,128)(2,1)S(1)} %shard_map.124), channel_id=1, source_target_pairs={{0,2},{1,3},{2,0},{3,1},{16,18},{17,19},{18,16},{19,17},{4,6},{5,7... | collective-permute-start | bytes 1179656 | tf_op jit(solution)/shard_map/ppermute | solution.py:360
  148.7 46.9 %collective-permute-start.15 = (bf16[2,64,6144]{2,1,0:T(8,128)(2,1)S(1)}, bf16[2,64,6144]{2,1,0:T(8,128)(2,1)S(1)}, u32[]{:S(2)}, u32[]{:S(2)}) collective-permute-start(bf16[2,64,6144]{2,1,0:T(8,128)(2,1)S(1)} %bitcast.13), channel_id=1, source_target_pairs={{0,1},{1,0},{2,3},{3,2},{4,5},{5,4},{6,7},{7,6},{8,9},{9,8},{10,11... | collective-permute-start | bytes 4718600 | tf_op jit(solution)/shard_map/ppermute | solution.py:352
  171.0 32.0 %collective-permute-start.39 = (bf16[2,64,6144]{2,1,0:T(8,128)(2,1)S(1)}, bf16[2,64,6144]{2,1,0:T(8,128)(2,1)S(1)}, u32[]{:S(2)}, u32[]{:S(2)}) collective-permute-start(bf16[2,64,6144]{2,1,0:T(8,128)(2,1)S(1)} %bitcast.16), channel_id=1, source_target_pairs={{0,1},{1,0},{2,3},{3,2},{4,5},{5,4},{6,7},{7,6},{8,9},{9,8},{10,11... | collective-permute-start | bytes 4718600 | tf_op jit(solution)/shard_map/ppermute | solution.py:352
  183.6 31.5 %collective-permute-start.53 = (bf16[2,2,32,3072]{3,2,1,0:T(8,128)(2,1)}, bf16[2,2,32,3072]{3,2,1,0:T(8,128)(2,1)S(1)}, u32[]{:S(2)}, u32[]{:S(2)}) collective-permute-start(bf16[2,2,32,3072]{3,2,1,0:T(8,128)(2,1)} %pad_maximum_fusion.2.refs_3_), channel_id=1, source_target_pairs={{0,12},{4,0},{8,4},{12,8},{1,13},{5,1},{9,5},{13,9},{2,14},{6,2},{... | collective-permute-start | bytes 2359304 | tf_op jit(solution)/shard_map/ppermute | solution.py:346
  188.6 73.1 %collective-permute-start.52 = (bf16[2,2,32,3072]{3,2,1,0:T(8,128)(2,1)}, bf16[2,2,32,3072]{3,2,1,0:T(8,128)(2,1)}, u32[]{:S(2)}, u32[]{:S(2)}) collective-permute-start(bf16[2,2,32,3072]{3,2,1,0:T(8,128)(2,1)} %pad_maximum_fusion.2.refs_3_), channel_id=1, source_target_pairs={{0,8},{4,12},{8,0},{12,4},{1,9},{5,13},{9,1},{13,5},{2,10},{6,14},... | collective-permute-start | bytes 2359304 | tf_op jit(solution)/shard_map/ppermute | solution.py:346
  193.5 68.1 %collective-permute-start.51 = (bf16[2,2,32,3072]{3,2,1,0:T(8,128)(2,1)}, bf16[2,2,32,3072]{3,2,1,0:T(8,128)(2,1)}, u32[]{:S(2)}, u32[]{:S(2)}) collective-permute-start(bf16[2,2,32,3072]{3,2,1,0:T(8,128)(2,1)} %pad_maximum_fusion.2.refs_3_), channel_id=1, source_target_pairs={{0,4},{4,8},{8,12},{12,0},{1,5},{5,9},{9,13},{13,1},{2,6},{6,10},{... | collective-permute-start | bytes 2359304 | tf_op jit(solution)/shard_map/ppermute | solution.py:346
  203.0 78.5 %collective-permute-start.19 = (f32[128,1536]{1,0:T(8,128)}, f32[128,1536]{1,0:T(8,128)}, u32[]{:S(2)}, u32[]{:S(2)}) collective-permute-start(f32[128,1536]{1,0:T(8,128)} %get-tuple-element.75), channel_id=1, source_target_pairs={{0,16},{16,0},{1,17},{17,1},{2,18},{18,2},{3,19},{19,3},{4,20},{20... | collective-permute-start | bytes 2359304 | tf_op jit(solution)/shard_map/ppermute | solution.py:349
  203.1 80.0 %collective-permute-start.23 = (f32[128,1536]{1,0:T(8,128)}, f32[128,1536]{1,0:T(8,128)}, u32[]{:S(2)}, u32[]{:S(2)}) collective-permute-start(f32[128,1536]{1,0:T(8,128)} %get-tuple-element.77), channel_id=1, source_target_pairs={{0,16},{16,0},{1,17},{17,1},{2,18},{18,2},{3,19},{19,3},{4,20},{20... | collective-permute-start | bytes 2359304 | tf_op jit(solution)/shard_map/ppermute | solution.py:349
  216.0 68.5 %collective-permute-start.40 = (f32[128,1536]{1,0:T(8,128)}, f32[128,1536]{1,0:T(8,128)}, u32[]{:S(2)}, u32[]{:S(2)}) collective-permute-start(f32[128,1536]{1,0:T(8,128)} %get-tuple-element.90), channel_id=1, source_target_pairs={{0,16},{16,0},{1,17},{17,1},{2,18},{18,2},{3,19},{19,3},{4,20},{20... | collective-permute-start | bytes 2359304 | tf_op jit(solution)/shard_map/ppermute | solution.py:349
  272.8 81.8 %collective-permute-start.55 = (f32[2,18,128,128]{3,2,1,0:T(8,128)S(1)}, f32[2,18,128,128]{3,2,1,0:T(8,128)S(1)}, u32[]{:S(2)}, u32[]{:S(2)}) collective-permute-start(f32[2,18,128,128]{3,2,1,0:T(8,128)S(1)} %get-tuple-element.98), channel_id=1, source_target_pairs={{0,1},{1,0},{2,3},{3,2},{4,5},{5,4},{6,7},{7,6},{8,9},{9,8},{10,11... | collective-permute-start | bytes 7077896 | tf_op jit(solution)/shard_map/ppermute | solution.py:352
  281.6 87.3 %collective-permute-start.54 = (f32[2,18,128,128]{3,2,1,0:T(8,128)S(1)}, f32[2,18,128,128]{3,2,1,0:T(8,128)S(1)}, u32[]{:S(2)}, u32[]{:S(2)}) collective-permute-start(f32[2,18,128,128]{3,2,1,0:T(8,128)S(1)} %get-tuple-element.95), channel_id=1, source_target_pairs={{0,1},{1,0},{2,3},{3,2},{4,5},{5,4},{6,7},{7,6},{8,9},{9,8},{10,11... | collective-permute-start | bytes 7077896 | tf_op jit(solution)/shard_map/ppermute | solution.py:352
  308.4 20.2 %collective-permute-start.41 = (f32[32,1536]{1,0:T(8,128)S(1)}, f32[32,1536]{1,0:T(8,128)S(1)}, u32[]{:S(2)}, u32[]{:S(2)}) collective-permute-start(f32[32,1536]{1,0:T(8,128)S(1)} %get-tuple-element.105), channel_id=1, source_target_pairs={{0,12},{4,0},{8,4},{12,8},{1,13},{5,1},{9,5},{13,9},{2,14},{6,2},{... | collective-permute-start | bytes 589832 | tf_op jit(solution)/shard_map/ppermute | solution.py:346
  (50 other events, 549.6 us)

commit v6 on v5

--- a/solution.py
+++ b/solution.py
@@ -272,9 +272,10 @@
 
 def activate_kernel(split, *refs):
     *part_refs, hidden_ref, preact_ref = refs
-    span = preact_ref.shape[1] // 2
-    for side, side_refs in enumerate((part_refs[:split], part_refs[split:])):
-        at = slice(side * span, (side + 1) * span)
+    start = 0
+    for side_refs in (part_refs[:split], part_refs[split:]):
+        at = slice(start, start + side_refs[0].shape[1])
+        start = at.stop
         preact = total_of(side_refs)
         preact_ref[:, at] = preact
         hidden_ref[:, at] = activate(preact).astype(jnp.bfloat16)
@@ -282,9 +283,10 @@
 
 def slope_kernel(split, *refs):
     *part_refs, preact_ref, out_ref = refs
-    span = preact_ref.shape[1] // 2
-    for side, side_refs in enumerate((part_refs[:split], part_refs[split:])):
-        at = slice(side * span, (side + 1) * span)
+    start = 0
+    for side_refs in (part_refs[:split], part_refs[split:]):
+        at = slice(start, start + side_refs[0].shape[1])
+        start = at.stop
         slope = gelu_slope(preact_ref[:, at])
         out_ref[:, at] = (total_of(side_refs) * slope).astype(jnp.bfloat16)
 
@@ -359,8 +361,6 @@
                 table.append((m * tok_count + t, to))
         return lax.ppermute(array, (MEM, TOK), table)
 
-    peers = [(j, b) for j in range(mem_count) for b in range(other)][1:]
-
     def gather_rows(array):
         pieces = [array] + [shift_hid(array, k) for k in range(1, hid_count)]
         near = jnp.concatenate(pieces, axis=0)
@@ -408,16 +408,19 @@
         flops = 2 * mem_count * rows * local_slots * block_size * block_size
         return call(kernel, outs, scalars, [*row_groups, *weights], flops)
 
-    def half_columns(kernel, outs, arrays, side, steps):
-        span = hidden_span // 2 // steps
+    mem_span = hidden_span * 5 // 8
+
+    def side_columns(kernel, outs, arrays, side, steps=3):
+        whole = hidden_span - mem_span if side else mem_span
+        span = whole // steps
 
         def spec(shape, shift):
             lead = len(shape) - 1
             return pl.BlockSpec(tuple(shape[:-1]) + (span,), lambda i: (0,) * lead + (i + shift,))
 
-        shift = side * steps
-        needed = sum(math_size(a) for a in outs) // steps * 2
-        needed += sum(math_size(a) for a in arrays) // steps
+        shift = side * mem_span // span
+        needed = 2 * (sum(math_size(a) for a in outs) // steps)
+        needed += 2 * (sum(math_size(a) // a.shape[-1] * span for a in arrays))
         return pl.pallas_call(
             kernel,
             grid=(steps,),
@@ -434,39 +437,39 @@
 
     def reduce_plane(keep, send):
         swap = flip_tok(send, 1)
-        span = hidden_span // 2
-
-        def array(*lead):
-            return jax.ShapeDtypeStruct((*lead, span), f32)
-
-        by_mem = half_columns(
-            functools.partial(join_kernel, False),
-            [array(other, part)] * mem_count,
-            [keep, swap],
-            0,
-            2,
-        )
-        by_pair = half_columns(
-            functools.partial(join_kernel, True),
-            [array(mem_count, part)] * other,
-            [keep, swap],
-            1,
-            2,
-        )
+
+        def array(side, *lead):
+            return jax.ShapeDtypeStruct((*lead, hidden_span - mem_span if side else mem_span), f32)
+
+        kernel = functools.partial(join_kernel, False)
+        outs = [array(0, other, part)] * mem_count
+        by_mem = side_columns(kernel, outs, [keep, swap], 0)
+        kernel = functools.partial(join_kernel, True)
+        outs = [array(1, mem_count, part)] * other
+        by_pair = side_columns(kernel, outs, [keep, swap], 1)
         mem_terms = [by_mem[0]] + [shift_mem(by_mem[j], -j) for j in range(1, mem_count)]
         pair_terms = [by_pair[0]] + [flip_tok(by_pair[b], 2 * b) for b in range(1, other)]
-        mine, *rest = call(split_kernel, [array(part)] * other, (), mem_terms, part)
+        mine, *rest = call(split_kernel, [array(0, part)] * other, (), mem_terms, part)
         first = [mine] + [flip_tok(x, 2 * b) for b, x in enumerate(rest, 1)]
-        mine, *rest = call(split_kernel, [array(part)] * mem_count, (), pair_terms, part)
+        mine, *rest = call(split_kernel, [array(1, part)] * mem_count, (), pair_terms, part)
         second = [mine] + [shift_mem(x, -j) for j, x in enumerate(rest, 1)]
         return first, second
 
     def gather_plane(piece):
-        found = {(0, 0): piece}
-        for j, b in peers:
-            found[(-j) % mem_count, b] = across(piece, j, b)
+        cut = part // 2
+        found = {(0, 0): [piece]}
+        for j in range(1, mem_count):
+            found[(-j) % mem_count, 0] = [across(piece, j, 0)]
+        for b in range(1, other):
+            found[0, b] = [across(piece, 0, b)]
+        for j in range(1, mem_count):
+            for b in range(1, other):
+                found[j, b] = [across(found[j, 0][0][:cut], 0, b)]
+        for j in range(1, mem_count):
+            for b in range(1, other):
+                found[(-j) % mem_count, b].append(across(found[0, b][0][cut:], j, 0))
         near = jnp.concatenate(
-            [found[j, b] for j in range(mem_count) for b in range(other)], axis=0
+            [x for j in range(mem_count) for b in range(other) for x in found[j, b]], axis=0
         ).reshape(mem_count, half, hidden_span)
         return near, flip_tok(near, 1)
 

time: 384 us -> 381 us (level)
    ppermute x6 -> x8, waiting for transfers between devices: 36.8 us -> 14.3 us  [across(): return lax.ppermute(array, (MEM, TOK), table)]
    ppermute x11, waiting for transfers between devices: 34 us -> 49.7 us  [shift_mem(): lax.ppermute(array, MEM, [(i, (i + shift) % mem_count) for i in range(mem...]
    ppermute x21, starting transfers between devices: 48.7 us -> 40.4 us  [shift_hid(): lax.ppermute(array, HID, [(i, (i + shift) % hid_count) for i in range(hid...]
    ppermute x18, waiting for transfers between devices: 39.3 us -> 45.3 us  [flip_tok(): return lax.ppermute(array, TOK, [(i, i ^ bit) for i in range(tok_count)])]
    ppermute x6 -> x8, starting transfers between devices: 5.13 us -> 10.3 us  [across(): return lax.ppermute(array, (MEM, TOK), table)]
    unnamed x56 -> x64, local copies, waits for them, and re-layouts: 15.5 us -> 15.6 us
  transfers between devices with their start and end apart: 56 -> 58, of which waited for: 29 -> 29; matrix products, arithmetic and copies ran while one was open for 2% -> 2% of each run, Pallas kernels for 14% -> 14%
where the time goes in v6:
time: 381 us
  waiting for transfers between devices  217 us (57%)
  starting transfers between devices  71.2 us (19%)
  Pallas kernels  68.8 us (18%)
  local copies, waits for them, and re-layouts  15.9 us (4%)
  other arithmetic  6.62 us (2%)
    ppermute x21, waiting for transfers between devices, shift_hid(): lax.ppermute(array, HID, [(i, (i + shift) % hid_count) for i in range(hid...  108 us
    ppermute x11, waiting for transfers between devices, shift_mem(): lax.ppermute(array, MEM, [(i, (i + shift) % mem_count) for i in range(mem...  49.7 us
    ppermute x18, waiting for transfers between devices, flip_tok(): return lax.ppermute(array, TOK, [(i, i ^ bit) for i in range(tok_count)])  45.3 us
    ppermute x21, starting transfers between devices, shift_hid(): lax.ppermute(array, HID, [(i, (i + shift) % hid_count) for i in range(hid...  40.4 us
    pallas_call x12, Pallas kernels, call(): pl.pallas_call(kernel, out_shape=outs, in_specs=[SCALARS] * len(scalars)...  37.1 us
    pallas_call x2, Pallas kernels, update(): pl.pallas_call(functools.partial(update_kernel, matrix, owned_slots), gri...  28.3 us
    unnamed x64, local copies, waits for them, and re-layouts  15.6 us
    ppermute x8, waiting for transfers between devices, across(): return lax.ppermute(array, (MEM, TOK), table)  14.3 us
  transfers between devices with their start and end apart: 58, of which 29 were waited for; matrix products, arithmetic and copies ran while one was open for 2% of the time, Pallas kernels for 14%

profile of v6, /device:TPU:0, one launch (start us, length us, event | category | flops | bytes accessed | tf_op | source)
XLA Modules:
  0.0 380.6 jit_solution(7701791673196281207)
XLA Ops:
  0.6 5.1 %collective-permute-start.2 = (bf16[32,3072]{1,0:T(8,128)(2,1)}, bf16[32,3072]{1,0:T(8,128)(2,1)S(1)}, u32[]{:S(2)}, u32[]{:S(2)}) collective-permute-start(bf16[32,3072]{1,0:T(8,128)(2,1)} %param.7), channel_id=1, source_target_pairs={{0,12},{4,0},{8,4},{12,8},{1,13},{5,1},{9,5},{13,9},{2,14},{6,2},{... | collective-permute-start | bytes 589832 | tf_op jit(solution)/shard_map/ppermute | solution.py:348
  8.3 3.7 copy-done
  13.5 6.1 %collective-permute-done = bf16[32,3072]{1,0:T(8,128)(2,1)S(1)} collective-permute-done((bf16[32,3072]{1,0:T(8,128)(2,1)}, bf16[32,3072]{1,0:T(8,128)(2,1)S(1)}, u32[]{:S(2)}, u32[]{:S(2)}) %collective-permute-start) | collective-permute-done | bytes 196640 | tf_op jit(solution)/shard_map/ppermute | solution.py:348
  29.2 11.2 %collective-permute-done.5.refs_4_.refs_2_ = bf16[18,128,128]{2,1,0:T(8,128)(2,1)S(1)} collective-permute-done((bf16[18,128,128]{2,1,0:T(8,128)(2,1)S(1)}, bf16[18,128,128]{2,1,0:T(8,128)(2,1)S(1)}, u32[]{:S(2)}, u32[]{:S(2)}) %collective-permute-start.5) | collective-permute-done | bytes 589856 | tf_op jit(solution)/shard_map/ppermute | solution.py:354
  40.5 9.5 %collective-permute-done.6.refs_5_.refs_3_ = bf16[18,128,128]{2,1,0:T(8,128)(2,1)S(1)} collective-permute-done((bf16[18,128,128]{2,1,0:T(8,128)(2,1)S(1)}, bf16[18,128,128]{2,1,0:T(8,128)(2,1)S(1)}, u32[]{:S(2)}, u32[]{:S(2)}) %collective-permute-start.6) | collective-permute-done | bytes 589856 | tf_op jit(solution)/shard_map/ppermute | solution.py:354
  52.4 5.9 %shard_map.111 = (bf16[256,3072]{1,0:T(8,128)(2,1)S(1)}, f32[2,64,6144]{2,1,0:T(8,128)S(1)}, f32[2,64,6144]{2,1,0:T(8,128)S(1)}) custom-call(s32[2,4]{1,0:T(2,128)S(1)} %bitcast.26, s32[2,144]{1,0:T(2,128)S(1)} %bitcast.19, bf16[128,3072]{1,0:T(8,128)(2,1)S(1)} %constant_dynamic-update-slice_fusion.refs_0_, ...), custom_call_target="tpu_custom_call" | custom-call | flops 603979776 | bytes 11796480 | tf_op jit(solution)/shard_map/pallas_call | solution.py:309
  61.1 11.8 %collective-permute-done.29.refs_1_ = bf16[2,32,3072]{2,1,0:T(8,128)(2,1)S(1)} collective-permute-done((bf16[2,32,3072]{2,1,0:T(8,128)(2,1)S(1)}, bf16[2,32,3072]{2,1,0:T(8,128)(2,1)S(1)}, u32[]{:S(2)}, u32[]{:S(2)}) %collective-permute-start.29) | collective-permute-done | bytes 393248 | tf_op jit(solution)/shard_map/ppermute | solution.py:348
  72.8 6.0 %collective-permute-done.19.refs_3_.refs_7_ = bf16[18,128,128]{2,1,0:T(8,128)(2,1)S(1)} collective-permute-done((bf16[18,128,128]{2,1,0:T(8,128)(2,1)S(1)}, bf16[18,128,128]{2,1,0:T(8,128)(2,1)S(1)}, u32[]{:S(2)}, u32[]{:S(2)}) %collective-permute-start.19) | collective-permute-done | bytes 589856 | tf_op jit(solution)/shard_map/ppermute | solution.py:354
  83.1 4.6 %collective-permute-done.32.swap_ref = f32[2,64,6144]{2,1,0:T(8,128)S(1)} collective-permute-done((f32[2,64,6144]{2,1,0:T(8,128)S(1)}, f32[2,64,6144]{2,1,0:T(8,128)S(1)}, u32[]{:S(2)}, u32[]{:S(2)}) %collective-permute-start.32) | collective-permute-done | bytes 3145760 | tf_op jit(solution)/shard_map/ppermute | solution.py:354
  91.7 16.0 %collective-permute-done.8.refs_1_ = f32[2,32,3840]{2,1,0:T(8,128)S(1)} collective-permute-done((f32[2,32,3840]{2,1,0:T(8,128)S(1)}, f32[2,32,3840]{2,1,0:T(8,128)S(1)}, u32[]{:S(2)}, u32[]{:S(2)}) %collective-permute-start.8) | collective-permute-done | bytes 983072 | tf_op jit(solution)/shard_map/ppermute | solution.py:351
  110.1 7.9 %collective-permute-done.35.refs_1_ = f32[2,32,2304]{2,1,0:T(8,128)S(1)} collective-permute-done((f32[2,32,2304]{2,1,0:T(8,128)S(1)}, f32[2,32,2304]{2,1,0:T(8,128)S(1)}, u32[]{:S(2)}, u32[]{:S(2)}) %collective-permute-start.35) | collective-permute-done | bytes 589856 | tf_op jit(solution)/shard_map/ppermute | solution.py:354
  120.1 8.6 %collective-permute-done.33.refs_1_ = f32[2,32,3840]{2,1,0:T(8,128)S(1)} collective-permute-done((f32[2,32,3840]{2,1,0:T(8,128)S(1)}, f32[2,32,3840]{2,1,0:T(8,128)S(1)}, u32[]{:S(2)}, u32[]{:S(2)}) %collective-permute-start.33) | collective-permute-done | bytes 983072 | tf_op jit(solution)/shard_map/ppermute | solution.py:351
  129.8 5.3 %collective-permute-done.11.refs_3_ = f32[32,2304]{1,0:T(8,128)S(1)} collective-permute-done((f32[32,2304]{1,0:T(8,128)S(1)}, f32[32,2304]{1,0:T(8,128)S(1)}, u32[]{:S(2)}, u32[]{:S(2)}) %collective-permute-start.11) | collective-permute-done | bytes 294944 | tf_op jit(solution)/shard_map/ppermute | solution.py:351
  136.5 5.0 %collective-permute-done.36.refs_3_ = f32[32,2304]{1,0:T(8,128)S(1)} collective-permute-done((f32[32,2304]{1,0:T(8,128)S(1)}, f32[32,2304]{1,0:T(8,128)S(1)}, u32[]{:S(2)}, u32[]{:S(2)}) %collective-permute-start.36) | collective-permute-done | bytes 294944 | tf_op jit(solution)/shard_map/ppermute | solution.py:351
  141.4 6.1 %collective-permute-done.34.refs_1_ = f32[32,3840]{1,0:T(8,128)S(1)} collective-permute-done((f32[32,3840]{1,0:T(8,128)S(1)}, f32[32,3840]{1,0:T(8,128)S(1)}, u32[]{:S(2)}, u32[]{:S(2)}) %collective-permute-start.34) | collective-permute-done | bytes 491552 | tf_op jit(solution)/shard_map/ppermute | solution.py:354
  159.3 5.0 %collective-permute-done.37 = bf16[32,6144]{1,0:T(8,128)(2,1)S(1)} collective-permute-done((bf16[32,6144]{1,0:T(8,128)(2,1)S(1)}, bf16[32,6144]{1,0:T(8,128)(2,1)S(1)}, u32[]{:S(2)}, u32[]{:S(2)}) %collective-permute-start.37) | collective-permute-done | bytes 393248 | tf_op jit(solution)/shard_map/ppermute | solution.py:362
  173.9 9.7 %collective-permute-done.52 = bf16[2,32,3072]{2,1,0:T(8,128)(2,1)S(1)} collective-permute-done((bf16[2,32,3072]{2,1,0:T(8,128)(2,1)S(1)}, bf16[2,32,3072]{2,1,0:T(8,128)(2,1)S(1)}, u32[]{:S(2)}, u32[]{:S(2)}) %collective-permute-start.52) | collective-permute-done | bytes 393248 | tf_op jit(solution)/shard_map/ppermute | solution.py:351
  193.5 4.1 %shard_map.118 = (f32[128,1536]{1,0:T(8,128)S(1)}, f32[128,1536]{1,0:T(8,128)}, f32[128,1536]{1,0:T(8,128)S(1)}, f32[128,1536]{1,0:T(8,128)}) custom-call(s32[2,4]{1,0:T(2,128)S(1)} %bitcast.28, s32[2,144]{1,0:T(2,128)S(1)} %bitcast.22, bf16[2,64,6144]{2,1,0:T(8,128)(2,1)S(1)} %bitcast.14, bf16[2,64,6144]{2,1,0:T(8,128)(2,1)S(1)} %collective-permute-done.16.pair_ref.refs_2_, ...), custom_call_target="tpu_custom_call" | custom-call | flops 603979776 | bytes 8650752 | tf_op jit(solution)/shard_map/pallas_call | solution.py:309
  201.4 7.1 %shard_map.125 = (f32[128,1536]{1,0:T(8,128)S(1)}, f32[128,1536]{1,0:T(8,128)}, f32[128,1536]{1,0:T(8,128)S(1)}, f32[128,1536]{1,0:T(8,128)S(1)}) custom-call(s32[2,4]{1,0:T(2,128)S(1)} %bitcast.29, s32[2,144]{1,0:T(2,128)S(1)} %bitcast.23, bf16[2,64,6144]{2,1,0:T(8,128)(2,1)S(1)} %bitcast.17, ...), custom_call_target="tpu_custom_call" | custom-call | flops 603979776 | bytes 8650752 | tf_op jit(solution)/shard_map/pallas_call | solution.py:309
  212.1 45.8 %collective-permute-done.54.refs_5_ = bf16[2,2,32,3072]{3,2,1,0:T(8,128)(2,1)} collective-permute-done((bf16[2,2,32,3072]{3,2,1,0:T(8,128)(2,1)}, bf16[2,2,32,3072]{3,2,1,0:T(8,128)(2,1)}, u32[]{:S(2)}, u32[]{:S(2)}) %collective-permute-start.54) | collective-permute-done | bytes 786464 | tf_op jit(solution)/shard_map/ppermute | solution.py:348
  261.9 7.2 %shard_map.127 = (f32[2,18,128,128]{3,2,1,0:T(8,128)S(1)}, f32[2,18,128,128]{3,2,1,0:T(8,128)S(1)}) custom-call(s32[2,4]{1,0:T(2,128)S(1)} %bitcast.30, s32[2,144]{1,0:T(2,128)S(1)} %bitcast.24, s32[2,144]{1,0:T(2,128)S(1)} %collective-permute-done.50.far_place_ref, bf16[256,3072]{1,0:T(8,128)(2,1)S(1)} %copy-done.11, bf16[2,64,6144]{2,1,0:T(8,128)(2,1)S(1)} %bitcast.15, ...), custom_call_target="tpu_custom_call" | custom-call | flops 603979776 | bytes 12582912 | tf_op jit(solution)/shard_map/pallas_call | solution.py:309
  269.3 8.5 %shard_map.126 = (f32[2,18,128,128]{3,2,1,0:T(8,128)S(1)}, f32[2,18,128,128]{3,2,1,0:T(8,128)S(1)}) custom-call(s32[2,4]{1,0:T(2,128)S(1)} %bitcast.31, s32[2,144]{1,0:T(2,128)S(1)} %bitcast.25, s32[2,144]{1,0:T(2,128)S(1)} %collective-permute-done.50.far_place_ref, bf16[256,3072]{1,0:T(8,128)(2,1)S(1)} %copy-done.9, bf16[2,64,6144]{2,1,0:T(8,128)(2,1)S(1)} %bitcast.18, ...), custom_call_target="tpu_custom_call" | custom-call | flops 603979776 | bytes 12582912 | tf_op jit(solution)/shard_map/pallas_call | solution.py:309
  284.1 5.1 %collective-permute-done.46 = f32[128,1536]{1,0:T(8,128)S(1)} collective-permute-done((f32[128,1536]{1,0:T(8,128)S(1)}, f32[128,1536]{1,0:T(8,128)S(1)}, u32[]{:S(2)}, u32[]{:S(2)}) %collective-permute-start.46) | collective-permute-done | bytes 786464 | tf_op jit(solution)/shard_map/ppermute | solution.py:351
  293.5 8.6 %collective-permute-done.22 = f32[32,1536]{1,0:T(8,128)S(1)} collective-permute-done((f32[32,1536]{1,0:T(8,128)S(1)}, f32[32,1536]{1,0:T(8,128)S(1)}, u32[]{:S(2)}, u32[]{:S(2)}) %collective-permute-start.22) | collective-permute-done | bytes 196640 | tf_op jit(solution)/shard_map/ppermute | solution.py:348
  302.1 3.8 collective-permute-done.25
  306.3 9.7 %collective-permute-start.45 = (f32[32,1536]{1,0:T(8,128)S(1)}, f32[32,1536]{1,0:T(8,128)S(1)}, u32[]{:S(2)}, u32[]{:S(2)}) collective-permute-start(f32[32,1536]{1,0:T(8,128)S(1)} %get-tuple-element.106), channel_id=1, source_target_pairs={{0,4},{4,8},{8,12},{12,0},{1,5},{5,9},{9,13},{13,1},{2,6},{6,10},{... | collective-permute-start | bytes 589832 | tf_op jit(solution)/shard_map/ppermute | solution.py:348
  318.0 8.2 %collective-permute-done.43 = f32[32,1536]{1,0:T(8,128)S(1)} collective-permute-done((f32[32,1536]{1,0:T(8,128)S(1)}, f32[32,1536]{1,0:T(8,128)S(1)}, u32[]{:S(2)}, u32[]{:S(2)}) %collective-permute-start.43) | collective-permute-done | bytes 196640 | tf_op jit(solution)/shard_map/ppermute | solution.py:348
  326.1 6.6 %collective-permute-start.49 = (f32[32,1536]{1,0:T(8,128)S(1)}, f32[32,1536]{1,0:T(8,128)S(1)}, u32[]{:S(2)}, u32[]{:S(2)}) collective-permute-start(f32[32,1536]{1,0:T(8,128)S(1)} %get-tuple-element.109), channel_id=1, source_target_pairs={{0,4},{4,8},{8,12},{12,0},{1,5},{5,9},{9,13},{13,1},{2,6},{6,10},{... | collective-permute-start | bytes 589832 | tf_op jit(solution)/shard_map/ppermute | solution.py:348
  335.6 7.5 %collective-permute-done.47 = f32[32,1536]{1,0:T(8,128)S(1)} collective-permute-done((f32[32,1536]{1,0:T(8,128)S(1)}, f32[32,1536]{1,0:T(8,128)S(1)}, u32[]{:S(2)}, u32[]{:S(2)}) %collective-permute-start.47) | collective-permute-done | bytes 196640 | tf_op jit(solution)/shard_map/ppermute | solution.py:348
  343.0 8.5 %collective-permute-done.48 = f32[32,1536]{1,0:T(8,128)S(1)} collective-permute-done((f32[32,1536]{1,0:T(8,128)S(1)}, f32[32,1536]{1,0:T(8,128)S(1)}, u32[]{:S(2)}, u32[]{:S(2)}) %collective-permute-start.48) | collective-permute-done | bytes 196640 | tf_op jit(solution)/shard_map/ppermute | solution.py:348
  352.2 14.2 %shard_map.128 = (f32[2,4,1,18,128,128]{5,4,3,2,1,0:T(8,128)}, f32[2,4,1,18,128,128]{5,4,3,2,1,0:T(8,128)}, f32[2,4,1,18,128,128]{5,4,3,2,1,0:T(8,128)}) custom-call(s32[2,4]{1,0:T(2,128)S(1)} %bitcast.32, f32[2,18,128,128]{3,2,1,0:T(8,128)S(1)} %get-tuple-element.97.keep_ref, f32[2,18,128,128]{3,2,1,0:T(8,128)S(1)} %collective-permute-done.57.swap_ref, ...), custom_call_target="tpu_custom_call" | custom-call | flops 14155776 | bytes 33030144 | tf_op jit(solution)/shard_map/pallas_call | solution.py:534
  366.4 14.1 %shard_map.129 = (f32[2,4,1,18,128,128]{5,4,3,2,1,0:T(8,128)}, f32[2,4,1,18,128,128]{5,4,3,2,1,0:T(8,128)}, f32[2,4,1,18,128,128]{5,4,3,2,1,0:T(8,128)}) custom-call(s32[2,4]{1,0:T(2,128)S(1)} %bitcast.33, f32[2,18,128,128]{3,2,1,0:T(8,128)S(1)} %get-tuple-element.94.keep_ref, ...), custom_call_target="tpu_custom_call", output_to_operand_aliasing={{0}: (6, {}), {1}: (7, {}), {2}: (8, {})} | custom-call | flops 14155776 | bytes 33030144 | tf_op jit(solution)/shard_map/pallas_call | solution.py:534
  (191 shorter events, 93.0 us)
Async XLA Ops:
  0.6 22.1 %collective-permute-start.2 = (bf16[32,3072]{1,0:T(8,128)(2,1)}, bf16[32,3072]{1,0:T(8,128)(2,1)S(1)}, u32[]{:S(2)}, u32[]{:S(2)}) collective-permute-start(bf16[32,3072]{1,0:T(8,128)(2,1)} %param.7), channel_id=1, source_target_pairs={{0,12},{4,0},{8,4},{12,8},{1,13},{5,1},{9,5},{13,9},{2,14},{6,2},{... | collective-permute-start | bytes 589832 | tf_op jit(solution)/shard_map/ppermute | solution.py:348
  6.8 19.0 %collective-permute-start.28 = (bf16[32,3072]{1,0:T(8,128)(2,1)}, bf16[32,3072]{1,0:T(8,128)(2,1)S(1)}, u32[]{:S(2)}, u32[]{:S(2)}) collective-permute-start(bf16[32,3072]{1,0:T(8,128)(2,1)} %param.8), channel_id=1, source_target_pairs={{0,16},{16,0},{1,17},{17,1},{2,18},{18,2},{3,19},{19,3},{4,20},{20... | collective-permute-start | bytes 589832 | tf_op jit(solution)/shard_map/ppermute | solution.py:351
  22.7 27.8 %collective-permute-start.3 = (bf16[128,3072]{1,0:T(8,128)(2,1)S(1)}, bf16[128,3072]{1,0:T(8,128)(2,1)S(1)}, u32[]{:S(2)}, u32[]{:S(2)}) collective-permute-start(bf16[128,3072]{1,0:T(8,128)(2,1)S(1)} %constant_dynamic-update-slice_fusion.refs_0_), channel_id=1, source_target_pairs={{0,16},{16,0},{1,17},{17,1},{2,18},{18,2},{3,19},{19,3},{4,20},{20... | collective-permute-start | bytes 2359304 | tf_op jit(solution)/shard_map/ppermute | solution.py:351
  25.8 24.2 %collective-permute-start.6 = (bf16[18,128,128]{2,1,0:T(8,128)(2,1)S(1)}, bf16[18,128,128]{2,1,0:T(8,128)(2,1)S(1)}, u32[]{:S(2)}, u32[]{:S(2)}) collective-permute-start(bf16[18,128,128]{2,1,0:T(8,128)(2,1)S(1)} %get-tuple-element.58), channel_id=1, source_target_pairs={{0,3},{1,2},{2,1},{3,0},{4,7},{5,6},{6,5},{7,4},{8,11},{9,10},{10,... | collective-permute-start | bytes 1769480 | tf_op jit(solution)/shard_map/ppermute | solution.py:354
  25.9 33.6 %collective-permute-start.31 = (bf16[2,32,3072]{2,1,0:T(8,128)(2,1)S(1)}, bf16[2,32,3072]{2,1,0:T(8,128)(2,1)S(1)}, u32[]{:S(2)}, u32[]{:S(2)}) collective-permute-start(bf16[2,32,3072]{2,1,0:T(8,128)(2,1)S(1)} %get-tuple-element.118.refs_0_), channel_id=1, source_target_pairs={{0,12},{4,0},{8,4},{12,8},{1,13},{5,1},{9,5},{13,9},{2,14},{6,2},{... | collective-permute-start | bytes 1179656 | tf_op jit(solution)/shard_map/ppermute | solution.py:348
  26.3 33.2 %collective-permute-start.30 = (bf16[2,32,3072]{2,1,0:T(8,128)(2,1)S(1)}, bf16[2,32,3072]{2,1,0:T(8,128)(2,1)S(1)}, u32[]{:S(2)}, u32[]{:S(2)}) collective-permute-start(bf16[2,32,3072]{2,1,0:T(8,128)(2,1)S(1)} %get-tuple-element.118.refs_0_), channel_id=1, source_target_pairs={{0,8},{4,12},{8,0},{12,4},{1,9},{5,13},{9,1},{13,5},{2,10},{6,14},... | collective-permute-start | bytes 1179656 | tf_op jit(solution)/shard_map/ppermute | solution.py:348
  40.5 32.4 %collective-permute-start.17 = (bf16[18,128,128]{2,1,0:T(8,128)(2,1)S(1)}, bf16[18,128,128]{2,1,0:T(8,128)(2,1)S(1)}, u32[]{:S(2)}, u32[]{:S(2)}) collective-permute-start(bf16[18,128,128]{2,1,0:T(8,128)(2,1)S(1)} %get-tuple-element.71), channel_id=1, source_target_pairs={{0,1},{1,0},{2,3},{3,2},{4,5},{5,4},{6,7},{7,6},{8,9},{9,8},{10,11... | collective-permute-start | bytes 1769480 | tf_op jit(solution)/shard_map/ppermute | solution.py:354
  50.0 22.8 %collective-permute-start.18 = (bf16[18,128,128]{2,1,0:T(8,128)(2,1)S(1)}, bf16[18,128,128]{2,1,0:T(8,128)(2,1)S(1)}, u32[]{:S(2)}, u32[]{:S(2)}) collective-permute-start(bf16[18,128,128]{2,1,0:T(8,128)(2,1)S(1)} %get-tuple-element.72), channel_id=1, source_target_pairs={{0,2},{1,3},{2,0},{3,1},{4,6},{5,7},{6,4},{7,5},{8,10},{9,11},{10,... | collective-permute-start | bytes 1769480 | tf_op jit(solution)/shard_map/ppermute | solution.py:354
  50.5 28.3 %collective-permute-start.19 = (bf16[18,128,128]{2,1,0:T(8,128)(2,1)S(1)}, bf16[18,128,128]{2,1,0:T(8,128)(2,1)S(1)}, u32[]{:S(2)}, u32[]{:S(2)}) collective-permute-start(bf16[18,128,128]{2,1,0:T(8,128)(2,1)S(1)} %get-tuple-element.73), channel_id=1, source_target_pairs={{0,3},{1,2},{2,1},{3,0},{4,7},{5,6},{6,5},{7,4},{8,11},{9,10},{10,... | collective-permute-start | bytes 1769480 | tf_op jit(solution)/shard_map/ppermute | solution.py:354
  59.5 22.5 %collective-permute-start.7 = (f32[2,64,6144]{2,1,0:T(8,128)S(1)}, f32[2,64,6144]{2,1,0:T(8,128)S(1)}, u32[]{:S(2)}, u32[]{:S(2)}) collective-permute-start(f32[2,64,6144]{2,1,0:T(8,128)S(1)} %get-tuple-element.60), channel_id=1, source_target_pairs={{0,1},{1,0},{2,3},{3,2},{4,5},{5,4},{6,7},{7,6},{8,9},{9,8},{10,11... | collective-permute-start | bytes 9437192 | tf_op jit(solution)/shard_map/ppermute | solution.py:354
  83.1 24.6 %collective-permute-start.8 = (f32[2,32,3840]{2,1,0:T(8,128)S(1)}, f32[2,32,3840]{2,1,0:T(8,128)S(1)}, u32[]{:S(2)}, u32[]{:S(2)}) collective-permute-start(f32[2,32,3840]{2,1,0:T(8,128)S(1)} %get-tuple-element.62), channel_id=1, source_target_pairs={{0,16},{16,0},{1,17},{17,1},{2,18},{18,2},{3,19},{19,3},{4,20},{20... | collective-permute-start | bytes 2949128 | tf_op jit(solution)/shard_map/ppermute | solution.py:351
  88.6 40.2 %collective-permute-start.33 = (f32[2,32,3840]{2,1,0:T(8,128)S(1)}, f32[2,32,3840]{2,1,0:T(8,128)S(1)}, u32[]{:S(2)}, u32[]{:S(2)}) collective-permute-start(f32[2,32,3840]{2,1,0:T(8,128)S(1)} %get-tuple-element.81), channel_id=1, source_target_pairs={{0,16},{16,0},{1,17},{17,1},{2,18},{18,2},{3,19},{19,3},{4,20},{20... | collective-permute-start | bytes 2949128 | tf_op jit(solution)/shard_map/ppermute | solution.py:351
  89.1 19.7 %collective-permute-start.10 = (f32[2,32,2304]{2,1,0:T(8,128)S(1)}, f32[2,32,2304]{2,1,0:T(8,128)S(1)}, u32[]{:S(2)}, u32[]{:S(2)}) collective-permute-start(f32[2,32,2304]{2,1,0:T(8,128)S(1)} %get-tuple-element.66), channel_id=1, source_target_pairs={{0,2},{1,3},{2,0},{3,1},{4,6},{5,7},{6,4},{7,5},{8,10},{9,11},{10,... | collective-permute-start | bytes 1769480 | tf_op jit(solution)/shard_map/ppermute | solution.py:354
  90.5 27.5 %collective-permute-start.35 = (f32[2,32,2304]{2,1,0:T(8,128)S(1)}, f32[2,32,2304]{2,1,0:T(8,128)S(1)}, u32[]{:S(2)}, u32[]{:S(2)}) collective-permute-start(f32[2,32,2304]{2,1,0:T(8,128)S(1)} %get-tuple-element.85), channel_id=1, source_target_pairs={{0,2},{1,3},{2,0},{3,1},{4,6},{5,7},{6,4},{7,5},{8,10},{9,11},{10,... | collective-permute-start | bytes 1769480 | tf_op jit(solution)/shard_map/ppermute | solution.py:354
  107.8 27.3 %collective-permute-start.9 = (f32[32,3840]{1,0:T(8,128)S(1)}, f32[32,3840]{1,0:T(8,128)S(1)}, u32[]{:S(2)}, u32[]{:S(2)}) collective-permute-start(f32[32,3840]{1,0:T(8,128)S(1)} %get-tuple-element.64), channel_id=1, source_target_pairs={{0,2},{1,3},{2,0},{3,1},{4,6},{5,7},{6,4},{7,5},{8,10},{9,11},{10,... | collective-permute-start | bytes 1474568 | tf_op jit(solution)/shard_map/ppermute | solution.py:354
  108.8 26.3 %collective-permute-start.11 = (f32[32,2304]{1,0:T(8,128)S(1)}, f32[32,2304]{1,0:T(8,128)S(1)}, u32[]{:S(2)}, u32[]{:S(2)}) collective-permute-start(f32[32,2304]{1,0:T(8,128)S(1)} %get-tuple-element.68), channel_id=1, source_target_pairs={{0,16},{16,0},{1,17},{17,1},{2,18},{18,2},{3,19},{19,3},{4,20},{20... | collective-permute-start | bytes 884744 | tf_op jit(solution)/shard_map/ppermute | solution.py:351
  108.9 63.2 %collective-permute-start.51 = (bf16[2,32,3072]{2,1,0:T(8,128)(2,1)S(1)}, bf16[2,32,3072]{2,1,0:T(8,128)(2,1)S(1)}, u32[]{:S(2)}, u32[]{:S(2)}) collective-permute-start(bf16[2,32,3072]{2,1,0:T(8,128)(2,1)S(1)} %get-tuple-element.117), channel_id=1, source_target_pairs={{0,2},{1,3},{2,0},{3,1},{4,6},{5,7},{6,4},{7,5},{8,10},{9,11},{10,... | collective-permute-start | bytes 1179656 | tf_op jit(solution)/shard_map/ppermute | solution.py:354
  118.1 23.4 %collective-permute-start.36 = (f32[32,2304]{1,0:T(8,128)S(1)}, f32[32,2304]{1,0:T(8,128)S(1)}, u32[]{:S(2)}, u32[]{:S(2)}) collective-permute-start(f32[32,2304]{1,0:T(8,128)S(1)} %get-tuple-element.87), channel_id=1, source_target_pairs={{0,16},{16,0},{1,17},{17,1},{2,18},{18,2},{3,19},{19,3},{4,20},{20... | collective-permute-start | bytes 884744 | tf_op jit(solution)/shard_map/ppermute | solution.py:351
  135.5 20.4 %collective-permute-start.12 = (bf16[32,6144]{1,0:T(8,128)(2,1)S(1)}, bf16[32,6144]{1,0:T(8,128)(2,1)S(1)}, u32[]{:S(2)}, u32[]{:S(2)}) collective-permute-start(bf16[32,6144]{1,0:T(8,128)(2,1)S(1)} %get-tuple-element.69), channel_id=1, source_target_pairs={{0,2},{1,3},{2,0},{3,1},{16,18},{17,19},{18,16},{19,17},{4,6},{5,7... | collective-permute-start | bytes 1179656 | tf_op jit(solution)/shard_map/ppermute | solution.py:362
  168.6 23.1 %collective-permute-start.16 = (bf16[2,64,6144]{2,1,0:T(8,128)(2,1)S(1)}, bf16[2,64,6144]{2,1,0:T(8,128)(2,1)S(1)}, u32[]{:S(2)}, u32[]{:S(2)}) collective-permute-start(bf16[2,64,6144]{2,1,0:T(8,128)(2,1)S(1)} %bitcast.13), channel_id=1, source_target_pairs={{0,1},{1,0},{2,3},{3,2},{4,5},{5,4},{6,7},{7,6},{8,9},{9,8},{10,11... | collective-permute-start | bytes 4718600 | tf_op jit(solution)/shard_map/ppermute | solution.py:354
  172.0 27.4 %collective-permute-start.41 = (bf16[2,64,6144]{2,1,0:T(8,128)(2,1)S(1)}, bf16[2,64,6144]{2,1,0:T(8,128)(2,1)S(1)}, u32[]{:S(2)}, u32[]{:S(2)}) collective-permute-start(bf16[2,64,6144]{2,1,0:T(8,128)(2,1)S(1)} %bitcast.16), channel_id=1, source_target_pairs={{0,1},{1,0},{2,3},{3,2},{4,5},{5,4},{6,7},{7,6},{8,9},{9,8},{10,11... | collective-permute-start | bytes 4718600 | tf_op jit(solution)/shard_map/ppermute | solution.py:354
  184.6 26.7 %collective-permute-start.55 = (bf16[2,2,32,3072]{3,2,1,0:T(8,128)(2,1)}, bf16[2,2,32,3072]{3,2,1,0:T(8,128)(2,1)S(1)}, u32[]{:S(2)}, u32[]{:S(2)}) collective-permute-start(bf16[2,2,32,3072]{3,2,1,0:T(8,128)(2,1)} %pad_maximum_fusion.refs_3_), channel_id=1, source_target_pairs={{0,12},{4,0},{8,4},{12,8},{1,13},{5,1},{9,5},{13,9},{2,14},{6,2},{... | collective-permute-start | bytes 2359304 | tf_op jit(solution)/shard_map/ppermute | solution.py:348
  188.0 69.9 %collective-permute-start.54 = (bf16[2,2,32,3072]{3,2,1,0:T(8,128)(2,1)}, bf16[2,2,32,3072]{3,2,1,0:T(8,128)(2,1)}, u32[]{:S(2)}, u32[]{:S(2)}) collective-permute-start(bf16[2,2,32,3072]{3,2,1,0:T(8,128)(2,1)} %pad_maximum_fusion.refs_3_), channel_id=1, source_target_pairs={{0,8},{4,12},{8,0},{12,4},{1,9},{5,13},{9,1},{13,5},{2,10},{6,14},... | collective-permute-start | bytes 2359304 | tf_op jit(solution)/shard_map/ppermute | solution.py:348
  190.1 67.9 %collective-permute-start.53 = (bf16[2,2,32,3072]{3,2,1,0:T(8,128)(2,1)}, bf16[2,2,32,3072]{3,2,1,0:T(8,128)(2,1)}, u32[]{:S(2)}, u32[]{:S(2)}) collective-permute-start(bf16[2,2,32,3072]{3,2,1,0:T(8,128)(2,1)} %pad_maximum_fusion.refs_3_), channel_id=1, source_target_pairs={{0,4},{4,8},{8,12},{12,0},{1,5},{5,9},{9,13},{13,1},{2,6},{6,10},{... | collective-permute-start | bytes 2359304 | tf_op jit(solution)/shard_map/ppermute | solution.py:348
  199.4 78.4 %collective-permute-start.20 = (f32[128,1536]{1,0:T(8,128)}, f32[128,1536]{1,0:T(8,128)}, u32[]{:S(2)}, u32[]{:S(2)}) collective-permute-start(f32[128,1536]{1,0:T(8,128)} %get-tuple-element.75), channel_id=1, source_target_pairs={{0,16},{16,0},{1,17},{17,1},{2,18},{18,2},{3,19},{19,3},{4,20},{20... | collective-permute-start | bytes 2359304 | tf_op jit(solution)/shard_map/ppermute | solution.py:351
  199.4 79.9 %collective-permute-start.24 = (f32[128,1536]{1,0:T(8,128)}, f32[128,1536]{1,0:T(8,128)}, u32[]{:S(2)}, u32[]{:S(2)}) collective-permute-start(f32[128,1536]{1,0:T(8,128)} %get-tuple-element.77), channel_id=1, source_target_pairs={{0,16},{16,0},{1,17},{17,1},{2,18},{18,2},{3,19},{19,3},{4,20},{20... | collective-permute-start | bytes 2359304 | tf_op jit(solution)/shard_map/ppermute | solution.py:351
  212.1 68.6 %collective-permute-start.42 = (f32[128,1536]{1,0:T(8,128)}, f32[128,1536]{1,0:T(8,128)}, u32[]{:S(2)}, u32[]{:S(2)}) collective-permute-start(f32[128,1536]{1,0:T(8,128)} %get-tuple-element.90), channel_id=1, source_target_pairs={{0,16},{16,0},{1,17},{17,1},{2,18},{18,2},{3,19},{19,3},{4,20},{20... | collective-permute-start | bytes 2359304 | tf_op jit(solution)/shard_map/ppermute | solution.py:351
  269.1 83.2 %collective-permute-start.57 = (f32[2,18,128,128]{3,2,1,0:T(8,128)S(1)}, f32[2,18,128,128]{3,2,1,0:T(8,128)S(1)}, u32[]{:S(2)}, u32[]{:S(2)}) collective-permute-start(f32[2,18,128,128]{3,2,1,0:T(8,128)S(1)} %get-tuple-element.98), channel_id=1, source_target_pairs={{0,1},{1,0},{2,3},{3,2},{4,5},{5,4},{6,7},{7,6},{8,9},{9,8},{10,11... | collective-permute-start | bytes 7077896 | tf_op jit(solution)/shard_map/ppermute | solution.py:354
  269.2 19.9 %collective-permute-start.46 = (f32[128,1536]{1,0:T(8,128)S(1)}, f32[128,1536]{1,0:T(8,128)S(1)}, u32[]{:S(2)}, u32[]{:S(2)}) collective-permute-start(f32[128,1536]{1,0:T(8,128)S(1)} %copy-done.22), channel_id=1, source_target_pairs={{0,16},{16,0},{1,17},{17,1},{2,18},{18,2},{3,19},{19,3},{4,20},{20... | collective-permute-start | bytes 2359304 | tf_op jit(solution)/shard_map/ppermute | solution.py:351
  277.8 88.6 %collective-permute-start.56 = (f32[2,18,128,128]{3,2,1,0:T(8,128)S(1)}, f32[2,18,128,128]{3,2,1,0:T(8,128)S(1)}, u32[]{:S(2)}, u32[]{:S(2)}) collective-permute-start(f32[2,18,128,128]{3,2,1,0:T(8,128)S(1)} %get-tuple-element.95), channel_id=1, source_target_pairs={{0,1},{1,0},{2,3},{3,2},{4,5},{5,4},{6,7},{7,6},{8,9},{9,8},{10,11... | collective-permute-start | bytes 7077896 | tf_op jit(solution)/shard_map/ppermute | solution.py:354
  305.9 20.2 %collective-permute-start.43 = (f32[32,1536]{1,0:T(8,128)S(1)}, f32[32,1536]{1,0:T(8,128)S(1)}, u32[]{:S(2)}, u32[]{:S(2)}) collective-permute-start(f32[32,1536]{1,0:T(8,128)S(1)} %get-tuple-element.105), channel_id=1, source_target_pairs={{0,12},{4,0},{8,4},{12,8},{1,13},{5,1},{9,5},{13,9},{2,14},{6,2},{... | collective-permute-start | bytes 589832 | tf_op jit(solution)/shard_map/ppermute | solution.py:348
  306.3 19.8 %collective-permute-start.45 = (f32[32,1536]{1,0:T(8,128)S(1)}, f32[32,1536]{1,0:T(8,128)S(1)}, u32[]{:S(2)}, u32[]{:S(2)}) collective-permute-start(f32[32,1536]{1,0:T(8,128)S(1)} %get-tuple-element.106), channel_id=1, source_target_pairs={{0,4},{4,8},{8,12},{12,0},{1,5},{5,9},{9,13},{13,1},{2,6},{6,10},{... | collective-permute-start | bytes 589832 | tf_op jit(solution)/shard_map/ppermute | solution.py:348
  (52 other events, 527.8 us)

commit v7 on v6

--- a/solution.py
+++ b/solution.py
@@ -81,6 +81,21 @@
     lax.fori_loop(groups * UNROLL, count, single, 0)
 
 
+def start_weights(sources, held_ref, sems):
+    copies = [
+        pltpu.make_async_copy(source, held_ref.at[index], sems.at[index])
+        for index, source in enumerate(sources)
+    ]
+    for copy in copies:
+        copy.start()
+
+    def finish():
+        for copy in copies:
+            copy.wait()
+
+    return [held_ref.at[index] for index in range(len(sources))], finish
+
+
 def over_owners(matrix, kept_ref, weight_refs, body):
     tok = lax.axis_index(TOK)
     for turn, weight_ref in enumerate(weight_refs):
@@ -100,9 +115,10 @@
     sources = hid_count if matrix else mem_count
     own_refs, weight_refs, (row_ref, keep_ref, send_ref) = (
         refs[:sources],
-        refs[sources:-3],
-        refs[-3:],
+        refs[sources : sources + tok_count],
+        refs[sources + tok_count : -2],
     )
+    weight_refs, finish = start_weights(weight_refs, *refs[-2:])
     half = keep_ref.shape[1]
     _, size = weight_refs[0].shape[:2]
     rows = row_ref.shape[0] // mem_count
@@ -132,6 +148,7 @@
                 keep_ref[group, :, spot] += product[start : start + half]
                 send_ref[group, :, spot] += product[start + half : start + rows]
 
+    finish()
     over_owners(matrix, kept_ref, weight_refs, body)
 
 
@@ -139,7 +156,8 @@
     matrix, transposed, width_blocks, mem_count, kept_ref, place_ref, own_ref, pair_ref, *refs
 ):
     tok_count = lax.axis_size(TOK)
-    weight_refs, out_refs, total_ref = refs[:tok_count], refs[tok_count:-1], refs[-1]
+    out_refs, total_ref = refs[tok_count:-3], refs[-1]
+    weight_refs, finish = start_weights(refs[:tok_count], *refs[-3:-1])
     size = weight_refs[0].shape[-1]
     half = own_ref.shape[1]
     total_ref[...] = jnp.zeros(total_ref.shape, jnp.float32)
@@ -159,6 +177,7 @@
         for spot, product in found:
             total_ref[:, spot] += product
 
+    finish()
     over_owners(matrix, kept_ref, weight_refs, body)
     for index, out_ref in enumerate(out_refs):
         chunk, group = index // mem_count, index % mem_count
@@ -168,54 +187,53 @@
         ]
 
 
-def gradient_kernel(matrix, width_blocks, mem_count, hid_count, kept_ref, place_ref, far_place_ref, *refs):
-    row_ref, own_ref, pair_ref = refs[:3]
-    late_refs = refs[3 : 3 + hid_count]
-    keep_ref, send_ref, late_ref = refs[3 + hid_count :]
-    cells, owned, size = keep_ref.shape[:3]
+def gradient_kernel(
+    matrix, cell, width_blocks, mem_count, kept_ref, place_ref, row_ref, own_ref, pair_ref, *out_refs
+):
+    owned, size = out_refs[0].shape[:2]
     tok_count = lax.axis_size(TOK)
     tok = lax.axis_index(TOK)
     rows = row_ref.shape[0] // mem_count
     part = rows // tok_count
-    step = rows // hid_count
-    turn = relative(tok_count)
-    for block, source in enumerate(late_refs):
-        start = block * step
-        spot = ((start // part) ^ turn) * part + start % part
-        for group in range(mem_count):
-            late_ref[pl.ds(pl.multiple_of(spot + group * rows, step), step), :] = source[matrix, group]
-
-    for cell in range(cells):
-        places, values = ((place_ref, row_ref), (far_place_ref, late_ref))[cell]
-        for side, out_ref in enumerate((keep_ref, send_ref)):
-            first, count = owner_count(kept_ref, matrix, tok ^ (2 * cell), tok ^ side, owned)
-
-            def body(slots):
-                for slot in slots:
-                    place = places[matrix, first + slot]
-                    hidden = lanes(place // width_blocks, size)
-                    width = lanes(place % width_blocks, size)
-                    total = None
-                    for group in range(mem_count):
-                        wide = values[group * rows : (group + 1) * rows, width]
-                        deep = jnp.concatenate(
-                            [own_ref[group, :, hidden], pair_ref[group, :, hidden]], axis=0
-                        )
-                        left, right = (wide, deep) if matrix == 0 else (deep, wide)
-                        term = dot(left, right, 0, 0).astype(jnp.bfloat16).astype(jnp.float32)
-                        total = term if total is None else total + term
-                    out_ref[cell, slot] = total
-
-            over_slots(count, body)
-
-            def clear(slot, carry):
-                out_ref[cell, slot] = jnp.zeros((size, size), jnp.float32)
-                return carry
-
-            lax.fori_loop(count, owned, clear, 0)
-
-
-def update_kernel(matrix, owned, kept_ref, keep_ref, swap_ref, weight_ref, moment_ref, variance_ref, *refs):
+
+    def wide_rows(group, width):
+        if cell == 0:
+            return row_ref[group * rows : (group + 1) * rows, width]
+        starts = [group * rows + (p ^ cell) * part for p in range(tok_count)]
+        return jnp.concatenate([row_ref[start : start + part, width] for start in starts], axis=0)
+
+    for side, out_ref in enumerate(out_refs):
+        first, count = owner_count(kept_ref, matrix, tok ^ (2 * cell), tok ^ side, owned)
+
+        def body(slots):
+            for slot in slots:
+                place = place_ref[matrix, first + slot]
+                hidden = lanes(place // width_blocks, size)
+                width = lanes(place % width_blocks, size)
+                total = None
+                for group in range(mem_count):
+                    wide = wide_rows(group, width)
+                    deep = jnp.concatenate(
+                        [own_ref[group, :, hidden], pair_ref[group, :, hidden]], axis=0
+                    )
+                    left, right = (wide, deep) if matrix == 0 else (deep, wide)
+                    term = dot(left, right, 0, 0).astype(jnp.bfloat16).astype(jnp.float32)
+                    total = term if total is None else total + term
+                out_ref[slot] = total
+
+        over_slots(count, body)
+
+        def clear(slot, carry):
+            out_ref[slot] = jnp.zeros((size, size), jnp.float32)
+            return carry
+
+        lax.fori_loop(count, owned, clear, 0)
+
+
+def update_kernel(matrix, owned, kept_ref, *refs):
+    tok_count = lax.axis_size(TOK)
+    grad_refs = refs[:tok_count]
+    weight_ref, moment_ref, variance_ref = refs[tok_count : tok_count + 3]
     out_refs = refs[-3:]
     turn = pl.program_id(0)
     tok = lax.axis_index(TOK)
@@ -226,15 +244,15 @@
     def update_from(grad_ref):
         def update(slot, carry):
             at = (0, 0, 0, slot)
-            fresh = adam_step(weight_ref[at], moment_ref[at], variance_ref[at], grad_ref[0, slot])
+            fresh = adam_step(weight_ref[at], moment_ref[at], variance_ref[at], grad_ref[slot])
             for out_ref, value in zip(out_refs, fresh):
                 out_ref[at] = value
             return carry
 
         lax.fori_loop(0, count, update, 0)
 
-    pl.when(turn % 2 == 0)(functools.partial(update_from, keep_ref))
-    pl.when(turn % 2 == 1)(functools.partial(update_from, swap_ref))
+    for index, grad_ref in enumerate(grad_refs):
+        pl.when(turn == index)(functools.partial(update_from, grad_ref))
 
     def keep(slot, carry):
         at = (0, 0, 0, slot)
@@ -301,20 +319,28 @@
 
 SCALARS = pl.BlockSpec(memory_space=pltpu.SMEM)
 WHOLE = pl.BlockSpec(memory_space=pltpu.VMEM)
+OUTSIDE = pl.BlockSpec(memory_space=pltpu.HBM)
 ANYWHERE = pl.BlockSpec(memory_space=pl.ANY)
 
 
-def call(kernel, outs, scalars, arrays, flops, scratch=(), scratch_sizes=()):
-    moved = sum(math_size(a) for a in (*arrays, *outs))
+def call(kernel, outs, scalars, arrays, flops, outside=(), scratch=()):
+    if outside:
+        scratch = [
+            pltpu.VMEM((len(outside), *outside[0].shape), outside[0].dtype),
+            pltpu.SemaphoreType.DMA((len(outside),)),
+            *scratch,
+        ]
+    moved = sum(math_size(a) for a in (*arrays, *outs, *outside))
+    needed = moved + sum(math_size(x) for x in scratch[2:])
     return pl.pallas_call(
         kernel,
         out_shape=outs,
-        in_specs=[SCALARS] * len(scalars) + [WHOLE] * len(arrays),
+        in_specs=[SCALARS] * len(scalars) + [WHOLE] * len(arrays) + [OUTSIDE] * len(outside),
         out_specs=[WHOLE] * len(outs),
         scratch_shapes=scratch,
-        compiler_params=grant(moved + sum(scratch_sizes)),
+        compiler_params=grant(needed),
         cost_estimate=pl.CostEstimate(flops=flops, bytes_accessed=moved, transcendentals=0),
-    )(*scalars, *arrays)
+    )(*scalars, *arrays, *outside)
 
 
 def math_size(array):
@@ -371,12 +397,6 @@
         own = jnp.stack(found)
         return [own] + [shift_hid(own, k) for k in range(1, hid_count)]
 
-    def gather_late():
-        both = flip_tok(jnp.stack([inputs, cotangent]), 2)
-        found = [both] + [shift_mem(both, j) for j in range(1, mem_count)]
-        moved = jnp.stack(found, axis=1)
-        return [moved] + [shift_hid(moved, k) for k in range(1, hid_count)]
-
     def gather_weights(matrix):
         shape = (owned_slots, block_size, block_size)
         narrow = pl.pallas_call(
@@ -406,9 +426,9 @@
             jax.ShapeDtypeStruct((mem_count, half, hidden_span), f32),
         ]
         flops = 2 * mem_count * rows * local_slots * block_size * block_size
-        return call(kernel, outs, scalars, [*row_groups, *weights], flops)
-
-    mem_span = hidden_span * 5 // 8
+        return call(kernel, outs, scalars, row_groups, flops, weights)
+
+    mem_span = hidden_span // 2
 
     def side_columns(kernel, outs, arrays, side, steps=3):
         whole = hidden_span - mem_span if side else mem_span
@@ -455,21 +475,14 @@
         second = [mine] + [shift_mem(x, -j) for j, x in enumerate(rest, 1)]
         return first, second
 
+    peers = [(j, b) for j in range(mem_count) for b in range(other)][1:]
+
     def gather_plane(piece):
-        cut = part // 2
-        found = {(0, 0): [piece]}
-        for j in range(1, mem_count):
-            found[(-j) % mem_count, 0] = [across(piece, j, 0)]
-        for b in range(1, other):
-            found[0, b] = [across(piece, 0, b)]
-        for j in range(1, mem_count):
-            for b in range(1, other):
-                found[j, b] = [across(found[j, 0][0][:cut], 0, b)]
-        for j in range(1, mem_count):
-            for b in range(1, other):
-                found[(-j) % mem_count, b].append(across(found[0, b][0][cut:], j, 0))
+        found = {(0, 0): piece}
+        for j, b in peers:
+            found[(-j) % mem_count, b] = across(piece, j, b)
         near = jnp.concatenate(
-            [x for j in range(mem_count) for b in range(other) for x in found[j, b]], axis=0
+            [found[j, b] for j in range(mem_count) for b in range(other)], axis=0
         ).reshape(mem_count, half, hidden_span)
         return near, flip_tok(near, 1)
 
@@ -479,8 +492,7 @@
         outs = [jax.ShapeDtypeStruct((rows, span), f32)] * (mem_count * chunks)
         flops = 2 * mem_count * rows * local_slots * block_size * block_size
         scratch = [pltpu.VMEM((mem_count * rows, inputs.shape[1]), f32)]
-        sizes = [mem_count * rows * inputs.shape[1] * 4]
-        return call(kernel, outs, scalars, [near, far, *weights], flops, scratch, sizes)
+        return call(kernel, outs, scalars, [near, far], flops, weights, scratch)
 
     turn = relative(tok_count)
     step = inputs.shape[0]
@@ -503,22 +515,11 @@
             results.append(result.astype(bf16))
         return jnp.concatenate(results, axis=1)
 
-    def gradient(matrix, row_values, near, far, late):
-        kernel = functools.partial(gradient_kernel, matrix, width_blocks, mem_count, hid_count)
-        outs = [
-            jax.ShapeDtypeStruct((other, owned_slots, block_size, block_size), f32),
-            jax.ShapeDtypeStruct((other, owned_slots, block_size, block_size), f32),
-        ]
-        flops = 2 * mem_count * rows * local_slots * block_size * block_size
-        keep, send = call(
-            kernel,
-            outs,
-            (kept, place_ids, far_place_ids),
-            [row_values, near, far, *late],
-            flops,
-            [pltpu.VMEM(row_values.shape, bf16)],
-            [math_size(row_values)],
-        )
+    def gradient(matrix, cell, ids, row_values, near, far):
+        kernel = functools.partial(gradient_kernel, matrix, cell, width_blocks, mem_count)
+        outs = [jax.ShapeDtypeStruct((owned_slots, block_size, block_size), f32)] * 2
+        flops = 2 * mem_count * rows * owned_slots * 2 * block_size * block_size
+        keep, send = call(kernel, outs, (kept, ids), [row_values, near, far], flops)
         return keep, flip_tok(send, 1)
 
     def update(matrix, grads, held):
@@ -528,16 +529,25 @@
             (1, 1, 1, run, block_size, block_size),
             lambda i, j: (matrix, lax.axis_index(TOK) ^ i, 0, j, 0, 0),
         )
-        grad_spec = pl.BlockSpec((1, run, block_size, block_size), lambda i, j: (i // 2, j, 0, 0))
+
+        def grad_spec(turn):
+            return pl.BlockSpec(
+                (run, block_size, block_size),
+                lambda i, j: (jnp.where(i < turn, 0, jnp.where(i > turn, splits - 1, j)), 0, 0),
+            )
+
         state = (blocks, first_moment, second_moment)
         size = local_slots * block_size * block_size
         return pl.pallas_call(
             functools.partial(update_kernel, matrix, owned_slots),
             grid=(tok_count, splits),
             out_shape=[jax.ShapeDtypeStruct(s.shape, f32) for s in state],
-            in_specs=[SCALARS, grad_spec, grad_spec] + [state_spec] * 3 + [ANYWHERE] * len(held),
+            in_specs=[SCALARS]
+            + [grad_spec(turn) for turn in range(tok_count)]
+            + [state_spec] * 3
+            + [ANYWHERE] * len(held),
             out_specs=[state_spec] * 3,
-            input_output_aliases={6 + i: i for i in range(len(held))},
+            input_output_aliases={4 + tok_count + i: i for i in range(len(held))},
             compiler_params=grant(44 * 2**20),
             cost_estimate=pl.CostEstimate(
                 flops=size * 12, bytes_accessed=size * 28, transcendentals=size
@@ -549,7 +559,6 @@
     weights_first = gather_weights(0)
     cotangent_groups = gather_small(cotangent)
     weights_second = gather_weights(1)
-    late = gather_late()
     token_rows, *pre_part = forward(0, False, input_groups, weights_first)
     pre_terms = reduce_plane(*pre_part)
     grad_rows, *back_part = forward(1, True, cotangent_groups, weights_second)
@@ -565,8 +574,16 @@
     pre_grad = gather_plane(grad_piece)
     layer_out = reduce_rows(backward(1, False, *hidden, weights_second))
     grad_in = reduce_rows(backward(0, True, *pre_grad, weights_first))
-    second_grad = gradient(1, grad_rows, *hidden, late)
-    first_grad = gradient(0, token_rows, *pre_grad, late)
+    far_grad_rows = flip_tok(grad_rows, 2)
+    far_token_rows = flip_tok(token_rows, 2)
+    second_grad = [
+        *gradient(1, 0, place_ids, grad_rows, *hidden),
+        *gradient(1, 1, far_place_ids, far_grad_rows, *hidden),
+    ]
+    first_grad = [
+        *gradient(0, 0, place_ids, token_rows, *pre_grad),
+        *gradient(0, 1, far_place_ids, far_token_rows, *pre_grad),
+    ]
     held = update(1, second_grad, ())
     return (layer_out, grad_in, *update(0, first_grad, held))
 

time: 381 us -> 381 us (level)
  waiting for transfers between devices: 217 us -> 205 us
  starting transfers between devices: 71.2 us -> 82.5 us
  Pallas kernels: 68.8 us -> 75.4 us
  local copies, waits for them, and re-layouts: 15.9 us -> 10.1 us
    ppermute x18 -> x21, waiting for transfers between devices: 45.3 us -> 82.5 us  [flip_tok(): return lax.ppermute(array, TOK, [(i, i ^ bit) for i in range(tok_count)])]
    ppermute x11 -> x10, waiting for transfers between devices: 49.7 us -> 17.5 us  [shift_mem(): lax.ppermute(array, MEM, [(i, (i + shift) % mem_count) for i in range(mem...]
    ppermute x21 -> x18, waiting for transfers between devices: 108 us -> 76.4 us  [shift_hid(): lax.ppermute(array, HID, [(i, (i + shift) % hid_count) for i in range(hid...]
    ppermute x21 -> x18, starting transfers between devices: 40.4 us -> 57.9 us  [shift_hid(): lax.ppermute(array, HID, [(i, (i + shift) % hid_count) for i in range(hid...]
    ppermute x8 -> x6, waiting for transfers between devices: 14.3 us -> 28.7 us  [across(): return lax.ppermute(array, (MEM, TOK), table)]
    pallas_call x12 -> x14, Pallas kernels: 37.1 us -> 43.9 us  [call(): pl.pallas_call(kernel, out_shape=outs, in_specs=[SCALARS] * len(scalars)...]
    unnamed x64 -> x44, local copies, waits for them, and re-layouts: 15.6 us -> 9.85 us
    ppermute x11 -> x10, starting transfers between devices: 9.13 us -> 5.77 us  [shift_mem(): lax.ppermute(array, MEM, [(i, (i + shift) % mem_count) for i in range(mem...]
  transfers between devices with their start and end apart: 58 -> 55, of which waited for: 29 -> 25; matrix products, arithmetic and copies ran while one was open for 2% -> 2% of each run, Pallas kernels for 14% -> 16%
where the time goes in v7:
time: 381 us; the launch traced here: 380 us
  waiting for transfers between devices  205 us (54%)
  starting transfers between devices  82.5 us (22%)
  Pallas kernels  75.4 us (20%)
  local copies, waits for them, and re-layouts  10.1 us (3%)
  other arithmetic  5.77 us (2%)
    ppermute x21, waiting for transfers between devices, flip_tok(): return lax.ppermute(array, TOK, [(i, i ^ bit) for i in range(tok_count)])  82.5 us
    ppermute x18, waiting for transfers between devices, shift_hid(): lax.ppermute(array, HID, [(i, (i + shift) % hid_count) for i in range(hid...  76.4 us
    ppermute x18, starting transfers between devices, shift_hid(): lax.ppermute(array, HID, [(i, (i + shift) % hid_count) for i in range(hid...  57.9 us
    pallas_call x14, Pallas kernels, call(): pl.pallas_call(kernel, out_shape=outs, in_specs=[SCALARS] * len(scalars)...  43.9 us
    ppermute x6, waiting for transfers between devices, across(): return lax.ppermute(array, (MEM, TOK), table)  28.7 us
    pallas_call x2, Pallas kernels, update(): pl.pallas_call(functools.partial(update_kernel, matrix, owned_slots), gri...  28.6 us
    ppermute x10, waiting for transfers between devices, shift_mem(): lax.ppermute(array, MEM, [(i, (i + shift) % mem_count) for i in range(mem...  17.5 us
    ppermute x21, starting transfers between devices, flip_tok(): return lax.ppermute(array, TOK, [(i, i ^ bit) for i in range(tok_count)])  11.8 us
  transfers between devices with their start and end apart: 55, of which 25 were waited for; matrix products, arithmetic and copies ran while one was open for 2% of the time, Pallas kernels for 16%

profile of v7, /device:TPU:0, one launch (start us, length us, event | category | flops | bytes accessed | tf_op | source)
XLA Modules:
  0.0 380.0 jit_solution(16484499576297416505)
XLA Ops:
  0.6 4.1 %collective-permute-start.1 = (bf16[32,3072]{1,0:T(8,128)(2,1)}, bf16[32,3072]{1,0:T(8,128)(2,1)S(1)}, u32[]{:S(2)}, u32[]{:S(2)}) collective-permute-start(bf16[32,3072]{1,0:T(8,128)(2,1)} %param.7), channel_id=1, source_target_pairs={{0,8},{4,12},{8,0},{12,4},{1,9},{5,13},{9,1},{13,5},{2,10},{6,14},... | collective-permute-start | bytes 589832 | tf_op jit(solution)/shard_map/ppermute | solution.py:374
  23.7 20.6 %collective-permute-done.30.refs_3_ = bf16[2,32,3072]{2,1,0:T(8,128)(2,1)S(1)} collective-permute-done((bf16[2,32,3072]{2,1,0:T(8,128)(2,1)S(1)}, bf16[2,32,3072]{2,1,0:T(8,128)(2,1)S(1)}, u32[]{:S(2)}, u32[]{:S(2)}) %collective-permute-start.30) | collective-permute-done | bytes 393248 | tf_op jit(solution)/shard_map/ppermute | solution.py:374
  52.9 7.6 %shard_map.111 = (bf16[256,3072]{1,0:T(8,128)(2,1)}, f32[2,64,6144]{2,1,0:T(8,128)S(1)}, f32[2,64,6144]{2,1,0:T(8,128)S(1)}) custom-call(s32[2,4]{1,0:T(2,128)S(1)} %bitcast.16, s32[2,144]{1,0:T(2,128)S(1)} %bitcast.26, bf16[128,3072]{1,0:T(8,128)(2,1)S(1)} %constant_dynamic-update-slice_fusion.refs_0_, ...), custom_call_target="tpu_custom_call" | custom-call | flops 603979776 | bytes 11796480 | tf_op jit(solution)/shard_map/pallas_call | solution.py:335
  60.4 12.4 %collective-permute-done.29.refs_2_ = bf16[2,32,3072]{2,1,0:T(8,128)(2,1)S(1)} collective-permute-done((bf16[2,32,3072]{2,1,0:T(8,128)(2,1)S(1)}, bf16[2,32,3072]{2,1,0:T(8,128)(2,1)S(1)}, u32[]{:S(2)}, u32[]{:S(2)}) %collective-permute-start.29) | collective-permute-done | bytes 393248 | tf_op jit(solution)/shard_map/ppermute | solution.py:374
  76.6 4.8 %shard_map.119 = (bf16[256,3072]{1,0:T(8,128)(2,1)}, f32[2,64,6144]{2,1,0:T(8,128)S(1)}, f32[2,64,6144]{2,1,0:T(8,128)S(1)}) custom-call(s32[2,4]{1,0:T(2,128)S(1)} %bitcast.17, s32[2,144]{1,0:T(2,128)S(1)} %bitcast.27, bf16[2,32,3072]{2,1,0:T(8,128)(2,1)S(1)} %pad_maximum_fusion.2.refs_0_, bf16[2,32,3072]{2,1,0:T(8,128)(2,1)S(1)} %collective-permute-done.28.refs_1_, ...), custom_call_target="tpu_custom_call" | custom-call | flops 603979776 | bytes 11796480 | tf_op jit(solution)/shard_map/pallas_call | solution.py:335
  90.2 12.3 %collective-permute-done.10.refs_1_ = f32[2,32,3072]{2,1,0:T(8,128)S(1)} collective-permute-done((f32[2,32,3072]{2,1,0:T(8,128)S(1)}, f32[2,32,3072]{2,1,0:T(8,128)S(1)}, u32[]{:S(2)}, u32[]{:S(2)}) %collective-permute-start.10) | collective-permute-done | bytes 786464 | tf_op jit(solution)/shard_map/ppermute | solution.py:380
  105.3 14.1 %collective-permute-done.34.refs_1_ = f32[2,32,3072]{2,1,0:T(8,128)S(1)} collective-permute-done((f32[2,32,3072]{2,1,0:T(8,128)S(1)}, f32[2,32,3072]{2,1,0:T(8,128)S(1)}, u32[]{:S(2)}, u32[]{:S(2)}) %collective-permute-start.34) | collective-permute-done | bytes 786464 | tf_op jit(solution)/shard_map/ppermute | solution.py:380
  122.2 8.2 %collective-permute-done.11.refs_3_ = f32[32,3072]{1,0:T(8,128)S(1)} collective-permute-done((f32[32,3072]{1,0:T(8,128)S(1)}, f32[32,3072]{1,0:T(8,128)S(1)}, u32[]{:S(2)}, u32[]{:S(2)}) %collective-permute-start.11) | collective-permute-done | bytes 393248 | tf_op jit(solution)/shard_map/ppermute | solution.py:377
  134.2 4.6 %collective-permute-done.35.refs_3_ = f32[32,3072]{1,0:T(8,128)S(1)} collective-permute-done((f32[32,3072]{1,0:T(8,128)S(1)}, f32[32,3072]{1,0:T(8,128)S(1)}, u32[]{:S(2)}, u32[]{:S(2)}) %collective-permute-start.35) | collective-permute-done | bytes 393248 | tf_op jit(solution)/shard_map/ppermute | solution.py:377
  141.0 5.8 %collective-permute-done.14 = bf16[32,6144]{1,0:T(8,128)(2,1)S(1)} collective-permute-done((bf16[32,6144]{1,0:T(8,128)(2,1)S(1)}, bf16[32,6144]{1,0:T(8,128)(2,1)S(1)}, u32[]{:S(2)}, u32[]{:S(2)}) %collective-permute-start.14) | collective-permute-done | bytes 393248 | tf_op jit(solution)/shard_map/ppermute | solution.py:388
  148.7 7.0 %collective-permute-done.13 = bf16[32,6144]{1,0:T(8,128)(2,1)S(1)} collective-permute-done((bf16[32,6144]{1,0:T(8,128)(2,1)S(1)}, bf16[32,6144]{1,0:T(8,128)(2,1)S(1)}, u32[]{:S(2)}, u32[]{:S(2)}) %collective-permute-start.13) | collective-permute-done | bytes 393248 | tf_op jit(solution)/shard_map/ppermute | solution.py:388
  155.9 7.8 %collective-permute-done.38 = bf16[32,6144]{1,0:T(8,128)(2,1)S(1)} collective-permute-done((bf16[32,6144]{1,0:T(8,128)(2,1)S(1)}, bf16[32,6144]{1,0:T(8,128)(2,1)S(1)}, u32[]{:S(2)}, u32[]{:S(2)}) %collective-permute-start.38) | collective-permute-done | bytes 393248 | tf_op jit(solution)/shard_map/ppermute | solution.py:388
  163.7 8.1 %collective-permute-done.37 = bf16[32,6144]{1,0:T(8,128)(2,1)S(1)} collective-permute-done((bf16[32,6144]{1,0:T(8,128)(2,1)S(1)}, bf16[32,6144]{1,0:T(8,128)(2,1)S(1)}, u32[]{:S(2)}, u32[]{:S(2)}) %collective-permute-start.37) | collective-permute-done | bytes 393248 | tf_op jit(solution)/shard_map/ppermute | solution.py:388
  174.0 4.5 %shard_map.118 = (f32[128,1536]{1,0:T(8,128)S(1)}, f32[128,1536]{1,0:T(8,128)}, f32[128,1536]{1,0:T(8,128)S(1)}, f32[128,1536]{1,0:T(8,128)}) custom-call(s32[2,4]{1,0:T(2,128)S(1)} %bitcast.18, s32[2,144]{1,0:T(2,128)S(1)} %bitcast.28, bf16[2,64,6144]{2,1,0:T(8,128)(2,1)S(1)} %bitcast.9, bf16[2,64,6144]{2,1,0:T(8,128)(2,1)S(1)} %collective-permute-done.15.pair_ref, ...), custom_call_target="tpu_custom_call" | custom-call | flops 603979776 | bytes 8650752 | tf_op jit(solution)/shard_map/pallas_call | solution.py:335
  182.2 7.9 %shard_map.125 = (f32[128,1536]{1,0:T(8,128)S(1)}, f32[128,1536]{1,0:T(8,128)}, f32[128,1536]{1,0:T(8,128)S(1)}, f32[128,1536]{1,0:T(8,128)S(1)}) custom-call(s32[2,4]{1,0:T(2,128)S(1)} %bitcast.19, s32[2,144]{1,0:T(2,128)S(1)} %bitcast.30, bf16[2,64,6144]{2,1,0:T(8,128)(2,1)S(1)} %bitcast.13, bf16[2,64,6144]{2,1,0:T(8,128)(2,1)S(1)} %collective-permute-done.39.pair_ref, ...), custom_call_target="tpu_custom_call" | custom-call | flops 603979776 | bytes 8650752 | tf_op jit(solution)/shard_map/pallas_call | solution.py:335
  192.8 50.0 %collective-permute-done.49.place_ref = s32[2,144]{1,0:T(2,128)S(1)} collective-permute-done((s32[2,144]{1,0:T(2,128)S(1)}, s32[2,144]{1,0:T(2,128)S(1)}, u32[]{:S(2)}, u32[]{:S(2)}) %collective-permute-start.49) | collective-permute-done | bytes 1184 | tf_op jit(solution)/shard_map/ppermute | solution.py:380
  244.5 4.0 %shard_map.128 = (f32[18,128,128]{2,1,0:T(8,128)S(1)}, f32[18,128,128]{2,1,0:T(8,128)S(1)}) custom-call(s32[2,4]{1,0:T(2,128)S(1)} %bitcast.20, s32[2,144]{1,0:T(2,128)S(1)} %bitcast.31, bf16[256,3072]{1,0:T(8,128)(2,1)} %get-tuple-element.102.row_ref, bf16[2,64,6144]{2,1,0:T(8,128)(2,1)S(1)} %bitcast.10, bf16[2,64,6144]{2,1,0:T(8,128)(2,1)S(1)} %copy-done.3), custom_call_target="tpu_custom_call" | custom-call | flops 301989888 | bytes 7077888 | tf_op jit(solution)/shard_map/pallas_call | solution.py:335
  248.5 4.9 %shard_map.126 = (f32[18,128,128]{2,1,0:T(8,128)S(1)}, f32[18,128,128]{2,1,0:T(8,128)S(1)}) custom-call(s32[2,4]{1,0:T(2,128)S(1)} %bitcast.21, s32[2,144]{1,0:T(2,128)S(1)} %bitcast.32, bf16[256,3072]{1,0:T(8,128)(2,1)} %get-tuple-element.97.row_ref, bf16[2,64,6144]{2,1,0:T(8,128)(2,1)S(1)} %bitcast.14, bf16[2,64,6144]{2,1,0:T(8,128)(2,1)S(1)} %copy-done.6), custom_call_target="tpu_custom_call" | custom-call | flops 301989888 | bytes 7077888 | tf_op jit(solution)/shard_map/pallas_call | solution.py:335
  253.6 4.3 %shard_map.129 = (f32[18,128,128]{2,1,0:T(8,128)S(1)}, f32[18,128,128]{2,1,0:T(8,128)S(1)}) custom-call(s32[2,4]{1,0:T(2,128)S(1)} %bitcast.22, s32[2,144]{1,0:T(2,128)S(1)} %collective-permute-done.49.place_ref, bf16[256,3072]{1,0:T(8,128)(2,1)} %collective-permute-done.53.row_ref, bf16[2,64,6144]{2,1,0:T(8,128)(2,1)S(1)} %bitcast.11, ...), custom_call_target="tpu_custom_call" | custom-call | flops 301989888 | bytes 7077888 | tf_op jit(solution)/shard_map/pallas_call | solution.py:335
  257.9 4.8 %shard_map.127 = (f32[18,128,128]{2,1,0:T(8,128)S(1)}, f32[18,128,128]{2,1,0:T(8,128)S(1)}) custom-call(s32[2,4]{1,0:T(2,128)S(1)} %bitcast.23, s32[2,144]{1,0:T(2,128)S(1)} %collective-permute-done.49.place_ref, bf16[256,3072]{1,0:T(8,128)(2,1)} %collective-permute-done.50.row_ref, bf16[2,64,6144]{2,1,0:T(8,128)(2,1)S(1)} %bitcast.15, ...), custom_call_target="tpu_custom_call" | custom-call | flops 301989888 | bytes 7077888 | tf_op jit(solution)/shard_map/pallas_call | solution.py:335
  264.2 6.1 %collective-permute-start.20 = (f32[32,1536]{1,0:T(8,128)S(1)}, f32[32,1536]{1,0:T(8,128)S(1)}, u32[]{:S(2)}, u32[]{:S(2)}) collective-permute-start(f32[32,1536]{1,0:T(8,128)S(1)} %get-tuple-element.119), channel_id=1, source_target_pairs={{0,12},{4,0},{8,4},{12,8},{1,13},{5,1},{9,5},{13,9},{2,14},{6,2},{... | collective-permute-start | bytes 589832 | tf_op jit(solution)/shard_map/ppermute | solution.py:374
  271.6 10.6 %collective-permute-start.21 = (f32[32,1536]{1,0:T(8,128)S(1)}, f32[32,1536]{1,0:T(8,128)S(1)}, u32[]{:S(2)}, u32[]{:S(2)}) collective-permute-start(f32[32,1536]{1,0:T(8,128)S(1)} %get-tuple-element.121), channel_id=1, source_target_pairs={{0,8},{4,12},{8,0},{12,4},{1,9},{5,13},{9,1},{13,5},{2,10},{6,14},... | collective-permute-start | bytes 589832 | tf_op jit(solution)/shard_map/ppermute | solution.py:374
  285.9 4.5 %collective-permute-done.22 = f32[32,1536]{1,0:T(8,128)S(1)} collective-permute-done((f32[32,1536]{1,0:T(8,128)S(1)}, f32[32,1536]{1,0:T(8,128)S(1)}, u32[]{:S(2)}, u32[]{:S(2)}) %collective-permute-start.22) | collective-permute-done | bytes 196640 | tf_op jit(solution)/shard_map/ppermute | solution.py:374
  290.4 4.7 %collective-permute-start.25 = (f32[32,1536]{1,0:T(8,128)S(1)}, f32[32,1536]{1,0:T(8,128)S(1)}, u32[]{:S(2)}, u32[]{:S(2)}) collective-permute-start(f32[32,1536]{1,0:T(8,128)S(1)} %get-tuple-element.124), channel_id=1, source_target_pairs={{0,8},{4,12},{8,0},{12,4},{1,9},{5,13},{9,1},{13,5},{2,10},{6,14},... | collective-permute-start | bytes 589832 | tf_op jit(solution)/shard_map/ppermute | solution.py:374
  297.3 7.2 %collective-permute-start.41 = (f32[32,1536]{1,0:T(8,128)S(1)}, f32[32,1536]{1,0:T(8,128)S(1)}, u32[]{:S(2)}, u32[]{:S(2)}) collective-permute-start(f32[32,1536]{1,0:T(8,128)S(1)} %get-tuple-element.113), channel_id=1, source_target_pairs={{0,12},{4,0},{8,4},{12,8},{1,13},{5,1},{9,5},{13,9},{2,14},{6,2},{... | collective-permute-start | bytes 589832 | tf_op jit(solution)/shard_map/ppermute | solution.py:374
  304.5 6.0 %collective-permute-start.43 = (f32[32,1536]{1,0:T(8,128)S(1)}, f32[32,1536]{1,0:T(8,128)S(1)}, u32[]{:S(2)}, u32[]{:S(2)}) collective-permute-start(f32[32,1536]{1,0:T(8,128)S(1)} %get-tuple-element.114), channel_id=1, source_target_pairs={{0,4},{4,8},{8,12},{12,0},{1,5},{5,9},{9,13},{13,1},{2,6},{6,10},{... | collective-permute-start | bytes 589832 | tf_op jit(solution)/shard_map/ppermute | solution.py:374
  312.0 10.6 %collective-permute-done.25 = f32[32,1536]{1,0:T(8,128)S(1)} collective-permute-done((f32[32,1536]{1,0:T(8,128)S(1)}, f32[32,1536]{1,0:T(8,128)S(1)}, u32[]{:S(2)}, u32[]{:S(2)}) %collective-permute-start.25) | collective-permute-done | bytes 196640 | tf_op jit(solution)/shard_map/ppermute | solution.py:374
  323.2 7.8 %collective-permute-done.42 = f32[32,1536]{1,0:T(8,128)S(1)} collective-permute-done((f32[32,1536]{1,0:T(8,128)S(1)}, f32[32,1536]{1,0:T(8,128)S(1)}, u32[]{:S(2)}, u32[]{:S(2)}) %collective-permute-start.42) | collective-permute-done | bytes 196640 | tf_op jit(solution)/shard_map/ppermute | solution.py:374
  335.6 5.0 %collective-permute-done.47 = f32[32,1536]{1,0:T(8,128)S(1)} collective-permute-done((f32[32,1536]{1,0:T(8,128)S(1)}, f32[32,1536]{1,0:T(8,128)S(1)}, u32[]{:S(2)}, u32[]{:S(2)}) %collective-permute-start.47) | collective-permute-done | bytes 196640 | tf_op jit(solution)/shard_map/ppermute | solution.py:374
  342.7 8.0 %collective-permute-done.46 = f32[32,1536]{1,0:T(8,128)S(1)} collective-permute-done((f32[32,1536]{1,0:T(8,128)S(1)}, f32[32,1536]{1,0:T(8,128)S(1)}, u32[]{:S(2)}, u32[]{:S(2)}) %collective-permute-start.46) | collective-permute-done | bytes 196640 | tf_op jit(solution)/shard_map/ppermute | solution.py:374
  351.4 14.3 %shard_map.130 = (f32[2,4,1,18,128,128]{5,4,3,2,1,0:T(8,128)}, f32[2,4,1,18,128,128]{5,4,3,2,1,0:T(8,128)}, f32[2,4,1,18,128,128]{5,4,3,2,1,0:T(8,128)}) custom-call(s32[2,4]{1,0:T(2,128)S(1)} %bitcast.24, f32[18,128,128]{2,1,0:T(8,128)S(1)} %get-tuple-element.103.refs_0_, f32[18,128,128]{2,1,0:T(8,128)S(1)} %collective-permute-done.52.refs_1_, ...), custom_call_target="tpu_custom_call" | custom-call | flops 14155776 | bytes 33030144 | tf_op jit(solution)/shard_map/pallas_call | solution.py:541
  365.7 14.3 %shard_map.131 = (f32[2,4,1,18,128,128]{5,4,3,2,1,0:T(8,128)}, f32[2,4,1,18,128,128]{5,4,3,2,1,0:T(8,128)}, f32[2,4,1,18,128,128]{5,4,3,2,1,0:T(8,128)}) custom-call(s32[2,4]{1,0:T(2,128)S(1)} %bitcast.25, f32[18,128,128]{2,1,0:T(8,128)S(1)} %get-tuple-element.98.refs_0_, ...), custom_call_target="tpu_custom_call", output_to_operand_aliasing={{0}: (8, {}), {1}: (9, {}), {2}: (10, {})} | custom-call | flops 14155776 | bytes 33030144 | tf_op jit(solution)/shard_map/pallas_call | solution.py:541
  (162 shorter events, 82.0 us)
Async XLA Ops:
  14.1 34.0 %collective-permute-start.4 = (bf16[18,128,128]{2,1,0:T(8,128)(2,1)S(1)}, bf16[18,128,128]{2,1,0:T(8,128)(2,1)S(1)}, u32[]{:S(2)}, u32[]{:S(2)}) collective-permute-start(bf16[18,128,128]{2,1,0:T(8,128)(2,1)S(1)} %get-tuple-element.60), channel_id=1, source_target_pairs={{0,1},{1,0},{2,3},{3,2},{4,5},{5,4},{6,7},{7,6},{8,9},{9,8},{10,11... | collective-permute-start | bytes 1769480 | tf_op jit(solution)/shard_map/ppermute | solution.py:380
  16.4 31.8 %collective-permute-start.5 = (bf16[18,128,128]{2,1,0:T(8,128)(2,1)S(1)}, bf16[18,128,128]{2,1,0:T(8,128)(2,1)S(1)}, u32[]{:S(2)}, u32[]{:S(2)}) collective-permute-start(bf16[18,128,128]{2,1,0:T(8,128)(2,1)S(1)} %get-tuple-element.61), channel_id=1, source_target_pairs={{0,2},{1,3},{2,0},{3,1},{4,6},{5,7},{6,4},{7,5},{8,10},{9,11},{10,... | collective-permute-start | bytes 1769480 | tf_op jit(solution)/shard_map/ppermute | solution.py:380
  19.2 31.1 %collective-permute-start.6 = (bf16[18,128,128]{2,1,0:T(8,128)(2,1)S(1)}, bf16[18,128,128]{2,1,0:T(8,128)(2,1)S(1)}, u32[]{:S(2)}, u32[]{:S(2)}) collective-permute-start(bf16[18,128,128]{2,1,0:T(8,128)(2,1)S(1)} %get-tuple-element.62), channel_id=1, source_target_pairs={{0,3},{1,2},{2,1},{3,0},{4,7},{5,6},{6,5},{7,4},{8,11},{9,10},{10,... | collective-permute-start | bytes 1769480 | tf_op jit(solution)/shard_map/ppermute | solution.py:380
  19.9 30.5 %collective-permute-start.3 = (bf16[128,3072]{1,0:T(8,128)(2,1)S(1)}, bf16[128,3072]{1,0:T(8,128)(2,1)S(1)}, u32[]{:S(2)}, u32[]{:S(2)}) collective-permute-start(bf16[128,3072]{1,0:T(8,128)(2,1)S(1)} %constant_dynamic-update-slice_fusion.refs_0_), channel_id=1, source_target_pairs={{0,16},{16,0},{1,17},{17,1},{2,18},{18,2},{3,19},{19,3},{4,20},{20... | collective-permute-start | bytes 2359304 | tf_op jit(solution)/shard_map/ppermute | solution.py:377
  44.3 28.6 %collective-permute-start.29 = (bf16[2,32,3072]{2,1,0:T(8,128)(2,1)S(1)}, bf16[2,32,3072]{2,1,0:T(8,128)(2,1)S(1)}, u32[]{:S(2)}, u32[]{:S(2)}) collective-permute-start(bf16[2,32,3072]{2,1,0:T(8,128)(2,1)S(1)} %pad_maximum_fusion.2.refs_0_), channel_id=1, source_target_pairs={{0,8},{4,12},{8,0},{12,4},{1,9},{5,13},{9,1},{13,5},{2,10},{6,14},... | collective-permute-start | bytes 1179656 | tf_op jit(solution)/shard_map/ppermute | solution.py:374
  48.1 24.7 %collective-permute-start.16 = (bf16[18,128,128]{2,1,0:T(8,128)(2,1)S(1)}, bf16[18,128,128]{2,1,0:T(8,128)(2,1)S(1)}, u32[]{:S(2)}, u32[]{:S(2)}) collective-permute-start(bf16[18,128,128]{2,1,0:T(8,128)(2,1)S(1)} %get-tuple-element.75), channel_id=1, source_target_pairs={{0,1},{1,0},{2,3},{3,2},{4,5},{5,4},{6,7},{7,6},{8,9},{9,8},{10,11... | collective-permute-start | bytes 1769480 | tf_op jit(solution)/shard_map/ppermute | solution.py:380
  48.2 24.7 %collective-permute-start.17 = (bf16[18,128,128]{2,1,0:T(8,128)(2,1)S(1)}, bf16[18,128,128]{2,1,0:T(8,128)(2,1)S(1)}, u32[]{:S(2)}, u32[]{:S(2)}) collective-permute-start(bf16[18,128,128]{2,1,0:T(8,128)(2,1)S(1)} %get-tuple-element.76), channel_id=1, source_target_pairs={{0,2},{1,3},{2,0},{3,1},{4,6},{5,7},{6,4},{7,5},{8,10},{9,11},{10,... | collective-permute-start | bytes 1769480 | tf_op jit(solution)/shard_map/ppermute | solution.py:380
  50.3 26.3 %collective-permute-start.18 = (bf16[18,128,128]{2,1,0:T(8,128)(2,1)S(1)}, bf16[18,128,128]{2,1,0:T(8,128)(2,1)S(1)}, u32[]{:S(2)}, u32[]{:S(2)}) collective-permute-start(bf16[18,128,128]{2,1,0:T(8,128)(2,1)S(1)} %get-tuple-element.77), channel_id=1, source_target_pairs={{0,3},{1,2},{2,1},{3,0},{4,7},{5,6},{6,5},{7,4},{8,11},{9,10},{10,... | collective-permute-start | bytes 1769480 | tf_op jit(solution)/shard_map/ppermute | solution.py:380
  87.7 31.7 %collective-permute-start.34 = (f32[2,32,3072]{2,1,0:T(8,128)S(1)}, f32[2,32,3072]{2,1,0:T(8,128)S(1)}, u32[]{:S(2)}, u32[]{:S(2)}) collective-permute-start(f32[2,32,3072]{2,1,0:T(8,128)S(1)} %get-tuple-element.89), channel_id=1, source_target_pairs={{0,2},{1,3},{2,0},{3,1},{4,6},{5,7},{6,4},{7,5},{8,10},{9,11},{10,... | collective-permute-start | bytes 2359304 | tf_op jit(solution)/shard_map/ppermute | solution.py:380
  90.2 31.8 %collective-permute-start.32 = (f32[2,32,3072]{2,1,0:T(8,128)S(1)}, f32[2,32,3072]{2,1,0:T(8,128)S(1)}, u32[]{:S(2)}, u32[]{:S(2)}) collective-permute-start(f32[2,32,3072]{2,1,0:T(8,128)S(1)} %get-tuple-element.85), channel_id=1, source_target_pairs={{0,16},{16,0},{1,17},{17,1},{2,18},{18,2},{3,19},{19,3},{4,20},{20... | collective-permute-start | bytes 2359304 | tf_op jit(solution)/shard_map/ppermute | solution.py:377
  102.6 27.7 %collective-permute-start.11 = (f32[32,3072]{1,0:T(8,128)S(1)}, f32[32,3072]{1,0:T(8,128)S(1)}, u32[]{:S(2)}, u32[]{:S(2)}) collective-permute-start(f32[32,3072]{1,0:T(8,128)S(1)} %get-tuple-element.72), channel_id=1, source_target_pairs={{0,16},{16,0},{1,17},{17,1},{2,18},{18,2},{3,19},{19,3},{4,20},{20... | collective-permute-start | bytes 1179656 | tf_op jit(solution)/shard_map/ppermute | solution.py:377
  105.1 25.2 %collective-permute-start.9 = (f32[32,3072]{1,0:T(8,128)S(1)}, f32[32,3072]{1,0:T(8,128)S(1)}, u32[]{:S(2)}, u32[]{:S(2)}) collective-permute-start(f32[32,3072]{1,0:T(8,128)S(1)} %get-tuple-element.68), channel_id=1, source_target_pairs={{0,2},{1,3},{2,0},{3,1},{4,6},{5,7},{6,4},{7,5},{8,10},{9,11},{10,... | collective-permute-start | bytes 1179656 | tf_op jit(solution)/shard_map/ppermute | solution.py:380
  130.7 24.9 %collective-permute-start.13 = (bf16[32,6144]{1,0:T(8,128)(2,1)S(1)}, bf16[32,6144]{1,0:T(8,128)(2,1)S(1)}, u32[]{:S(2)}, u32[]{:S(2)}) collective-permute-start(bf16[32,6144]{1,0:T(8,128)(2,1)S(1)} %get-tuple-element.73), channel_id=1, source_target_pairs={{0,16},{1,17},{2,18},{3,19},{16,0},{17,1},{18,2},{19,3},{4,20},{5,... | collective-permute-start | bytes 1179656 | tf_op jit(solution)/shard_map/ppermute | solution.py:388
  132.3 23.4 %collective-permute-start.12 = (bf16[32,6144]{1,0:T(8,128)(2,1)S(1)}, bf16[32,6144]{1,0:T(8,128)(2,1)S(1)}, u32[]{:S(2)}, u32[]{:S(2)}) collective-permute-start(bf16[32,6144]{1,0:T(8,128)(2,1)S(1)} %get-tuple-element.73), channel_id=1, source_target_pairs={{0,2},{1,3},{2,0},{3,1},{16,18},{17,19},{18,16},{19,17},{4,6},{5,7... | collective-permute-start | bytes 1179656 | tf_op jit(solution)/shard_map/ppermute | solution.py:388
  139.3 24.4 %collective-permute-start.38 = (bf16[32,6144]{1,0:T(8,128)(2,1)S(1)}, bf16[32,6144]{1,0:T(8,128)(2,1)S(1)}, u32[]{:S(2)}, u32[]{:S(2)}) collective-permute-start(bf16[32,6144]{1,0:T(8,128)(2,1)S(1)} %shard_map.124), channel_id=1, source_target_pairs={{0,18},{1,19},{2,16},{3,17},{16,2},{17,3},{18,0},{19,1},{4,22},{5,... | collective-permute-start | bytes 1179656 | tf_op jit(solution)/shard_map/ppermute | solution.py:388
  139.4 32.3 %collective-permute-start.37 = (bf16[32,6144]{1,0:T(8,128)(2,1)S(1)}, bf16[32,6144]{1,0:T(8,128)(2,1)S(1)}, u32[]{:S(2)}, u32[]{:S(2)}) collective-permute-start(bf16[32,6144]{1,0:T(8,128)(2,1)S(1)} %shard_map.124), channel_id=1, source_target_pairs={{0,16},{1,17},{2,18},{3,19},{16,0},{17,1},{18,2},{19,3},{4,20},{5,... | collective-permute-start | bytes 1179656 | tf_op jit(solution)/shard_map/ppermute | solution.py:388
  146.8 25.0 %collective-permute-start.36 = (bf16[32,6144]{1,0:T(8,128)(2,1)S(1)}, bf16[32,6144]{1,0:T(8,128)(2,1)S(1)}, u32[]{:S(2)}, u32[]{:S(2)}) collective-permute-start(bf16[32,6144]{1,0:T(8,128)(2,1)S(1)} %shard_map.124), channel_id=1, source_target_pairs={{0,2},{1,3},{2,0},{3,1},{16,18},{17,19},{18,16},{19,17},{4,6},{5,7... | collective-permute-start | bytes 1179656 | tf_op jit(solution)/shard_map/ppermute | solution.py:388
  172.0 81.5 %collective-permute-start.53 = (bf16[256,3072]{1,0:T(8,128)(2,1)}, bf16[256,3072]{1,0:T(8,128)(2,1)}, u32[]{:S(2)}, u32[]{:S(2)}) collective-permute-start(bf16[256,3072]{1,0:T(8,128)(2,1)} %get-tuple-element.102.row_ref), channel_id=1, source_target_pairs={{0,2},{1,3},{2,0},{3,1},{4,6},{5,7},{6,4},{7,5},{8,10},{9,11},{10,... | collective-permute-start | bytes 4718600 | tf_op jit(solution)/shard_map/ppermute | solution.py:380
  172.3 85.5 %collective-permute-start.50 = (bf16[256,3072]{1,0:T(8,128)(2,1)}, bf16[256,3072]{1,0:T(8,128)(2,1)}, u32[]{:S(2)}, u32[]{:S(2)}) collective-permute-start(bf16[256,3072]{1,0:T(8,128)(2,1)} %get-tuple-element.97.row_ref), channel_id=1, source_target_pairs={{0,2},{1,3},{2,0},{3,1},{4,6},{5,7},{6,4},{7,5},{8,10},{9,11},{10,... | collective-permute-start | bytes 4718600 | tf_op jit(solution)/shard_map/ppermute | solution.py:380
  179.5 83.3 %collective-permute-start.19 = (f32[128,1536]{1,0:T(8,128)}, f32[128,1536]{1,0:T(8,128)}, u32[]{:S(2)}, u32[]{:S(2)}) collective-permute-start(f32[128,1536]{1,0:T(8,128)} %get-tuple-element.79), channel_id=1, source_target_pairs={{0,16},{16,0},{1,17},{17,1},{2,18},{18,2},{3,19},{19,3},{4,20},{20... | collective-permute-start | bytes 2359304 | tf_op jit(solution)/shard_map/ppermute | solution.py:377
  179.5 63.3 %collective-permute-start.49 = (s32[2,144]{1,0:T(2,128)S(1)}, s32[2,144]{1,0:T(2,128)S(1)}, u32[]{:S(2)}, u32[]{:S(2)}) collective-permute-start(s32[2,144]{1,0:T(2,128)S(1)} %bitcast.29), channel_id=1, source_target_pairs={{0,2},{1,3},{2,0},{3,1},{4,6},{5,7},{6,4},{7,5},{8,10},{9,11},{10,... | collective-permute-start | bytes 3464 | tf_op jit(solution)/shard_map/ppermute | solution.py:380
  180.2 90.1 %collective-permute-start.23 = (f32[128,1536]{1,0:T(8,128)}, f32[128,1536]{1,0:T(8,128)}, u32[]{:S(2)}, u32[]{:S(2)}) collective-permute-start(f32[128,1536]{1,0:T(8,128)} %get-tuple-element.81), channel_id=1, source_target_pairs={{0,16},{16,0},{1,17},{17,1},{2,18},{18,2},{3,19},{19,3},{4,20},{20... | collective-permute-start | bytes 2359304 | tf_op jit(solution)/shard_map/ppermute | solution.py:377
  242.8 28.8 %collective-permute-start.40 = (f32[128,1536]{1,0:T(8,128)}, f32[128,1536]{1,0:T(8,128)}, u32[]{:S(2)}, u32[]{:S(2)}) collective-permute-start(f32[128,1536]{1,0:T(8,128)} %get-tuple-element.94), channel_id=1, source_target_pairs={{0,16},{16,0},{1,17},{17,1},{2,18},{18,2},{3,19},{19,3},{4,20},{20... | collective-permute-start | bytes 2359304 | tf_op jit(solution)/shard_map/ppermute | solution.py:377
  253.5 30.1 %collective-permute-start.44 = (f32[128,1536]{1,0:T(8,128)S(1)}, f32[128,1536]{1,0:T(8,128)S(1)}, u32[]{:S(2)}, u32[]{:S(2)}) collective-permute-start(f32[128,1536]{1,0:T(8,128)S(1)} %copy-done.17), channel_id=1, source_target_pairs={{0,16},{16,0},{1,17},{17,1},{2,18},{18,2},{3,19},{19,3},{4,20},{20... | collective-permute-start | bytes 2359304 | tf_op jit(solution)/shard_map/ppermute | solution.py:377
  257.8 93.6 %collective-permute-start.54 = (f32[18,128,128]{2,1,0:T(8,128)S(1)}, f32[18,128,128]{2,1,0:T(8,128)S(1)}, u32[]{:S(2)}, u32[]{:S(2)}) collective-permute-start(f32[18,128,128]{2,1,0:T(8,128)S(1)} %get-tuple-element.106), channel_id=1, source_target_pairs={{0,1},{1,0},{2,3},{3,2},{4,5},{5,4},{6,7},{7,6},{8,9},{9,8},{10,11... | collective-permute-start | bytes 3538952 | tf_op jit(solution)/shard_map/ppermute | solution.py:380
  271.6 25.7 %collective-permute-start.21 = (f32[32,1536]{1,0:T(8,128)S(1)}, f32[32,1536]{1,0:T(8,128)S(1)}, u32[]{:S(2)}, u32[]{:S(2)}) collective-permute-start(f32[32,1536]{1,0:T(8,128)S(1)} %get-tuple-element.121), channel_id=1, source_target_pairs={{0,8},{4,12},{8,0},{12,4},{1,9},{5,13},{9,1},{13,5},{2,10},{6,14},... | collective-permute-start | bytes 589832 | tf_op jit(solution)/shard_map/ppermute | solution.py:374
  284.8 25.7 %collective-permute-start.26 = (f32[32,1536]{1,0:T(8,128)S(1)}, f32[32,1536]{1,0:T(8,128)S(1)}, u32[]{:S(2)}, u32[]{:S(2)}) collective-permute-start(f32[32,1536]{1,0:T(8,128)S(1)} %get-tuple-element.123), channel_id=1, source_target_pairs={{0,4},{4,8},{8,12},{12,0},{1,5},{5,9},{9,13},{13,1},{2,6},{6,10},{... | collective-permute-start | bytes 589832 | tf_op jit(solution)/shard_map/ppermute | solution.py:374
  290.4 32.1 %collective-permute-start.25 = (f32[32,1536]{1,0:T(8,128)S(1)}, f32[32,1536]{1,0:T(8,128)S(1)}, u32[]{:S(2)}, u32[]{:S(2)}) collective-permute-start(f32[32,1536]{1,0:T(8,128)S(1)} %get-tuple-element.124), channel_id=1, source_target_pairs={{0,8},{4,12},{8,0},{12,4},{1,9},{5,13},{9,1},{13,5},{2,10},{6,14},... | collective-permute-start | bytes 589832 | tf_op jit(solution)/shard_map/ppermute | solution.py:374
  297.3 25.3 %collective-permute-start.41 = (f32[32,1536]{1,0:T(8,128)S(1)}, f32[32,1536]{1,0:T(8,128)S(1)}, u32[]{:S(2)}, u32[]{:S(2)}) collective-permute-start(f32[32,1536]{1,0:T(8,128)S(1)} %get-tuple-element.113), channel_id=1, source_target_pairs={{0,12},{4,0},{8,4},{12,8},{1,13},{5,1},{9,5},{13,9},{2,14},{6,2},{... | collective-permute-start | bytes 589832 | tf_op jit(solution)/shard_map/ppermute | solution.py:374
  322.6 28.8 %collective-permute-start.52 = (f32[18,128,128]{2,1,0:T(8,128)S(1)}, f32[18,128,128]{2,1,0:T(8,128)S(1)}, u32[]{:S(2)}, u32[]{:S(2)}) collective-permute-start(f32[18,128,128]{2,1,0:T(8,128)S(1)} %get-tuple-element.104), channel_id=1, source_target_pairs={{0,1},{1,0},{2,3},{3,2},{4,5},{5,4},{6,7},{7,6},{8,9},{9,8},{10,11... | collective-permute-start | bytes 3538952 | tf_op jit(solution)/shard_map/ppermute | solution.py:380
  322.7 43.0 %collective-permute-start.48 = (f32[18,128,128]{2,1,0:T(8,128)S(1)}, f32[18,128,128]{2,1,0:T(8,128)S(1)}, u32[]{:S(2)}, u32[]{:S(2)}) collective-permute-start(f32[18,128,128]{2,1,0:T(8,128)S(1)} %get-tuple-element.99), channel_id=1, source_target_pairs={{0,1},{1,0},{2,3},{3,2},{4,5},{5,4},{6,7},{7,6},{8,9},{9,8},{10,11... | collective-permute-start | bytes 3538952 | tf_op jit(solution)/shard_map/ppermute | solution.py:380
  331.1 34.7 %collective-permute-start.51 = (f32[18,128,128]{2,1,0:T(8,128)S(1)}, f32[18,128,128]{2,1,0:T(8,128)S(1)}, u32[]{:S(2)}, u32[]{:S(2)}) collective-permute-start(f32[18,128,128]{2,1,0:T(8,128)S(1)} %get-tuple-element.101), channel_id=1, source_target_pairs={{0,1},{1,0},{2,3},{3,2},{4,5},{5,4},{6,7},{7,6},{8,9},{9,8},{10,11... | collective-permute-start | bytes 3538952 | tf_op jit(solution)/shard_map/ppermute | solution.py:380
  (43 other events, 547.9 us)

commit v8 on v7

--- a/solution.py
+++ b/solution.py
@@ -113,12 +113,9 @@
     matrix, transposed, width_blocks, tok_count, hid_count, mem_count, kept_ref, place_ref, *refs
 ):
     sources = hid_count if matrix else mem_count
-    own_refs, weight_refs, (row_ref, keep_ref, send_ref) = (
-        refs[:sources],
-        refs[sources : sources + tok_count],
-        refs[sources + tok_count : -2],
-    )
-    weight_refs, finish = start_weights(weight_refs, *refs[-2:])
+    own_refs = refs[:sources]
+    row_ref, keep_ref, send_ref, held_ref, sems = refs[sources + tok_count :]
+    weight_refs, finish = start_weights(refs[sources : sources + tok_count], held_ref, sems)
     half = keep_ref.shape[1]
     _, size = weight_refs[0].shape[:2]
     rows = row_ref.shape[0] // mem_count
@@ -156,9 +153,9 @@
     matrix, transposed, width_blocks, mem_count, kept_ref, place_ref, own_ref, pair_ref, *refs
 ):
     tok_count = lax.axis_size(TOK)
-    out_refs, total_ref = refs[tok_count:-3], refs[-1]
-    weight_refs, finish = start_weights(refs[:tok_count], *refs[-3:-1])
-    size = weight_refs[0].shape[-1]
+    held_ref, out_refs, total_ref = refs[0], refs[1:-1], refs[-1]
+    weight_refs = [held_ref.at[turn] for turn in range(tok_count)]
+    size = held_ref.shape[-1]
     half = own_ref.shape[1]
     total_ref[...] = jnp.zeros(total_ref.shape, jnp.float32)
 
@@ -177,7 +174,6 @@
         for spot, product in found:
             total_ref[:, spot] += product
 
-    finish()
     over_owners(matrix, kept_ref, weight_refs, body)
     for index, out_ref in enumerate(out_refs):
         chunk, group = index // mem_count, index % mem_count
@@ -230,15 +226,13 @@
         lax.fori_loop(count, owned, clear, 0)
 
 
-def update_kernel(matrix, owned, kept_ref, *refs):
-    tok_count = lax.axis_size(TOK)
-    grad_refs = refs[:tok_count]
-    weight_ref, moment_ref, variance_ref = refs[tok_count : tok_count + 3]
+def update_kernel(matrix, cell, owned, kept_ref, own_ref, pair_ref, *refs):
+    weight_ref, moment_ref, variance_ref = refs[:3]
     out_refs = refs[-3:]
     turn = pl.program_id(0)
     tok = lax.axis_index(TOK)
     run = weight_ref.shape[3]
-    _, count = owner_count(kept_ref, matrix, tok ^ turn, tok, owned)
+    _, count = owner_count(kept_ref, matrix, tok ^ (2 * cell + turn), tok, owned)
     count = jnp.clip(count - pl.program_id(1) * run, 0, run)
 
     def update_from(grad_ref):
@@ -251,8 +245,8 @@
 
         lax.fori_loop(0, count, update, 0)
 
-    for index, grad_ref in enumerate(grad_refs):
-        pl.when(turn == index)(functools.partial(update_from, grad_ref))
+    pl.when(turn == 0)(functools.partial(update_from, own_ref))
+    pl.when(turn == 1)(functools.partial(update_from, pair_ref))
 
     def keep(slot, carry):
         at = (0, 0, 0, slot)
@@ -324,14 +318,12 @@
 
 
 def call(kernel, outs, scalars, arrays, flops, outside=(), scratch=()):
+    moved = sum(math_size(a) for a in (*arrays, *outs))
+    needed = moved
     if outside:
-        scratch = [
-            pltpu.VMEM((len(outside), *outside[0].shape), outside[0].dtype),
-            pltpu.SemaphoreType.DMA((len(outside),)),
-            *scratch,
-        ]
-    moved = sum(math_size(a) for a in (*arrays, *outs, *outside))
-    needed = moved + sum(math_size(x) for x in scratch[2:])
+        scratch = [pltpu.SemaphoreType.DMA((len(outside),))]
+    else:
+        needed += sum(math_size(x) for x in scratch)
     return pl.pallas_call(
         kernel,
         out_shape=outs,
@@ -424,6 +416,7 @@
             jax.ShapeDtypeStruct((mem_count * rows, width), bf16),
             jax.ShapeDtypeStruct((mem_count, half, hidden_span), f32),
             jax.ShapeDtypeStruct((mem_count, half, hidden_span), f32),
+            jax.ShapeDtypeStruct((tok_count, owned_slots, block_size, block_size), bf16),
         ]
         flops = 2 * mem_count * rows * local_slots * block_size * block_size
         return call(kernel, outs, scalars, row_groups, flops, weights)
@@ -492,7 +485,8 @@
         outs = [jax.ShapeDtypeStruct((rows, span), f32)] * (mem_count * chunks)
         flops = 2 * mem_count * rows * local_slots * block_size * block_size
         scratch = [pltpu.VMEM((mem_count * rows, inputs.shape[1]), f32)]
-        return call(kernel, outs, scalars, [near, far], flops, weights, scratch)
+        arrays = [near, far, weights]
+        return call(kernel, outs, scalars, arrays, flops, (), scratch)
 
     turn = relative(tok_count)
     step = inputs.shape[0]
@@ -522,32 +516,28 @@
         keep, send = call(kernel, outs, (kept, ids), [row_values, near, far], flops)
         return keep, flip_tok(send, 1)
 
-    def update(matrix, grads, held):
+    def update(matrix, cell, grads, held):
         splits = 2 if owned_slots % 2 == 0 else 1
         run = owned_slots // splits
         state_spec = pl.BlockSpec(
             (1, 1, 1, run, block_size, block_size),
-            lambda i, j: (matrix, lax.axis_index(TOK) ^ i, 0, j, 0, 0),
+            lambda i, j: (matrix, lax.axis_index(TOK) ^ (2 * cell + i), 0, j, 0, 0),
         )
-
-        def grad_spec(turn):
-            return pl.BlockSpec(
-                (run, block_size, block_size),
-                lambda i, j: (jnp.where(i < turn, 0, jnp.where(i > turn, splits - 1, j)), 0, 0),
-            )
-
+        own_spec = pl.BlockSpec(
+            (run, block_size, block_size), lambda i, j: (jnp.where(i == 0, j, splits - 1), 0, 0)
+        )
+        pair_spec = pl.BlockSpec(
+            (run, block_size, block_size), lambda i, j: (jnp.where(i == 0, 0, j), 0, 0)
+        )
         state = (blocks, first_moment, second_moment)
-        size = local_slots * block_size * block_size
+        size = 2 * owned_slots * block_size * block_size
         return pl.pallas_call(
-            functools.partial(update_kernel, matrix, owned_slots),
-            grid=(tok_count, splits),
+            functools.partial(update_kernel, matrix, cell, owned_slots),
+            grid=(2, splits),
             out_shape=[jax.ShapeDtypeStruct(s.shape, f32) for s in state],
-            in_specs=[SCALARS]
-            + [grad_spec(turn) for turn in range(tok_count)]
-            + [state_spec] * 3
-            + [ANYWHERE] * len(held),
+            in_specs=[SCALARS, own_spec, pair_spec] + [state_spec] * 3 + [ANYWHERE] * len(held),
             out_specs=[state_spec] * 3,
-            input_output_aliases={4 + tok_count + i: i for i in range(len(held))},
+            input_output_aliases={6 + i: i for i in range(len(held))},
             compiler_params=grant(44 * 2**20),
             cost_estimate=pl.CostEstimate(
                 flops=size * 12, bytes_accessed=size * 28, transcendentals=size
@@ -559,9 +549,9 @@
     weights_first = gather_weights(0)
     cotangent_groups = gather_small(cotangent)
     weights_second = gather_weights(1)
-    token_rows, *pre_part = forward(0, False, input_groups, weights_first)
+    token_rows, *pre_part, weights_first = forward(0, False, input_groups, weights_first)
     pre_terms = reduce_plane(*pre_part)
-    grad_rows, *back_part = forward(1, True, cotangent_groups, weights_second)
+    grad_rows, *back_part, weights_second = forward(1, True, cotangent_groups, weights_second)
     back_terms = reduce_plane(*back_part)
     piece = (part, hidden_span)
     outs = [jax.ShapeDtypeStruct(piece, bf16), jax.ShapeDtypeStruct(piece, f32)]
@@ -576,16 +566,14 @@
     grad_in = reduce_rows(backward(0, True, *pre_grad, weights_first))
     far_grad_rows = flip_tok(grad_rows, 2)
     far_token_rows = flip_tok(token_rows, 2)
-    second_grad = [
-        *gradient(1, 0, place_ids, grad_rows, *hidden),
-        *gradient(1, 1, far_place_ids, far_grad_rows, *hidden),
-    ]
-    first_grad = [
-        *gradient(0, 0, place_ids, token_rows, *pre_grad),
-        *gradient(0, 1, far_place_ids, far_token_rows, *pre_grad),
-    ]
-    held = update(1, second_grad, ())
-    return (layer_out, grad_in, *update(0, first_grad, held))
+    grads = gradient(1, 0, place_ids, grad_rows, *hidden)
+    state = update(1, 0, grads, ())
+    grads = gradient(0, 0, place_ids, token_rows, *pre_grad)
+    state = update(0, 0, grads, state)
+    grads = gradient(1, 1, far_place_ids, far_grad_rows, *hidden)
+    state = update(1, 1, grads, state)
+    grads = gradient(0, 1, far_place_ids, far_token_rows, *pre_grad)
+    return (layer_out, grad_in, *update(0, 1, grads, state))
 
 
 def solution(mesh):

time: 381 us -> 382 us (level)
    pallas_call x2 -> x4, Pallas kernels: 28.6 us -> 29.8 us  [update(): pl.pallas_call(functools.partial(update_kernel, matrix, cell, owned_slots...]
  transfers between devices with their start and end apart: 55 -> 55, of which waited for: 25 -> 25; matrix products, arithmetic and copies ran while one was open for 2% -> 2% of each run, Pallas kernels for 16% -> 18%
where the time goes in v8:
time: 382 us; the launch traced here: 381 us
  waiting for transfers between devices  205 us (54%)
  starting transfers between devices  82.5 us (22%)
  Pallas kernels  75.5 us (20%)
  local copies, waits for them, and re-layouts  11.1 us (3%)
  other arithmetic  5.77 us (2%)
    ppermute x21, waiting for transfers between devices, flip_tok(): return lax.ppermute(array, TOK, [(i, i ^ bit) for i in range(tok_count)])  82.8 us
    ppermute x18, waiting for transfers between devices, shift_hid(): lax.ppermute(array, HID, [(i, (i + shift) % hid_count) for i in range(hid...  76.1 us
    ppermute x18, starting transfers between devices, shift_hid(): lax.ppermute(array, HID, [(i, (i + shift) % hid_count) for i in range(hid...  57.9 us
    pallas_call x14, Pallas kernels, call(): pl.pallas_call(kernel, out_shape=outs, in_specs=[SCALARS] * len(scalars)...  42.9 us
    pallas_call x4, Pallas kernels, update(): pl.pallas_call(functools.partial(update_kernel, matrix, cell, owned_slots...  29.8 us
    ppermute x6, waiting for transfers between devices, across(): return lax.ppermute(array, (MEM, TOK), table)  28.6 us
    ppermute x10, waiting for transfers between devices, shift_mem(): lax.ppermute(array, MEM, [(i, (i + shift) % mem_count) for i in range(mem...  17.5 us
    ppermute x21, starting transfers between devices, flip_tok(): return lax.ppermute(array, TOK, [(i, i ^ bit) for i in range(tok_count)])  11.7 us
  transfers between devices with their start and end apart: 55, of which 25 were waited for; matrix products, arithmetic and copies ran while one was open for 2% of the time, Pallas kernels for 18%

profile of v8, /device:TPU:0, one launch (start us, length us, event | category | flops | bytes accessed | tf_op | source)
XLA Modules:
  0.0 381.1 jit_solution(2115834442949465710)
XLA Ops:
  0.6 4.1 %collective-permute-start.1 = (bf16[32,3072]{1,0:T(8,128)(2,1)}, bf16[32,3072]{1,0:T(8,128)(2,1)S(1)}, u32[]{:S(2)}, u32[]{:S(2)}) collective-permute-start(bf16[32,3072]{1,0:T(8,128)(2,1)} %param.7), channel_id=1, source_target_pairs={{0,8},{4,12},{8,0},{12,4},{1,9},{5,13},{9,1},{13,5},{2,10},{6,14},... | collective-permute-start | bytes 589832 | tf_op jit(solution)/shard_map/ppermute | solution.py:366
  23.7 20.6 %collective-permute-done.19.refs_3_ = bf16[2,32,3072]{2,1,0:T(8,128)(2,1)S(1)} collective-permute-done((bf16[2,32,3072]{2,1,0:T(8,128)(2,1)S(1)}, bf16[2,32,3072]{2,1,0:T(8,128)(2,1)S(1)}, u32[]{:S(2)}, u32[]{:S(2)}) %collective-permute-start.19) | collective-permute-done | bytes 393248 | tf_op jit(solution)/shard_map/ppermute | solution.py:366
  52.9 7.6 %shard_map.111 = (bf16[256,3072]{1,0:T(8,128)(2,1)}, f32[2,64,6144]{2,1,0:T(8,128)S(1)}, f32[2,64,6144]{2,1,0:T(8,128)S(1)}, bf16[4,18,128,128]{3,2,1,0:T(8,128)(2,1)S(1)}) custom-call(s32[2,4]{1,0:T(2,128)S(1)} %bitcast.16, s32[2,144]{1,0:T(2,128)S(1)} %bitcast.28, bf16[128,3072]{1,0:T(8,128)(2,1)S(1)} %constant_dynamic-update-slice_fusion.refs_0_, ...), custom_call_target="tpu_custom_call" | custom-call | flops 603979776 | bytes 11796480 | tf_op jit(solution)/shard_map/pallas_call | solution.py:327
  60.5 12.4 %collective-permute-done.18.refs_2_ = bf16[2,32,3072]{2,1,0:T(8,128)(2,1)S(1)} collective-permute-done((bf16[2,32,3072]{2,1,0:T(8,128)(2,1)S(1)}, bf16[2,32,3072]{2,1,0:T(8,128)(2,1)S(1)}, u32[]{:S(2)}, u32[]{:S(2)}) %collective-permute-start.18) | collective-permute-done | bytes 393248 | tf_op jit(solution)/shard_map/ppermute | solution.py:366
  76.6 4.8 %shard_map.118 = (bf16[256,3072]{1,0:T(8,128)(2,1)}, f32[2,64,6144]{2,1,0:T(8,128)S(1)}, f32[2,64,6144]{2,1,0:T(8,128)S(1)}, bf16[4,18,128,128]{3,2,1,0:T(8,128)(2,1)S(1)}) custom-call(s32[2,4]{1,0:T(2,128)S(1)} %bitcast.17, s32[2,144]{1,0:T(2,128)S(1)} %bitcast.29, bf16[2,32,3072]{2,1,0:T(8,128)(2,1)S(1)} %pad_maximum_fusion.2.refs_0_, ...), custom_call_target="tpu_custom_call" | custom-call | flops 603979776 | bytes 11796480 | tf_op jit(solution)/shard_map/pallas_call | solution.py:327
  90.2 12.3 %collective-permute-done.10.refs_1_ = f32[2,32,3072]{2,1,0:T(8,128)S(1)} collective-permute-done((f32[2,32,3072]{2,1,0:T(8,128)S(1)}, f32[2,32,3072]{2,1,0:T(8,128)S(1)}, u32[]{:S(2)}, u32[]{:S(2)}) %collective-permute-start.10) | collective-permute-done | bytes 786464 | tf_op jit(solution)/shard_map/ppermute | solution.py:372
  105.3 14.1 %collective-permute-done.34.refs_1_ = f32[2,32,3072]{2,1,0:T(8,128)S(1)} collective-permute-done((f32[2,32,3072]{2,1,0:T(8,128)S(1)}, f32[2,32,3072]{2,1,0:T(8,128)S(1)}, u32[]{:S(2)}, u32[]{:S(2)}) %collective-permute-start.34) | collective-permute-done | bytes 786464 | tf_op jit(solution)/shard_map/ppermute | solution.py:372
  122.2 8.2 %collective-permute-done.11.refs_3_ = f32[32,3072]{1,0:T(8,128)S(1)} collective-permute-done((f32[32,3072]{1,0:T(8,128)S(1)}, f32[32,3072]{1,0:T(8,128)S(1)}, u32[]{:S(2)}, u32[]{:S(2)}) %collective-permute-start.11) | collective-permute-done | bytes 393248 | tf_op jit(solution)/shard_map/ppermute | solution.py:369
  134.2 4.6 %collective-permute-done.35.refs_3_ = f32[32,3072]{1,0:T(8,128)S(1)} collective-permute-done((f32[32,3072]{1,0:T(8,128)S(1)}, f32[32,3072]{1,0:T(8,128)S(1)}, u32[]{:S(2)}, u32[]{:S(2)}) %collective-permute-start.35) | collective-permute-done | bytes 393248 | tf_op jit(solution)/shard_map/ppermute | solution.py:369
  141.0 5.8 %collective-permute-done.14 = bf16[32,6144]{1,0:T(8,128)(2,1)S(1)} collective-permute-done((bf16[32,6144]{1,0:T(8,128)(2,1)S(1)}, bf16[32,6144]{1,0:T(8,128)(2,1)S(1)}, u32[]{:S(2)}, u32[]{:S(2)}) %collective-permute-start.14) | collective-permute-done | bytes 393248 | tf_op jit(solution)/shard_map/ppermute | solution.py:380
  148.7 7.0 %collective-permute-done.13 = bf16[32,6144]{1,0:T(8,128)(2,1)S(1)} collective-permute-done((bf16[32,6144]{1,0:T(8,128)(2,1)S(1)}, bf16[32,6144]{1,0:T(8,128)(2,1)S(1)}, u32[]{:S(2)}, u32[]{:S(2)}) %collective-permute-start.13) | collective-permute-done | bytes 393248 | tf_op jit(solution)/shard_map/ppermute | solution.py:380
  155.9 7.8 %collective-permute-done.38 = bf16[32,6144]{1,0:T(8,128)(2,1)S(1)} collective-permute-done((bf16[32,6144]{1,0:T(8,128)(2,1)S(1)}, bf16[32,6144]{1,0:T(8,128)(2,1)S(1)}, u32[]{:S(2)}, u32[]{:S(2)}) %collective-permute-start.38) | collective-permute-done | bytes 393248 | tf_op jit(solution)/shard_map/ppermute | solution.py:380
  163.7 8.0 %collective-permute-done.37 = bf16[32,6144]{1,0:T(8,128)(2,1)S(1)} collective-permute-done((bf16[32,6144]{1,0:T(8,128)(2,1)S(1)}, bf16[32,6144]{1,0:T(8,128)(2,1)S(1)}, u32[]{:S(2)}, u32[]{:S(2)}) %collective-permute-start.37) | collective-permute-done | bytes 393248 | tf_op jit(solution)/shard_map/ppermute | solution.py:380
  182.5 7.3 %shard_map.125 = (f32[128,1536]{1,0:T(8,128)S(1)}, f32[128,1536]{1,0:T(8,128)}, f32[128,1536]{1,0:T(8,128)S(1)}, f32[128,1536]{1,0:T(8,128)S(1)}) custom-call(s32[2,4]{1,0:T(2,128)S(1)} %bitcast.19, s32[2,144]{1,0:T(2,128)S(1)} %bitcast.32, bf16[2,64,6144]{2,1,0:T(8,128)(2,1)S(1)} %bitcast.13, bf16[2,64,6144]{2,1,0:T(8,128)(2,1)S(1)} %collective-permute-done.39.pair_ref, ...), custom_call_target="tpu_custom_call" | custom-call | flops 603979776 | bytes 8650752 | tf_op jit(solution)/shard_map/pallas_call | solution.py:327
  192.6 50.2 %collective-permute-done.48.place_ref = s32[2,144]{1,0:T(2,128)S(1)} collective-permute-done((s32[2,144]{1,0:T(2,128)S(1)}, s32[2,144]{1,0:T(2,128)S(1)}, u32[]{:S(2)}, u32[]{:S(2)}) %collective-permute-start.48) | collective-permute-done | bytes 1184 | tf_op jit(solution)/shard_map/ppermute | solution.py:372
  248.5 4.9 %shard_map.128 = (f32[18,128,128]{2,1,0:T(8,128)S(1)}, f32[18,128,128]{2,1,0:T(8,128)S(1)}) custom-call(s32[2,4]{1,0:T(2,128)S(1)} %bitcast.21, s32[2,144]{1,0:T(2,128)S(1)} %bitcast.34, bf16[256,3072]{1,0:T(8,128)(2,1)} %get-tuple-element.107.row_ref, bf16[2,64,6144]{2,1,0:T(8,128)(2,1)S(1)} %bitcast.14, bf16[2,64,6144]{2,1,0:T(8,128)(2,1)S(1)} %copy-done.6), custom_call_target="tpu_custom_call" | custom-call | flops 301989888 | bytes 7077888 | tf_op jit(solution)/shard_map/pallas_call | solution.py:327
  253.5 4.3 %shard_map.127 = (f32[18,128,128]{2,1,0:T(8,128)S(1)}, f32[18,128,128]{2,1,0:T(8,128)S(1)}) custom-call(s32[2,4]{1,0:T(2,128)S(1)} %bitcast.22, s32[2,144]{1,0:T(2,128)S(1)} %collective-permute-done.48.place_ref, bf16[256,3072]{1,0:T(8,128)(2,1)} %collective-permute-done.51.row_ref, bf16[2,64,6144]{2,1,0:T(8,128)(2,1)S(1)} %bitcast.11, ...), custom_call_target="tpu_custom_call" | custom-call | flops 301989888 | bytes 7077888 | tf_op jit(solution)/shard_map/pallas_call | solution.py:327
  257.9 4.9 %shard_map.126 = (f32[18,128,128]{2,1,0:T(8,128)S(1)}, f32[18,128,128]{2,1,0:T(8,128)S(1)}) custom-call(s32[2,4]{1,0:T(2,128)S(1)} %bitcast.23, s32[2,144]{1,0:T(2,128)S(1)} %collective-permute-done.48.place_ref, bf16[256,3072]{1,0:T(8,128)(2,1)} %collective-permute-done.49.row_ref, bf16[2,64,6144]{2,1,0:T(8,128)(2,1)S(1)} %bitcast.15, ...), custom_call_target="tpu_custom_call" | custom-call | flops 301989888 | bytes 7077888 | tf_op jit(solution)/shard_map/pallas_call | solution.py:327
  264.2 6.2 %collective-permute-start.24 = (f32[32,1536]{1,0:T(8,128)S(1)}, f32[32,1536]{1,0:T(8,128)S(1)}, u32[]{:S(2)}, u32[]{:S(2)}) collective-permute-start(f32[32,1536]{1,0:T(8,128)S(1)} %get-tuple-element.135), channel_id=1, source_target_pairs={{0,12},{4,0},{8,4},{12,8},{1,13},{5,1},{9,5},{13,9},{2,14},{6,2},{... | collective-permute-start | bytes 589832 | tf_op jit(solution)/shard_map/ppermute | solution.py:366
  271.7 10.7 %collective-permute-start.25 = (f32[32,1536]{1,0:T(8,128)S(1)}, f32[32,1536]{1,0:T(8,128)S(1)}, u32[]{:S(2)}, u32[]{:S(2)}) collective-permute-start(f32[32,1536]{1,0:T(8,128)S(1)} %get-tuple-element.137), channel_id=1, source_target_pairs={{0,8},{4,12},{8,0},{12,4},{1,9},{5,13},{9,1},{13,5},{2,10},{6,14},... | collective-permute-start | bytes 589832 | tf_op jit(solution)/shard_map/ppermute | solution.py:366
  286.0 4.5 %collective-permute-done.26 = f32[32,1536]{1,0:T(8,128)S(1)} collective-permute-done((f32[32,1536]{1,0:T(8,128)S(1)}, f32[32,1536]{1,0:T(8,128)S(1)}, u32[]{:S(2)}, u32[]{:S(2)}) %collective-permute-start.26) | collective-permute-done | bytes 196640 | tf_op jit(solution)/shard_map/ppermute | solution.py:366
  290.5 4.7 %collective-permute-start.29 = (f32[32,1536]{1,0:T(8,128)S(1)}, f32[32,1536]{1,0:T(8,128)S(1)}, u32[]{:S(2)}, u32[]{:S(2)}) collective-permute-start(f32[32,1536]{1,0:T(8,128)S(1)} %get-tuple-element.140), channel_id=1, source_target_pairs={{0,8},{4,12},{8,0},{12,4},{1,9},{5,13},{9,1},{13,5},{2,10},{6,14},... | collective-permute-start | bytes 589832 | tf_op jit(solution)/shard_map/ppermute | solution.py:366
  297.4 7.2 %collective-permute-start.41 = (f32[32,1536]{1,0:T(8,128)S(1)}, f32[32,1536]{1,0:T(8,128)S(1)}, u32[]{:S(2)}, u32[]{:S(2)}) collective-permute-start(f32[32,1536]{1,0:T(8,128)S(1)} %get-tuple-element.129), channel_id=1, source_target_pairs={{0,12},{4,0},{8,4},{12,8},{1,13},{5,1},{9,5},{13,9},{2,14},{6,2},{... | collective-permute-start | bytes 589832 | tf_op jit(solution)/shard_map/ppermute | solution.py:366
  304.6 6.0 %collective-permute-start.43 = (f32[32,1536]{1,0:T(8,128)S(1)}, f32[32,1536]{1,0:T(8,128)S(1)}, u32[]{:S(2)}, u32[]{:S(2)}) collective-permute-start(f32[32,1536]{1,0:T(8,128)S(1)} %get-tuple-element.130), channel_id=1, source_target_pairs={{0,4},{4,8},{8,12},{12,0},{1,5},{5,9},{9,13},{13,1},{2,6},{6,10},{... | collective-permute-start | bytes 589832 | tf_op jit(solution)/shard_map/ppermute | solution.py:366
  312.1 10.6 %collective-permute-done.29 = f32[32,1536]{1,0:T(8,128)S(1)} collective-permute-done((f32[32,1536]{1,0:T(8,128)S(1)}, f32[32,1536]{1,0:T(8,128)S(1)}, u32[]{:S(2)}, u32[]{:S(2)}) %collective-permute-start.29) | collective-permute-done | bytes 196640 | tf_op jit(solution)/shard_map/ppermute | solution.py:366
  323.3 7.8 %collective-permute-done.42 = f32[32,1536]{1,0:T(8,128)S(1)} collective-permute-done((f32[32,1536]{1,0:T(8,128)S(1)}, f32[32,1536]{1,0:T(8,128)S(1)}, u32[]{:S(2)}, u32[]{:S(2)}) %collective-permute-start.42) | collective-permute-done | bytes 196640 | tf_op jit(solution)/shard_map/ppermute | solution.py:366
  335.7 5.0 %collective-permute-done.47 = f32[32,1536]{1,0:T(8,128)S(1)} collective-permute-done((f32[32,1536]{1,0:T(8,128)S(1)}, f32[32,1536]{1,0:T(8,128)S(1)}, u32[]{:S(2)}, u32[]{:S(2)}) %collective-permute-start.47) | collective-permute-done | bytes 196640 | tf_op jit(solution)/shard_map/ppermute | solution.py:366
  342.6 8.0 %collective-permute-done.46 = f32[32,1536]{1,0:T(8,128)S(1)} collective-permute-done((f32[32,1536]{1,0:T(8,128)S(1)}, f32[32,1536]{1,0:T(8,128)S(1)}, u32[]{:S(2)}, u32[]{:S(2)}) %collective-permute-start.46) | collective-permute-done | bytes 196640 | tf_op jit(solution)/shard_map/ppermute | solution.py:366
  351.4 7.4 %shard_map.130 = (f32[2,4,1,18,128,128]{5,4,3,2,1,0:T(8,128)}, f32[2,4,1,18,128,128]{5,4,3,2,1,0:T(8,128)}, f32[2,4,1,18,128,128]{5,4,3,2,1,0:T(8,128)}) custom-call(s32[2,4]{1,0:T(2,128)S(1)} %bitcast.24, f32[18,128,128]{2,1,0:T(8,128)S(1)} %get-tuple-element.115.own_ref, f32[18,128,128]{2,1,0:T(8,128)S(1)} %collective-permute-done.54.pair_ref, ...), custom_call_target="tpu_custom_call" | custom-call | flops 7077888 | bytes 16515072 | tf_op jit(solution)/shard_map/pallas_call | solution.py:534
  358.8 7.4 %shard_map.131 = (f32[2,4,1,18,128,128]{5,4,3,2,1,0:T(8,128)}, f32[2,4,1,18,128,128]{5,4,3,2,1,0:T(8,128)}, f32[2,4,1,18,128,128]{5,4,3,2,1,0:T(8,128)}) custom-call(s32[2,4]{1,0:T(2,128)S(1)} %bitcast.25, f32[18,128,128]{2,1,0:T(8,128)S(1)} %get-tuple-element.113.own_ref, ...), custom_call_target="tpu_custom_call", output_to_operand_aliasing={{0}: (6, {}), {1}: (7, {}), {2}: (8, {})} | custom-call | flops 7077888 | bytes 16515072 | tf_op jit(solution)/shard_map/pallas_call | solution.py:534
  366.2 7.4 %shard_map.132 = (f32[2,4,1,18,128,128]{5,4,3,2,1,0:T(8,128)}, f32[2,4,1,18,128,128]{5,4,3,2,1,0:T(8,128)}, f32[2,4,1,18,128,128]{5,4,3,2,1,0:T(8,128)}) custom-call(s32[2,4]{1,0:T(2,128)S(1)} %bitcast.26, f32[18,128,128]{2,1,0:T(8,128)S(1)} %get-tuple-element.111.own_ref, ...), custom_call_target="tpu_custom_call", output_to_operand_aliasing={{0}: (6, {}), {1}: (7, {}), {2}: (8, {})} | custom-call | flops 7077888 | bytes 16515072 | tf_op jit(solution)/shard_map/pallas_call | solution.py:534
  373.7 7.4 %shard_map.133 = (f32[2,4,1,18,128,128]{5,4,3,2,1,0:T(8,128)}, f32[2,4,1,18,128,128]{5,4,3,2,1,0:T(8,128)}, f32[2,4,1,18,128,128]{5,4,3,2,1,0:T(8,128)}) custom-call(s32[2,4]{1,0:T(2,128)S(1)} %bitcast.27, f32[18,128,128]{2,1,0:T(8,128)S(1)} %get-tuple-element.108.own_ref, ...), custom_call_target="tpu_custom_call", output_to_operand_aliasing={{0}: (6, {}), {1}: (7, {}), {2}: (8, {})} | custom-call | flops 7077888 | bytes 16515072 | tf_op jit(solution)/shard_map/pallas_call | solution.py:534
  (164 shorter events, 90.9 us)
Async XLA Ops:
  14.1 34.0 %collective-permute-start.4 = (bf16[18,128,128]{2,1,0:T(8,128)(2,1)S(1)}, bf16[18,128,128]{2,1,0:T(8,128)(2,1)S(1)}, u32[]{:S(2)}, u32[]{:S(2)}) collective-permute-start(bf16[18,128,128]{2,1,0:T(8,128)(2,1)S(1)} %get-tuple-element.68), channel_id=1, source_target_pairs={{0,1},{1,0},{2,3},{3,2},{4,5},{5,4},{6,7},{7,6},{8,9},{9,8},{10,11... | collective-permute-start | bytes 1769480 | tf_op jit(solution)/shard_map/ppermute | solution.py:372
  16.4 31.8 %collective-permute-start.5 = (bf16[18,128,128]{2,1,0:T(8,128)(2,1)S(1)}, bf16[18,128,128]{2,1,0:T(8,128)(2,1)S(1)}, u32[]{:S(2)}, u32[]{:S(2)}) collective-permute-start(bf16[18,128,128]{2,1,0:T(8,128)(2,1)S(1)} %get-tuple-element.69), channel_id=1, source_target_pairs={{0,2},{1,3},{2,0},{3,1},{4,6},{5,7},{6,4},{7,5},{8,10},{9,11},{10,... | collective-permute-start | bytes 1769480 | tf_op jit(solution)/shard_map/ppermute | solution.py:372
  19.2 31.1 %collective-permute-start.6 = (bf16[18,128,128]{2,1,0:T(8,128)(2,1)S(1)}, bf16[18,128,128]{2,1,0:T(8,128)(2,1)S(1)}, u32[]{:S(2)}, u32[]{:S(2)}) collective-permute-start(bf16[18,128,128]{2,1,0:T(8,128)(2,1)S(1)} %get-tuple-element.70), channel_id=1, source_target_pairs={{0,3},{1,2},{2,1},{3,0},{4,7},{5,6},{6,5},{7,4},{8,11},{9,10},{10,... | collective-permute-start | bytes 1769480 | tf_op jit(solution)/shard_map/ppermute | solution.py:372
  19.9 30.5 %collective-permute-start.3 = (bf16[128,3072]{1,0:T(8,128)(2,1)S(1)}, bf16[128,3072]{1,0:T(8,128)(2,1)S(1)}, u32[]{:S(2)}, u32[]{:S(2)}) collective-permute-start(bf16[128,3072]{1,0:T(8,128)(2,1)S(1)} %constant_dynamic-update-slice_fusion.refs_0_), channel_id=1, source_target_pairs={{0,16},{16,0},{1,17},{17,1},{2,18},{18,2},{3,19},{19,3},{4,20},{20... | collective-permute-start | bytes 2359304 | tf_op jit(solution)/shard_map/ppermute | solution.py:369
  44.3 28.6 %collective-permute-start.18 = (bf16[2,32,3072]{2,1,0:T(8,128)(2,1)S(1)}, bf16[2,32,3072]{2,1,0:T(8,128)(2,1)S(1)}, u32[]{:S(2)}, u32[]{:S(2)}) collective-permute-start(bf16[2,32,3072]{2,1,0:T(8,128)(2,1)S(1)} %pad_maximum_fusion.2.refs_0_), channel_id=1, source_target_pairs={{0,8},{4,12},{8,0},{12,4},{1,9},{5,13},{9,1},{13,5},{2,10},{6,14},... | collective-permute-start | bytes 1179656 | tf_op jit(solution)/shard_map/ppermute | solution.py:366
  48.2 24.7 %collective-permute-start.20 = (bf16[18,128,128]{2,1,0:T(8,128)(2,1)S(1)}, bf16[18,128,128]{2,1,0:T(8,128)(2,1)S(1)}, u32[]{:S(2)}, u32[]{:S(2)}) collective-permute-start(bf16[18,128,128]{2,1,0:T(8,128)(2,1)S(1)} %get-tuple-element.83), channel_id=1, source_target_pairs={{0,1},{1,0},{2,3},{3,2},{4,5},{5,4},{6,7},{7,6},{8,9},{9,8},{10,11... | collective-permute-start | bytes 1769480 | tf_op jit(solution)/shard_map/ppermute | solution.py:372
  48.2 24.7 %collective-permute-start.21 = (bf16[18,128,128]{2,1,0:T(8,128)(2,1)S(1)}, bf16[18,128,128]{2,1,0:T(8,128)(2,1)S(1)}, u32[]{:S(2)}, u32[]{:S(2)}) collective-permute-start(bf16[18,128,128]{2,1,0:T(8,128)(2,1)S(1)} %get-tuple-element.84), channel_id=1, source_target_pairs={{0,2},{1,3},{2,0},{3,1},{4,6},{5,7},{6,4},{7,5},{8,10},{9,11},{10,... | collective-permute-start | bytes 1769480 | tf_op jit(solution)/shard_map/ppermute | solution.py:372
  50.3 26.3 %collective-permute-start.22 = (bf16[18,128,128]{2,1,0:T(8,128)(2,1)S(1)}, bf16[18,128,128]{2,1,0:T(8,128)(2,1)S(1)}, u32[]{:S(2)}, u32[]{:S(2)}) collective-permute-start(bf16[18,128,128]{2,1,0:T(8,128)(2,1)S(1)} %get-tuple-element.85), channel_id=1, source_target_pairs={{0,3},{1,2},{2,1},{3,0},{4,7},{5,6},{6,5},{7,4},{8,11},{9,10},{10,... | collective-permute-start | bytes 1769480 | tf_op jit(solution)/shard_map/ppermute | solution.py:372
  87.7 31.7 %collective-permute-start.34 = (f32[2,32,3072]{2,1,0:T(8,128)S(1)}, f32[2,32,3072]{2,1,0:T(8,128)S(1)}, u32[]{:S(2)}, u32[]{:S(2)}) collective-permute-start(f32[2,32,3072]{2,1,0:T(8,128)S(1)} %get-tuple-element.98), channel_id=1, source_target_pairs={{0,2},{1,3},{2,0},{3,1},{4,6},{5,7},{6,4},{7,5},{8,10},{9,11},{10,... | collective-permute-start | bytes 2359304 | tf_op jit(solution)/shard_map/ppermute | solution.py:372
  90.1 31.8 %collective-permute-start.32 = (f32[2,32,3072]{2,1,0:T(8,128)S(1)}, f32[2,32,3072]{2,1,0:T(8,128)S(1)}, u32[]{:S(2)}, u32[]{:S(2)}) collective-permute-start(f32[2,32,3072]{2,1,0:T(8,128)S(1)} %get-tuple-element.94), channel_id=1, source_target_pairs={{0,16},{16,0},{1,17},{17,1},{2,18},{18,2},{3,19},{19,3},{4,20},{20... | collective-permute-start | bytes 2359304 | tf_op jit(solution)/shard_map/ppermute | solution.py:369
  102.6 27.7 %collective-permute-start.11 = (f32[32,3072]{1,0:T(8,128)S(1)}, f32[32,3072]{1,0:T(8,128)S(1)}, u32[]{:S(2)}, u32[]{:S(2)}) collective-permute-start(f32[32,3072]{1,0:T(8,128)S(1)} %get-tuple-element.80), channel_id=1, source_target_pairs={{0,16},{16,0},{1,17},{17,1},{2,18},{18,2},{3,19},{19,3},{4,20},{20... | collective-permute-start | bytes 1179656 | tf_op jit(solution)/shard_map/ppermute | solution.py:369
  105.1 25.2 %collective-permute-start.9 = (f32[32,3072]{1,0:T(8,128)S(1)}, f32[32,3072]{1,0:T(8,128)S(1)}, u32[]{:S(2)}, u32[]{:S(2)}) collective-permute-start(f32[32,3072]{1,0:T(8,128)S(1)} %get-tuple-element.76), channel_id=1, source_target_pairs={{0,2},{1,3},{2,0},{3,1},{4,6},{5,7},{6,4},{7,5},{8,10},{9,11},{10,... | collective-permute-start | bytes 1179656 | tf_op jit(solution)/shard_map/ppermute | solution.py:372
  130.7 24.9 %collective-permute-start.13 = (bf16[32,6144]{1,0:T(8,128)(2,1)S(1)}, bf16[32,6144]{1,0:T(8,128)(2,1)S(1)}, u32[]{:S(2)}, u32[]{:S(2)}) collective-permute-start(bf16[32,6144]{1,0:T(8,128)(2,1)S(1)} %get-tuple-element.81), channel_id=1, source_target_pairs={{0,16},{1,17},{2,18},{3,19},{16,0},{17,1},{18,2},{19,3},{4,20},{5,... | collective-permute-start | bytes 1179656 | tf_op jit(solution)/shard_map/ppermute | solution.py:380
  132.3 23.4 %collective-permute-start.12 = (bf16[32,6144]{1,0:T(8,128)(2,1)S(1)}, bf16[32,6144]{1,0:T(8,128)(2,1)S(1)}, u32[]{:S(2)}, u32[]{:S(2)}) collective-permute-start(bf16[32,6144]{1,0:T(8,128)(2,1)S(1)} %get-tuple-element.81), channel_id=1, source_target_pairs={{0,2},{1,3},{2,0},{3,1},{16,18},{17,19},{18,16},{19,17},{4,6},{5,7... | collective-permute-start | bytes 1179656 | tf_op jit(solution)/shard_map/ppermute | solution.py:380
  139.3 24.4 %collective-permute-start.38 = (bf16[32,6144]{1,0:T(8,128)(2,1)S(1)}, bf16[32,6144]{1,0:T(8,128)(2,1)S(1)}, u32[]{:S(2)}, u32[]{:S(2)}) collective-permute-start(bf16[32,6144]{1,0:T(8,128)(2,1)S(1)} %shard_map.124), channel_id=1, source_target_pairs={{0,18},{1,19},{2,16},{3,17},{16,2},{17,3},{18,0},{19,1},{4,22},{5,... | collective-permute-start | bytes 1179656 | tf_op jit(solution)/shard_map/ppermute | solution.py:380
  139.4 32.3 %collective-permute-start.37 = (bf16[32,6144]{1,0:T(8,128)(2,1)S(1)}, bf16[32,6144]{1,0:T(8,128)(2,1)S(1)}, u32[]{:S(2)}, u32[]{:S(2)}) collective-permute-start(bf16[32,6144]{1,0:T(8,128)(2,1)S(1)} %shard_map.124), channel_id=1, source_target_pairs={{0,16},{1,17},{2,18},{3,19},{16,0},{17,1},{18,2},{19,3},{4,20},{5,... | collective-permute-start | bytes 1179656 | tf_op jit(solution)/shard_map/ppermute | solution.py:380
  146.8 24.9 %collective-permute-start.36 = (bf16[32,6144]{1,0:T(8,128)(2,1)S(1)}, bf16[32,6144]{1,0:T(8,128)(2,1)S(1)}, u32[]{:S(2)}, u32[]{:S(2)}) collective-permute-start(bf16[32,6144]{1,0:T(8,128)(2,1)S(1)} %shard_map.124), channel_id=1, source_target_pairs={{0,2},{1,3},{2,0},{3,1},{16,18},{17,19},{18,16},{19,17},{4,6},{5,7... | collective-permute-start | bytes 1179656 | tf_op jit(solution)/shard_map/ppermute | solution.py:380
  171.9 81.5 %collective-permute-start.51 = (bf16[256,3072]{1,0:T(8,128)(2,1)}, bf16[256,3072]{1,0:T(8,128)(2,1)}, u32[]{:S(2)}, u32[]{:S(2)}) collective-permute-start(bf16[256,3072]{1,0:T(8,128)(2,1)} %get-tuple-element.110.row_ref), channel_id=1, source_target_pairs={{0,2},{1,3},{2,0},{3,1},{4,6},{5,7},{6,4},{7,5},{8,10},{9,11},{10,... | collective-permute-start | bytes 4718600 | tf_op jit(solution)/shard_map/ppermute | solution.py:372
  172.3 85.5 %collective-permute-start.49 = (bf16[256,3072]{1,0:T(8,128)(2,1)}, bf16[256,3072]{1,0:T(8,128)(2,1)}, u32[]{:S(2)}, u32[]{:S(2)}) collective-permute-start(bf16[256,3072]{1,0:T(8,128)(2,1)} %get-tuple-element.107.row_ref), channel_id=1, source_target_pairs={{0,2},{1,3},{2,0},{3,1},{4,6},{5,7},{6,4},{7,5},{8,10},{9,11},{10,... | collective-permute-start | bytes 4718600 | tf_op jit(solution)/shard_map/ppermute | solution.py:372
  179.8 83.0 %collective-permute-start.23 = (f32[128,1536]{1,0:T(8,128)}, f32[128,1536]{1,0:T(8,128)}, u32[]{:S(2)}, u32[]{:S(2)}) collective-permute-start(f32[128,1536]{1,0:T(8,128)} %get-tuple-element.88), channel_id=1, source_target_pairs={{0,16},{16,0},{1,17},{17,1},{2,18},{18,2},{3,19},{19,3},{4,20},{20... | collective-permute-start | bytes 2359304 | tf_op jit(solution)/shard_map/ppermute | solution.py:369
  179.8 63.0 %collective-permute-start.48 = (s32[2,144]{1,0:T(2,128)S(1)}, s32[2,144]{1,0:T(2,128)S(1)}, u32[]{:S(2)}, u32[]{:S(2)}) collective-permute-start(s32[2,144]{1,0:T(2,128)S(1)} %bitcast.31), channel_id=1, source_target_pairs={{0,2},{1,3},{2,0},{3,1},{4,6},{5,7},{6,4},{7,5},{8,10},{9,11},{10,... | collective-permute-start | bytes 3464 | tf_op jit(solution)/shard_map/ppermute | solution.py:372
  180.5 89.9 %collective-permute-start.27 = (f32[128,1536]{1,0:T(8,128)}, f32[128,1536]{1,0:T(8,128)}, u32[]{:S(2)}, u32[]{:S(2)}) collective-permute-start(f32[128,1536]{1,0:T(8,128)} %get-tuple-element.90), channel_id=1, source_target_pairs={{0,16},{16,0},{1,17},{17,1},{2,18},{18,2},{3,19},{19,3},{4,20},{20... | collective-permute-start | bytes 2359304 | tf_op jit(solution)/shard_map/ppermute | solution.py:369
  242.8 28.9 %collective-permute-start.40 = (f32[128,1536]{1,0:T(8,128)}, f32[128,1536]{1,0:T(8,128)}, u32[]{:S(2)}, u32[]{:S(2)}) collective-permute-start(f32[128,1536]{1,0:T(8,128)} %get-tuple-element.104), channel_id=1, source_target_pairs={{0,16},{16,0},{1,17},{17,1},{2,18},{18,2},{3,19},{19,3},{4,20},{20... | collective-permute-start | bytes 2359304 | tf_op jit(solution)/shard_map/ppermute | solution.py:369
  253.5 30.2 %collective-permute-start.44 = (f32[128,1536]{1,0:T(8,128)S(1)}, f32[128,1536]{1,0:T(8,128)S(1)}, u32[]{:S(2)}, u32[]{:S(2)}) collective-permute-start(f32[128,1536]{1,0:T(8,128)S(1)} %copy-done.17), channel_id=1, source_target_pairs={{0,16},{16,0},{1,17},{17,1},{2,18},{18,2},{3,19},{19,3},{4,20},{20... | collective-permute-start | bytes 2359304 | tf_op jit(solution)/shard_map/ppermute | solution.py:369
  257.8 108.4 %collective-permute-start.52 = (f32[18,128,128]{2,1,0:T(8,128)S(1)}, f32[18,128,128]{2,1,0:T(8,128)S(1)}, u32[]{:S(2)}, u32[]{:S(2)}) collective-permute-start(f32[18,128,128]{2,1,0:T(8,128)S(1)} %get-tuple-element.112), channel_id=1, source_target_pairs={{0,1},{1,0},{2,3},{3,2},{4,5},{5,4},{6,7},{7,6},{8,9},{9,8},{10,11... | collective-permute-start | bytes 3538952 | tf_op jit(solution)/shard_map/ppermute | solution.py:372
  271.7 25.7 %collective-permute-start.25 = (f32[32,1536]{1,0:T(8,128)S(1)}, f32[32,1536]{1,0:T(8,128)S(1)}, u32[]{:S(2)}, u32[]{:S(2)}) collective-permute-start(f32[32,1536]{1,0:T(8,128)S(1)} %get-tuple-element.137), channel_id=1, source_target_pairs={{0,8},{4,12},{8,0},{12,4},{1,9},{5,13},{9,1},{13,5},{2,10},{6,14},... | collective-permute-start | bytes 589832 | tf_op jit(solution)/shard_map/ppermute | solution.py:366
  284.9 25.7 %collective-permute-start.30 = (f32[32,1536]{1,0:T(8,128)S(1)}, f32[32,1536]{1,0:T(8,128)S(1)}, u32[]{:S(2)}, u32[]{:S(2)}) collective-permute-start(f32[32,1536]{1,0:T(8,128)S(1)} %get-tuple-element.139), channel_id=1, source_target_pairs={{0,4},{4,8},{8,12},{12,0},{1,5},{5,9},{9,13},{13,1},{2,6},{6,10},{... | collective-permute-start | bytes 589832 | tf_op jit(solution)/shard_map/ppermute | solution.py:366
  290.5 32.1 %collective-permute-start.29 = (f32[32,1536]{1,0:T(8,128)S(1)}, f32[32,1536]{1,0:T(8,128)S(1)}, u32[]{:S(2)}, u32[]{:S(2)}) collective-permute-start(f32[32,1536]{1,0:T(8,128)S(1)} %get-tuple-element.140), channel_id=1, source_target_pairs={{0,8},{4,12},{8,0},{12,4},{1,9},{5,13},{9,1},{13,5},{2,10},{6,14},... | collective-permute-start | bytes 589832 | tf_op jit(solution)/shard_map/ppermute | solution.py:366
  297.4 25.3 %collective-permute-start.41 = (f32[32,1536]{1,0:T(8,128)S(1)}, f32[32,1536]{1,0:T(8,128)S(1)}, u32[]{:S(2)}, u32[]{:S(2)}) collective-permute-start(f32[32,1536]{1,0:T(8,128)S(1)} %get-tuple-element.129), channel_id=1, source_target_pairs={{0,12},{4,0},{8,4},{12,8},{1,13},{5,1},{9,5},{13,9},{2,14},{6,2},{... | collective-permute-start | bytes 589832 | tf_op jit(solution)/shard_map/ppermute | solution.py:366
  322.7 28.6 %collective-permute-start.54 = (f32[18,128,128]{2,1,0:T(8,128)S(1)}, f32[18,128,128]{2,1,0:T(8,128)S(1)}, u32[]{:S(2)}, u32[]{:S(2)}) collective-permute-start(f32[18,128,128]{2,1,0:T(8,128)S(1)} %get-tuple-element.116), channel_id=1, source_target_pairs={{0,1},{1,0},{2,3},{3,2},{4,5},{5,4},{6,7},{7,6},{8,9},{9,8},{10,11... | collective-permute-start | bytes 3538952 | tf_op jit(solution)/shard_map/ppermute | solution.py:372
  322.8 36.0 %collective-permute-start.53 = (f32[18,128,128]{2,1,0:T(8,128)S(1)}, f32[18,128,128]{2,1,0:T(8,128)S(1)}, u32[]{:S(2)}, u32[]{:S(2)}) collective-permute-start(f32[18,128,128]{2,1,0:T(8,128)S(1)} %get-tuple-element.114), channel_id=1, source_target_pairs={{0,1},{1,0},{2,3},{3,2},{4,5},{5,4},{6,7},{7,6},{8,9},{9,8},{10,11... | collective-permute-start | bytes 3538952 | tf_op jit(solution)/shard_map/ppermute | solution.py:372
  331.1 42.6 %collective-permute-start.50 = (f32[18,128,128]{2,1,0:T(8,128)S(1)}, f32[18,128,128]{2,1,0:T(8,128)S(1)}, u32[]{:S(2)}, u32[]{:S(2)}) collective-permute-start(f32[18,128,128]{2,1,0:T(8,128)S(1)} %get-tuple-element.109), channel_id=1, source_target_pairs={{0,1},{1,0},{2,3},{3,2},{4,5},{5,4},{6,7},{7,6},{8,9},{9,8},{10,11... | collective-permute-start | bytes 3538952 | tf_op jit(solution)/shard_map/ppermute | solution.py:372
  (43 other events, 622.1 us)

commit v9 on v8

--- a/solution.py
+++ b/solution.py
@@ -40,13 +40,11 @@
 
 def adam_step(weight, moment, variance, gradient):
     new_moment = BETA_FIRST * moment + (1.0 - BETA_FIRST) * gradient
-    new_variance = BETA_SECOND * variance + (1.0 - BETA_SECOND) * gradient * gradient
-    scaled = (
-        new_moment
-        / (1.0 - BETA_FIRST**STEP)
-        / (jnp.sqrt(new_variance / (1.0 - BETA_SECOND**STEP)) + ADAM_EPSILON)
-    )
-    new_weight = weight - LEARN_RATE * (scaled + WEIGHT_DECAY * weight)
+    new_variance = BETA_SECOND * variance + (1.0 - BETA_SECOND) * (gradient * gradient)
+    scaled = new_variance * (1.0 / (1.0 - BETA_SECOND**STEP))
+    root = scaled * lax.rsqrt(scaled)
+    step = new_moment * (LEARN_RATE / (1.0 - BETA_FIRST**STEP)) / (root + ADAM_EPSILON)
+    new_weight = weight * (1.0 - LEARN_RATE * WEIGHT_DECAY) - step
     return new_weight, new_moment, new_variance
 
 
@@ -421,7 +419,7 @@
         flops = 2 * mem_count * rows * local_slots * block_size * block_size
         return call(kernel, outs, scalars, row_groups, flops, weights)
 
-    mem_span = hidden_span // 2
+    mem_span = hidden_span * 5 // 8
 
     def side_columns(kernel, outs, arrays, side, steps=3):
         whole = hidden_span - mem_span if side else mem_span
@@ -491,22 +489,40 @@
     turn = relative(tok_count)
     step = inputs.shape[0]
 
-    def reduce_rows(found):
+    def spot_of(k):
+        start = k * step
+        return ((start // part) ^ turn) * part + start % part
+
+    def mem_first(groups):
+        total = groups[0]
+        for j in range(1, mem_count):
+            total = total + shift_mem(groups[j], -j)
+        result = lax.dynamic_slice_in_dim(total, spot_of(0), step, 0)
+        for k in range(1, hid_count):
+            piece = lax.dynamic_slice_in_dim(total, spot_of(k), step, 0)
+            result = result + shift_hid(piece, -k)
+        return result.astype(bf16)
+
+    def hid_first(groups):
+        def rows_of(k):
+            return jnp.stack([lax.dynamic_slice_in_dim(g, spot_of(k), step, 0) for g in groups])
+
+        total = rows_of(0)
+        for k in range(1, hid_count):
+            total = total + shift_hid(rows_of(k), -k)
+        result = total[0]
+        for j in range(1, mem_count):
+            result = result + shift_mem(total[j], -j)
+        return result.astype(bf16)
+
+    def reduce_rows(found, hid_chunks=0):
         results = []
         for chunk in range(chunks):
             groups = found[chunk * mem_count : (chunk + 1) * mem_count]
-            total = groups[0]
-            for j in range(1, mem_count):
-                total = total + shift_mem(groups[j], -j)
-            result = None
-            for k in range(hid_count):
-                start = k * step
-                spot = ((start // part) ^ turn) * part + start % part
-                piece = lax.dynamic_slice_in_dim(total, spot, step, 0)
-                if k:
-                    piece = shift_hid(piece, -k)
-                result = piece if result is None else result + piece
-            results.append(result.astype(bf16))
+            if chunk < chunks - hid_chunks:
+                results.append(mem_first(groups))
+            else:
+                results.append(hid_first(groups))
         return jnp.concatenate(results, axis=1)
 
     def gradient(matrix, cell, ids, row_values, near, far):
@@ -562,7 +578,7 @@
     arrays = [*back_terms[0], *back_terms[1], preact]
     (grad_piece,) = call(kernel, outs[:1], (), arrays, part)
     pre_grad = gather_plane(grad_piece)
-    layer_out = reduce_rows(backward(1, False, *hidden, weights_second))
+    layer_out = reduce_rows(backward(1, False, *hidden, weights_second), 1)
     grad_in = reduce_rows(backward(0, True, *pre_grad, weights_first))
     far_grad_rows = flip_tok(grad_rows, 2)
     far_token_rows = flip_tok(token_rows, 2)

time: 382 us -> 405 us (1.060)
  waiting for transfers between devices: 205 us -> 253 us
  Pallas kernels: 75.5 us -> 66.3 us
  starting transfers between devices: 82.5 us -> 74.5 us
  local copies, waits for them, and re-layouts: 11.1 us -> 5.97 us
    ppermute x10, waiting for transfers between devices: 17.5 us -> 78 us  [shift_mem(): lax.ppermute(array, MEM, [(i, (i + shift) % mem_count) for i in range(mem...]
    ppermute x21, waiting for transfers between devices: 82.8 us -> 42.7 us  [flip_tok(): return lax.ppermute(array, TOK, [(i, i ^ bit) for i in range(tok_count)])]
    ppermute x18, waiting for transfers between devices: 76.1 us -> 105 us  [shift_hid(): lax.ppermute(array, HID, [(i, (i + shift) % hid_count) for i in range(hid...]
    ppermute x18, starting transfers between devices: 57.9 us -> 46.8 us  [shift_hid(): lax.ppermute(array, HID, [(i, (i + shift) % hid_count) for i in range(hid...]
    pallas_call x14, Pallas kernels: 42.9 us -> 34.7 us  [call(): pl.pallas_call(kernel, out_shape=outs, in_specs=[SCALARS] * len(scalars)...]
    unnamed x44 -> x30, local copies, waits for them, and re-layouts: 10.9 us -> 5.66 us
    ppermute x21, starting transfers between devices: 11.7 us -> 16.6 us  [flip_tok(): return lax.ppermute(array, TOK, [(i, i ^ bit) for i in range(tok_count)])]
  transfers between devices with their start and end apart: 55 -> 55, of which waited for: 25 -> 26; matrix products, arithmetic and copies ran while one was open for 2% -> 1% of each run, Pallas kernels for 18% -> 15%
where the time goes in v9:
time: 405 us
  waiting for transfers between devices  253 us (62%)
  starting transfers between devices  74.5 us (18%)
  Pallas kernels  66.3 us (16%)
  local copies, waits for them, and re-layouts  5.97 us (1%)
    ppermute x18, waiting for transfers between devices, shift_hid(): lax.ppermute(array, HID, [(i, (i + shift) % hid_count) for i in range(hid...  105 us
    ppermute x10, waiting for transfers between devices, shift_mem(): lax.ppermute(array, MEM, [(i, (i + shift) % mem_count) for i in range(mem...  78 us
    ppermute x18, starting transfers between devices, shift_hid(): lax.ppermute(array, HID, [(i, (i + shift) % hid_count) for i in range(hid...  46.8 us
    ppermute x21, waiting for transfers between devices, flip_tok(): return lax.ppermute(array, TOK, [(i, i ^ bit) for i in range(tok_count)])  42.7 us
    pallas_call x14, Pallas kernels, call(): pl.pallas_call(kernel, out_shape=outs, in_specs=[SCALARS] * len(scalars)...  34.7 us
    pallas_call x4, Pallas kernels, update(): pl.pallas_call(functools.partial(update_kernel, matrix, cell, owned_slots...  28.2 us
    ppermute x6, waiting for transfers between devices, across(): return lax.ppermute(array, (MEM, TOK), table)  27 us
    ppermute x21, starting transfers between devices, flip_tok(): return lax.ppermute(array, TOK, [(i, i ^ bit) for i in range(tok_count)])  16.6 us
  transfers between devices with their start and end apart: 55, of which 26 were waited for; matrix products, arithmetic and copies ran while one was open for 1% of the time, Pallas kernels for 15%

profile of v9, /device:TPU:0, one launch (start us, length us, event | category | flops | bytes accessed | tf_op | source)
XLA Modules:
  0.0 404.5 jit_solution(8486452757895454250)
XLA Ops:
  9.6 6.8 %collective-permute-done = bf16[32,3072]{1,0:T(8,128)(2,1)S(1)} collective-permute-done((bf16[32,3072]{1,0:T(8,128)(2,1)}, bf16[32,3072]{1,0:T(8,128)(2,1)S(1)}, u32[]{:S(2)}, u32[]{:S(2)}) %collective-permute-start) | collective-permute-done | bytes 196640 | tf_op jit(solution)/shard_map/ppermute | solution.py:364
  28.0 13.4 %collective-permute-done.16 = bf16[32,3072]{1,0:T(8,128)(2,1)S(1)} collective-permute-done((bf16[32,3072]{1,0:T(8,128)(2,1)}, bf16[32,3072]{1,0:T(8,128)(2,1)S(1)}, u32[]{:S(2)}, u32[]{:S(2)}) %collective-permute-start.16) | collective-permute-done | bytes 196640 | tf_op jit(solution)/shard_map/ppermute | solution.py:367
  44.8 9.2 %collective-permute-done.6.refs_5_ = bf16[18,128,128]{2,1,0:T(8,128)(2,1)S(1)} collective-permute-done((bf16[18,128,128]{2,1,0:T(8,128)(2,1)S(1)}, bf16[18,128,128]{2,1,0:T(8,128)(2,1)S(1)}, u32[]{:S(2)}, u32[]{:S(2)}) %collective-permute-start.6) | collective-permute-done | bytes 589856 | tf_op jit(solution)/shard_map/ppermute | solution.py:370
  54.0 6.3 %shard_map.111 = (bf16[256,3072]{1,0:T(8,128)(2,1)S(1)}, f32[2,64,6144]{2,1,0:T(8,128)S(1)}, f32[2,64,6144]{2,1,0:T(8,128)S(1)}, bf16[4,18,128,128]{3,2,1,0:T(8,128)(2,1)S(1)}) custom-call(s32[2,4]{1,0:T(2,128)S(1)} %bitcast.40, s32[2,144]{1,0:T(2,128)S(1)} %bitcast.52, bf16[128,3072]{1,0:T(8,128)(2,1)S(1)} %constant_dynamic-update-slice_fusion.refs_0_, ...), custom_call_target="tpu_custom_call" | custom-call | flops 603979776 | bytes 11796480 | tf_op jit(solution)/shard_map/pallas_call | solution.py:325
  60.4 6.0 %collective-permute-start.18 = (bf16[2,32,3072]{2,1,0:T(8,128)(2,1)S(1)}, bf16[2,32,3072]{2,1,0:T(8,128)(2,1)S(1)}, u32[]{:S(2)}, u32[]{:S(2)}) collective-permute-start(bf16[2,32,3072]{2,1,0:T(8,128)(2,1)S(1)} %pad_maximum_fusion.2.refs_0_), channel_id=1, source_target_pairs={{0,8},{4,12},{8,0},{12,4},{1,9},{5,13},{9,1},{13,5},{2,10},{6,14},... | collective-permute-start | bytes 1179656 | tf_op jit(solution)/shard_map/ppermute | solution.py:364
  68.8 15.8 %collective-permute-done.18.refs_2_ = bf16[2,32,3072]{2,1,0:T(8,128)(2,1)S(1)} collective-permute-done((bf16[2,32,3072]{2,1,0:T(8,128)(2,1)S(1)}, bf16[2,32,3072]{2,1,0:T(8,128)(2,1)S(1)}, u32[]{:S(2)}, u32[]{:S(2)}) %collective-permute-start.18) | collective-permute-done | bytes 393248 | tf_op jit(solution)/shard_map/ppermute | solution.py:364
  84.5 12.7 %collective-permute-done.17.refs_1_ = bf16[2,32,3072]{2,1,0:T(8,128)(2,1)S(1)} collective-permute-done((bf16[2,32,3072]{2,1,0:T(8,128)(2,1)S(1)}, bf16[2,32,3072]{2,1,0:T(8,128)(2,1)S(1)}, u32[]{:S(2)}, u32[]{:S(2)}) %collective-permute-start.17) | collective-permute-done | bytes 393248 | tf_op jit(solution)/shard_map/ppermute | solution.py:364
  108.0 19.4 %collective-permute-done.8.refs_1_ = f32[2,32,3840]{2,1,0:T(8,128)S(1)} collective-permute-done((f32[2,32,3840]{2,1,0:T(8,128)S(1)}, f32[2,32,3840]{2,1,0:T(8,128)S(1)}, u32[]{:S(2)}, u32[]{:S(2)}) %collective-permute-start.8) | collective-permute-done | bytes 983072 | tf_op jit(solution)/shard_map/ppermute | solution.py:367
  129.4 24.0 %collective-permute-done.11.refs_3_ = f32[32,2304]{1,0:T(8,128)S(1)} collective-permute-done((f32[32,2304]{1,0:T(8,128)S(1)}, f32[32,2304]{1,0:T(8,128)S(1)}, u32[]{:S(2)}, u32[]{:S(2)}) %collective-permute-start.11) | collective-permute-done | bytes 294944 | tf_op jit(solution)/shard_map/ppermute | solution.py:367
  160.0 6.7 %collective-permute-done.14 = bf16[32,6144]{1,0:T(8,128)(2,1)S(1)} collective-permute-done((bf16[32,6144]{1,0:T(8,128)(2,1)S(1)}, bf16[32,6144]{1,0:T(8,128)(2,1)S(1)}, u32[]{:S(2)}, u32[]{:S(2)}) %collective-permute-start.14) | collective-permute-done | bytes 393248 | tf_op jit(solution)/shard_map/ppermute | solution.py:378
  166.7 6.5 %collective-permute-done.13 = bf16[32,6144]{1,0:T(8,128)(2,1)S(1)} collective-permute-done((bf16[32,6144]{1,0:T(8,128)(2,1)S(1)}, bf16[32,6144]{1,0:T(8,128)(2,1)S(1)}, u32[]{:S(2)}, u32[]{:S(2)}) %collective-permute-start.13) | collective-permute-done | bytes 393248 | tf_op jit(solution)/shard_map/ppermute | solution.py:378
  173.5 12.2 %collective-permute-done.34.refs_1_ = f32[2,32,2304]{2,1,0:T(8,128)S(1)} collective-permute-done((f32[2,32,2304]{2,1,0:T(8,128)S(1)}, f32[2,32,2304]{2,1,0:T(8,128)S(1)}, u32[]{:S(2)}, u32[]{:S(2)}) %collective-permute-start.34) | collective-permute-done | bytes 589856 | tf_op jit(solution)/shard_map/ppermute | solution.py:370
  186.3 8.3 %collective-permute-done.35.refs_3_ = f32[32,2304]{1,0:T(8,128)S(1)} collective-permute-done((f32[32,2304]{1,0:T(8,128)S(1)}, f32[32,2304]{1,0:T(8,128)S(1)}, u32[]{:S(2)}, u32[]{:S(2)}) %collective-permute-start.35) | collective-permute-done | bytes 294944 | tf_op jit(solution)/shard_map/ppermute | solution.py:367
  201.9 7.8 %collective-permute-done.38 = bf16[32,6144]{1,0:T(8,128)(2,1)} collective-permute-done((bf16[32,6144]{1,0:T(8,128)(2,1)S(1)}, bf16[32,6144]{1,0:T(8,128)(2,1)}, u32[]{:S(2)}, u32[]{:S(2)}) %collective-permute-start.38) | collective-permute-done | bytes 393248 | tf_op jit(solution)/shard_map/ppermute | solution.py:378
  211.5 6.0 %collective-permute-done.37 = bf16[32,6144]{1,0:T(8,128)(2,1)} collective-permute-done((bf16[32,6144]{1,0:T(8,128)(2,1)S(1)}, bf16[32,6144]{1,0:T(8,128)(2,1)}, u32[]{:S(2)}, u32[]{:S(2)}) %collective-permute-start.37) | collective-permute-done | bytes 393248 | tf_op jit(solution)/shard_map/ppermute | solution.py:378
  222.0 6.8 %collective-permute-start.27 = (f32[2,32,1536]{2,1,0:T(8,128)S(1)}, f32[2,32,1536]{2,1,0:T(8,128)S(1)}, u32[]{:S(2)}, u32[]{:S(2)}) collective-permute-start(f32[2,32,1536]{2,1,0:T(8,128)S(1)} %pad_maximum_fusion.3), channel_id=1, source_target_pairs={{0,12},{4,0},{8,4},{12,8},{1,13},{5,1},{9,5},{13,9},{2,14},{6,2},{... | collective-permute-start | bytes 1179656 | tf_op jit(solution)/shard_map/ppermute | solution.py:364
  228.9 9.4 %collective-permute-done.27 = f32[2,32,1536]{2,1,0:T(8,128)S(1)} collective-permute-done((f32[2,32,1536]{2,1,0:T(8,128)S(1)}, f32[2,32,1536]{2,1,0:T(8,128)S(1)}, u32[]{:S(2)}, u32[]{:S(2)}) %collective-permute-start.27) | collective-permute-done | bytes 393248 | tf_op jit(solution)/shard_map/ppermute | solution.py:364
  238.4 24.7 %collective-permute-done.28 = f32[2,32,1536]{2,1,0:T(8,128)S(1)} collective-permute-done((f32[2,32,1536]{2,1,0:T(8,128)S(1)}, f32[2,32,1536]{2,1,0:T(8,128)S(1)}, u32[]{:S(2)}, u32[]{:S(2)}) %collective-permute-start.28) | collective-permute-done | bytes 393248 | tf_op jit(solution)/shard_map/ppermute | solution.py:364
  266.2 18.3 %collective-permute-done.48.place_ref = s32[2,144]{1,0:T(2,128)S(1)} collective-permute-done((s32[2,144]{1,0:T(2,128)S(1)}, s32[2,144]{1,0:T(2,128)S(1)}, u32[]{:S(2)}, u32[]{:S(2)}) %collective-permute-start.48) | collective-permute-done | bytes 1184 | tf_op jit(solution)/shard_map/ppermute | solution.py:370
  288.6 6.4 %shard_map.125 = (f32[128,1536]{1,0:T(8,128)S(1)}, f32[128,1536]{1,0:T(8,128)S(1)}, f32[128,1536]{1,0:T(8,128)S(1)}, f32[128,1536]{1,0:T(8,128)S(1)}) custom-call(s32[2,4]{1,0:T(2,128)S(1)} %bitcast.44, s32[2,144]{1,0:T(2,128)S(1)} %bitcast.56, bf16[2,64,6144]{2,1,0:T(8,128)(2,1)S(1)} %bitcast.37, bf16[2,64,6144]{2,1,0:T(8,128)(2,1)S(1)} %collective-permute-done.39.pair_ref, ...), custom_call_target="tpu_custom_call" | custom-call | flops 603979776 | bytes 8650752 | tf_op jit(solution)/shard_map/pallas_call | solution.py:325
  310.4 5.1 %collective-permute-done.40 = f32[128,1536]{1,0:T(8,128)S(1)} collective-permute-done((f32[128,1536]{1,0:T(8,128)S(1)}, f32[128,1536]{1,0:T(8,128)S(1)}, u32[]{:S(2)}, u32[]{:S(2)}) %collective-permute-start.40) | collective-permute-done | bytes 786464 | tf_op jit(solution)/shard_map/ppermute | solution.py:367
  315.5 5.4 %collective-permute-start.25 = (f32[32,1536]{1,0:T(8,128)S(1)}, f32[32,1536]{1,0:T(8,128)S(1)}, u32[]{:S(2)}, u32[]{:S(2)}) collective-permute-start(f32[32,1536]{1,0:T(8,128)S(1)} %get-tuple-element.137), channel_id=1, source_target_pairs={{0,8},{4,12},{8,0},{12,4},{1,9},{5,13},{9,1},{13,5},{2,10},{6,14},... | collective-permute-start | bytes 589832 | tf_op jit(solution)/shard_map/ppermute | solution.py:364
  321.0 7.8 %collective-permute-done.44 = f32[128,1536]{1,0:T(8,128)S(1)} collective-permute-done((f32[128,1536]{1,0:T(8,128)S(1)}, f32[128,1536]{1,0:T(8,128)S(1)}, u32[]{:S(2)}, u32[]{:S(2)}) %collective-permute-start.44) | collective-permute-done | bytes 786464 | tf_op jit(solution)/shard_map/ppermute | solution.py:367
  328.8 4.3 %collective-permute-start.41 = (f32[32,1536]{1,0:T(8,128)S(1)}, f32[32,1536]{1,0:T(8,128)S(1)}, u32[]{:S(2)}, u32[]{:S(2)}) collective-permute-start(f32[32,1536]{1,0:T(8,128)S(1)} %get-tuple-element.129), channel_id=1, source_target_pairs={{0,12},{4,0},{8,4},{12,8},{1,13},{5,1},{9,5},{13,9},{2,14},{6,2},{... | collective-permute-start | bytes 589832 | tf_op jit(solution)/shard_map/ppermute | solution.py:364
  339.3 8.1 %collective-permute-done.43 = f32[32,1536]{1,0:T(8,128)S(1)} collective-permute-done((f32[32,1536]{1,0:T(8,128)S(1)}, f32[32,1536]{1,0:T(8,128)S(1)}, u32[]{:S(2)}, u32[]{:S(2)}) %collective-permute-start.43) | collective-permute-done | bytes 196640 | tf_op jit(solution)/shard_map/ppermute | solution.py:364
  347.5 6.6 %collective-permute-done.42 = f32[32,1536]{1,0:T(8,128)S(1)} collective-permute-done((f32[32,1536]{1,0:T(8,128)S(1)}, f32[32,1536]{1,0:T(8,128)S(1)}, u32[]{:S(2)}, u32[]{:S(2)}) %collective-permute-start.42) | collective-permute-done | bytes 196640 | tf_op jit(solution)/shard_map/ppermute | solution.py:364
  357.1 7.7 %collective-permute-done.47 = f32[32,1536]{1,0:T(8,128)S(1)} collective-permute-done((f32[32,1536]{1,0:T(8,128)S(1)}, f32[32,1536]{1,0:T(8,128)S(1)}, u32[]{:S(2)}, u32[]{:S(2)}) %collective-permute-start.47) | collective-permute-done | bytes 196640 | tf_op jit(solution)/shard_map/ppermute | solution.py:364
  365.6 10.0 %collective-permute-done.46 = f32[32,1536]{1,0:T(8,128)S(1)} collective-permute-done((f32[32,1536]{1,0:T(8,128)S(1)}, f32[32,1536]{1,0:T(8,128)S(1)}, u32[]{:S(2)}, u32[]{:S(2)}) %collective-permute-start.46) | collective-permute-done | bytes 196640 | tf_op jit(solution)/shard_map/ppermute | solution.py:364
  376.3 7.1 %shard_map.130 = (f32[2,4,1,18,128,128]{5,4,3,2,1,0:T(8,128)}, f32[2,4,1,18,128,128]{5,4,3,2,1,0:T(8,128)}, f32[2,4,1,18,128,128]{5,4,3,2,1,0:T(8,128)}) custom-call(s32[2,4]{1,0:T(2,128)S(1)} %bitcast.48, f32[18,128,128]{2,1,0:T(8,128)S(1)} %get-tuple-element.115.own_ref, f32[18,128,128]{2,1,0:T(8,128)S(1)} %collective-permute-done.54.pair_ref, ...), custom_call_target="tpu_custom_call" | custom-call | flops 7077888 | bytes 16515072 | tf_op jit(solution)/shard_map/pallas_call | solution.py:550
  383.3 7.1 %shard_map.131 = (f32[2,4,1,18,128,128]{5,4,3,2,1,0:T(8,128)}, f32[2,4,1,18,128,128]{5,4,3,2,1,0:T(8,128)}, f32[2,4,1,18,128,128]{5,4,3,2,1,0:T(8,128)}) custom-call(s32[2,4]{1,0:T(2,128)S(1)} %bitcast.49, f32[18,128,128]{2,1,0:T(8,128)S(1)} %get-tuple-element.113.own_ref, ...), custom_call_target="tpu_custom_call", output_to_operand_aliasing={{0}: (6, {}), {1}: (7, {}), {2}: (8, {})} | custom-call | flops 7077888 | bytes 16515072 | tf_op jit(solution)/shard_map/pallas_call | solution.py:550
  390.4 7.1 %shard_map.132 = (f32[2,4,1,18,128,128]{5,4,3,2,1,0:T(8,128)}, f32[2,4,1,18,128,128]{5,4,3,2,1,0:T(8,128)}, f32[2,4,1,18,128,128]{5,4,3,2,1,0:T(8,128)}) custom-call(s32[2,4]{1,0:T(2,128)S(1)} %bitcast.50, f32[18,128,128]{2,1,0:T(8,128)S(1)} %get-tuple-element.111.own_ref, ...), custom_call_target="tpu_custom_call", output_to_operand_aliasing={{0}: (6, {}), {1}: (7, {}), {2}: (8, {})} | custom-call | flops 7077888 | bytes 16515072 | tf_op jit(solution)/shard_map/pallas_call | solution.py:550
  397.5 7.1 %shard_map.133 = (f32[2,4,1,18,128,128]{5,4,3,2,1,0:T(8,128)}, f32[2,4,1,18,128,128]{5,4,3,2,1,0:T(8,128)}, f32[2,4,1,18,128,128]{5,4,3,2,1,0:T(8,128)}) custom-call(s32[2,4]{1,0:T(2,128)S(1)} %bitcast.51, f32[18,128,128]{2,1,0:T(8,128)S(1)} %get-tuple-element.108.own_ref, ...), custom_call_target="tpu_custom_call", output_to_operand_aliasing={{0}: (6, {}), {1}: (7, {}), {2}: (8, {})} | custom-call | flops 7077888 | bytes 16515072 | tf_op jit(solution)/shard_map/pallas_call | solution.py:550
  (154 shorter events, 93.5 us)
Async XLA Ops:
  19.9 34.0 %collective-permute-start.3 = (bf16[128,3072]{1,0:T(8,128)(2,1)S(1)}, bf16[128,3072]{1,0:T(8,128)(2,1)S(1)}, u32[]{:S(2)}, u32[]{:S(2)}) collective-permute-start(bf16[128,3072]{1,0:T(8,128)(2,1)S(1)} %constant_dynamic-update-slice_fusion.refs_0_), channel_id=1, source_target_pairs={{0,16},{16,0},{1,17},{17,1},{2,18},{18,2},{3,19},{19,3},{4,20},{20... | collective-permute-start | bytes 2359304 | tf_op jit(solution)/shard_map/ppermute | solution.py:367
  27.8 26.2 %collective-permute-start.6 = (bf16[18,128,128]{2,1,0:T(8,128)(2,1)S(1)}, bf16[18,128,128]{2,1,0:T(8,128)(2,1)S(1)}, u32[]{:S(2)}, u32[]{:S(2)}) collective-permute-start(bf16[18,128,128]{2,1,0:T(8,128)(2,1)S(1)} %get-tuple-element.70), channel_id=1, source_target_pairs={{0,3},{1,2},{2,1},{3,0},{4,7},{5,6},{6,5},{7,4},{8,11},{9,10},{10,... | collective-permute-start | bytes 1769480 | tf_op jit(solution)/shard_map/ppermute | solution.py:370
  41.5 27.3 %collective-permute-start.19 = (bf16[2,32,3072]{2,1,0:T(8,128)(2,1)S(1)}, bf16[2,32,3072]{2,1,0:T(8,128)(2,1)S(1)}, u32[]{:S(2)}, u32[]{:S(2)}) collective-permute-start(bf16[2,32,3072]{2,1,0:T(8,128)(2,1)S(1)} %pad_maximum_fusion.2.refs_0_), channel_id=1, source_target_pairs={{0,12},{4,0},{8,4},{12,8},{1,13},{5,1},{9,5},{13,9},{2,14},{6,2},{... | collective-permute-start | bytes 1179656 | tf_op jit(solution)/shard_map/ppermute | solution.py:364
  60.3 40.6 %collective-permute-start.7 = (f32[2,64,6144]{2,1,0:T(8,128)S(1)}, f32[2,64,6144]{2,1,0:T(8,128)S(1)}, u32[]{:S(2)}, u32[]{:S(2)}) collective-permute-start(f32[2,64,6144]{2,1,0:T(8,128)S(1)} %get-tuple-element.72), channel_id=1, source_target_pairs={{0,1},{1,0},{2,3},{3,2},{4,5},{5,4},{6,7},{7,6},{8,9},{9,8},{10,11... | collective-permute-start | bytes 9437192 | tf_op jit(solution)/shard_map/ppermute | solution.py:370
  60.4 24.1 %collective-permute-start.18 = (bf16[2,32,3072]{2,1,0:T(8,128)(2,1)S(1)}, bf16[2,32,3072]{2,1,0:T(8,128)(2,1)S(1)}, u32[]{:S(2)}, u32[]{:S(2)}) collective-permute-start(bf16[2,32,3072]{2,1,0:T(8,128)(2,1)S(1)} %pad_maximum_fusion.2.refs_0_), channel_id=1, source_target_pairs={{0,8},{4,12},{8,0},{12,4},{1,9},{5,13},{9,1},{13,5},{2,10},{6,14},... | collective-permute-start | bytes 1179656 | tf_op jit(solution)/shard_map/ppermute | solution.py:364
  66.8 30.4 %collective-permute-start.20 = (bf16[18,128,128]{2,1,0:T(8,128)(2,1)S(1)}, bf16[18,128,128]{2,1,0:T(8,128)(2,1)S(1)}, u32[]{:S(2)}, u32[]{:S(2)}) collective-permute-start(bf16[18,128,128]{2,1,0:T(8,128)(2,1)S(1)} %get-tuple-element.83), channel_id=1, source_target_pairs={{0,1},{1,0},{2,3},{3,2},{4,5},{5,4},{6,7},{7,6},{8,9},{9,8},{10,11... | collective-permute-start | bytes 1769480 | tf_op jit(solution)/shard_map/ppermute | solution.py:370
  67.0 30.2 %collective-permute-start.21 = (bf16[18,128,128]{2,1,0:T(8,128)(2,1)S(1)}, bf16[18,128,128]{2,1,0:T(8,128)(2,1)S(1)}, u32[]{:S(2)}, u32[]{:S(2)}) collective-permute-start(bf16[18,128,128]{2,1,0:T(8,128)(2,1)S(1)} %get-tuple-element.84), channel_id=1, source_target_pairs={{0,2},{1,3},{2,0},{3,1},{4,6},{5,7},{6,4},{7,5},{8,10},{9,11},{10,... | collective-permute-start | bytes 1769480 | tf_op jit(solution)/shard_map/ppermute | solution.py:370
  68.7 28.5 %collective-permute-start.22 = (bf16[18,128,128]{2,1,0:T(8,128)(2,1)S(1)}, bf16[18,128,128]{2,1,0:T(8,128)(2,1)S(1)}, u32[]{:S(2)}, u32[]{:S(2)}) collective-permute-start(bf16[18,128,128]{2,1,0:T(8,128)(2,1)S(1)} %get-tuple-element.85), channel_id=1, source_target_pairs={{0,3},{1,2},{2,1},{3,0},{4,7},{5,6},{6,5},{7,4},{8,11},{9,10},{10,... | collective-permute-start | bytes 1769480 | tf_op jit(solution)/shard_map/ppermute | solution.py:370
  102.7 24.6 %collective-permute-start.8 = (f32[2,32,3840]{2,1,0:T(8,128)S(1)}, f32[2,32,3840]{2,1,0:T(8,128)S(1)}, u32[]{:S(2)}, u32[]{:S(2)}) collective-permute-start(f32[2,32,3840]{2,1,0:T(8,128)S(1)} %get-tuple-element.74), channel_id=1, source_target_pairs={{0,16},{16,0},{1,17},{17,1},{2,18},{18,2},{3,19},{19,3},{4,20},{20... | collective-permute-start | bytes 2949128 | tf_op jit(solution)/shard_map/ppermute | solution.py:367
  103.2 26.1 %collective-permute-start.10 = (f32[2,32,2304]{2,1,0:T(8,128)S(1)}, f32[2,32,2304]{2,1,0:T(8,128)S(1)}, u32[]{:S(2)}, u32[]{:S(2)}) collective-permute-start(f32[2,32,2304]{2,1,0:T(8,128)S(1)} %get-tuple-element.78), channel_id=1, source_target_pairs={{0,2},{1,3},{2,0},{3,1},{4,6},{5,7},{6,4},{7,5},{8,10},{9,11},{10,... | collective-permute-start | bytes 1769480 | tf_op jit(solution)/shard_map/ppermute | solution.py:370
  107.4 52.1 %collective-permute-start.32 = (f32[2,32,3840]{2,1,0:T(8,128)S(1)}, f32[2,32,3840]{2,1,0:T(8,128)S(1)}, u32[]{:S(2)}, u32[]{:S(2)}) collective-permute-start(f32[2,32,3840]{2,1,0:T(8,128)S(1)} %get-tuple-element.94), channel_id=1, source_target_pairs={{0,16},{16,0},{1,17},{17,1},{2,18},{18,2},{3,19},{19,3},{4,20},{20... | collective-permute-start | bytes 2949128 | tf_op jit(solution)/shard_map/ppermute | solution.py:367
  127.5 25.9 %collective-permute-start.9 = (f32[32,3840]{1,0:T(8,128)S(1)}, f32[32,3840]{1,0:T(8,128)S(1)}, u32[]{:S(2)}, u32[]{:S(2)}) collective-permute-start(f32[32,3840]{1,0:T(8,128)S(1)} %get-tuple-element.76), channel_id=1, source_target_pairs={{0,2},{1,3},{2,0},{3,1},{4,6},{5,7},{6,4},{7,5},{8,10},{9,11},{10,... | collective-permute-start | bytes 1474568 | tf_op jit(solution)/shard_map/ppermute | solution.py:370
  129.4 24.1 %collective-permute-start.11 = (f32[32,2304]{1,0:T(8,128)S(1)}, f32[32,2304]{1,0:T(8,128)S(1)}, u32[]{:S(2)}, u32[]{:S(2)}) collective-permute-start(f32[32,2304]{1,0:T(8,128)S(1)} %get-tuple-element.80), channel_id=1, source_target_pairs={{0,16},{16,0},{1,17},{17,1},{2,18},{18,2},{3,19},{19,3},{4,20},{20... | collective-permute-start | bytes 884744 | tf_op jit(solution)/shard_map/ppermute | solution.py:367
  157.7 27.9 %collective-permute-start.34 = (f32[2,32,2304]{2,1,0:T(8,128)S(1)}, f32[2,32,2304]{2,1,0:T(8,128)S(1)}, u32[]{:S(2)}, u32[]{:S(2)}) collective-permute-start(f32[2,32,2304]{2,1,0:T(8,128)S(1)} %get-tuple-element.98), channel_id=1, source_target_pairs={{0,2},{1,3},{2,0},{3,1},{4,6},{5,7},{6,4},{7,5},{8,10},{9,11},{10,... | collective-permute-start | bytes 1769480 | tf_op jit(solution)/shard_map/ppermute | solution.py:370
  159.6 36.4 %collective-permute-start.33 = (f32[32,3840]{1,0:T(8,128)S(1)}, f32[32,3840]{1,0:T(8,128)S(1)}, u32[]{:S(2)}, u32[]{:S(2)}) collective-permute-start(f32[32,3840]{1,0:T(8,128)S(1)} %get-tuple-element.96), channel_id=1, source_target_pairs={{0,2},{1,3},{2,0},{3,1},{4,6},{5,7},{6,4},{7,5},{8,10},{9,11},{10,... | collective-permute-start | bytes 1474568 | tf_op jit(solution)/shard_map/ppermute | solution.py:370
  173.4 45.5 %collective-permute-start.15 = (bf16[2,64,6144]{2,1,0:T(8,128)(2,1)S(1)}, bf16[2,64,6144]{2,1,0:T(8,128)(2,1)S(1)}, u32[]{:S(2)}, u32[]{:S(2)}) collective-permute-start(bf16[2,64,6144]{2,1,0:T(8,128)(2,1)S(1)} %bitcast.32), channel_id=1, source_target_pairs={{0,1},{1,0},{2,3},{3,2},{4,5},{5,4},{6,7},{7,6},{8,9},{9,8},{10,11... | collective-permute-start | bytes 4718600 | tf_op jit(solution)/shard_map/ppermute | solution.py:370
  200.2 84.9 %collective-permute-start.51 = (bf16[256,3072]{1,0:T(8,128)(2,1)}, bf16[256,3072]{1,0:T(8,128)(2,1)S(1)}, u32[]{:S(2)}, u32[]{:S(2)}) collective-permute-start(bf16[256,3072]{1,0:T(8,128)(2,1)} %copy-done.8), channel_id=1, source_target_pairs={{0,2},{1,3},{2,0},{3,1},{4,6},{5,7},{6,4},{7,5},{8,10},{9,11},{10,... | collective-permute-start | bytes 4718600 | tf_op jit(solution)/shard_map/ppermute | solution.py:370
  209.7 92.4 %collective-permute-start.49 = (bf16[256,3072]{1,0:T(8,128)(2,1)}, bf16[256,3072]{1,0:T(8,128)(2,1)S(1)}, u32[]{:S(2)}, u32[]{:S(2)}) collective-permute-start(bf16[256,3072]{1,0:T(8,128)(2,1)} %copy-done.6), channel_id=1, source_target_pairs={{0,2},{1,3},{2,0},{3,1},{4,6},{5,7},{6,4},{7,5},{8,10},{9,11},{10,... | collective-permute-start | bytes 4718600 | tf_op jit(solution)/shard_map/ppermute | solution.py:370
  218.8 69.8 %collective-permute-start.39 = (bf16[2,64,6144]{2,1,0:T(8,128)(2,1)S(1)}, bf16[2,64,6144]{2,1,0:T(8,128)(2,1)S(1)}, u32[]{:S(2)}, u32[]{:S(2)}) collective-permute-start(bf16[2,64,6144]{2,1,0:T(8,128)(2,1)S(1)} %bitcast.36), channel_id=1, source_target_pairs={{0,1},{1,0},{2,3},{3,2},{4,5},{5,4},{6,7},{7,6},{8,9},{9,8},{10,11... | collective-permute-start | bytes 4718600 | tf_op jit(solution)/shard_map/ppermute | solution.py:370
  228.8 34.3 %collective-permute-start.28 = (f32[2,32,1536]{2,1,0:T(8,128)S(1)}, f32[2,32,1536]{2,1,0:T(8,128)S(1)}, u32[]{:S(2)}, u32[]{:S(2)}) collective-permute-start(f32[2,32,1536]{2,1,0:T(8,128)S(1)} %pad_maximum_fusion.4), channel_id=1, source_target_pairs={{0,8},{4,12},{8,0},{12,4},{1,9},{5,13},{9,1},{13,5},{2,10},{6,14},... | collective-permute-start | bytes 1179656 | tf_op jit(solution)/shard_map/ppermute | solution.py:364
  238.3 27.8 %collective-permute-start.29 = (f32[2,32,1536]{2,1,0:T(8,128)S(1)}, f32[2,32,1536]{2,1,0:T(8,128)S(1)}, u32[]{:S(2)}, u32[]{:S(2)}) collective-permute-start(f32[2,32,1536]{2,1,0:T(8,128)S(1)} %pad_maximum_fusion.5), channel_id=1, source_target_pairs={{0,4},{4,8},{8,12},{12,0},{1,5},{5,9},{9,13},{13,1},{2,6},{6,10},{... | collective-permute-start | bytes 1179656 | tf_op jit(solution)/shard_map/ppermute | solution.py:364
  263.1 21.4 %collective-permute-start.48 = (s32[2,144]{1,0:T(2,128)S(1)}, s32[2,144]{1,0:T(2,128)S(1)}, u32[]{:S(2)}, u32[]{:S(2)}) collective-permute-start(s32[2,144]{1,0:T(2,128)S(1)} %bitcast.55), channel_id=1, source_target_pairs={{0,2},{1,3},{2,0},{3,1},{4,6},{5,7},{6,4},{7,5},{8,10},{9,11},{10,... | collective-permute-start | bytes 3464 | tf_op jit(solution)/shard_map/ppermute | solution.py:370
  266.1 40.1 %collective-permute-start.23 = (f32[128,1536]{1,0:T(8,128)S(1)}, f32[128,1536]{1,0:T(8,128)S(1)}, u32[]{:S(2)}, u32[]{:S(2)}) collective-permute-start(f32[128,1536]{1,0:T(8,128)S(1)} %get-tuple-element.88), channel_id=1, source_target_pairs={{0,16},{16,0},{1,17},{17,1},{2,18},{18,2},{3,19},{19,3},{4,20},{20... | collective-permute-start | bytes 2359304 | tf_op jit(solution)/shard_map/ppermute | solution.py:367
  284.5 21.7 %collective-permute-start.30 = (f32[32,1536]{1,0:T(8,128)S(1)}, f32[32,1536]{1,0:T(8,128)S(1)}, u32[]{:S(2)}, u32[]{:S(2)}) collective-permute-start(f32[32,1536]{1,0:T(8,128)S(1)} %slice_bitcast_fusion), channel_id=1, source_target_pairs={{0,16},{16,0},{1,17},{17,1},{2,18},{18,2},{3,19},{19,3},{4,20},{20... | collective-permute-start | bytes 589832 | tf_op jit(solution)/shard_map/ppermute | solution.py:367
  288.5 101.9 %collective-permute-start.52 = (f32[18,128,128]{2,1,0:T(8,128)S(1)}, f32[18,128,128]{2,1,0:T(8,128)S(1)}, u32[]{:S(2)}, u32[]{:S(2)}) collective-permute-start(f32[18,128,128]{2,1,0:T(8,128)S(1)} %get-tuple-element.112), channel_id=1, source_target_pairs={{0,1},{1,0},{2,3},{3,2},{4,5},{5,4},{6,7},{7,6},{8,9},{9,8},{10,11... | collective-permute-start | bytes 3538952 | tf_op jit(solution)/shard_map/ppermute | solution.py:370
  302.1 26.7 %collective-permute-start.44 = (f32[128,1536]{1,0:T(8,128)S(1)}, f32[128,1536]{1,0:T(8,128)S(1)}, u32[]{:S(2)}, u32[]{:S(2)}) collective-permute-start(f32[128,1536]{1,0:T(8,128)S(1)} %get-tuple-element.106), channel_id=1, source_target_pairs={{0,16},{16,0},{1,17},{17,1},{2,18},{18,2},{3,19},{19,3},{4,20},{20... | collective-permute-start | bytes 2359304 | tf_op jit(solution)/shard_map/ppermute | solution.py:367
  306.4 26.9 %collective-permute-start.24 = (f32[32,1536]{1,0:T(8,128)S(1)}, f32[32,1536]{1,0:T(8,128)S(1)}, u32[]{:S(2)}, u32[]{:S(2)}) collective-permute-start(f32[32,1536]{1,0:T(8,128)S(1)} %get-tuple-element.135), channel_id=1, source_target_pairs={{0,12},{4,0},{8,4},{12,8},{1,13},{5,1},{9,5},{13,9},{2,14},{6,2},{... | collective-permute-start | bytes 589832 | tf_op jit(solution)/shard_map/ppermute | solution.py:364
  309.6 24.8 %collective-permute-start.26 = (f32[32,1536]{1,0:T(8,128)S(1)}, f32[32,1536]{1,0:T(8,128)S(1)}, u32[]{:S(2)}, u32[]{:S(2)}) collective-permute-start(f32[32,1536]{1,0:T(8,128)S(1)} %get-tuple-element.136), channel_id=1, source_target_pairs={{0,4},{4,8},{8,12},{12,0},{1,5},{5,9},{9,13},{13,1},{2,6},{6,10},{... | collective-permute-start | bytes 589832 | tf_op jit(solution)/shard_map/ppermute | solution.py:364
  315.5 22.8 %collective-permute-start.25 = (f32[32,1536]{1,0:T(8,128)S(1)}, f32[32,1536]{1,0:T(8,128)S(1)}, u32[]{:S(2)}, u32[]{:S(2)}) collective-permute-start(f32[32,1536]{1,0:T(8,128)S(1)} %get-tuple-element.137), channel_id=1, source_target_pairs={{0,8},{4,12},{8,0},{12,4},{1,9},{5,13},{9,1},{13,5},{2,10},{6,14},... | collective-permute-start | bytes 589832 | tf_op jit(solution)/shard_map/ppermute | solution.py:364
  339.3 37.0 %collective-permute-start.54 = (f32[18,128,128]{2,1,0:T(8,128)S(1)}, f32[18,128,128]{2,1,0:T(8,128)S(1)}, u32[]{:S(2)}, u32[]{:S(2)}) collective-permute-start(f32[18,128,128]{2,1,0:T(8,128)S(1)} %get-tuple-element.116), channel_id=1, source_target_pairs={{0,1},{1,0},{2,3},{3,2},{4,5},{5,4},{6,7},{7,6},{8,9},{9,8},{10,11... | collective-permute-start | bytes 3538952 | tf_op jit(solution)/shard_map/ppermute | solution.py:370
  347.5 35.9 %collective-permute-start.53 = (f32[18,128,128]{2,1,0:T(8,128)S(1)}, f32[18,128,128]{2,1,0:T(8,128)S(1)}, u32[]{:S(2)}, u32[]{:S(2)}) collective-permute-start(f32[18,128,128]{2,1,0:T(8,128)S(1)} %get-tuple-element.114), channel_id=1, source_target_pairs={{0,1},{1,0},{2,3},{3,2},{4,5},{5,4},{6,7},{7,6},{8,9},{9,8},{10,11... | collective-permute-start | bytes 3538952 | tf_op jit(solution)/shard_map/ppermute | solution.py:370
  354.0 43.4 %collective-permute-start.50 = (f32[18,128,128]{2,1,0:T(8,128)S(1)}, f32[18,128,128]{2,1,0:T(8,128)S(1)}, u32[]{:S(2)}, u32[]{:S(2)}) collective-permute-start(f32[18,128,128]{2,1,0:T(8,128)S(1)} %get-tuple-element.109), channel_id=1, source_target_pairs={{0,1},{1,0},{2,3},{3,2},{4,5},{5,4},{6,7},{7,6},{8,9},{9,8},{10,11... | collective-permute-start | bytes 3538952 | tf_op jit(solution)/shard_map/ppermute | solution.py:370
  (36 other events, 535.6 us)

commit v10 on v9

--- a/solution.py
+++ b/solution.py
@@ -21,7 +21,7 @@
 WEIGHT_DECAY = 0.1
 ADAM_EPSILON = 1e-08
 VMEM_SPARE = 3 * 2**19
-UNROLL = 4
+UNROLL = 6
 CHUNKS = 2
 MEM, HID, TOK = "mem", "hid", "tok"
 
@@ -387,23 +387,27 @@
         own = jnp.stack(found)
         return [own] + [shift_hid(own, k) for k in range(1, hid_count)]
 
-    def gather_weights(matrix):
+    def narrow(matrix, turns):
         shape = (owned_slots, block_size, block_size)
-        narrow = pl.pallas_call(
+        return pl.pallas_call(
             narrow_kernel,
-            grid=(tok_count,),
-            out_shape=[jax.ShapeDtypeStruct(shape, bf16)] * tok_count,
+            grid=(len(turns),),
+            out_shape=[jax.ShapeDtypeStruct(shape, bf16)] * len(turns),
             in_specs=[
                 pl.BlockSpec(
                     (1, 1, 1) + blocks.shape[3:],
-                    lambda i: (matrix, lax.axis_index(TOK) ^ i, 0, 0, 0, 0),
+                    lambda i: (matrix, lax.axis_index(TOK) ^ (turns[0] + i), 0, 0, 0, 0),
                 )
             ],
-            out_specs=[pl.BlockSpec(shape, lambda i: (0, 0, 0))] * tok_count,
-            compiler_params=grant(owned_slots * block_size**2 * 4 * (2 + tok_count)),
+            out_specs=[pl.BlockSpec(shape, lambda i: (0, 0, 0))] * len(turns),
+            compiler_params=grant(44 * 2**20),
         )(blocks)
-        moved = [flip_tok(narrow[r], r) for r in range(1, tok_count)]
-        return [narrow[0], *moved]
+
+    def gather_weights(matrix):
+        near, far = range(2), range(2, tok_count)
+        sent = [flip_tok(x, r) for r, x in zip(far, narrow(matrix, far))]
+        own, pair = narrow(matrix, near)
+        return [own, flip_tok(pair, 1), *sent]
 
     def forward(matrix, transposed, row_groups, weights):
         kernel = functools.partial(
@@ -533,7 +537,7 @@
         return keep, flip_tok(send, 1)
 
     def update(matrix, cell, grads, held):
-        splits = 2 if owned_slots % 2 == 0 else 1
+        splits = 1
         run = owned_slots // splits
         state_spec = pl.BlockSpec(
             (1, 1, 1, run, block_size, block_size),

time: 405 us -> 395 us (0.975)
  waiting for transfers between devices: 253 us -> 246 us
    pallas_call x2 -> x4, Pallas kernels: 0.69 us -> 6.91 us  [narrow(): pl.pallas_call(narrow_kernel, grid=(len(turns),), out_shape=[jax.ShapeDty...]
    ppermute x21, waiting for transfers between devices: 42.7 us -> 36.6 us  [flip_tok(): return lax.ppermute(array, TOK, [(i, i ^ bit) for i in range(tok_count)])]
    pallas_call x14, Pallas kernels: 34.7 us -> 29 us  [call(): pl.pallas_call(kernel, out_shape=outs, in_specs=[SCALARS] * len(scalars)...]
    ppermute x18, waiting for transfers between devices: 105 us -> 100 us  [shift_hid(): lax.ppermute(array, HID, [(i, (i + shift) % hid_count) for i in range(hid...]
    ppermute x10, waiting for transfers between devices: 78 us -> 82.8 us  [shift_mem(): lax.ppermute(array, MEM, [(i, (i + shift) % mem_count) for i in range(mem...]
    pallas_call x4, Pallas kernels: 28.2 us -> 23.8 us  [update(): pl.pallas_call(functools.partial(update_kernel, matrix, cell, owned_slots...]
  transfers between devices with their start and end apart: 55 -> 55, of which waited for: 26 -> 26; matrix products, arithmetic and copies ran while one was open for 1% -> 1% of each run, Pallas kernels for 15% -> 14%
where the time goes in v10:
time: 395 us
  waiting for transfers between devices  246 us (62%)
  starting transfers between devices  76.6 us (19%)
  Pallas kernels  62.3 us (16%)
  local copies, waits for them, and re-layouts  4.81 us (1%)
    ppermute x18, waiting for transfers between devices, shift_hid(): lax.ppermute(array, HID, [(i, (i + shift) % hid_count) for i in range(hid...  100 us
    ppermute x10, waiting for transfers between devices, shift_mem(): lax.ppermute(array, MEM, [(i, (i + shift) % mem_count) for i in range(mem...  82.8 us
    ppermute x18, starting transfers between devices, shift_hid(): lax.ppermute(array, HID, [(i, (i + shift) % hid_count) for i in range(hid...  43.2 us
    ppermute x21, waiting for transfers between devices, flip_tok(): return lax.ppermute(array, TOK, [(i, i ^ bit) for i in range(tok_count)])  36.6 us
    pallas_call x14, Pallas kernels, call(): pl.pallas_call(kernel, out_shape=outs, in_specs=[SCALARS] * len(scalars)...  29 us
    ppermute x6, waiting for transfers between devices, across(): return lax.ppermute(array, (MEM, TOK), table)  26.7 us
    pallas_call x4, Pallas kernels, update(): pl.pallas_call(functools.partial(update_kernel, matrix, cell, owned_slots...  23.8 us
    ppermute x21, starting transfers between devices, flip_tok(): return lax.ppermute(array, TOK, [(i, i ^ bit) for i in range(tok_count)])  19.9 us
  transfers between devices with their start and end apart: 55, of which 26 were waited for; matrix products, arithmetic and copies ran while one was open for 1% of the time, Pallas kernels for 14%

profile of v10, /device:TPU:0, one launch (start us, length us, event | category | flops | bytes accessed | tf_op | source)
XLA Modules:
  0.0 394.6 jit_solution(7761450763020409280)
XLA Ops:
  0.6 4.1 %collective-permute-start.1 = (bf16[32,3072]{1,0:T(8,128)(2,1)}, bf16[32,3072]{1,0:T(8,128)(2,1)S(1)}, u32[]{:S(2)}, u32[]{:S(2)}) collective-permute-start(bf16[32,3072]{1,0:T(8,128)(2,1)} %param.7), channel_id=1, source_target_pairs={{0,8},{4,12},{8,0},{12,4},{1,9},{5,13},{9,1},{13,5},{2,10},{6,14},... | collective-permute-start | bytes 589832 | tf_op jit(solution)/shard_map/ppermute | solution.py:364
  9.6 6.8 %collective-permute-done = bf16[32,3072]{1,0:T(8,128)(2,1)S(1)} collective-permute-done((bf16[32,3072]{1,0:T(8,128)(2,1)}, bf16[32,3072]{1,0:T(8,128)(2,1)S(1)}, u32[]{:S(2)}, u32[]{:S(2)}) %collective-permute-start) | collective-permute-done | bytes 196640 | tf_op jit(solution)/shard_map/ppermute | solution.py:364
  27.7 13.7 %collective-permute-done.16 = bf16[32,3072]{1,0:T(8,128)(2,1)S(1)} collective-permute-done((bf16[32,3072]{1,0:T(8,128)(2,1)}, bf16[32,3072]{1,0:T(8,128)(2,1)S(1)}, u32[]{:S(2)}, u32[]{:S(2)}) %collective-permute-start.16) | collective-permute-done | bytes 196640 | tf_op jit(solution)/shard_map/ppermute | solution.py:367
  47.7 5.2 %shard_map.112 = (bf16[256,3072]{1,0:T(8,128)(2,1)S(1)}, f32[2,64,6144]{2,1,0:T(8,128)S(1)}, f32[2,64,6144]{2,1,0:T(8,128)S(1)}, bf16[4,18,128,128]{3,2,1,0:T(8,128)(2,1)S(1)}) custom-call(s32[2,4]{1,0:T(2,128)S(1)} %bitcast.40, s32[2,144]{1,0:T(2,128)S(1)} %bitcast.52, bf16[128,3072]{1,0:T(8,128)(2,1)S(1)} %constant_dynamic-update-slice_fusion.refs_0_, ...), custom_call_target="tpu_custom_call" | custom-call | flops 603979776 | bytes 11796480 | tf_op jit(solution)/shard_map/pallas_call | solution.py:325
  55.4 8.5 %collective-permute-start.18 = (bf16[2,32,3072]{2,1,0:T(8,128)(2,1)S(1)}, bf16[2,32,3072]{2,1,0:T(8,128)(2,1)S(1)}, u32[]{:S(2)}, u32[]{:S(2)}) collective-permute-start(bf16[2,32,3072]{2,1,0:T(8,128)(2,1)S(1)} %pad_maximum_fusion.2.refs_0_), channel_id=1, source_target_pairs={{0,8},{4,12},{8,0},{12,4},{1,9},{5,13},{9,1},{13,5},{2,10},{6,14},... | collective-permute-start | bytes 1179656 | tf_op jit(solution)/shard_map/ppermute | solution.py:364
  69.9 11.8 %collective-permute-done.18.refs_2_ = bf16[2,32,3072]{2,1,0:T(8,128)(2,1)S(1)} collective-permute-done((bf16[2,32,3072]{2,1,0:T(8,128)(2,1)S(1)}, bf16[2,32,3072]{2,1,0:T(8,128)(2,1)S(1)}, u32[]{:S(2)}, u32[]{:S(2)}) %collective-permute-start.18) | collective-permute-done | bytes 393248 | tf_op jit(solution)/shard_map/ppermute | solution.py:364
  81.7 12.3 %collective-permute-done.17.refs_1_ = bf16[2,32,3072]{2,1,0:T(8,128)(2,1)S(1)} collective-permute-done((bf16[2,32,3072]{2,1,0:T(8,128)(2,1)S(1)}, bf16[2,32,3072]{2,1,0:T(8,128)(2,1)S(1)}, u32[]{:S(2)}, u32[]{:S(2)}) %collective-permute-start.17) | collective-permute-done | bytes 393248 | tf_op jit(solution)/shard_map/ppermute | solution.py:364
  105.0 18.8 %collective-permute-done.8.refs_1_ = f32[2,32,3840]{2,1,0:T(8,128)S(1)} collective-permute-done((f32[2,32,3840]{2,1,0:T(8,128)S(1)}, f32[2,32,3840]{2,1,0:T(8,128)S(1)}, u32[]{:S(2)}, u32[]{:S(2)}) %collective-permute-start.8) | collective-permute-done | bytes 983072 | tf_op jit(solution)/shard_map/ppermute | solution.py:367
  126.5 23.4 %collective-permute-done.11.refs_3_ = f32[32,2304]{1,0:T(8,128)S(1)} collective-permute-done((f32[32,2304]{1,0:T(8,128)S(1)}, f32[32,2304]{1,0:T(8,128)S(1)}, u32[]{:S(2)}, u32[]{:S(2)}) %collective-permute-start.11) | collective-permute-done | bytes 294944 | tf_op jit(solution)/shard_map/ppermute | solution.py:367
  156.8 6.4 %collective-permute-done.14 = bf16[32,6144]{1,0:T(8,128)(2,1)S(1)} collective-permute-done((bf16[32,6144]{1,0:T(8,128)(2,1)S(1)}, bf16[32,6144]{1,0:T(8,128)(2,1)S(1)}, u32[]{:S(2)}, u32[]{:S(2)}) %collective-permute-start.14) | collective-permute-done | bytes 393248 | tf_op jit(solution)/shard_map/ppermute | solution.py:378
  163.2 7.1 %collective-permute-done.13 = bf16[32,6144]{1,0:T(8,128)(2,1)S(1)} collective-permute-done((bf16[32,6144]{1,0:T(8,128)(2,1)S(1)}, bf16[32,6144]{1,0:T(8,128)(2,1)S(1)}, u32[]{:S(2)}, u32[]{:S(2)}) %collective-permute-start.13) | collective-permute-done | bytes 393248 | tf_op jit(solution)/shard_map/ppermute | solution.py:378
  170.5 11.6 %collective-permute-done.34.refs_1_ = f32[2,32,2304]{2,1,0:T(8,128)S(1)} collective-permute-done((f32[2,32,2304]{2,1,0:T(8,128)S(1)}, f32[2,32,2304]{2,1,0:T(8,128)S(1)}, u32[]{:S(2)}, u32[]{:S(2)}) %collective-permute-start.34) | collective-permute-done | bytes 589856 | tf_op jit(solution)/shard_map/ppermute | solution.py:370
  183.4 7.7 %collective-permute-done.35.refs_3_ = f32[32,2304]{1,0:T(8,128)S(1)} collective-permute-done((f32[32,2304]{1,0:T(8,128)S(1)}, f32[32,2304]{1,0:T(8,128)S(1)}, u32[]{:S(2)}, u32[]{:S(2)}) %collective-permute-start.35) | collective-permute-done | bytes 294944 | tf_op jit(solution)/shard_map/ppermute | solution.py:367
  199.0 7.2 %collective-permute-done.38 = bf16[32,6144]{1,0:T(8,128)(2,1)} collective-permute-done((bf16[32,6144]{1,0:T(8,128)(2,1)S(1)}, bf16[32,6144]{1,0:T(8,128)(2,1)}, u32[]{:S(2)}, u32[]{:S(2)}) %collective-permute-start.38) | collective-permute-done | bytes 393248 | tf_op jit(solution)/shard_map/ppermute | solution.py:378
  208.5 6.0 %collective-permute-done.37 = bf16[32,6144]{1,0:T(8,128)(2,1)} collective-permute-done((bf16[32,6144]{1,0:T(8,128)(2,1)S(1)}, bf16[32,6144]{1,0:T(8,128)(2,1)}, u32[]{:S(2)}, u32[]{:S(2)}) %collective-permute-start.37) | collective-permute-done | bytes 393248 | tf_op jit(solution)/shard_map/ppermute | solution.py:378
  218.9 5.4 %collective-permute-start.27 = (f32[2,32,1536]{2,1,0:T(8,128)S(1)}, f32[2,32,1536]{2,1,0:T(8,128)S(1)}, u32[]{:S(2)}, u32[]{:S(2)}) collective-permute-start(f32[2,32,1536]{2,1,0:T(8,128)S(1)} %pad_maximum_fusion.3), channel_id=1, source_target_pairs={{0,12},{4,0},{8,4},{12,8},{1,13},{5,1},{9,5},{13,9},{2,14},{6,2},{... | collective-permute-start | bytes 1179656 | tf_op jit(solution)/shard_map/ppermute | solution.py:364
  224.4 9.4 %collective-permute-done.27 = f32[2,32,1536]{2,1,0:T(8,128)S(1)} collective-permute-done((f32[2,32,1536]{2,1,0:T(8,128)S(1)}, f32[2,32,1536]{2,1,0:T(8,128)S(1)}, u32[]{:S(2)}, u32[]{:S(2)}) %collective-permute-start.27) | collective-permute-done | bytes 393248 | tf_op jit(solution)/shard_map/ppermute | solution.py:364
  233.8 24.4 %collective-permute-done.28 = f32[2,32,1536]{2,1,0:T(8,128)S(1)} collective-permute-done((f32[2,32,1536]{2,1,0:T(8,128)S(1)}, f32[2,32,1536]{2,1,0:T(8,128)S(1)}, u32[]{:S(2)}, u32[]{:S(2)}) %collective-permute-start.28) | collective-permute-done | bytes 393248 | tf_op jit(solution)/shard_map/ppermute | solution.py:364
  261.4 19.5 %collective-permute-done.48.place_ref = s32[2,144]{1,0:T(2,128)S(1)} collective-permute-done((s32[2,144]{1,0:T(2,128)S(1)}, s32[2,144]{1,0:T(2,128)S(1)}, u32[]{:S(2)}, u32[]{:S(2)}) %collective-permute-start.48) | collective-permute-done | bytes 1184 | tf_op jit(solution)/shard_map/ppermute | solution.py:370
  285.4 4.9 %shard_map.127 = (f32[128,1536]{1,0:T(8,128)S(1)}, f32[128,1536]{1,0:T(8,128)S(1)}, f32[128,1536]{1,0:T(8,128)S(1)}, f32[128,1536]{1,0:T(8,128)S(1)}) custom-call(s32[2,4]{1,0:T(2,128)S(1)} %bitcast.44, s32[2,144]{1,0:T(2,128)S(1)} %bitcast.56, bf16[2,64,6144]{2,1,0:T(8,128)(2,1)S(1)} %bitcast.37, bf16[2,64,6144]{2,1,0:T(8,128)(2,1)S(1)} %collective-permute-done.39.pair_ref, ...), custom_call_target="tpu_custom_call" | custom-call | flops 603979776 | bytes 8650752 | tf_op jit(solution)/shard_map/pallas_call | solution.py:325
  301.9 9.0 %collective-permute-done.40 = f32[128,1536]{1,0:T(8,128)S(1)} collective-permute-done((f32[128,1536]{1,0:T(8,128)S(1)}, f32[128,1536]{1,0:T(8,128)S(1)}, u32[]{:S(2)}, u32[]{:S(2)}) %collective-permute-start.40) | collective-permute-done | bytes 786464 | tf_op jit(solution)/shard_map/ppermute | solution.py:367
  314.6 10.3 %collective-permute-done.44 = f32[128,1536]{1,0:T(8,128)S(1)} collective-permute-done((f32[128,1536]{1,0:T(8,128)S(1)}, f32[128,1536]{1,0:T(8,128)S(1)}, u32[]{:S(2)}, u32[]{:S(2)}) %collective-permute-start.44) | collective-permute-done | bytes 786464 | tf_op jit(solution)/shard_map/ppermute | solution.py:367
  328.5 3.9 collective-permute-start.42
  333.9 7.2 %collective-permute-done.43 = f32[32,1536]{1,0:T(8,128)S(1)} collective-permute-done((f32[32,1536]{1,0:T(8,128)S(1)}, f32[32,1536]{1,0:T(8,128)S(1)}, u32[]{:S(2)}, u32[]{:S(2)}) %collective-permute-start.43) | collective-permute-done | bytes 196640 | tf_op jit(solution)/shard_map/ppermute | solution.py:364
  341.0 6.8 %collective-permute-done.42 = f32[32,1536]{1,0:T(8,128)S(1)} collective-permute-done((f32[32,1536]{1,0:T(8,128)S(1)}, f32[32,1536]{1,0:T(8,128)S(1)}, u32[]{:S(2)}, u32[]{:S(2)}) %collective-permute-start.42) | collective-permute-done | bytes 196640 | tf_op jit(solution)/shard_map/ppermute | solution.py:364
  347.8 3.7 collective-permute-start.47
  351.5 7.9 %collective-permute-done.47 = f32[32,1536]{1,0:T(8,128)S(1)} collective-permute-done((f32[32,1536]{1,0:T(8,128)S(1)}, f32[32,1536]{1,0:T(8,128)S(1)}, u32[]{:S(2)}, u32[]{:S(2)}) %collective-permute-start.47) | collective-permute-done | bytes 196640 | tf_op jit(solution)/shard_map/ppermute | solution.py:364
  360.1 10.0 %collective-permute-done.46 = f32[32,1536]{1,0:T(8,128)S(1)} collective-permute-done((f32[32,1536]{1,0:T(8,128)S(1)}, f32[32,1536]{1,0:T(8,128)S(1)}, u32[]{:S(2)}, u32[]{:S(2)}) %collective-permute-start.46) | collective-permute-done | bytes 196640 | tf_op jit(solution)/shard_map/ppermute | solution.py:364
  370.8 5.9 %shard_map.132 = (f32[2,4,1,18,128,128]{5,4,3,2,1,0:T(8,128)}, f32[2,4,1,18,128,128]{5,4,3,2,1,0:T(8,128)}, f32[2,4,1,18,128,128]{5,4,3,2,1,0:T(8,128)}) custom-call(s32[2,4]{1,0:T(2,128)S(1)} %bitcast.48, f32[18,128,128]{2,1,0:T(8,128)S(1)} %get-tuple-element.115.own_ref, f32[18,128,128]{2,1,0:T(8,128)S(1)} %collective-permute-done.54.pair_ref, ...), custom_call_target="tpu_custom_call" | custom-call | flops 7077888 | bytes 16515072 | tf_op jit(solution)/shard_map/pallas_call | solution.py:554
  376.7 6.0 %shard_map.133 = (f32[2,4,1,18,128,128]{5,4,3,2,1,0:T(8,128)}, f32[2,4,1,18,128,128]{5,4,3,2,1,0:T(8,128)}, f32[2,4,1,18,128,128]{5,4,3,2,1,0:T(8,128)}) custom-call(s32[2,4]{1,0:T(2,128)S(1)} %bitcast.49, f32[18,128,128]{2,1,0:T(8,128)S(1)} %get-tuple-element.113.own_ref, ...), custom_call_target="tpu_custom_call", output_to_operand_aliasing={{0}: (6, {}), {1}: (7, {}), {2}: (8, {})} | custom-call | flops 7077888 | bytes 16515072 | tf_op jit(solution)/shard_map/pallas_call | solution.py:554
  382.7 6.0 %shard_map.134 = (f32[2,4,1,18,128,128]{5,4,3,2,1,0:T(8,128)}, f32[2,4,1,18,128,128]{5,4,3,2,1,0:T(8,128)}, f32[2,4,1,18,128,128]{5,4,3,2,1,0:T(8,128)}) custom-call(s32[2,4]{1,0:T(2,128)S(1)} %bitcast.50, f32[18,128,128]{2,1,0:T(8,128)S(1)} %get-tuple-element.111.own_ref, ...), custom_call_target="tpu_custom_call", output_to_operand_aliasing={{0}: (6, {}), {1}: (7, {}), {2}: (8, {})} | custom-call | flops 7077888 | bytes 16515072 | tf_op jit(solution)/shard_map/pallas_call | solution.py:554
  388.6 6.0 %shard_map.135 = (f32[2,4,1,18,128,128]{5,4,3,2,1,0:T(8,128)}, f32[2,4,1,18,128,128]{5,4,3,2,1,0:T(8,128)}, f32[2,4,1,18,128,128]{5,4,3,2,1,0:T(8,128)}) custom-call(s32[2,4]{1,0:T(2,128)S(1)} %bitcast.51, f32[18,128,128]{2,1,0:T(8,128)S(1)} %get-tuple-element.108.own_ref, ...), custom_call_target="tpu_custom_call", output_to_operand_aliasing={{0}: (6, {}), {1}: (7, {}), {2}: (8, {})} | custom-call | flops 7077888 | bytes 16515072 | tf_op jit(solution)/shard_map/pallas_call | solution.py:554
  (152 shorter events, 96.7 us)
Async XLA Ops:
  19.9 27.8 %collective-permute-start.3 = (bf16[128,3072]{1,0:T(8,128)(2,1)S(1)}, bf16[128,3072]{1,0:T(8,128)(2,1)S(1)}, u32[]{:S(2)}, u32[]{:S(2)}) collective-permute-start(bf16[128,3072]{1,0:T(8,128)(2,1)S(1)} %constant_dynamic-update-slice_fusion.refs_0_), channel_id=1, source_target_pairs={{0,16},{16,0},{1,17},{17,1},{2,18},{18,2},{3,19},{19,3},{4,20},{20... | collective-permute-start | bytes 2359304 | tf_op jit(solution)/shard_map/ppermute | solution.py:367
  23.7 21.0 %collective-permute-start.5 = (bf16[18,128,128]{2,1,0:T(8,128)(2,1)S(1)}, bf16[18,128,128]{2,1,0:T(8,128)(2,1)S(1)}, u32[]{:S(2)}, u32[]{:S(2)}) collective-permute-start(bf16[18,128,128]{2,1,0:T(8,128)(2,1)S(1)} %get-tuple-element.69), channel_id=1, source_target_pairs={{0,2},{1,3},{2,0},{3,1},{4,6},{5,7},{6,4},{7,5},{8,10},{9,11},{10,... | collective-permute-start | bytes 1769480 | tf_op jit(solution)/shard_map/ppermute | solution.py:370
  25.4 22.3 %collective-permute-start.6 = (bf16[18,128,128]{2,1,0:T(8,128)(2,1)S(1)}, bf16[18,128,128]{2,1,0:T(8,128)(2,1)S(1)}, u32[]{:S(2)}, u32[]{:S(2)}) collective-permute-start(bf16[18,128,128]{2,1,0:T(8,128)(2,1)S(1)} %get-tuple-element.70), channel_id=1, source_target_pairs={{0,3},{1,2},{2,1},{3,0},{4,7},{5,6},{6,5},{7,4},{8,11},{9,10},{10,... | collective-permute-start | bytes 1769480 | tf_op jit(solution)/shard_map/ppermute | solution.py:370
  41.4 28.2 %collective-permute-start.19 = (bf16[2,32,3072]{2,1,0:T(8,128)(2,1)S(1)}, bf16[2,32,3072]{2,1,0:T(8,128)(2,1)S(1)}, u32[]{:S(2)}, u32[]{:S(2)}) collective-permute-start(bf16[2,32,3072]{2,1,0:T(8,128)(2,1)S(1)} %pad_maximum_fusion.2.refs_0_), channel_id=1, source_target_pairs={{0,12},{4,0},{8,4},{12,8},{1,13},{5,1},{9,5},{13,9},{2,14},{6,2},{... | collective-permute-start | bytes 1179656 | tf_op jit(solution)/shard_map/ppermute | solution.py:364
  55.4 42.0 %collective-permute-start.7 = (f32[2,64,6144]{2,1,0:T(8,128)S(1)}, f32[2,64,6144]{2,1,0:T(8,128)S(1)}, u32[]{:S(2)}, u32[]{:S(2)}) collective-permute-start(f32[2,64,6144]{2,1,0:T(8,128)S(1)} %get-tuple-element.72), channel_id=1, source_target_pairs={{0,1},{1,0},{2,3},{3,2},{4,5},{5,4},{6,7},{7,6},{8,9},{9,8},{10,11... | collective-permute-start | bytes 9437192 | tf_op jit(solution)/shard_map/ppermute | solution.py:370
  55.4 26.3 %collective-permute-start.18 = (bf16[2,32,3072]{2,1,0:T(8,128)(2,1)S(1)}, bf16[2,32,3072]{2,1,0:T(8,128)(2,1)S(1)}, u32[]{:S(2)}, u32[]{:S(2)}) collective-permute-start(bf16[2,32,3072]{2,1,0:T(8,128)(2,1)S(1)} %pad_maximum_fusion.2.refs_0_), channel_id=1, source_target_pairs={{0,8},{4,12},{8,0},{12,4},{1,9},{5,13},{9,1},{13,5},{2,10},{6,14},... | collective-permute-start | bytes 1179656 | tf_op jit(solution)/shard_map/ppermute | solution.py:364
  65.7 28.4 %collective-permute-start.21 = (bf16[18,128,128]{2,1,0:T(8,128)(2,1)S(1)}, bf16[18,128,128]{2,1,0:T(8,128)(2,1)S(1)}, u32[]{:S(2)}, u32[]{:S(2)}) collective-permute-start(bf16[18,128,128]{2,1,0:T(8,128)(2,1)S(1)} %get-tuple-element.84), channel_id=1, source_target_pairs={{0,2},{1,3},{2,0},{3,1},{4,6},{5,7},{6,4},{7,5},{8,10},{9,11},{10,... | collective-permute-start | bytes 1769480 | tf_op jit(solution)/shard_map/ppermute | solution.py:370
  67.9 26.1 %collective-permute-start.22 = (bf16[18,128,128]{2,1,0:T(8,128)(2,1)S(1)}, bf16[18,128,128]{2,1,0:T(8,128)(2,1)S(1)}, u32[]{:S(2)}, u32[]{:S(2)}) collective-permute-start(bf16[18,128,128]{2,1,0:T(8,128)(2,1)S(1)} %get-tuple-element.85), channel_id=1, source_target_pairs={{0,3},{1,2},{2,1},{3,0},{4,7},{5,6},{6,5},{7,4},{8,11},{9,10},{10,... | collective-permute-start | bytes 1769480 | tf_op jit(solution)/shard_map/ppermute | solution.py:370
  69.7 24.4 %collective-permute-start.20 = (bf16[18,128,128]{2,1,0:T(8,128)(2,1)S(1)}, bf16[18,128,128]{2,1,0:T(8,128)(2,1)S(1)}, u32[]{:S(2)}, u32[]{:S(2)}) collective-permute-start(bf16[18,128,128]{2,1,0:T(8,128)(2,1)S(1)} %get-tuple-element.83), channel_id=1, source_target_pairs={{0,1},{1,0},{2,3},{3,2},{4,5},{5,4},{6,7},{7,6},{8,9},{9,8},{10,11... | collective-permute-start | bytes 1769480 | tf_op jit(solution)/shard_map/ppermute | solution.py:370
  99.2 24.6 %collective-permute-start.8 = (f32[2,32,3840]{2,1,0:T(8,128)S(1)}, f32[2,32,3840]{2,1,0:T(8,128)S(1)}, u32[]{:S(2)}, u32[]{:S(2)}) collective-permute-start(f32[2,32,3840]{2,1,0:T(8,128)S(1)} %get-tuple-element.74), channel_id=1, source_target_pairs={{0,16},{16,0},{1,17},{17,1},{2,18},{18,2},{3,19},{19,3},{4,20},{20... | collective-permute-start | bytes 2949128 | tf_op jit(solution)/shard_map/ppermute | solution.py:367
  99.7 26.7 %collective-permute-start.10 = (f32[2,32,2304]{2,1,0:T(8,128)S(1)}, f32[2,32,2304]{2,1,0:T(8,128)S(1)}, u32[]{:S(2)}, u32[]{:S(2)}) collective-permute-start(f32[2,32,2304]{2,1,0:T(8,128)S(1)} %get-tuple-element.78), channel_id=1, source_target_pairs={{0,2},{1,3},{2,0},{3,1},{4,6},{5,7},{6,4},{7,5},{8,10},{9,11},{10,... | collective-permute-start | bytes 1769480 | tf_op jit(solution)/shard_map/ppermute | solution.py:370
  103.9 52.7 %collective-permute-start.32 = (f32[2,32,3840]{2,1,0:T(8,128)S(1)}, f32[2,32,3840]{2,1,0:T(8,128)S(1)}, u32[]{:S(2)}, u32[]{:S(2)}) collective-permute-start(f32[2,32,3840]{2,1,0:T(8,128)S(1)} %get-tuple-element.94), channel_id=1, source_target_pairs={{0,16},{16,0},{1,17},{17,1},{2,18},{18,2},{3,19},{19,3},{4,20},{20... | collective-permute-start | bytes 2949128 | tf_op jit(solution)/shard_map/ppermute | solution.py:367
  124.0 25.9 %collective-permute-start.9 = (f32[32,3840]{1,0:T(8,128)S(1)}, f32[32,3840]{1,0:T(8,128)S(1)}, u32[]{:S(2)}, u32[]{:S(2)}) collective-permute-start(f32[32,3840]{1,0:T(8,128)S(1)} %get-tuple-element.76), channel_id=1, source_target_pairs={{0,2},{1,3},{2,0},{3,1},{4,6},{5,7},{6,4},{7,5},{8,10},{9,11},{10,... | collective-permute-start | bytes 1474568 | tf_op jit(solution)/shard_map/ppermute | solution.py:370
  126.4 23.5 %collective-permute-start.11 = (f32[32,2304]{1,0:T(8,128)S(1)}, f32[32,2304]{1,0:T(8,128)S(1)}, u32[]{:S(2)}, u32[]{:S(2)}) collective-permute-start(f32[32,2304]{1,0:T(8,128)S(1)} %get-tuple-element.80), channel_id=1, source_target_pairs={{0,16},{16,0},{1,17},{17,1},{2,18},{18,2},{3,19},{19,3},{4,20},{20... | collective-permute-start | bytes 884744 | tf_op jit(solution)/shard_map/ppermute | solution.py:367
  154.5 27.6 %collective-permute-start.34 = (f32[2,32,2304]{2,1,0:T(8,128)S(1)}, f32[2,32,2304]{2,1,0:T(8,128)S(1)}, u32[]{:S(2)}, u32[]{:S(2)}) collective-permute-start(f32[2,32,2304]{2,1,0:T(8,128)S(1)} %get-tuple-element.98), channel_id=1, source_target_pairs={{0,2},{1,3},{2,0},{3,1},{4,6},{5,7},{6,4},{7,5},{8,10},{9,11},{10,... | collective-permute-start | bytes 1769480 | tf_op jit(solution)/shard_map/ppermute | solution.py:370
  156.7 35.9 %collective-permute-start.33 = (f32[32,3840]{1,0:T(8,128)S(1)}, f32[32,3840]{1,0:T(8,128)S(1)}, u32[]{:S(2)}, u32[]{:S(2)}) collective-permute-start(f32[32,3840]{1,0:T(8,128)S(1)} %get-tuple-element.96), channel_id=1, source_target_pairs={{0,2},{1,3},{2,0},{3,1},{4,6},{5,7},{6,4},{7,5},{8,10},{9,11},{10,... | collective-permute-start | bytes 1474568 | tf_op jit(solution)/shard_map/ppermute | solution.py:370
  170.4 45.5 %collective-permute-start.15 = (bf16[2,64,6144]{2,1,0:T(8,128)(2,1)S(1)}, bf16[2,64,6144]{2,1,0:T(8,128)(2,1)S(1)}, u32[]{:S(2)}, u32[]{:S(2)}) collective-permute-start(bf16[2,64,6144]{2,1,0:T(8,128)(2,1)S(1)} %bitcast.32), channel_id=1, source_target_pairs={{0,1},{1,0},{2,3},{3,2},{4,5},{5,4},{6,7},{7,6},{8,9},{9,8},{10,11... | collective-permute-start | bytes 4718600 | tf_op jit(solution)/shard_map/ppermute | solution.py:370
  196.9 85.2 %collective-permute-start.51 = (bf16[256,3072]{1,0:T(8,128)(2,1)}, bf16[256,3072]{1,0:T(8,128)(2,1)S(1)}, u32[]{:S(2)}, u32[]{:S(2)}) collective-permute-start(bf16[256,3072]{1,0:T(8,128)(2,1)} %copy-done.6), channel_id=1, source_target_pairs={{0,2},{1,3},{2,0},{3,1},{4,6},{5,7},{6,4},{7,5},{8,10},{9,11},{10,... | collective-permute-start | bytes 4718600 | tf_op jit(solution)/shard_map/ppermute | solution.py:370
  206.2 89.9 %collective-permute-start.49 = (bf16[256,3072]{1,0:T(8,128)(2,1)}, bf16[256,3072]{1,0:T(8,128)(2,1)S(1)}, u32[]{:S(2)}, u32[]{:S(2)}) collective-permute-start(bf16[256,3072]{1,0:T(8,128)(2,1)} %copy-done.4), channel_id=1, source_target_pairs={{0,2},{1,3},{2,0},{3,1},{4,6},{5,7},{6,4},{7,5},{8,10},{9,11},{10,... | collective-permute-start | bytes 4718600 | tf_op jit(solution)/shard_map/ppermute | solution.py:370
  215.9 69.5 %collective-permute-start.39 = (bf16[2,64,6144]{2,1,0:T(8,128)(2,1)S(1)}, bf16[2,64,6144]{2,1,0:T(8,128)(2,1)S(1)}, u32[]{:S(2)}, u32[]{:S(2)}) collective-permute-start(bf16[2,64,6144]{2,1,0:T(8,128)(2,1)S(1)} %bitcast.36), channel_id=1, source_target_pairs={{0,1},{1,0},{2,3},{3,2},{4,5},{5,4},{6,7},{7,6},{8,9},{9,8},{10,11... | collective-permute-start | bytes 4718600 | tf_op jit(solution)/shard_map/ppermute | solution.py:370
  224.3 33.9 %collective-permute-start.28 = (f32[2,32,1536]{2,1,0:T(8,128)S(1)}, f32[2,32,1536]{2,1,0:T(8,128)S(1)}, u32[]{:S(2)}, u32[]{:S(2)}) collective-permute-start(f32[2,32,1536]{2,1,0:T(8,128)S(1)} %pad_maximum_fusion.4), channel_id=1, source_target_pairs={{0,8},{4,12},{8,0},{12,4},{1,9},{5,13},{9,1},{13,5},{2,10},{6,14},... | collective-permute-start | bytes 1179656 | tf_op jit(solution)/shard_map/ppermute | solution.py:364
  233.8 27.5 %collective-permute-start.29 = (f32[2,32,1536]{2,1,0:T(8,128)S(1)}, f32[2,32,1536]{2,1,0:T(8,128)S(1)}, u32[]{:S(2)}, u32[]{:S(2)}) collective-permute-start(f32[2,32,1536]{2,1,0:T(8,128)S(1)} %pad_maximum_fusion.5), channel_id=1, source_target_pairs={{0,4},{4,8},{8,12},{12,0},{1,5},{5,9},{9,13},{13,1},{2,6},{6,10},{... | collective-permute-start | bytes 1179656 | tf_op jit(solution)/shard_map/ppermute | solution.py:364
  258.2 22.8 %collective-permute-start.48 = (s32[2,144]{1,0:T(2,128)S(1)}, s32[2,144]{1,0:T(2,128)S(1)}, u32[]{:S(2)}, u32[]{:S(2)}) collective-permute-start(s32[2,144]{1,0:T(2,128)S(1)} %bitcast.55), channel_id=1, source_target_pairs={{0,2},{1,3},{2,0},{3,1},{4,6},{5,7},{6,4},{7,5},{8,10},{9,11},{10,... | collective-permute-start | bytes 3464 | tf_op jit(solution)/shard_map/ppermute | solution.py:370
  261.3 38.0 %collective-permute-start.23 = (f32[128,1536]{1,0:T(8,128)S(1)}, f32[128,1536]{1,0:T(8,128)S(1)}, u32[]{:S(2)}, u32[]{:S(2)}) collective-permute-start(f32[128,1536]{1,0:T(8,128)S(1)} %get-tuple-element.88), channel_id=1, source_target_pairs={{0,16},{16,0},{1,17},{17,1},{2,18},{18,2},{3,19},{19,3},{4,20},{20... | collective-permute-start | bytes 2359304 | tf_op jit(solution)/shard_map/ppermute | solution.py:367
  285.3 97.3 %collective-permute-start.52 = (f32[18,128,128]{2,1,0:T(8,128)S(1)}, f32[18,128,128]{2,1,0:T(8,128)S(1)}, u32[]{:S(2)}, u32[]{:S(2)}) collective-permute-start(f32[18,128,128]{2,1,0:T(8,128)S(1)} %get-tuple-element.112), channel_id=1, source_target_pairs={{0,1},{1,0},{2,3},{3,2},{4,5},{5,4},{6,7},{7,6},{8,9},{9,8},{10,11... | collective-permute-start | bytes 3538952 | tf_op jit(solution)/shard_map/ppermute | solution.py:370
  296.1 28.8 %collective-permute-start.44 = (f32[128,1536]{1,0:T(8,128)S(1)}, f32[128,1536]{1,0:T(8,128)S(1)}, u32[]{:S(2)}, u32[]{:S(2)}) collective-permute-start(f32[128,1536]{1,0:T(8,128)S(1)} %get-tuple-element.106), channel_id=1, source_target_pairs={{0,16},{16,0},{1,17},{17,1},{2,18},{18,2},{3,19},{19,3},{4,20},{20... | collective-permute-start | bytes 2359304 | tf_op jit(solution)/shard_map/ppermute | solution.py:367
  299.5 28.9 %collective-permute-start.24 = (f32[32,1536]{1,0:T(8,128)S(1)}, f32[32,1536]{1,0:T(8,128)S(1)}, u32[]{:S(2)}, u32[]{:S(2)}) collective-permute-start(f32[32,1536]{1,0:T(8,128)S(1)} %get-tuple-element.135), channel_id=1, source_target_pairs={{0,12},{4,0},{8,4},{12,8},{1,13},{5,1},{9,5},{13,9},{2,14},{6,2},{... | collective-permute-start | bytes 589832 | tf_op jit(solution)/shard_map/ppermute | solution.py:364
  301.9 26.6 %collective-permute-start.26 = (f32[32,1536]{1,0:T(8,128)S(1)}, f32[32,1536]{1,0:T(8,128)S(1)}, u32[]{:S(2)}, u32[]{:S(2)}) collective-permute-start(f32[32,1536]{1,0:T(8,128)S(1)} %get-tuple-element.136), channel_id=1, source_target_pairs={{0,4},{4,8},{8,12},{12,0},{1,5},{5,9},{9,13},{13,1},{2,6},{6,10},{... | collective-permute-start | bytes 589832 | tf_op jit(solution)/shard_map/ppermute | solution.py:364
  310.8 21.6 %collective-permute-start.25 = (f32[32,1536]{1,0:T(8,128)S(1)}, f32[32,1536]{1,0:T(8,128)S(1)}, u32[]{:S(2)}, u32[]{:S(2)}) collective-permute-start(f32[32,1536]{1,0:T(8,128)S(1)} %get-tuple-element.137), channel_id=1, source_target_pairs={{0,8},{4,12},{8,0},{12,4},{1,9},{5,13},{9,1},{13,5},{2,10},{6,14},... | collective-permute-start | bytes 589832 | tf_op jit(solution)/shard_map/ppermute | solution.py:364
  333.3 37.5 %collective-permute-start.54 = (f32[18,128,128]{2,1,0:T(8,128)S(1)}, f32[18,128,128]{2,1,0:T(8,128)S(1)}, u32[]{:S(2)}, u32[]{:S(2)}) collective-permute-start(f32[18,128,128]{2,1,0:T(8,128)S(1)} %get-tuple-element.116), channel_id=1, source_target_pairs={{0,1},{1,0},{2,3},{3,2},{4,5},{5,4},{6,7},{7,6},{8,9},{9,8},{10,11... | collective-permute-start | bytes 3538952 | tf_op jit(solution)/shard_map/ppermute | solution.py:370
  341.0 35.7 %collective-permute-start.53 = (f32[18,128,128]{2,1,0:T(8,128)S(1)}, f32[18,128,128]{2,1,0:T(8,128)S(1)}, u32[]{:S(2)}, u32[]{:S(2)}) collective-permute-start(f32[18,128,128]{2,1,0:T(8,128)S(1)} %get-tuple-element.114), channel_id=1, source_target_pairs={{0,1},{1,0},{2,3},{3,2},{4,5},{5,4},{6,7},{7,6},{8,9},{9,8},{10,11... | collective-permute-start | bytes 3538952 | tf_op jit(solution)/shard_map/ppermute | solution.py:370
  347.8 40.8 %collective-permute-start.50 = (f32[18,128,128]{2,1,0:T(8,128)S(1)}, f32[18,128,128]{2,1,0:T(8,128)S(1)}, u32[]{:S(2)}, u32[]{:S(2)}) collective-permute-start(f32[18,128,128]{2,1,0:T(8,128)S(1)} %get-tuple-element.109), channel_id=1, source_target_pairs={{0,1},{1,0},{2,3},{3,2},{4,5},{5,4},{6,7},{7,6},{8,9},{9,8},{10,11... | collective-permute-start | bytes 3538952 | tf_op jit(solution)/shard_map/ppermute | solution.py:370
  (34 other events, 454.4 us)
